TPU v7x, 32 devices: a whole 2x2x4 slice. The times are simulated.
32 devices in a mesh: seq: 8 (over z, y), dp: 4 (over x, core).
Axes of the slice: x: 2, y: 2, z: 4, core: 2. Of those that a mesh axis runs over, the one named last changes fastest.
Arguments:
- blocks: bfloat16 [4, 2048, 768], P('dp', 'seq'), may hold values from -6 to 6
- lengths: int32 [4, 4], P('dp'), may hold values from 1 to 1024, 1920 in all within a row
- bucket_table: int32 [2047], replicated, may hold values from 0 to 31, as said below
- first_gain: float32 [768], P(('seq', 'dp')), may hold values from 0.5 to 1.5
- query_weight: float32 [768, 768], P(('seq', 'dp')), may hold values from -0.109375 to 0.109375
- key_weight: float32 [768, 768], P(('seq', 'dp')), may hold values from -0.109375 to 0.109375
- value_weight: float32 [768, 768], P(('seq', 'dp')), may hold values from -0.21875 to 0.21875
- output_weight: float32 [768, 768], P(('seq', 'dp')), may hold values from -0.625 to 0.625
- table_weight: float32 [32, 12], replicated, may hold values from -4 to 4
- second_gain: float32 [768], P(('seq', 'dp')), may hold values from 0.5 to 1.5
- gate_weight: float32 [768, 2048], P(('seq', 'dp')), may hold values from -0.21875 to 0.21875
- up_weight: float32 [768, 2048], P(('seq', 'dp')), may hold values from -0.21875 to 0.21875
- down_weight: float32 [2048, 768], P(('seq', 'dp')), may hold values from -0.25 to 0.25
- cotangent: bfloat16 [4, 2048, 768], P('dp', 'seq'), may hold values from -6 to 6
Outputs:
- output: bfloat16 [4, 2048, 768], P('dp', 'seq')
- grad_blocks: float32 [4, 2048, 768], P('dp', 'seq')
- grad_first_gain: float32 [768], P(('seq', 'dp'))
- grad_query_weight: float32 [768, 768], P(('seq', 'dp'))
- grad_key_weight: float32 [768, 768], P(('seq', 'dp'))
- grad_value_weight: float32 [768, 768], P(('seq', 'dp'))
- grad_output_weight: float32 [768, 768], P(('seq', 'dp'))
- grad_table_weight: float32 [32, 12], replicated
- grad_second_gain: float32 [768], P(('seq', 'dp'))
- grad_gate_weight: float32 [768, 2048], P(('seq', 'dp'))
- grad_up_weight: float32 [768, 2048], P(('seq', 'dp'))
- grad_down_weight: float32 [2048, 768], P(('seq', 'dp'))
Inputs may be any that keep to these rules, and one draw needn't show every extreme that they name: Each row of lengths sums to 1920, and its largest entry is 1024. bucket_table[1023 + r] is 0 for r = 0, between 1 and 15 for r < 0 and between 17 and 31 for r > 0, never falling as |r| grows on either side; it is 31 at r = 1023.
All inputs are finite; a program needn't handle non-finite values.
Results may differ from a plain program's by a relative error of at most 0.025.
Values may be sent and summed in bfloat16 or wider, within the bound.
No kernel may reach another device: no remote copies, remote signals or barrier semaphores. Data moves between devices by JAX's collectives and lax.ppermute only.
A program may use at most 128 MiB of HBM per device.

v0:
```python
import jax
import jax.numpy as jnp
from jax import lax
from jax.sharding import PartitionSpec as P

EPSILON = 1e-06
MASKED = -1e30
HIGHEST = lax.Precision.HIGHEST


def shifted(value, axis, steps):
    count = lax.axis_size(axis)
    pairs = [(source, (source + steps) % count) for source in range(count)]
    return lax.ppermute(value, axis, pairs)


def rms_scale(values, scaling):
    return values * lax.rsqrt(jnp.mean(values * values, axis=-1, keepdims=True) + EPSILON) * scaling


def segment_of(seq_ends, places):
    return jnp.sum(
        (places[:, None] >= seq_ends[None, :]).astype(jnp.int32), axis=1, dtype=jnp.int32
    )


def contract_rows(left_side, right_side):
    return lax.dot_general(
        left_side, right_side, (((0,), (0,)), ((), ())), preferred_element_type=jnp.float32
    )


def times_transposed(left_side, right_side):
    return lax.dot_general(
        left_side, right_side, (((1,), (1,)), ((), ())), preferred_element_type=jnp.float32
    )


def bias_block(table_weight, one_hot, query_first, key_first, row_count, pack_rows):
    head_count = table_weight.shape[1]
    half_span = (one_hot.shape[0] + 1) // 2
    bias_line = jnp.dot(one_hot, table_weight, precision=HIGHEST).T
    extended = jnp.concatenate(
        [
            jnp.broadcast_to(bias_line[:, :1], (head_count, pack_rows - half_span)),
            bias_line,
            jnp.broadcast_to(bias_line[:, -1:], (head_count, pack_rows - half_span + 1)),
        ],
        axis=1,
    )
    offset = key_first - query_first + pack_rows - row_count
    window = lax.dynamic_slice_in_dim(extended, offset, 2 * row_count, 1)
    circle = jnp.concatenate([window[:, row_count - 1 :], window[:, : row_count - 1]], axis=1)
    period = 2 * row_count
    tiled_rows = jnp.broadcast_to(circle[:, None, :], (head_count, row_count, period)).reshape(
        head_count, row_count * period
    )
    return tiled_rows[:, : row_count * (period - 1)].reshape(head_count, row_count, period - 1)[
        :, :, :row_count
    ]


def body(
    blocks,
    lengths,
    bucket_table,
    first_gain,
    query_weight,
    key_weight,
    value_weight,
    output_weight,
    table_weight,
    second_gain,
    gate_weight,
    up_weight,
    down_weight,
    cotangent,
):
    seq_count = lax.axis_size("seq")
    seq_rank = lax.axis_index("seq")
    row_count = blocks.shape[1]
    model_width = blocks.shape[2]
    pack_rows = row_count * seq_count
    head_count = table_weight.shape[1]
    head_dim = model_width // head_count
    seq_total = lengths.shape[1]
    seq_ends = jnp.cumsum(lengths[0], dtype=jnp.int32)
    query_first = seq_rank * row_count
    row_places = jnp.arange(row_count, dtype=jnp.int32)
    query_seg = segment_of(seq_ends, query_first + row_places)
    valid_rows = (query_seg < seq_total).astype(jnp.float32)
    one_hot = (
        bucket_table[:, None] == jnp.arange(table_weight.shape[0], dtype=jnp.int32)[None, :]
    ).astype(jnp.float32)
    attn_full = (
        lax.all_gather(first_gain.astype(jnp.bfloat16), ("seq", "dp"), axis=0, tiled=True),
        lax.all_gather(query_weight.astype(jnp.bfloat16), ("seq", "dp"), axis=0, tiled=True),
        lax.all_gather(key_weight.astype(jnp.bfloat16), ("seq", "dp"), axis=0, tiled=True),
        lax.all_gather(value_weight.astype(jnp.bfloat16), ("seq", "dp"), axis=0, tiled=True),
        lax.all_gather(output_weight.astype(jnp.bfloat16), ("seq", "dp"), axis=0, tiled=True),
    )
    gain_one = attn_full[0].astype(jnp.float32)
    weight_query, weight_key, weight_value, weight_output = (
        attn_full[1],
        attn_full[2],
        attn_full[3],
        attn_full[4],
    )
    tokens = blocks[0].astype(jnp.float32)
    normed, norm_pull = jax.vjp(rms_scale, tokens, gain_one)
    normed_low = normed.astype(jnp.bfloat16)
    queries = jnp.dot(normed_low, weight_query, preferred_element_type=jnp.float32).astype(
        jnp.bfloat16
    )
    key_rows = jnp.dot(normed_low, weight_key, preferred_element_type=jnp.float32).astype(
        jnp.bfloat16
    )
    values = jnp.dot(normed_low, weight_value, preferred_element_type=jnp.float32).astype(
        jnp.bfloat16
    )
    query_heads = queries.reshape(row_count, head_count, head_dim)

    def score_block(key_block, key_first, bias_values):
        key_heads = key_block.reshape(row_count, head_count, head_dim)
        scores = (
            jnp.einsum("qhd,khd->hqk", query_heads, key_heads, preferred_element_type=jnp.float32)
            + bias_values
        )
        key_seg = segment_of(seq_ends, key_first + row_places)
        same_seq = query_seg[:, None] == key_seg[None, :]
        return jnp.where(same_seq[None], scores, MASKED)

    start_state = (
        jnp.full((head_count, row_count), MASKED, jnp.float32),
        jnp.zeros((head_count, row_count), jnp.float32),
        jnp.zeros((head_count, row_count, head_dim), jnp.float32),
    )
    fold_state = start_state
    key_piece = (
        lax.all_gather(key_rows, "seq", axis=0, tiled=True),
        lax.all_gather(values, "seq", axis=0, tiled=True),
    )
    shard_count = key_piece[0].shape[0] // row_count
    key_stack = key_piece[0].reshape(shard_count, row_count, model_width)
    value_stack = key_piece[1].reshape(shard_count, row_count, model_width)
    block_firsts = row_count * jnp.arange(shard_count, dtype=jnp.int32)

    def fold_step(carry_state, block_item):
        running_max, running_sum, accumulated = carry_state
        key_block, value_block, key_first = block_item
        bias_values = bias_block(
            table_weight, one_hot, query_first, key_first, row_count, pack_rows
        )
        scores = score_block(key_block, key_first, bias_values)
        new_max = jnp.maximum(running_max, jnp.max(scores, axis=-1))
        factor = jnp.exp(running_max - new_max)
        weights = jnp.exp(scores - new_max[..., None])
        running_sum = running_sum * factor + jnp.sum(weights, axis=-1)
        value_heads = value_block.reshape(row_count, head_count, head_dim)
        accumulated = accumulated * factor[..., None] + jnp.einsum(
            "hqk,khd->hqd",
            weights.astype(jnp.bfloat16),
            value_heads,
            preferred_element_type=jnp.float32,
        )
        return ((new_max, running_sum, accumulated), None)

    fold_state, ignored = lax.scan(fold_step, fold_state, (key_stack, value_stack, block_firsts))
    running_max, running_sum, accumulated = fold_state
    log_sum = running_max + jnp.log(running_sum)
    attended_heads = accumulated / running_sum[..., None]
    attended = (
        jnp.transpose(attended_heads, (1, 0, 2)).reshape(row_count, model_width)
        * valid_rows[:, None]
    )
    mixed_low = attended.astype(jnp.bfloat16)
    middle = tokens + jnp.dot(mixed_low, weight_output, preferred_element_type=jnp.float32)
    ffn_full = (
        lax.all_gather(second_gain.astype(jnp.bfloat16), ("seq", "dp"), axis=0, tiled=True),
        lax.all_gather(gate_weight.astype(jnp.bfloat16), ("seq", "dp"), axis=0, tiled=True),
        lax.all_gather(up_weight.astype(jnp.bfloat16), ("seq", "dp"), axis=0, tiled=True),
        lax.all_gather(down_weight.astype(jnp.bfloat16), ("seq", "dp"), axis=0, tiled=True),
    )
    gain_two = ffn_full[0].astype(jnp.float32)
    weight_gate, weight_up, weight_down = (ffn_full[1], ffn_full[2], ffn_full[3])
    normed_two, norm_pull_two = jax.vjp(rms_scale, middle, gain_two)
    second_low = normed_two.astype(jnp.bfloat16)
    gate_values = jnp.dot(second_low, weight_gate, preferred_element_type=jnp.float32)
    upward = jnp.dot(second_low, weight_up, preferred_element_type=jnp.float32)
    activated, gelu_pull = jax.vjp(
        lambda gate_in: jax.nn.gelu(gate_in, approximate=True), gate_values
    )
    hidden = (activated * upward).astype(jnp.bfloat16)
    output = middle + jnp.dot(hidden, weight_down, preferred_element_type=jnp.float32)
    grad_out = cotangent[0]
    grad_down = contract_rows(hidden, grad_out)
    grad_hidden = times_transposed(grad_out, weight_down)
    grad_gate = gelu_pull(grad_hidden * upward)[0].astype(jnp.bfloat16)
    grad_upward = (grad_hidden * activated).astype(jnp.bfloat16)
    grad_gate_weight = contract_rows(second_low, grad_gate)
    grad_up_weight = contract_rows(second_low, grad_upward)
    grad_second = times_transposed(grad_gate, weight_gate) + times_transposed(
        grad_upward, weight_up
    )
    grad_middle_norm, grad_gain_two = norm_pull_two(grad_second)
    grad_middle = grad_out.astype(jnp.float32) + grad_middle_norm
    grad_branch = grad_middle.astype(jnp.bfloat16)
    grad_output_weight = contract_rows(mixed_low, grad_branch)
    grad_mixed = times_transposed(grad_branch, weight_output).astype(jnp.bfloat16)
    grad_heads = (
        (grad_mixed.astype(jnp.float32) * valid_rows[:, None])
        .astype(jnp.bfloat16)
        .reshape(row_count, head_count, head_dim)
    )
    row_delta = jnp.sum(
        jnp.transpose(grad_heads.astype(jnp.float32), (1, 0, 2)) * attended_heads, axis=-1
    )

    def block_grads(key_block, value_block, key_first):
        key_heads = key_block.reshape(row_count, head_count, head_dim)
        value_heads = value_block.reshape(row_count, head_count, head_dim)
        bias_values, bias_pull = jax.vjp(
            lambda table_in: bias_block(
                table_in, one_hot, query_first, key_first, row_count, pack_rows
            ),
            table_weight,
        )
        scores = score_block(key_block, key_first, bias_values)
        probabilities = jnp.exp(scores - log_sum[..., None])
        grad_value = jnp.einsum(
            "hqk,qhd->khd",
            probabilities.astype(jnp.bfloat16),
            grad_heads,
            preferred_element_type=jnp.float32,
        )
        grad_probs = jnp.einsum(
            "qhd,khd->hqk", grad_heads, value_heads, preferred_element_type=jnp.float32
        )
        grad_scores = (probabilities * (grad_probs - row_delta[..., None])).astype(jnp.bfloat16)
        grad_query = jnp.einsum(
            "hqk,khd->qhd", grad_scores, key_heads, preferred_element_type=jnp.float32
        )
        grad_key = jnp.einsum(
            "hqk,qhd->khd", grad_scores, query_heads, preferred_element_type=jnp.float32
        )
        grad_table = bias_pull(grad_scores.astype(jnp.float32))[0]
        return (
            grad_query,
            grad_key.reshape(row_count, model_width),
            grad_value.reshape(row_count, model_width),
            grad_table,
        )

    zero_query = jnp.zeros((row_count, head_count, head_dim), jnp.float32)
    zero_table = jnp.zeros(table_weight.shape, jnp.float32)

    def cycle_step(counter, carry_state):
        key_block, value_block, grad_keys, grad_values, grad_query, grad_table = carry_state
        key_first = (seq_rank - counter) % seq_count * row_count
        part_query, part_key, part_value, part_table = block_grads(
            key_block, value_block, key_first
        )
        key_block, value_block = shifted((key_block, value_block), "seq", 1)
        grad_keys, grad_values = (
            shifted((grad_keys + part_key).astype(jnp.bfloat16), "seq", 1).astype(jnp.float32),
            shifted((grad_values + part_value).astype(jnp.bfloat16), "seq", 1).astype(jnp.float32),
        )
        return (
            key_block,
            value_block,
            grad_keys,
            grad_values,
            grad_query + part_query,
            grad_table + part_table,
        )

    zero_rows = jnp.zeros((row_count, model_width), jnp.float32)
    final_state = lax.fori_loop(
        0, seq_count, cycle_step, (key_rows, values, zero_rows, zero_rows, zero_query, zero_table)
    )
    grad_keys, grad_values, grad_query, grad_table = (
        final_state[2],
        final_state[3],
        final_state[4],
        final_state[5],
    )
    grad_queries_low = grad_query.reshape(row_count, model_width).astype(jnp.bfloat16)
    grad_keys_low = grad_keys.astype(jnp.bfloat16)
    grad_values_low = grad_values.astype(jnp.bfloat16)
    grad_query_weight = contract_rows(normed_low, grad_queries_low)
    grad_key_weight = contract_rows(normed_low, grad_keys_low)
    grad_value_weight = contract_rows(normed_low, grad_values_low)
    grad_normed = (
        times_transposed(grad_queries_low, weight_query)
        + times_transposed(grad_keys_low, weight_key)
        + times_transposed(grad_values_low, weight_value)
    )
    grad_tokens_norm, grad_gain_one = norm_pull(grad_normed)
    grad_blocks = (grad_middle + grad_tokens_norm)[None]
    attn_sums = (
        lax.psum_scatter(grad_gain_one, ("seq", "dp"), scatter_dimension=0, tiled=True),
        lax.psum_scatter(grad_query_weight, ("seq", "dp"), scatter_dimension=0, tiled=True),
        lax.psum_scatter(grad_key_weight, ("seq", "dp"), scatter_dimension=0, tiled=True),
        lax.psum_scatter(grad_value_weight, ("seq", "dp"), scatter_dimension=0, tiled=True),
        lax.psum_scatter(grad_output_weight, ("seq", "dp"), scatter_dimension=0, tiled=True),
    )
    ffn_sums = (
        lax.psum_scatter(grad_gain_two, ("seq", "dp"), scatter_dimension=0, tiled=True),
        lax.psum_scatter(grad_gate_weight, ("seq", "dp"), scatter_dimension=0, tiled=True),
        lax.psum_scatter(grad_up_weight, ("seq", "dp"), scatter_dimension=0, tiled=True),
        lax.psum_scatter(grad_down, ("seq", "dp"), scatter_dimension=0, tiled=True),
    )
    table_sum = lax.psum(grad_table, ("seq", "dp"))
    return (
        output.astype(jnp.bfloat16)[None],
        grad_blocks,
        attn_sums[0],
        attn_sums[1],
        attn_sums[2],
        attn_sums[3],
        attn_sums[4],
        table_sum,
        ffn_sums[0],
        ffn_sums[1],
        ffn_sums[2],
        ffn_sums[3],
    )


def solution(mesh):
    return jax.shard_map(
        body,
        mesh=mesh,
        in_specs=(
            P("dp", "seq", None),
            P("dp", None),
            P(),
            P(("seq", "dp")),
            P(("seq", "dp"), None),
            P(("seq", "dp"), None),
            P(("seq", "dp"), None),
            P(("seq", "dp"), None),
            P(),
            P(("seq", "dp")),
            P(("seq", "dp"), None),
            P(("seq", "dp"), None),
            P(("seq", "dp"), None),
            P("dp", "seq", None),
        ),
        out_specs=(
            P("dp", "seq", None),
            P("dp", "seq", None),
            P(("seq", "dp")),
            P(("seq", "dp"), None),
            P(("seq", "dp"), None),
            P(("seq", "dp"), None),
            P(("seq", "dp"), None),
            P(),
            P(("seq", "dp")),
            P(("seq", "dp"), None),
            P(("seq", "dp"), None),
            P(("seq", "dp"), None),
        ),
        check_vma=False,
    )
```

profile of v0, /device:TPU:0, one launch (start us, length us, event | category | flops | bytes accessed | tf_op | source)
XLA Modules:
  0.0 2011.9 jit_solution(13417099302365523115)
XLA Ops:
  13.8 42.1 %all-reduce.11 = (bf16[768]{0:T(1024)(128)(2,1)S(1)}, bf16[768]{0:T(1024)(128)(2,1)S(1)}) all-reduce(bf16[768]{0:T(1024)(128)(2,1)S(1)} %dynamic-update-slice, bf16[768]{0:T(1024)(128)(2,1)S(1)} %dynamic-update-slice.1), channel_id=1, replica_groups=mesh['seq'=8,'dp'=4] {'seq','dp'}, use_global_device_ids=true, to_apply=%add.6 | all-reduce | flops 1536 | bytes 6144
  57.6 10.7 all-gather.10.cloned.1.call-done
  71.1 53.7 %all-gather.16.cloned.1.call-done = bf16[768,768]{1,0:T(8,128)(2,1)} async-done(((bf16[24,768]{1,0:T(8,128)(2,1)}), bf16[768,768]{1,0:T(8,128)(2,1)}) %all-gather.16.cloned.1.call-update) | async-done | bytes 1179664 | tf_op jit(solution)/shard_map/all_gather | solution.py:99
  136.9 44.5 %all-gather.14.cloned.1.call-done = bf16[768,768]{1,0:T(8,128)(2,1)} async-done(((bf16[24,768]{1,0:T(8,128)(2,1)}), bf16[768,768]{1,0:T(8,128)(2,1)}) %all-gather.14.cloned.1.call-update) | async-done | bytes 1179664 | tf_op jit(solution)/shard_map/all_gather | solution.py:97
  183.3 60.0 %all-gather.12.cloned.1.call-done = bf16[2048,768]{1,0:T(8,128)(2,1)} async-done(((bf16[256,768]{1,0:T(8,128)(2,1)}), bf16[2048,768]{1,0:T(8,128)(2,1)}) %all-gather.12.cloned.1.call-update) | async-done | bytes 3145744 | tf_op jit(solution)/shard_map/all_gather | solution.py:140
  243.4 61.1 %all-gather.18.cloned.1.call-done = bf16[2048,768]{1,0:T(8,128)(2,1)} async-done(((bf16[256,768]{1,0:T(8,128)(2,1)}), bf16[2048,768]{1,0:T(8,128)(2,1)}) %all-gather.18.cloned.1.call-update) | async-done | bytes 3145744 | tf_op jit(solution)/shard_map/all_gather | solution.py:141
  304.5 347.6 %while.47 = (s32[]{:T(128)}, f32[12,256]{1,0:T(8,128)}, f32[12,256]{1,0:T(8,128)}, f32[12,256,64]{1,2,0:T(8,128)}, s32[256]{0:T(256)S(1)}, /*index=5*/s32[8]{0:T...) while((s32[]{:T(128)}, f32[12,256]{1,0:T(8,128)}, ...), condition=%wide.region_7.8_spmd.clone, body=%wide.region_3.7_spmd.clone.sunk | while | flops 207511552 | bytes 98072240 | solution.py:168
  310.7 4.9 copy.97
  319.4 9.0 reshape.388
  353.2 4.9 copy.97
  361.9 9.0 reshape.388
  396.7 4.9 copy.97
  405.4 9.0 reshape.388
  440.3 4.9 copy.97
  448.9 9.0 reshape.388
  483.7 4.9 copy.97
  492.4 9.1 reshape.388
  527.3 4.9 copy.97
  535.9 9.0 reshape.388
  570.8 4.9 copy.97
  579.4 9.0 reshape.388
  622.9 9.0 reshape.388
  664.9 6.6 multiply_convert_fusion.1
  678.8 549.5 %while.48 = (s32[]{:T(128)}, bf16[256,768]{0,1:T(8,128)(2,1)}, bf16[256,768]{0,1:T(8,128)(2,1)}, f32[256,768]{0,1:T(8,128)}, f32[256,768]{0,1:T(8,128)}, /*index...) while((s32[]{:T(128)}, bf16[256,768]{0,1:T(8,128)(2,1)}, ...), condition=%wide.region_16.17_spmd.clone, body=%wide.region_11.16_spmd.clone.sunk | while | flops 523646112 | bytes 158935280 | solution.py:278
  688.8 4.9 copy.101
  697.5 9.0 reshape.390
  719.9 9.1 reshape.391
  731.7 4.9 copy.102
  757.6 4.9 copy.101
  766.2 9.0 reshape.390
  788.0 9.1 reshape.391
  799.8 4.9 copy.102
  834.7 9.0 reshape.390
  857.2 9.1 reshape.391
  869.0 4.9 copy.102
  894.9 4.9 copy.101
  903.5 9.0 reshape.390
  925.3 9.1 reshape.391
  937.1 4.9 copy.102
  972.0 9.0 reshape.390
  994.4 9.1 reshape.391
  1006.3 4.9 copy.102
  1032.1 4.9 copy.101
  1040.8 9.0 reshape.390
  1062.6 9.1 reshape.391
  1074.4 4.9 copy.102
  1100.7 4.9 copy.101
  1109.3 9.0 reshape.390
  1131.7 9.1 reshape.391
  1143.6 4.9 copy.102
  1178.1 9.0 reshape.390
  1199.9 9.1 reshape.391
  1211.7 4.9 copy.102
  1240.3 4.9 fusion.92
  1245.3 4.9 fusion.93
  1251.2 4.9 fusion.64
  1260.8 40.4 %all-reduce.10 = (f32[768]{0:T(1024)S(1)}, f32[32,12]{0,1:T(8,128)}, f32[768]{0:T(1024)S(1)}) all-reduce(f32[768]{0:T(1024)S(1)} %get-tuple-element.1093, f32[32,12]{0,1:T(8,128)S(1)} %copy-done.50, f32[768]{0:T(1024)S(1)} %copy-done.47), channel_id=2, replica_groups=mesh['seq'=8,'dp'=4] {'seq','dp'}, use_global_device_ids=true, to_apply=%region_19.20.clone | all-reduce | flops 1920 | bytes 15360
  1308.7 23.0 %reduce-scatter.8.cloned.1.call-done = f32[24,768]{1,0:T(8,128)} async-done(((f32[768,768]{1,0:T(8,128)}), f32[24,768]{1,0:T(8,128)}) %reduce-scatter.8.cloned.1.call-update) | async-done | bytes 73744 | tf_op jit(solution)/shard_map/reduce_scatter | solution.py:302
  1331.6 104.8 %reduce-scatter.10.cloned.1.call-done = f32[24,768]{1,0:T(8,128)} async-done(((f32[768,768]{1,0:T(8,128)}), f32[24,768]{1,0:T(8,128)}) %reduce-scatter.10.cloned.1.call-update) | async-done | bytes 73744 | tf_op jit(solution)/shard_map/reduce_scatter | solution.py:303
  1436.4 103.8 %reduce-scatter.12.cloned.1.call-done = f32[24,768]{1,0:T(8,128)} async-done(((f32[768,768]{1,0:T(8,128)}), f32[24,768]{1,0:T(8,128)}) %reduce-scatter.12.cloned.1.call-update) | async-done | bytes 73744 | tf_op jit(solution)/shard_map/reduce_scatter | solution.py:304
  1540.2 104.7 %reduce-scatter.14.cloned.1.call-done = f32[24,768]{1,0:T(8,128)} async-done(((f32[768,768]{1,0:T(8,128)}), f32[24,768]{1,0:T(8,128)}) %reduce-scatter.14.cloned.1.call-update) | async-done | bytes 73744 | tf_op jit(solution)/shard_map/reduce_scatter | solution.py:305
  1644.9 119.7 %reduce-scatter.16.cloned.1.call-done = f32[24,2048]{1,0:T(8,128)} async-done(((f32[768,2048]{1,0:T(8,128)}), f32[24,2048]{1,0:T(8,128)}) %reduce-scatter.16.cloned.1.call-update) | async-done | bytes 196624 | tf_op jit(solution)/shard_map/reduce_scatter | solution.py:309
  1764.6 120.8 %reduce-scatter.18.cloned.1.call-done = f32[24,2048]{1,0:T(8,128)} async-done(((f32[768,2048]{1,0:T(8,128)}), f32[24,2048]{1,0:T(8,128)}) %reduce-scatter.18.cloned.1.call-update) | async-done | bytes 196624 | tf_op jit(solution)/shard_map/reduce_scatter | solution.py:310
  1885.4 119.6 %reduce-scatter.20.cloned.1.call-done = f32[64,768]{1,0:T(8,128)} async-done(((f32[2048,768]{1,0:T(8,128)}), f32[64,768]{1,0:T(8,128)}) %reduce-scatter.20.cloned.1.call-update) | async-done | bytes 196624 | tf_op jit(solution)/shard_map/reduce_scatter | solution.py:311
  (854 shorter events, 644.2 us)
Async XLA Ops:
  7.2 126.4 %copy-start = (f32[32,12]{0,1:T(8,128)S(1)}, f32[32,12]{0,1:T(8,128)}, u32[]{:S(2)}) copy-start(f32[32,12]{0,1:T(8,128)} %param.26) | copy-start | bytes 4612
  7.2 117.6 %copy-start.9 = (bf16[1,256,768]{2,1,0:T(8,128)(2,1)S(1)}, bf16[1,256,768]{2,1,0:T(8,128)(2,1)}, u32[]{:S(2)}) copy-start(bf16[1,256,768]{2,1,0:T(8,128)(2,1)} %param.18) | copy-start | bytes 1179652
  7.2 61.1 %all-gather.10.cloned.1.call-start = ((), (), s32[]{:S(2)}) async-start(), calls=%async_computation.7 | async-start | bytes 1216512 | tf_op jit(solution)/shard_map/all_gather | solution.py:98
  8.8 116.0 %all-gather.16.cloned.1.call-start = ((), (), s32[]{:S(2)}) async-start(), calls=%async_computation.10 | async-start | bytes 1216512 | tf_op jit(solution)/shard_map/all_gather | solution.py:99
  10.4 170.9 %all-gather.14.cloned.1.call-start = ((), (), s32[]{:S(2)}) async-start(), calls=%async_computation.9 | async-start | bytes 1216512 | tf_op jit(solution)/shard_map/all_gather | solution.py:97
  12.0 231.4 %all-gather.12.cloned.1.call-start = ((), (), s32[]{:S(2)}) async-start(), calls=%async_computation.8 | async-start | bytes 3538944 | tf_op jit(solution)/shard_map/all_gather | solution.py:140
  55.8 125.5 %copy-start.39 = (f32[768]{0:T(1024)}, f32[768]{0:T(1024)S(1)}, u32[]{:S(2)}) copy-start(f32[768]{0:T(1024)S(1)} %convert_element_type.243) | copy-start | bytes 9220
  57.6 123.8 %copy-start.43 = (f32[256]{0:T(256)}, f32[256]{0:T(256)S(1)}, u32[]{:S(2)}) copy-start(f32[256]{0:T(256)S(1)} %fusion.79) | copy-start | bytes 3076
  57.6 69.9 %copy-start.41 = (f32[24,768]{1,0:T(8,128)S(1)}, f32[24,768]{1,0:T(8,128)}, u32[]{:S(2)}) copy-start(f32[24,768]{1,0:T(8,128)} %param.25) | copy-start | bytes 221188
  57.6 70.6 %copy-start.36 = (f32[24,2048]{1,0:T(8,128)S(1)}, f32[24,2048]{1,0:T(8,128)}, u32[]{:S(2)}) copy-start(f32[24,2048]{1,0:T(8,128)} %param.28) | copy-start | bytes 589828
  57.6 71.3 %copy-start.37 = (f32[24,2048]{1,0:T(8,128)S(1)}, f32[24,2048]{1,0:T(8,128)}, u32[]{:S(2)}) copy-start(f32[24,2048]{1,0:T(8,128)} %param.29) | copy-start | bytes 589828
  71.0 58.7 %copy-start.38 = (f32[64,768]{1,0:T(8,128)S(1)}, f32[64,768]{1,0:T(8,128)}, u32[]{:S(2)}) copy-start(f32[64,768]{1,0:T(8,128)} %param.30) | copy-start | bytes 589828
  71.0 60.0 %copy-start.52 = (s32[1,4]{1,0:T(1,128)S(1)}, s32[1,4]{1,0:T(1,128)}, u32[]{:S(2)}) copy-start(s32[1,4]{1,0:T(1,128)} %param.19) | copy-start | bytes 52
  71.0 62.6 %copy-start.51 = (s32[2047]{0:T(1024)S(1)}, s32[2047]{0:T(1024)}, u32[]{:S(2)}) copy-start(s32[2047]{0:T(1024)} %param.20) | copy-start | bytes 24568
  71.0 64.0 %copy-start.27 = (bf16[256,768]{1,0:T(8,128)(2,1)S(1)}, bf16[256,768]{1,0:T(8,128)(2,1)}, u32[]{:S(2)}) copy-start(bf16[256,768]{1,0:T(8,128)(2,1)} %convolution_convert_fusion.3) | copy-start | bytes 1179652
  71.0 233.5 %all-gather.18.cloned.1.call-start = ((), (), s32[]{:S(2)}) async-start(), calls=%async_computation.11 | async-start | bytes 3538944 | tf_op jit(solution)/shard_map/all_gather | solution.py:141
  127.4 526.3 %all-gather.20.cloned.1.call-start = ((), (), s32[]{:S(2)}) async-start(), calls=%async_computation.12 | async-start | bytes 1216512 | tf_op jit(solution)/shard_map/all_gather | solution.py:100
  128.1 528.0 %all-gather.22.cloned.1.call-start = ((), (), s32[]{:S(2)}) async-start(), calls=%async_computation.13 | async-start | bytes 3244032 | tf_op jit(solution)/shard_map/all_gather | solution.py:180
  128.8 531.7 %all-gather.24.cloned.1.call-start = ((), (), s32[]{:S(2)}) async-start(), calls=%async_computation.14 | async-start | bytes 3244032 | tf_op jit(solution)/shard_map/all_gather | solution.py:181
  129.6 535.3 %all-gather.26.cloned.1.call-start = ((), (), s32[]{:S(2)}) async-start(), calls=%async_computation.15 | async-start | bytes 3244032 | tf_op jit(solution)/shard_map/all_gather | solution.py:182
  130.3 1201.3 %reduce-scatter.8.cloned.1.call-start = ((), (), s32[]{:S(2)}) async-start(), calls=%async_computation.16 | async-start | bytes 2433024 | tf_op jit(solution)/shard_map/reduce_scatter | solution.py:302
  655.9 20.7 %copy-start.15 = (f32[256,768]{1,0:T(8,128)}, f32[256,768]{1,0:T(8,128)S(1)}, u32[]{:S(2)}) copy-start(f32[256,768]{1,0:T(8,128)S(1)} %get-tuple-element.1168) | copy-start | bytes 2359300
  678.8 550.7 %copy-start.40 = (f32[768]{0:T(1024)S(1)}, f32[768]{0:T(1024)}, u32[]{:S(2)}) copy-start(f32[768]{0:T(1024)} %copy-done.39) | copy-start | bytes 9220
  679.9 68.1 %collective-permute-start = (bf16[256,768]{0,1:T(8,128)(2,1)S(1)}, bf16[256,768]{0,1:T(8,128)(2,1)}, u32[]{:S(2)}, u32[]{:S(2)}) collective-permute-start(bf16[256,768]{0,1:T(8,128)(2,1)S(1)} %copy.127), channel_id=1, source_target_pairs={{0,4},{4,8},{8,12},{12,16},{16,20},{20,24},{24,28},{28,0},{1,5},{5... | collective-permute-start | bytes 1179656 | tf_op jit(solution)/shard_map/while/body/eval_jaxpr/ppermute | solution.py:14
  683.2 64.9 %collective-permute-start.1 = (bf16[256,768]{0,1:T(8,128)(2,1)}, bf16[256,768]{0,1:T(8,128)(2,1)}, u32[]{:S(2)}, u32[]{:S(2)}) collective-permute-start(bf16[256,768]{0,1:T(8,128)(2,1)} %copy.128), channel_id=1, source_target_pairs={{0,4},{4,8},{8,12},{12,16},{16,20},{20,24},{24,28},{28,0},{1,5},{5... | collective-permute-start | bytes 1179656 | tf_op jit(solution)/shard_map/while/body/eval_jaxpr/ppermute | solution.py:14
  713.7 30.1 %collective-permute-start.2 = (bf16[256,768]{0,1:T(8,128)(2,1)}, bf16[256,768]{0,1:T(8,128)(2,1)}, u32[]{:S(2)}, u32[]{:S(2)}) collective-permute-start(bf16[256,768]{0,1:T(8,128)(2,1)} %fusion.182), channel_id=1, source_target_pairs={{0,4},{4,8},{8,12},{12,16},{16,20},{20,24},{24,28},{28,0},{1,5},{5... | collective-permute-start | bytes 1179656 | tf_op jit(solution)/shard_map/while/body/eval_jaxpr/ppermute | solution.py:14
  716.4 29.7 %collective-permute-start.3 = (bf16[256,768]{0,1:T(8,128)(2,1)}, bf16[256,768]{0,1:T(8,128)(2,1)}, u32[]{:S(2)}, u32[]{:S(2)}) collective-permute-start(bf16[256,768]{0,1:T(8,128)(2,1)} %fusion.184), channel_id=1, source_target_pairs={{0,4},{4,8},{8,12},{12,16},{16,20},{20,24},{24,28},{28,0},{1,5},{5... | collective-permute-start | bytes 1179656 | tf_op jit(solution)/shard_map/while/body/eval_jaxpr/ppermute | solution.py:14
  749.1 67.1 %collective-permute-start = (bf16[256,768]{0,1:T(8,128)(2,1)S(1)}, bf16[256,768]{0,1:T(8,128)(2,1)}, u32[]{:S(2)}, u32[]{:S(2)}) collective-permute-start(bf16[256,768]{0,1:T(8,128)(2,1)S(1)} %copy.127), channel_id=1, source_target_pairs={{0,4},{4,8},{8,12},{12,16},{16,20},{20,24},{24,28},{28,0},{1,5},{5... | collective-permute-start | bytes 1179656 | tf_op jit(solution)/shard_map/while/body/eval_jaxpr/ppermute | solution.py:14
  751.9 64.2 %collective-permute-start.1 = (bf16[256,768]{0,1:T(8,128)(2,1)}, bf16[256,768]{0,1:T(8,128)(2,1)}, u32[]{:S(2)}, u32[]{:S(2)}) collective-permute-start(bf16[256,768]{0,1:T(8,128)(2,1)} %copy.128), channel_id=1, source_target_pairs={{0,4},{4,8},{8,12},{12,16},{16,20},{20,24},{24,28},{28,0},{1,5},{5... | collective-permute-start | bytes 1179656 | tf_op jit(solution)/shard_map/while/body/eval_jaxpr/ppermute | solution.py:14
  782.5 29.5 %collective-permute-start.2 = (bf16[256,768]{0,1:T(8,128)(2,1)}, bf16[256,768]{0,1:T(8,128)(2,1)}, u32[]{:S(2)}, u32[]{:S(2)}) collective-permute-start(bf16[256,768]{0,1:T(8,128)(2,1)} %fusion.182), channel_id=1, source_target_pairs={{0,4},{4,8},{8,12},{12,16},{16,20},{20,24},{24,28},{28,0},{1,5},{5... | collective-permute-start | bytes 1179656 | tf_op jit(solution)/shard_map/while/body/eval_jaxpr/ppermute | solution.py:14
  784.5 29.7 %collective-permute-start.3 = (bf16[256,768]{0,1:T(8,128)(2,1)}, bf16[256,768]{0,1:T(8,128)(2,1)}, u32[]{:S(2)}, u32[]{:S(2)}) collective-permute-start(bf16[256,768]{0,1:T(8,128)(2,1)} %fusion.184), channel_id=1, source_target_pairs={{0,4},{4,8},{8,12},{12,16},{16,20},{20,24},{24,28},{28,0},{1,5},{5... | collective-permute-start | bytes 1179656 | tf_op jit(solution)/shard_map/while/body/eval_jaxpr/ppermute | solution.py:14
  817.2 68.1 %collective-permute-start = (bf16[256,768]{0,1:T(8,128)(2,1)S(1)}, bf16[256,768]{0,1:T(8,128)(2,1)}, u32[]{:S(2)}, u32[]{:S(2)}) collective-permute-start(bf16[256,768]{0,1:T(8,128)(2,1)S(1)} %copy.127), channel_id=1, source_target_pairs={{0,4},{4,8},{8,12},{12,16},{16,20},{20,24},{24,28},{28,0},{1,5},{5... | collective-permute-start | bytes 1179656 | tf_op jit(solution)/shard_map/while/body/eval_jaxpr/ppermute | solution.py:14
  820.4 64.9 %collective-permute-start.1 = (bf16[256,768]{0,1:T(8,128)(2,1)}, bf16[256,768]{0,1:T(8,128)(2,1)}, u32[]{:S(2)}, u32[]{:S(2)}) collective-permute-start(bf16[256,768]{0,1:T(8,128)(2,1)} %copy.128), channel_id=1, source_target_pairs={{0,4},{4,8},{8,12},{12,16},{16,20},{20,24},{24,28},{28,0},{1,5},{5... | collective-permute-start | bytes 1179656 | tf_op jit(solution)/shard_map/while/body/eval_jaxpr/ppermute | solution.py:14
  851.0 30.2 %collective-permute-start.2 = (bf16[256,768]{0,1:T(8,128)(2,1)}, bf16[256,768]{0,1:T(8,128)(2,1)}, u32[]{:S(2)}, u32[]{:S(2)}) collective-permute-start(bf16[256,768]{0,1:T(8,128)(2,1)} %fusion.182), channel_id=1, source_target_pairs={{0,4},{4,8},{8,12},{12,16},{16,20},{20,24},{24,28},{28,0},{1,5},{5... | collective-permute-start | bytes 1179656 | tf_op jit(solution)/shard_map/while/body/eval_jaxpr/ppermute | solution.py:14
  853.7 29.7 %collective-permute-start.3 = (bf16[256,768]{0,1:T(8,128)(2,1)}, bf16[256,768]{0,1:T(8,128)(2,1)}, u32[]{:S(2)}, u32[]{:S(2)}) collective-permute-start(bf16[256,768]{0,1:T(8,128)(2,1)} %fusion.184), channel_id=1, source_target_pairs={{0,4},{4,8},{8,12},{12,16},{16,20},{20,24},{24,28},{28,0},{1,5},{5... | collective-permute-start | bytes 1179656 | tf_op jit(solution)/shard_map/while/body/eval_jaxpr/ppermute | solution.py:14
  886.3 67.1 %collective-permute-start = (bf16[256,768]{0,1:T(8,128)(2,1)S(1)}, bf16[256,768]{0,1:T(8,128)(2,1)}, u32[]{:S(2)}, u32[]{:S(2)}) collective-permute-start(bf16[256,768]{0,1:T(8,128)(2,1)S(1)} %copy.127), channel_id=1, source_target_pairs={{0,4},{4,8},{8,12},{12,16},{16,20},{20,24},{24,28},{28,0},{1,5},{5... | collective-permute-start | bytes 1179656 | tf_op jit(solution)/shard_map/while/body/eval_jaxpr/ppermute | solution.py:14
  889.2 64.2 %collective-permute-start.1 = (bf16[256,768]{0,1:T(8,128)(2,1)}, bf16[256,768]{0,1:T(8,128)(2,1)}, u32[]{:S(2)}, u32[]{:S(2)}) collective-permute-start(bf16[256,768]{0,1:T(8,128)(2,1)} %copy.128), channel_id=1, source_target_pairs={{0,4},{4,8},{8,12},{12,16},{16,20},{20,24},{24,28},{28,0},{1,5},{5... | collective-permute-start | bytes 1179656 | tf_op jit(solution)/shard_map/while/body/eval_jaxpr/ppermute | solution.py:14
  919.7 29.5 %collective-permute-start.2 = (bf16[256,768]{0,1:T(8,128)(2,1)}, bf16[256,768]{0,1:T(8,128)(2,1)}, u32[]{:S(2)}, u32[]{:S(2)}) collective-permute-start(bf16[256,768]{0,1:T(8,128)(2,1)} %fusion.182), channel_id=1, source_target_pairs={{0,4},{4,8},{8,12},{12,16},{16,20},{20,24},{24,28},{28,0},{1,5},{5... | collective-permute-start | bytes 1179656 | tf_op jit(solution)/shard_map/while/body/eval_jaxpr/ppermute | solution.py:14
  921.7 29.7 %collective-permute-start.3 = (bf16[256,768]{0,1:T(8,128)(2,1)}, bf16[256,768]{0,1:T(8,128)(2,1)}, u32[]{:S(2)}, u32[]{:S(2)}) collective-permute-start(bf16[256,768]{0,1:T(8,128)(2,1)} %fusion.184), channel_id=1, source_target_pairs={{0,4},{4,8},{8,12},{12,16},{16,20},{20,24},{24,28},{28,0},{1,5},{5... | collective-permute-start | bytes 1179656 | tf_op jit(solution)/shard_map/while/body/eval_jaxpr/ppermute | solution.py:14
  954.5 68.1 %collective-permute-start = (bf16[256,768]{0,1:T(8,128)(2,1)S(1)}, bf16[256,768]{0,1:T(8,128)(2,1)}, u32[]{:S(2)}, u32[]{:S(2)}) collective-permute-start(bf16[256,768]{0,1:T(8,128)(2,1)S(1)} %copy.127), channel_id=1, source_target_pairs={{0,4},{4,8},{8,12},{12,16},{16,20},{20,24},{24,28},{28,0},{1,5},{5... | collective-permute-start | bytes 1179656 | tf_op jit(solution)/shard_map/while/body/eval_jaxpr/ppermute | solution.py:14
  957.7 64.9 %collective-permute-start.1 = (bf16[256,768]{0,1:T(8,128)(2,1)}, bf16[256,768]{0,1:T(8,128)(2,1)}, u32[]{:S(2)}, u32[]{:S(2)}) collective-permute-start(bf16[256,768]{0,1:T(8,128)(2,1)} %copy.128), channel_id=1, source_target_pairs={{0,4},{4,8},{8,12},{12,16},{16,20},{20,24},{24,28},{28,0},{1,5},{5... | collective-permute-start | bytes 1179656 | tf_op jit(solution)/shard_map/while/body/eval_jaxpr/ppermute | solution.py:14
  988.3 30.2 %collective-permute-start.2 = (bf16[256,768]{0,1:T(8,128)(2,1)}, bf16[256,768]{0,1:T(8,128)(2,1)}, u32[]{:S(2)}, u32[]{:S(2)}) collective-permute-start(bf16[256,768]{0,1:T(8,128)(2,1)} %fusion.182), channel_id=1, source_target_pairs={{0,4},{4,8},{8,12},{12,16},{16,20},{20,24},{24,28},{28,0},{1,5},{5... | collective-permute-start | bytes 1179656 | tf_op jit(solution)/shard_map/while/body/eval_jaxpr/ppermute | solution.py:14
  991.0 29.7 %collective-permute-start.3 = (bf16[256,768]{0,1:T(8,128)(2,1)}, bf16[256,768]{0,1:T(8,128)(2,1)}, u32[]{:S(2)}, u32[]{:S(2)}) collective-permute-start(bf16[256,768]{0,1:T(8,128)(2,1)} %fusion.184), channel_id=1, source_target_pairs={{0,4},{4,8},{8,12},{12,16},{16,20},{20,24},{24,28},{28,0},{1,5},{5... | collective-permute-start | bytes 1179656 | tf_op jit(solution)/shard_map/while/body/eval_jaxpr/ppermute | solution.py:14
  1023.6 67.1 %collective-permute-start = (bf16[256,768]{0,1:T(8,128)(2,1)S(1)}, bf16[256,768]{0,1:T(8,128)(2,1)}, u32[]{:S(2)}, u32[]{:S(2)}) collective-permute-start(bf16[256,768]{0,1:T(8,128)(2,1)S(1)} %copy.127), channel_id=1, source_target_pairs={{0,4},{4,8},{8,12},{12,16},{16,20},{20,24},{24,28},{28,0},{1,5},{5... | collective-permute-start | bytes 1179656 | tf_op jit(solution)/shard_map/while/body/eval_jaxpr/ppermute | solution.py:14
  1026.5 64.2 %collective-permute-start.1 = (bf16[256,768]{0,1:T(8,128)(2,1)}, bf16[256,768]{0,1:T(8,128)(2,1)}, u32[]{:S(2)}, u32[]{:S(2)}) collective-permute-start(bf16[256,768]{0,1:T(8,128)(2,1)} %copy.128), channel_id=1, source_target_pairs={{0,4},{4,8},{8,12},{12,16},{16,20},{20,24},{24,28},{28,0},{1,5},{5... | collective-permute-start | bytes 1179656 | tf_op jit(solution)/shard_map/while/body/eval_jaxpr/ppermute | solution.py:14
  1057.0 29.5 %collective-permute-start.2 = (bf16[256,768]{0,1:T(8,128)(2,1)}, bf16[256,768]{0,1:T(8,128)(2,1)}, u32[]{:S(2)}, u32[]{:S(2)}) collective-permute-start(bf16[256,768]{0,1:T(8,128)(2,1)} %fusion.182), channel_id=1, source_target_pairs={{0,4},{4,8},{8,12},{12,16},{16,20},{20,24},{24,28},{28,0},{1,5},{5... | collective-permute-start | bytes 1179656 | tf_op jit(solution)/shard_map/while/body/eval_jaxpr/ppermute | solution.py:14
  1059.0 29.7 %collective-permute-start.3 = (bf16[256,768]{0,1:T(8,128)(2,1)}, bf16[256,768]{0,1:T(8,128)(2,1)}, u32[]{:S(2)}, u32[]{:S(2)}) collective-permute-start(bf16[256,768]{0,1:T(8,128)(2,1)} %fusion.184), channel_id=1, source_target_pairs={{0,4},{4,8},{8,12},{12,16},{16,20},{20,24},{24,28},{28,0},{1,5},{5... | collective-permute-start | bytes 1179656 | tf_op jit(solution)/shard_map/while/body/eval_jaxpr/ppermute | solution.py:14
  1091.8 68.1 %collective-permute-start = (bf16[256,768]{0,1:T(8,128)(2,1)S(1)}, bf16[256,768]{0,1:T(8,128)(2,1)}, u32[]{:S(2)}, u32[]{:S(2)}) collective-permute-start(bf16[256,768]{0,1:T(8,128)(2,1)S(1)} %copy.127), channel_id=1, source_target_pairs={{0,4},{4,8},{8,12},{12,16},{16,20},{20,24},{24,28},{28,0},{1,5},{5... | collective-permute-start | bytes 1179656 | tf_op jit(solution)/shard_map/while/body/eval_jaxpr/ppermute | solution.py:14
  1095.0 64.9 %collective-permute-start.1 = (bf16[256,768]{0,1:T(8,128)(2,1)}, bf16[256,768]{0,1:T(8,128)(2,1)}, u32[]{:S(2)}, u32[]{:S(2)}) collective-permute-start(bf16[256,768]{0,1:T(8,128)(2,1)} %copy.128), channel_id=1, source_target_pairs={{0,4},{4,8},{8,12},{12,16},{16,20},{20,24},{24,28},{28,0},{1,5},{5... | collective-permute-start | bytes 1179656 | tf_op jit(solution)/shard_map/while/body/eval_jaxpr/ppermute | solution.py:14
  1125.6 30.2 %collective-permute-start.2 = (bf16[256,768]{0,1:T(8,128)(2,1)}, bf16[256,768]{0,1:T(8,128)(2,1)}, u32[]{:S(2)}, u32[]{:S(2)}) collective-permute-start(bf16[256,768]{0,1:T(8,128)(2,1)} %fusion.182), channel_id=1, source_target_pairs={{0,4},{4,8},{8,12},{12,16},{16,20},{20,24},{24,28},{28,0},{1,5},{5... | collective-permute-start | bytes 1179656 | tf_op jit(solution)/shard_map/while/body/eval_jaxpr/ppermute | solution.py:14
  1128.2 29.7 %collective-permute-start.3 = (bf16[256,768]{0,1:T(8,128)(2,1)}, bf16[256,768]{0,1:T(8,128)(2,1)}, u32[]{:S(2)}, u32[]{:S(2)}) collective-permute-start(bf16[256,768]{0,1:T(8,128)(2,1)} %fusion.184), channel_id=1, source_target_pairs={{0,4},{4,8},{8,12},{12,16},{16,20},{20,24},{24,28},{28,0},{1,5},{5... | collective-permute-start | bytes 1179656 | tf_op jit(solution)/shard_map/while/body/eval_jaxpr/ppermute | solution.py:14
  1160.9 67.1 %collective-permute-start = (bf16[256,768]{0,1:T(8,128)(2,1)S(1)}, bf16[256,768]{0,1:T(8,128)(2,1)}, u32[]{:S(2)}, u32[]{:S(2)}) collective-permute-start(bf16[256,768]{0,1:T(8,128)(2,1)S(1)} %copy.127), channel_id=1, source_target_pairs={{0,4},{4,8},{8,12},{12,16},{16,20},{20,24},{24,28},{28,0},{1,5},{5... | collective-permute-start | bytes 1179656 | tf_op jit(solution)/shard_map/while/body/eval_jaxpr/ppermute | solution.py:14
  1163.8 64.2 %collective-permute-start.1 = (bf16[256,768]{0,1:T(8,128)(2,1)}, bf16[256,768]{0,1:T(8,128)(2,1)}, u32[]{:S(2)}, u32[]{:S(2)}) collective-permute-start(bf16[256,768]{0,1:T(8,128)(2,1)} %copy.128), channel_id=1, source_target_pairs={{0,4},{4,8},{8,12},{12,16},{16,20},{20,24},{24,28},{28,0},{1,5},{5... | collective-permute-start | bytes 1179656 | tf_op jit(solution)/shard_map/while/body/eval_jaxpr/ppermute | solution.py:14
  1194.3 29.5 %collective-permute-start.2 = (bf16[256,768]{0,1:T(8,128)(2,1)}, bf16[256,768]{0,1:T(8,128)(2,1)}, u32[]{:S(2)}, u32[]{:S(2)}) collective-permute-start(bf16[256,768]{0,1:T(8,128)(2,1)} %fusion.182), channel_id=1, source_target_pairs={{0,4},{4,8},{8,12},{12,16},{16,20},{20,24},{24,28},{28,0},{1,5},{5... | collective-permute-start | bytes 1179656 | tf_op jit(solution)/shard_map/while/body/eval_jaxpr/ppermute | solution.py:14
  1196.3 29.7 %collective-permute-start.3 = (bf16[256,768]{0,1:T(8,128)(2,1)}, bf16[256,768]{0,1:T(8,128)(2,1)}, u32[]{:S(2)}, u32[]{:S(2)}) collective-permute-start(bf16[256,768]{0,1:T(8,128)(2,1)} %fusion.184), channel_id=1, source_target_pairs={{0,4},{4,8},{8,12},{12,16},{16,20},{20,24},{24,28},{28,0},{1,5},{5... | collective-permute-start | bytes 1179656 | tf_op jit(solution)/shard_map/while/body/eval_jaxpr/ppermute | solution.py:14
  1232.6 203.8 %reduce-scatter.10.cloned.1.call-start = ((), (), s32[]{:S(2)}) async-start(), calls=%async_computation.17 | async-start | bytes 2433024 | tf_op jit(solution)/shard_map/reduce_scatter | solution.py:303
  1234.8 305.4 %reduce-scatter.12.cloned.1.call-start = ((), (), s32[]{:S(2)}) async-start(), calls=%async_computation.18 | async-start | bytes 2433024 | tf_op jit(solution)/shard_map/reduce_scatter | solution.py:304
  1236.9 407.9 %reduce-scatter.14.cloned.1.call-start = ((), (), s32[]{:S(2)}) async-start(), calls=%async_computation.19 | async-start | bytes 2433024 | tf_op jit(solution)/shard_map/reduce_scatter | solution.py:305
  1240.2 524.4 %reduce-scatter.16.cloned.1.call-start = ((), (), s32[]{:S(2)}) async-start(), calls=%async_computation.20 | async-start | bytes 6488064 | tf_op jit(solution)/shard_map/reduce_scatter | solution.py:309
  1245.2 640.2 %reduce-scatter.18.cloned.1.call-start = ((), (), s32[]{:S(2)}) async-start(), calls=%async_computation.21 | async-start | bytes 6488064 | tf_op jit(solution)/shard_map/reduce_scatter | solution.py:310
  1250.2 754.8 %reduce-scatter.20.cloned.1.call-start = ((), (), s32[]{:S(2)}) async-start(), calls=%async_computation.22 | async-start | bytes 6488064 | tf_op jit(solution)/shard_map/reduce_scatter | solution.py:311
  1259.3 43.1 %copy-start.49 = (f32[256]{0:T(256)S(1)}, f32[256]{0:T(256)}, u32[]{:S(2)}) copy-start(f32[256]{0:T(256)} %copy-done.48) | copy-start | bytes 3076
  1260.8 43.9 %copy-start.16 = (f32[256,768]{1,0:T(8,128)S(1)}, f32[256,768]{1,0:T(8,128)}, u32[]{:S(2)}) copy-start(f32[256,768]{1,0:T(8,128)} %copy-done.15) | copy-start | bytes 2359300
  1302.4 702.6 %copy-start.1 = (f32[32,12]{0,1:T(8,128)S(1)}, f32[32,12]{0,1:T(8,128)}, u32[]{:S(2)}) copy-start(f32[32,12]{0,1:T(8,128)} %param.26) | copy-start | bytes 4612
  (87 other events, 235.3 us)
Sparse Core Ops, SparseCore 0:
  11.5 56.7 all-gather.9
  71.8 52.9 all-gather.15
  128.3 53.0 all-gather.13
  184.0 59.3 all-gather.11
  245.4 59.0 all-gather.17
  307.8 52.6 all-gather.19
  364.0 57.8 all-gather.21
  425.4 57.7 all-gather.23
  486.1 57.7 all-gather.25
  1232.7 98.8 reduce-scatter.7
  1338.4 98.0 reduce-scatter.9
  1442.1 98.0 reduce-scatter.11
  1546.9 97.9 reduce-scatter.13
  1651.0 113.6 reduce-scatter.15
  1771.6 113.7 reduce-scatter.17
  1891.5 113.4 reduce-scatter.19
where the time goes:
time: 2020 us; the launch traced here: 2010 us
  waiting for transfers between devices  927 us (46%)
  local copies, waits for them, and re-layouts  614 us (30%)
  matrix products  185 us (9%)
  other arithmetic  136 us (7%)
  blocking collectives  82.5 us (4%)
  starting transfers between devices  43.9 us (2%)
    reshape x24, local copies, waits for them, and re-layouts, bias_block(): tiled_rows[:, :row_count * (period - 1)]  217 us
    while x168, local copies, waits for them, and re-layouts  184 us
    reduce_scatter x1, waiting for transfers between devices, body(): lax.psum_scatter(grad_up_weight, ('seq', 'dp'), scatter_dimension=0, tile...  121 us
    reduce_scatter x1, waiting for transfers between devices, body(): lax.psum_scatter(grad_gate_weight, ('seq', 'dp'), scatter_dimension=0, ti...  120 us
    reduce_scatter x1, waiting for transfers between devices, body(): lax.psum_scatter(grad_down, ('seq', 'dp'), scatter_dimension=0, tiled=True)  120 us
    reduce_scatter x1, waiting for transfers between devices, body(): lax.psum_scatter(grad_key_weight, ('seq', 'dp'), scatter_dimension=0, til...  105 us
    reduce_scatter x1, waiting for transfers between devices, body(): lax.psum_scatter(grad_output_weight, ('seq', 'dp'), scatter_dimension=0,...  105 us
    reduce_scatter x1, waiting for transfers between devices, body(): lax.psum_scatter(grad_value_weight, ('seq', 'dp'), scatter_dimension=0, t...  104 us
  transfers between devices with their start and end apart: 48, of which 12 were waited for; matrix products, arithmetic and copies ran while one was open for 44% of the time, Pallas kernels for 0%

commit v1 on v0

v1 whole, which is shorter than its diff:
```python
import functools

import jax
import jax.numpy as jnp
from jax import lax
from jax.experimental import pallas as pl
from jax.experimental.pallas import tpu as pltpu
from jax.sharding import PartitionSpec as P

EPSILON = 1e-06
BIG = -1e30
HIGHEST = lax.Precision.HIGHEST
BOTH = ("seq", "dp")
TILE = 128
STEP = 4
SPAN = STEP * TILE
F32 = jnp.float32
BF16 = jnp.bfloat16
LOWEST = -3.0e38


def bias_of(tiles_ref, pair, tile):
    halves_of = [tiles_ref[2 * pair + side, pl.ds(tile, STEP)].reshape(SPAN, TILE) for side in range(2)]
    return jnp.concatenate(halves_of, axis=1)


def dot(a, b):
    return jnp.dot(a, b, preferred_element_type=F32)


def tiles_kernel(line_ref, tiles_ref):
    tile_count = tiles_ref.shape[1]
    for index in range(tile_count):
        window = line_ref[0, :, pl.ds((tile_count - 1 - index) * TILE, 2 * TILE)]
        spread = jnp.broadcast_to(window, (TILE, 2 * TILE))
        rolled = pltpu.roll(spread, 0, 1, stride=1, stride_axis=0)
        tiles_ref[0, index] = rolled[:, TILE:]


def bias_tiles(lines, tile_count):
    heads, width = lines.shape
    return pl.pallas_call(
        tiles_kernel,
        out_shape=jax.ShapeDtypeStruct((heads, tile_count, TILE, TILE), F32),
        grid=(heads,),
        in_specs=[pl.BlockSpec((1, 1, width), lambda h: (h, 0, 0))],
        out_specs=pl.BlockSpec((1, tile_count, TILE, TILE), lambda h: (h, 0, 0, 0)),
    )(lines.reshape(heads, 1, width))


def halves(pair, head_dim):
    top = lax.broadcasted_iota(jnp.int32, pair.shape, 0) < head_dim
    zero = jnp.zeros_like(pair)
    return jnp.concatenate([jnp.where(top, pair, zero), jnp.where(top, zero, pair)], axis=1)


def halves_rows(pair, head_dim):
    left = lax.broadcasted_iota(jnp.int32, pair.shape, 1) < head_dim
    zero = jnp.zeros_like(pair)
    return jnp.concatenate([jnp.where(left, pair, zero), jnp.where(left, zero, pair)], axis=0)


def merge_halves(both, head_dim):
    top = lax.broadcasted_iota(jnp.int32, (both.shape[0], TILE), 0) < head_dim
    return jnp.where(top, both[:, :TILE], both[:, TILE:])


def fold(values, op):
    return op(values.reshape(values.shape[0] // 8, 8, values.shape[1]), axis=0)


def cols(pair):
    return slice(pair * TILE, (pair + 1) * TILE)


def wide(pair):
    return slice(pair * 2 * TILE, (pair + 1) * 2 * TILE)


def query_side(query_ref, query_feat_ref, block, pair, head_dim):
    rows = slice(block * TILE, (block + 1) * TILE)
    turned = query_ref[cols(pair), rows]
    feat = query_feat_ref[:, rows]
    return jnp.concatenate([halves(turned, head_dim), jnp.concatenate([feat, feat], axis=1)], axis=0)


def forward_kernel(
    first_ref, last_ref, query_ref, key_ref, value_turned_ref, key_feat_ref, query_feat_ref, tiles_ref,
    out_ref, log_ref, score_ref, total_ref, *, pairs, blocks, head_dim,
):
    for block in range(blocks):
        rows = slice(block * TILE, (block + 1) * TILE)
        first, last = first_ref[block], last_ref[block]
        query_sides = [query_side(query_ref, query_feat_ref, block, pair, head_dim) for pair in range(pairs)]

        def score_step(index, highest):
            start = pl.multiple_of((first + index * STEP) * TILE, TILE)
            feat = key_feat_ref[pl.ds(start, SPAN), :]
            tile = first + index * STEP - block + (blocks - 1)
            result = []
            for pair in range(pairs):
                left = jnp.concatenate([key_ref[pl.ds(start, SPAN), cols(pair)], feat], axis=1)
                bias = bias_of(tiles_ref, pair, tile)
                scores = dot(left, query_sides[pair]) + bias
                score_ref[pl.ds(start, SPAN), wide(pair)] = scores
                result.append(jnp.maximum(highest[pair], fold(scores, jnp.max)))
            return tuple(result)

        start_max = tuple(jnp.full((8, 2 * TILE), LOWEST, F32) for _ in range(pairs))
        highest = lax.fori_loop(0, last, score_step, start_max)
        peak = [jnp.max(value, axis=0, keepdims=True) for value in highest]
        total_ref[...] = jnp.zeros_like(total_ref)

        def value_step(index, sums):
            start = pl.multiple_of((first + index * STEP) * TILE, TILE)
            result = []
            for pair in range(pairs):
                weights = jnp.exp(score_ref[pl.ds(start, SPAN), wide(pair)] - peak[pair])
                result.append(sums[pair] + fold(weights, jnp.sum))
                total_ref[:, wide(pair)] += dot(
                    value_turned_ref[cols(pair), pl.ds(start, SPAN)], weights.astype(BF16)
                )
            return tuple(result)

        start_sum = tuple(jnp.zeros((8, 2 * TILE), F32) for _ in range(pairs))
        sums = lax.fori_loop(0, last, value_step, start_sum)
        for pair in range(pairs):
            denominator = jnp.sum(sums[pair], axis=0, keepdims=True)
            out_ref[cols(pair), rows] = merge_halves(total_ref[:, wide(pair)] / denominator, head_dim)
            log_ref[0, block * pairs + pair : block * pairs + pair + 1, :] = peak[pair] + jnp.log(denominator)


def attend(first, last, queries, keys, values_turned, key_feat, query_feat, tiles, head_dim, pairs):
    width, row_count = queries.shape
    window = keys.shape[0]
    blocks = row_count // TILE
    groups = width // (pairs * TILE)
    tile_count = tiles.shape[1]
    kernel = functools.partial(
        forward_kernel, pairs=pairs, blocks=blocks, head_dim=head_dim
    )
    work = row_count * 1280 * width
    return pl.pallas_call(
        kernel,
        out_shape=(
            jax.ShapeDtypeStruct((width, row_count), F32),
            jax.ShapeDtypeStruct((groups, blocks * pairs, 2 * TILE), F32),
        ),
        grid_spec=pltpu.PrefetchScalarGridSpec(
            num_scalar_prefetch=2,
            grid=(groups,),
            in_specs=[
                pl.BlockSpec((pairs * TILE, row_count), lambda g, a, b: (g, 0)),
                pl.BlockSpec((window, pairs * TILE), lambda g, a, b: (0, g)),
                pl.BlockSpec((pairs * TILE, window), lambda g, a, b: (g, 0)),
                pl.BlockSpec((window, TILE), lambda g, a, b: (0, 0)),
                pl.BlockSpec((TILE, row_count), lambda g, a, b: (0, 0)),
                pl.BlockSpec((2 * pairs, tile_count, TILE, TILE), lambda g, a, b: (g, 0, 0, 0)),
            ],
            out_specs=[
                pl.BlockSpec((pairs * TILE, row_count), lambda g, a, b: (g, 0)),
                pl.BlockSpec((1, blocks * pairs, 2 * TILE), lambda g, a, b: (g, 0, 0)),
            ],
            scratch_shapes=[
                pltpu.VMEM((window, pairs * 2 * TILE), F32),
                pltpu.VMEM((TILE, pairs * 2 * TILE), F32),
            ],
        ),
        compiler_params=pltpu.CompilerParams(vmem_limit_bytes=50 << 20),
        cost_estimate=pl.CostEstimate(flops=16 * work, bytes_accessed=24 << 20, transcendentals=row_count * 1280 * 12),
    )(first, last, queries, keys, values_turned, key_feat, query_feat, tiles)


def backward_kernel(
    first_ref, last_ref, query_ref, query_turned_ref, key_ref, key_turned_ref, value_ref, grad_ref, grad_turned_ref, out_ref, log_ref,
    key_feat_ref, query_feat_ref, tiles_ref,
    grad_query_ref, grad_key_ref, grad_value_ref, tile_total,
    key_total, value_total, query_total, *, pairs, blocks, head_dim,
):
    key_total[...] = jnp.zeros_like(key_total)
    value_total[...] = jnp.zeros_like(value_total)
    tile_total[...] = jnp.zeros_like(tile_total)
    for block in range(blocks):
        rows = slice(block * TILE, (block + 1) * TILE)
        first, last = first_ref[block], last_ref[block]
        query_sides, grad_sides, query_stacks, grad_stacks, logs, deltas = [], [], [], [], [], []
        for pair in range(pairs):
            query_sides.append(query_side(query_turned_ref, query_feat_ref, block, pair, head_dim))
            grad_pair = grad_ref[rows, cols(pair)]
            grad_turned = grad_turned_ref[cols(pair), rows]
            grad_sides.append(halves(grad_turned, head_dim))
            query_stacks.append(halves_rows(query_ref[rows, cols(pair)], head_dim))
            grad_stacks.append(halves_rows(grad_pair, head_dim))
            logs.append(log_ref[0, block * pairs + pair : block * pairs + pair + 1, :])
            both = halves(grad_turned.astype(F32) * out_ref[cols(pair), rows], head_dim)
            deltas.append(jnp.sum(both, axis=0, keepdims=True))
        query_total[...] = jnp.zeros_like(query_total)

        def step(index, carry):
            start = pl.multiple_of((first + index * STEP) * TILE, TILE)
            span = pl.ds(start, SPAN)
            feat = key_feat_ref[span, :]
            tile = first + index * STEP - block + (blocks - 1)
            for pair in range(pairs):
                left = jnp.concatenate([key_ref[span, cols(pair)], feat], axis=1)
                bias = bias_of(tiles_ref, pair, tile)
                weights = jnp.exp(dot(left, query_sides[pair]) + bias - logs[pair])
                grad_weights = dot(value_ref[span, cols(pair)], grad_sides[pair])
                grad_scores = weights * (grad_weights - deltas[pair])
                tile_total[2 * pair, pl.ds(tile, STEP)] += grad_scores[:, :TILE].reshape(STEP, TILE, TILE)
                tile_total[2 * pair + 1, pl.ds(tile, STEP)] += grad_scores[:, TILE:].reshape(STEP, TILE, TILE)
                scores_low = grad_scores.astype(BF16)
                value_total[span, cols(pair)] += dot(weights.astype(BF16), grad_stacks[pair])
                key_total[span, cols(pair)] += dot(scores_low, query_stacks[pair])
                query_total[:, wide(pair)] += dot(key_turned_ref[cols(pair), span], scores_low)
            return carry

        lax.fori_loop(0, last, step, 0)
        for pair in range(pairs):
            grad_query_ref[cols(pair), rows] = merge_halves(query_total[:, wide(pair)], head_dim).astype(BF16)
    grad_key_ref[...] = key_total[...].astype(BF16)
    grad_value_ref[...] = value_total[...].astype(BF16)


def attend_back(first, last, queries, queries_turned, keys, keys_turned, values, grads, grads_turned, outs, logs, key_feat, query_feat, tiles, head_dim, pairs):
    row_count, width = queries.shape
    window = keys.shape[0]
    blocks = row_count // TILE
    groups = width // (pairs * TILE)
    heads, tile_count = tiles.shape[:2]
    kernel = functools.partial(backward_kernel, pairs=pairs, blocks=blocks, head_dim=head_dim)
    rows_spec = pl.BlockSpec((row_count, pairs * TILE), lambda g, a, b: (0, g))
    turned_spec = pl.BlockSpec((pairs * TILE, row_count), lambda g, a, b: (g, 0))
    window_spec = pl.BlockSpec((window, pairs * TILE), lambda g, a, b: (0, g))
    work = row_count * 1280 * width
    return pl.pallas_call(
        kernel,
        out_shape=(
            jax.ShapeDtypeStruct((width, row_count), BF16),
            jax.ShapeDtypeStruct((window, width), BF16),
            jax.ShapeDtypeStruct((window, width), BF16),
            jax.ShapeDtypeStruct((heads, tile_count, TILE, TILE), F32),
        ),
        grid_spec=pltpu.PrefetchScalarGridSpec(
            num_scalar_prefetch=2,
            grid=(groups,),
            in_specs=[
                rows_spec,
                turned_spec,
                window_spec,
                pl.BlockSpec((pairs * TILE, window), lambda g, a, b: (g, 0)),
                window_spec,
                rows_spec,
                turned_spec,
                turned_spec,
                pl.BlockSpec((1, blocks * pairs, 2 * TILE), lambda g, a, b: (g, 0, 0)),
                pl.BlockSpec((window, TILE), lambda g, a, b: (0, 0)),
                pl.BlockSpec((TILE, row_count), lambda g, a, b: (0, 0)),
                pl.BlockSpec((2 * pairs, tile_count, TILE, TILE), lambda g, a, b: (g, 0, 0, 0)),
            ],
            out_specs=[
                turned_spec,
                window_spec,
                window_spec,
                pl.BlockSpec((2 * pairs, tile_count, TILE, TILE), lambda g, a, b: (g, 0, 0, 0)),
            ],
            scratch_shapes=[
                pltpu.VMEM((window, pairs * TILE), F32),
                pltpu.VMEM((window, pairs * TILE), F32),
                pltpu.VMEM((TILE, pairs * 2 * TILE), F32),
            ],
        ),
        input_output_aliases={13: 3},
        compiler_params=pltpu.CompilerParams(vmem_limit_bytes=56 << 20),
        cost_estimate=pl.CostEstimate(flops=40 * work, bytes_accessed=32 << 20, transcendentals=row_count * 1280 * 12),
    )(first, last, queries, queries_turned, keys, keys_turned, values, grads, grads_turned, outs, logs, key_feat, query_feat, tiles)


def diagonal_kernel(tiles_ref, line_ref):
    for index in range(tiles_ref.shape[1]):
        tile = tiles_ref[0, index]
        padded = jnp.concatenate([tile, jnp.zeros_like(tile)], axis=1)
        size = TILE // 2
        while size >= 8:
            padded = padded[:size] + pltpu.roll(padded[size:], 2 * TILE - size, 1)
            size //= 2
        line_ref[0, index] = padded


def diagonal_sums(tiles):
    heads, tile_count = tiles.shape[:2]
    return pl.pallas_call(
        diagonal_kernel,
        out_shape=jax.ShapeDtypeStruct((heads, tile_count, 8, 2 * TILE), F32),
        grid=(heads,),
        in_specs=[pl.BlockSpec((1, tile_count, TILE, TILE), lambda h: (h, 0, 0, 0))],
        out_specs=pl.BlockSpec((1, tile_count, 8, 2 * TILE), lambda h: (h, 0, 0, 0)),
    )(tiles)


def shifted(value, axis, steps):
    count = lax.axis_size(axis)
    pairs = [(source, source + steps) for source in range(count) if 0 <= source + steps < count]
    return lax.ppermute(value, axis, pairs)


def swapped(value, axis, bit):
    count = lax.axis_size(axis)
    return lax.ppermute(value, axis, [(source, source ^ bit) for source in range(count)])


def sum_everywhere(value):
    for axis in BOTH:
        count = lax.axis_size(axis)
        if count & (count - 1):
            value = lax.psum(value, axis)
            continue
        bit = 1
        while bit < count:
            value = value + swapped(value, axis, bit)
            bit *= 2
    return value


def rows_of(value, rows):
    height, width = value.shape
    columns = height * width // rows
    if height % 8 or rows % 8 or width % TILE or columns % TILE:
        return value.reshape(rows, columns)
    tiles = value.reshape(height // 8, 8, width // TILE, TILE).transpose(0, 2, 1, 3)
    tiles = tiles.reshape(rows // 8, columns // TILE, 8, TILE).transpose(0, 2, 1, 3)
    return tiles.reshape(rows, columns)


def parts_of(value, parts, to_rows):
    rows = value.shape[0] // parts
    columns = rows * value.shape[1] // to_rows
    if rows % 8 or to_rows % 8 or value.shape[1] % TILE or columns % TILE:
        return value.reshape(parts * to_rows, columns)
    tiles = value.reshape(parts, rows // 8, 8, value.shape[1] // TILE, TILE).transpose(0, 1, 3, 2, 4)
    tiles = tiles.reshape(parts, to_rows // 8, columns // TILE, 8, TILE).transpose(0, 1, 3, 2, 4)
    return tiles.reshape(parts * to_rows, columns)


def contract(left_side, right_side, left_dim, right_dim):
    return lax.dot_general(
        left_side, right_side, (((left_dim,), (right_dim,)), ((), ())), preferred_element_type=F32
    )


def gelu_pair(v):
    scale = 0.7978845608028654
    bent = jnp.tanh(scale * (v + 0.044715 * v * v * v))
    value = 0.5 * v * (1.0 + bent)
    slope = 0.5 * (1.0 + bent) + 0.5 * v * (1.0 - bent * bent) * scale * (1.0 + 3.0 * 0.044715 * v * v)
    return value, slope


def body(
    blocks,
    lengths,
    bucket_table,
    first_gain,
    query_weight,
    key_weight,
    value_weight,
    output_weight,
    table_weight,
    second_gain,
    gate_weight,
    up_weight,
    down_weight,
    cotangent,
):
    seq_count = lax.axis_size("seq")
    device_count = seq_count * lax.axis_size("dp")
    seq_rank = lax.axis_index("seq")
    row_count, width = blocks.shape[1:]
    pack_rows = row_count * seq_count
    bucket_count, heads = table_weight.shape
    head_dim = width // heads
    seq_total = lengths.shape[1]
    max_length = (bucket_table.shape[0] + 1) // 2
    shard_rows = query_weight.shape[0]
    hidden_width = gate_weight.shape[1]
    reach = min((max_length - 1 + row_count - 1) // row_count, seq_count - 1)
    query_blocks = row_count // TILE
    window = (2 * reach + 1) * row_count
    window_blocks = window // TILE
    tile_count = window_blocks + query_blocks - 1
    center = reach * query_blocks + query_blocks - 1
    pairs = 2 if window <= 2304 else 1

    own = blocks[0]
    near = [shifted(own, "seq", -step) for step in range(1, reach + 1)]
    far = [shifted(own, "seq", step) for step in range(1, reach + 1)]
    window_blocks_low = jnp.concatenate(far[::-1] + [own] + near, axis=0)

    gains = jnp.stack([first_gain.astype(BF16), second_gain.astype(BF16)], axis=1)
    gains = jnp.pad(gains, ((0, 0), (0, TILE - 2)))
    shard = jnp.concatenate(
        [
            query_weight.astype(BF16),
            key_weight.astype(BF16),
            value_weight.astype(BF16),
            gains,
            output_weight.astype(BF16),
            gate_weight.astype(BF16),
            up_weight.astype(BF16),
            rows_of(down_weight.astype(BF16), shard_rows),
        ],
        axis=1,
    )
    gathered = lax.all_gather(shard, BOTH, axis=0, tiled=True)
    down_columns = down_weight.shape[0] * width // shard_rows
    places = [width, width, width, TILE, width, 2 * hidden_width, down_columns]
    cuts = []
    start = 0
    for place in places:
        cuts.append(gathered[:, start : start + place])
        start += place
    weight_query, weight_key, weight_value, gain_columns, weight_output, weight_pair, weight_down = cuts
    weight_down = parts_of(weight_down, device_count, down_weight.shape[0])
    gain_one = gain_columns[:, 0].astype(F32)[None, :]
    gain_two = gain_columns[:, 1].astype(F32)[None, :]

    seq_ends = jnp.cumsum(lengths[0], dtype=jnp.int32)
    query_first = seq_rank * row_count
    window_first = query_first - reach * row_count

    def segments(at):
        return jnp.sum((at[:, None] >= seq_ends[None, :]).astype(jnp.int32), axis=1, dtype=jnp.int32)

    query_places = query_first + jnp.arange(row_count, dtype=jnp.int32)
    key_places = window_first + jnp.arange(window, dtype=jnp.int32)
    query_seg = segments(query_places)
    key_seg = jnp.where((key_places >= 0) & (key_places < pack_rows), segments(key_places), -1)
    lanes = jnp.arange(TILE, dtype=jnp.int32)
    key_feat = jnp.where(
        (key_seg[:, None] != lanes[None, :]) & (lanes[None, :] <= seq_total), BIG, 0.0
    ).astype(BF16)
    query_feat = (lanes[:, None] == query_seg[None, :]).astype(BF16)
    valid_rows = (query_seg < seq_total).astype(F32)
    seq_starts = jnp.concatenate([jnp.zeros((1,), jnp.int32), seq_ends])
    seq_stops = jnp.concatenate([seq_ends, jnp.full((1,), pack_rows, jnp.int32)])
    seq_ids = jnp.arange(seq_total + 1, dtype=jnp.int32)
    low_seg = query_seg[::TILE]
    high_seg = query_seg[TILE - 1 :: TILE]
    low = jnp.sum(jnp.where(low_seg[:, None] == seq_ids[None, :], seq_starts[None, :], 0), axis=1)
    high = jnp.sum(jnp.where(high_seg[:, None] == seq_ids[None, :], seq_stops[None, :], 0), axis=1)
    first = (low - window_first) // TILE
    last = (high - window_first + TILE - 1) // TILE
    steps = (last - first + STEP - 1) // STEP
    first = jnp.minimum(first, window_blocks - steps * STEP).astype(jnp.int32)
    steps = steps.astype(jnp.int32)

    line_width = (tile_count + 1) * TILE
    ahead = (tile_count - center) * TILE - (max_length - 1)
    behind = line_width - ahead - bucket_table.shape[0]
    bucket_line = jnp.pad(bucket_table[::-1], (max(ahead, 0), max(behind, 0)), mode="edge")
    bucket_line = bucket_line[max(-ahead, 0) : max(-ahead, 0) + line_width]
    bucket_ids = jnp.arange(bucket_count, dtype=jnp.int32)
    line_hot = (bucket_line[None, :] == bucket_ids[:, None]).astype(F32)
    lines = lax.dot_general(table_weight, line_hot, (((0,), (0,)), ((), ())), precision=HIGHEST)
    tiles = bias_tiles(lines, tile_count)

    window_rows = window_blocks_low.astype(F32)
    window_scale = lax.rsqrt(jnp.mean(window_rows * window_rows, axis=1, keepdims=True) + EPSILON)
    window_normed = (window_rows * window_scale * gain_one).astype(BF16)
    own_slice = slice(reach * row_count, (reach + 1) * row_count)
    tokens = own.astype(F32)
    scale_one = lax.rsqrt(jnp.mean(tokens * tokens, axis=1, keepdims=True) + EPSILON)
    normed_own = window_normed[own_slice]
    keys = contract(window_normed, weight_key, 1, 0).astype(BF16)
    values_turned = contract(weight_value, window_normed, 0, 1).astype(BF16)
    queries_turned = contract(weight_query, normed_own, 0, 1).astype(BF16)
    outs, logs = attend(
        first, steps, queries_turned, keys, values_turned, key_feat, query_feat, tiles, head_dim, pairs
    )
    attended = (outs * valid_rows[None, :]).astype(BF16)
    middle = tokens + contract(attended, weight_output, 0, 0)

    scale_two = lax.rsqrt(jnp.mean(middle * middle, axis=1, keepdims=True) + EPSILON)
    second = middle * scale_two
    second_low = (second * gain_two).astype(BF16)
    both_ways = contract(second_low, weight_pair, 1, 0)
    gate_values, upward = both_ways[:, :hidden_width], both_ways[:, hidden_width:]
    active, slope = gelu_pair(gate_values)
    hidden = (active * upward).astype(BF16)
    output = middle + contract(hidden, weight_down, 1, 0)
    grad_out = cotangent[0]
    grad_hidden = contract(grad_out, weight_down, 1, 1)
    grad_pair = jnp.concatenate(
        [(grad_hidden * upward * slope).astype(BF16), (grad_hidden * active).astype(BF16)], axis=1
    )
    grad_second = contract(grad_pair, weight_pair, 1, 1)
    grad_gain_two = jnp.sum(grad_second * second, axis=0)
    scaled = grad_second * gain_two
    grad_middle = grad_out.astype(F32) + scale_two * (
        scaled - second * jnp.mean(scaled * second, axis=1, keepdims=True)
    )
    grad_branch = grad_middle.astype(BF16)
    grad_mixed = (contract(grad_branch, weight_output, 1, 1).astype(BF16).astype(F32) * valid_rows[:, None]).astype(BF16)
    grad_mixed_turned = (
        contract(weight_output, grad_branch, 1, 1).astype(BF16).astype(F32) * valid_rows[None, :]
    ).astype(BF16)
    grad_down = contract(hidden, grad_out, 0, 0).astype(BF16)
    grad_pair_weight = contract(second_low, grad_pair, 0, 0).astype(BF16)
    grad_output_weight = contract(attended, grad_branch, 1, 0).astype(BF16)

    queries = contract(normed_own, weight_query, 1, 0).astype(BF16)
    keys_turned = contract(weight_key, window_normed, 0, 1).astype(BF16)
    values = contract(window_normed, weight_value, 1, 0).astype(BF16)
    grad_queries, grad_keys, grad_values, tile_sums = attend_back(
        first, steps, queries, queries_turned, keys, keys_turned, values, grad_mixed, grad_mixed_turned,
        outs, logs, key_feat, query_feat, tiles, head_dim, pairs,
    )
    partial = contract(grad_keys, weight_key, 1, 1) + contract(grad_values, weight_value, 1, 1)
    partial_low = partial.astype(BF16)
    grad_normed = partial[own_slice] + contract(grad_queries, weight_query, 0, 1)
    for step in range(1, reach + 1):
        ahead_part = partial_low[(reach + step) * row_count : (reach + step + 1) * row_count]
        behind_part = partial_low[(reach - step) * row_count : (reach - step + 1) * row_count]
        grad_normed = grad_normed + shifted(ahead_part, "seq", step).astype(F32)
        grad_normed = grad_normed + shifted(behind_part, "seq", -step).astype(F32)
    grad_query_weight = contract(normed_own, grad_queries, 0, 1).astype(BF16)
    grad_key_weight = contract(window_normed, grad_keys, 0, 0).astype(BF16)
    grad_value_weight = contract(window_normed, grad_values, 0, 0).astype(BF16)
    normed_rows = tokens * scale_one
    grad_gain_one = jnp.sum(grad_normed * normed_rows, axis=0)
    scaled_one = grad_normed * gain_one
    grad_blocks = grad_middle + scale_one * (
        scaled_one - normed_rows * jnp.mean(scaled_one * normed_rows, axis=1, keepdims=True)
    )

    sums = diagonal_sums(tile_sums)
    diagonals = sum(jnp.roll(sums[:, :, row], -row, axis=2) for row in range(8))
    flipped = bucket_line.reshape(tile_count + 1, TILE)[::-1]
    bucket_at = jnp.concatenate([flipped[:-1], flipped[1:]], axis=1).reshape(-1)
    bucket_hot = (bucket_at[:, None] == bucket_ids[None, :]).astype(F32)
    grad_table = lax.dot_general(
        bucket_hot, diagonals.reshape(heads, -1), (((0,), (1,)), ((), ())), precision=HIGHEST
    )
    grad_table = sum_everywhere(grad_table)

    grad_gains = jnp.stack([grad_gain_one, grad_gain_two], axis=1).astype(BF16)
    grad_gains = jnp.pad(grad_gains, ((0, 0), (0, TILE - 2)))
    grads = jnp.concatenate(
        [
            grad_query_weight,
            grad_key_weight,
            grad_value_weight,
            grad_gains,
            grad_output_weight,
            grad_pair_weight,
            parts_of(grad_down, device_count, shard_rows),
        ],
        axis=1,
    )
    summed = lax.psum_scatter(grads, BOTH, scatter_dimension=0, tiled=True).astype(F32)
    pieces = []
    start = 0
    for place in [width, width, width, TILE, width, hidden_width, hidden_width, down_columns]:
        pieces.append(summed[:, start : start + place])
        start += place
    return (
        output.astype(BF16)[None],
        grad_blocks[None],
        pieces[3][:, 0],
        pieces[0],
        pieces[1],
        pieces[2],
        pieces[4],
        grad_table,
        pieces[3][:, 1],
        pieces[5],
        pieces[6],
        rows_of(pieces[7], down_weight.shape[0]),
    )


def solution(mesh):
    return jax.shard_map(
        body,
        mesh=mesh,
        in_specs=(
            P("dp", "seq", None),
            P("dp", None),
            P(),
            P(("seq", "dp")),
            P(("seq", "dp"), None),
            P(("seq", "dp"), None),
            P(("seq", "dp"), None),
            P(("seq", "dp"), None),
            P(),
            P(("seq", "dp")),
            P(("seq", "dp"), None),
            P(("seq", "dp"), None),
            P(("seq", "dp"), None),
            P("dp", "seq", None),
        ),
        out_specs=(
            P("dp", "seq", None),
            P("dp", "seq", None),
            P(("seq", "dp")),
            P(("seq", "dp"), None),
            P(("seq", "dp"), None),
            P(("seq", "dp"), None),
            P(("seq", "dp"), None),
            P(),
            P(("seq", "dp")),
            P(("seq", "dp"), None),
            P(("seq", "dp"), None),
            P(("seq", "dp"), None),
        ),
        check_vma=False,
    )
```

time: 2020 us -> 535 us (0.26)
  waiting for transfers between devices: 927 us -> 231 us
  local copies, waits for them, and re-layouts: 614 us -> 46 us
  other arithmetic: 136 us -> 20.6 us
  matrix products: 185 us -> 79.4 us
  blocking collectives: 82.5 us -> 0 us
  Pallas kernels: 0 us -> 73.2 us
    reduce_scatter x7 -> x0, waiting for transfers between devices: 696 us -> none  [the longest x1 121 us: body(): lax.psum_scatter(grad_up_weight, ('seq', 'dp'), scatter_dimension=0, tile...]
    reshape x25 -> x3, local copies, waits for them, and re-layouts: 217 us -> 2.03 us  [the longest x2 1.29 us: body(): jnp.pad(bucket_table[::-1], (max(ahead, 0), max(behind, 0)), mode='edge')]
    all_gather x9 -> x1, waiting for transfers between devices: 230 us -> 37.7 us  [body(): gathered = lax.all_gather(shard, BOTH, axis=0, tiled=True)]
    while x168 -> x0, local copies, waits for them, and re-layouts: 184 us -> none
    dot_general x86 -> x24, matrix products: 185 us -> 79.4 us  [the longest x22 78.7 us: contract(): lax.dot_general(left_side, right_side, (((left_dim,), (right_dim,)), ((),...]
    unnamed x16 -> x3, waiting for transfers between devices: 0.29 us -> 103 us
    unnamed x2 -> x0, blocking collectives: 82.5 us -> none
    ppermute x32 -> x16, waiting for transfers between devices: 0.08 us -> 80.6 us  [shifted(): return lax.ppermute(value, axis, pairs)]
  transfers between devices with their start and end apart: 48 -> 23, of which waited for: 12 -> 12; matrix products, arithmetic and copies ran while one was open for 44% -> 8% of each run, Pallas kernels for 0% -> 8%
where the time goes in v1:
time: 535 us; the launch traced here: 528 us
  waiting for transfers between devices  231 us (43%)
  matrix products  79.4 us (15%)
  Pallas kernels  73.2 us (14%)
  starting transfers between devices  62.2 us (12%)
  local copies, waits for them, and re-layouts  46 us (9%)
  other arithmetic  20.6 us (4%)
  between operations  15.4 us (3%)
    unnamed x3, waiting for transfers between devices  103 us
    ppermute x16, waiting for transfers between devices, shifted(): return lax.ppermute(value, axis, pairs)  80.6 us
    dot_general x22, matrix products, contract(): lax.dot_general(left_side, right_side, (((left_dim,), (right_dim,)), ((),...  78.7 us
    ppermute x16, starting transfers between devices, shifted(): return lax.ppermute(value, axis, pairs)  53.3 us
    all_gather x1, waiting for transfers between devices, body(): gathered = lax.all_gather(shard, BOTH, axis=0, tiled=True)  37.7 us
    pallas_call x1, Pallas kernels, diagonal_sums(): pl.pallas_call(diagonal_kernel, out_shape=jax.ShapeDtypeStruct((heads, ti...  29 us
    pallas_call x1, Pallas kernels, attend_back(): pl.pallas_call(kernel, out_shape=(jax.ShapeDtypeStruct((width, row_count)...  22.3 us
    unnamed x124, local copies, waits for them, and re-layouts  13.4 us
  transfers between devices with their start and end apart: 23, of which 12 were waited for; matrix products, arithmetic and copies ran while one was open for 8% of the time, Pallas kernels for 8%

profile of v1, /device:TPU:0, one launch (start us, length us, event | category | flops | bytes accessed | tf_op | source)
XLA Modules:
  0.0 528.1 jit_solution(8219260912853755880)
XLA Ops:
  15.3 6.0 %collective-permute-start = (bf16[256,768]{1,0:T(8,128)(2,1)}, bf16[256,768]{1,0:T(8,128)(2,1)S(1)}, u32[]{:S(2)}, u32[]{:S(2)}) collective-permute-start(bf16[256,768]{1,0:T(8,128)(2,1)} %bitcast.135), channel_id=1, source_target_pairs={{0,16},{4,20},{8,24},{12,28},{1,17},{5,21},{9,25},{13,29},{2,18},{... | collective-permute-start | bytes 1179656 | tf_op jit(solution)/shard_map/ppermute | solution.py:304
  21.3 4.5 collective-permute-start.1
  25.7 1.3 collective-permute-start.2
  27.1 3.1 collective-permute-start.3
  30.2 1.3 collective-permute-start.4
  33.1 1.3 fusion.74
  40.5 12.2 %shard_map.229.tiles_ref = f32[12,19,128,128]{3,2,1,0:T(8,128)} custom-call(f32[12,1,2560]{2,1,0:T(1,128)} %reshape.210.line_ref), custom_call_target="tpu_custom_call" | custom-call | tf_op jit(solution)/shard_map/pallas_call | solution.py:42
  52.6 1.3 collective-permute-start.5
  54.0 1.3 collective-permute-start.6
  56.4 1.3 collective-permute-start.7
  57.9 9.5 %collective-permute-done.5 = bf16[256,768]{1,0:T(8,128)(2,1)S(1)} collective-permute-done((bf16[256,768]{1,0:T(8,128)(2,1)S(1)}, bf16[256,768]{1,0:T(8,128)(2,1)S(1)}, u32[]{:S(2)}, u32[]{:S(2)}) %collective-permute-start.5) | collective-permute-done | bytes 393248 | tf_op jit(solution)/shard_map/ppermute | solution.py:304
  67.4 29.7 %collective-permute-done.6 = bf16[256,768]{1,0:T(8,128)(2,1)S(1)} collective-permute-done((bf16[256,768]{1,0:T(8,128)(2,1)S(1)}, bf16[256,768]{1,0:T(8,128)(2,1)S(1)}, u32[]{:S(2)}, u32[]{:S(2)}) %collective-permute-start.6) | collective-permute-done | bytes 393248 | tf_op jit(solution)/shard_map/ppermute | solution.py:304
  97.2 25.1 %collective-permute-done.7 = bf16[256,768]{1,0:T(8,128)(2,1)S(1)} collective-permute-done((bf16[256,768]{1,0:T(8,128)(2,1)S(1)}, bf16[256,768]{1,0:T(8,128)(2,1)S(1)}, u32[]{:S(2)}, u32[]{:S(2)}) %collective-permute-start.7) | collective-permute-done | bytes 393248 | tf_op jit(solution)/shard_map/ppermute | solution.py:304
  122.4 1.7 copy-done.10
  124.9 37.7 %all-gather.2.cloned.1.call-done = bf16[768,9344]{1,0:T(8,128)(2,1)} async-done(((bf16[24,9344]{1,0:T(8,128)(2,1)}), bf16[768,9344]{1,0:T(8,128)(2,1)}) %all-gather.2.cloned.1.call-update) | async-done | bytes 14352400 | tf_op jit(solution)/shard_map/all_gather | solution.py:414
  162.5 1.3 convert_reduce_fusion
  163.8 2.9 fusion.2
  166.7 1.8 convolution_convert_fusion.13.query_ref.query_turned_ref
  168.5 5.8 %convolution_convert_fusion.4.key_ref = bf16[2304,768]{1,0:T(8,128)(2,1)} fusion(bf16[2304,768]{1,0:T(8,128)(2,1)S(1)} %fusion.2, bf16[768,9344]{1,0:T(8,128)(2,1)} %all-gather.2.cloned.1.call-done), kind=kOutput, calls=%fused_computation.15 | convolution fusion | flops 2719678464 | bytes 8257536 | tf_op jit(solution)/shard_map/dot_general | solution.py:346
  174.4 6.1 %convolution_convert_fusion.3.value_turned_ref = bf16[768,2304]{1,0:T(8,128)(2,1)} fusion(bf16[2304,768]{1,0:T(8,128)(2,1)S(1)} %fusion.2, bf16[768,9344]{1,0:T(8,128)(2,1)} %all-gather.2.cloned.1.call-done), kind=kOutput, calls=%fused_computation.14 | convolution fusion | flops 2719678464 | bytes 8257536 | tf_op jit(solution)/shard_map/dot_general | solution.py:346
  180.5 9.8 %shard_map.230 = (f32[768,256]{1,0:T(8,128)S(1)}, f32[3,4,256]{2,1,0:T(4,128)S(1)}) custom-call(s32[2]{0:T(128)S(1)} %get-tuple-element.33.first_ref, s32[2]{0:T(128)S(1)} %get-tuple-element.34.last_ref, bf16[768,256]{1,0:T(8,128)(2,1)S(1)} %convolution_convert_fusion.13.query_ref.query_turned_ref, bf16[2304,768]{1,0:T(8,128)(2,1)} %convolution_convert_fusion.4.key_ref, ...), custom_call_target="tpu_custom_call" | custom-call | flops 4026531840 | bytes 25165824 | tf_op jit(solution)/shard_map/pallas_call | solution.py:143
  190.3 2.2 multiply_reduce_fusion.2
  192.5 2.6 slice.296
  195.1 5.8 %fusion.6 = f32[256,4096]{1,0:T(8,128)S(1)} fusion(bf16[768,9344]{1,0:T(8,128)(2,1)} %all-gather.2.cloned.1.call-done, f32[256,768]{1,0:T(8,128)S(1)} %get-tuple-element.68, f32[768]{0:T(1024)S(1)} %get-tuple-element.24, f32[256]{0:T(256)S(1)} %add_rsqrt_fusion.2), kind=kOutput, calls=%fused_computation.10 | convolution fusion | flops 1611202560 | bytes 11276288 | tf_op jit(solution)/shard_map/dot_general | solution.py:346
  201.0 3.2 fusion.14
  204.2 2.5 multiply_reduce_fusion
  208.2 4.5 convolution_convert_fusion.2.key_turned_ref
  212.7 4.6 convolution_convert_fusion.1.value_ref
  219.9 22.3 %shard_map.231 = (bf16[768,256]{1,0:T(8,128)(2,1)}, bf16[2304,768]{1,0:T(8,128)(2,1)}, bf16[2304,768]{1,0:T(8,128)(2,1)}, f32[12,19,128,128]{3,2,1,0:T(8,128)}) custom-call(s32[2]{0:T(128)} %copy-done.7, s32[2]{0:T(128)} %copy-done.8, bf16[256,768]{1,0:T(8,128)(2,1)} %convolution_convert_fusion.12.query_ref, ...), custom_call_target="tpu_custom_call", output_to_operand_aliasing={{3}: (13, {})} | custom-call | flops 10066329600 | bytes 33554432 | tf_op jit(solution)/shard_map/pallas_call | solution.py:236
  242.1 6.3 %convolution_convert_fusion.7 = bf16[768,768]{0,1:T(8,128)(2,1)} fusion(bf16[2304,768]{1,0:T(8,128)(2,1)S(1)} %fusion.2, bf16[2304,768]{1,0:T(8,128)(2,1)} %get-tuple-element.20), kind=kOutput, calls=%fused_computation.33 | convolution fusion | flops 2718498816 | bytes 8257536 | tf_op jit(solution)/shard_map/dot_general | solution.py:346
  248.4 4.2 convolution_convert_fusion.6
  252.6 4.2 fusion.33
  256.8 6.4 %fusion.75 = (bf16[2304,768]{1,0:T(8,128)(2,1)S(1)}, f32[2304,768]{1,0:T(8,128)}) fusion(f32[2304,768]{1,0:T(8,128)S(1)} %fusion.33, bf16[2304,768]{1,0:T(8,128)(2,1)S(1)} %copy-done.11, bf16[768,9344]{1,0:T(8,128)(2,1)} %all-gather.2.cloned.1.call-done), kind=kOutput, calls=%fused_computation.195 | convolution fusion | flops 2721447936 | bytes 22413312 | tf_op jit(solution)/shard_map/dot_general | solution.py:346
  263.2 1.6 fusion.70
  266.1 10.8 %collective-permute-start.14 = (bf16[256,768]{1,0:T(8,128)(2,1)}, bf16[256,768]{1,0:T(8,128)(2,1)}, u32[]{:S(2)}, u32[]{:S(2)}) collective-permute-start(bf16[256,768]{1,0:T(8,128)(2,1)} %get-tuple-element.40), channel_id=1, source_target_pairs={{0,16},{4,20},{8,24},{12,28},{1,17},{5,21},{9,25},{13,29},{2,18},{... | collective-permute-start | bytes 1179656 | tf_op jit(solution)/shard_map/ppermute | solution.py:304
  278.1 6.2 %collective-permute-start.12 = (bf16[256,768]{1,0:T(8,128)(2,1)}, bf16[256,768]{1,0:T(8,128)(2,1)}, u32[]{:S(2)}, u32[]{:S(2)}) collective-permute-start(bf16[256,768]{1,0:T(8,128)(2,1)} %get-tuple-element.42), channel_id=1, source_target_pairs={{0,12},{4,16},{8,20},{12,24},{16,28},{1,13},{5,17},{9,21},{13,25},... | collective-permute-start | bytes 1179656 | tf_op jit(solution)/shard_map/ppermute | solution.py:304
  285.7 1.5 convolution_convert_fusion.8
  287.1 1.9 copy.51
  290.3 1.6 copy.52
  291.9 2.4 copy.53
  296.0 4.2 collective-permute-done.15
  300.1 2.0 collective-permute-start.10
  302.2 1.3 collective-permute-start.9
  303.5 9.2 %collective-permute-start.8 = (bf16[256,768]{1,0:T(8,128)(2,1)}, bf16[256,768]{1,0:T(8,128)(2,1)}, u32[]{:S(2)}, u32[]{:S(2)}) collective-permute-start(bf16[256,768]{1,0:T(8,128)(2,1)} %get-tuple-element.38), channel_id=1, source_target_pairs={{0,4},{4,8},{8,12},{12,16},{16,20},{20,24},{24,28},{1,5},{5,9},{9,... | collective-permute-start | bytes 1179656 | tf_op jit(solution)/shard_map/ppermute | solution.py:304
  313.9 1.5 copy.54
  315.4 2.4 convolution_convert_fusion.5
  317.8 10.9 %collective-permute-done.8 = bf16[256,768]{1,0:T(8,128)(2,1)} collective-permute-done((bf16[256,768]{1,0:T(8,128)(2,1)}, bf16[256,768]{1,0:T(8,128)(2,1)}, u32[]{:S(2)}, u32[]{:S(2)}) %collective-permute-start.8) | collective-permute-done | bytes 393248 | tf_op jit(solution)/shard_map/ppermute | solution.py:304
  328.8 4.9 fusion.45
  334.2 1.5 copy.50
  335.8 1.7 pad_dynamic-update-slice_fusion
  337.4 2.4 constant_dynamic-update-slice_fusion.16
  339.8 6.4 %fusion.3 = bf16[768,9344]{1,0:T(8,128)(2,1)} fusion(bf16[768,9344]{1,0:T(8,128)(2,1)} %constant_dynamic-update-slice_fusion.16, bf16[256,2048]{1,0:T(8,128)(2,1)} %copy-done.36, bf16[256,2048]{1,0:T(8,128)(2,1)} %copy-done.35, f32[256,768]{1,0:T(8,128)} %copy-done.20, f32[768]{0:T(1024)S(1)} %get-tuple-element.24, f32[256]{0:T(256)} %copy-done.32), kind=kOutput, calls=%fused_computation.6 | convolution fusion | flops 1618542592 | bytes 9179136 | tf_op jit(solution)/shard_map/dot_general | solution.py:346
  346.2 1.9 constant_dynamic-update-slice_fusion.15
  348.9 29.0 %shard_map.232 = f32[12,19,8,256]{3,2,1,0:T(8,128)} custom-call(f32[12,19,128,128]{3,2,1,0:T(8,128)} %get-tuple-element.23.tiles_ref), custom_call_target="tpu_custom_call" | custom-call | tf_op jit(solution)/shard_map/pallas_call | solution.py:292
  377.9 8.9 %fusion.71 = (f32[12,19,1,256]{3,2,1,0:T(1,128)S(1)}, f32[12,19,1,256]{3,2,1,0:T(1,128)S(1)}, f32[12,19,1,256]{3,2,1,0:T(1,128)S(1)}, f32[12,19,1,256]{3,2,1,0:T...) fusion(f32[12,19,8,256]{3,2,1,0:T(8,128)} %shard_map.232), kind=kLoop, calls=%fused_computation.191 | loop fusion | bytes 3735552 | tf_op jit(solution)/shard_map/slice | solution.py:537
  390.7 2.5 collective-permute-start.16
  393.2 1.6 collective-permute-done.16
  394.8 3.6 collective-permute-done.17
  399.0 4.0 collective-permute-done.18
  404.2 5.7 %collective-permute-start.20 = (f32[32,12]{0,1:T(8,128)S(1)}, f32[32,12]{0,1:T(8,128)S(1)}, u32[]{:S(2)}, u32[]{:S(2)}) collective-permute-start(f32[32,12]{0,1:T(8,128)S(1)} %add.202), channel_id=1, source_target_pairs={{0,2},{1,3},{2,0},{3,1},{4,6},{5,7},{6,4},{7,5},{8,10},{9,11},{10,... | collective-permute-start | bytes 4616 | tf_op jit(solution)/shard_map/ppermute | solution.py:309
  409.9 1.7 fusion.22
  413.5 102.5 %reduce-scatter.4.cloned.1.call-done = bf16[24,9344]{1,0:T(8,128)(2,1)} async-done(((bf16[768,9344]{1,0:T(8,128)(2,1)}), bf16[24,9344]{1,0:T(8,128)(2,1)}) %reduce-scatter.4.cloned.1.call-update) | async-done | bytes 448528
  517.7 1.5 fusion.73
  519.3 1.8 fusion.72
  (226 shorter events, 39.9 us)
Async XLA Ops:
  7.2 30.6 %copy-start = (f32[32,12]{0,1:T(8,128)S(1)}, f32[32,12]{0,1:T(8,128)}, u32[]{:S(2)}) copy-start(f32[32,12]{0,1:T(8,128)} %param.22) | copy-start | bytes 4612
  7.2 155.3 %all-gather.2.cloned.1.call-start = ((), (), s32[]{:S(2)}) async-start(), calls=%async_computation.1 | async-start | bytes 14800896 | tf_op jit(solution)/shard_map/all_gather | solution.py:414
  14.4 0.8 copy-start.23
  15.2 500.7 %reduce-scatter.4.cloned.1.call-start = ((), (), s32[]{:S(2)}) async-start(), calls=%async_computation.2 | async-start | bytes 14800896
  15.3 37.3 %collective-permute-start = (bf16[256,768]{1,0:T(8,128)(2,1)}, bf16[256,768]{1,0:T(8,128)(2,1)S(1)}, u32[]{:S(2)}, u32[]{:S(2)}) collective-permute-start(bf16[256,768]{1,0:T(8,128)(2,1)} %bitcast.135), channel_id=1, source_target_pairs={{0,16},{4,20},{8,24},{12,28},{1,17},{5,21},{9,25},{13,29},{2,18},{... | collective-permute-start | bytes 1179656 | tf_op jit(solution)/shard_map/ppermute | solution.py:304
  21.3 32.7 %collective-permute-start.1 = (bf16[256,768]{1,0:T(8,128)(2,1)}, bf16[256,768]{1,0:T(8,128)(2,1)S(1)}, u32[]{:S(2)}, u32[]{:S(2)}) collective-permute-start(bf16[256,768]{1,0:T(8,128)(2,1)} %bitcast.136), channel_id=1, source_target_pairs={{0,12},{4,16},{8,20},{12,24},{16,28},{1,13},{5,17},{9,21},{13,25},... | collective-permute-start | bytes 1179656 | tf_op jit(solution)/shard_map/ppermute | solution.py:304
  25.7 30.7 %collective-permute-start.2 = (bf16[256,768]{1,0:T(8,128)(2,1)}, bf16[256,768]{1,0:T(8,128)(2,1)S(1)}, u32[]{:S(2)}, u32[]{:S(2)}) collective-permute-start(bf16[256,768]{1,0:T(8,128)(2,1)} %bitcast.137), channel_id=1, source_target_pairs={{0,8},{4,12},{8,16},{12,20},{16,24},{20,28},{1,9},{5,13},{9,17},{1... | collective-permute-start | bytes 1179656 | tf_op jit(solution)/shard_map/ppermute | solution.py:304
  27.1 30.7 %collective-permute-start.3 = (bf16[256,768]{1,0:T(8,128)(2,1)}, bf16[256,768]{1,0:T(8,128)(2,1)S(1)}, u32[]{:S(2)}, u32[]{:S(2)}) collective-permute-start(bf16[256,768]{1,0:T(8,128)(2,1)} %bitcast.138), channel_id=1, source_target_pairs={{0,4},{4,8},{8,12},{12,16},{16,20},{20,24},{24,28},{1,5},{5,9},{9,... | collective-permute-start | bytes 1179656 | tf_op jit(solution)/shard_map/ppermute | solution.py:304
  30.2 27.7 %collective-permute-start.4 = (bf16[256,768]{1,0:T(8,128)(2,1)}, bf16[256,768]{1,0:T(8,128)(2,1)S(1)}, u32[]{:S(2)}, u32[]{:S(2)}) collective-permute-start(bf16[256,768]{1,0:T(8,128)(2,1)} %bitcast.139), channel_id=1, source_target_pairs={{4,0},{8,4},{12,8},{16,12},{20,16},{24,20},{28,24},{5,1},{9,5},{13... | collective-permute-start | bytes 1179656 | tf_op jit(solution)/shard_map/ppermute | solution.py:304
  35.8 2.0 copy-start.26
  37.2 181.4 %copy-start.28 = (f32[256]{0:T(256)}, f32[256]{0:T(256)S(1)}, u32[]{:S(2)}) copy-start(f32[256]{0:T(256)S(1)} %compare_convert_fusion) | copy-start | bytes 3076
  37.8 142.6 %copy-start.6 = (bf16[128,256]{1,0:T(8,128)(2,1)}, bf16[128,256]{1,0:T(8,128)(2,1)S(1)}, u32[]{:S(2)}) copy-start(bf16[128,256]{1,0:T(8,128)(2,1)S(1)} %fusion.62.query_feat_ref) | copy-start | bytes 196612
  39.2 141.3 %copy-start.2 = (bf16[2304,128]{1,0:T(8,128)(2,1)}, bf16[2304,128]{1,0:T(8,128)(2,1)S(1)}, u32[]{:S(2)}) copy-start(bf16[2304,128]{1,0:T(8,128)(2,1)S(1)} %select_convert_fusion.key_feat_ref) | copy-start | bytes 1769476
  39.7 140.7 %copy-start.7 = (s32[2]{0:T(128)}, s32[2]{0:T(128)S(1)}, u32[]{:S(2)}) copy-start(s32[2]{0:T(128)S(1)} %get-tuple-element.33.first_ref) | copy-start | bytes 28
  39.7 140.7 %copy-start.8 = (s32[2]{0:T(128)}, s32[2]{0:T(128)S(1)}, u32[]{:S(2)}) copy-start(s32[2]{0:T(128)S(1)} %get-tuple-element.34.last_ref) | copy-start | bytes 28
  40.5 12.2 %copy-start.16 = (bf16[1,256,768]{2,1,0:T(8,128)(2,1)S(1)}, bf16[1,256,768]{2,1,0:T(8,128)(2,1)}, u32[]{:S(2)}) copy-start(bf16[1,256,768]{2,1,0:T(8,128)(2,1)} %param.14) | copy-start | bytes 1179652
  52.6 14.7 %collective-permute-start.5 = (bf16[256,768]{1,0:T(8,128)(2,1)S(1)}, bf16[256,768]{1,0:T(8,128)(2,1)S(1)}, u32[]{:S(2)}, u32[]{:S(2)}) collective-permute-start(bf16[256,768]{1,0:T(8,128)(2,1)S(1)} %bitcast.140), channel_id=1, source_target_pairs={{8,0},{12,4},{16,8},{20,12},{24,16},{28,20},{9,1},{13,5},{17,9},{2... | collective-permute-start | bytes 1179656 | tf_op jit(solution)/shard_map/ppermute | solution.py:304
  54.0 43.2 %collective-permute-start.6 = (bf16[256,768]{1,0:T(8,128)(2,1)S(1)}, bf16[256,768]{1,0:T(8,128)(2,1)S(1)}, u32[]{:S(2)}, u32[]{:S(2)}) collective-permute-start(bf16[256,768]{1,0:T(8,128)(2,1)S(1)} %bitcast.141), channel_id=1, source_target_pairs={{12,0},{16,4},{20,8},{24,12},{28,16},{13,1},{17,5},{21,9},{25,13},... | collective-permute-start | bytes 1179656 | tf_op jit(solution)/shard_map/ppermute | solution.py:304
  56.4 65.9 %collective-permute-start.7 = (bf16[256,768]{1,0:T(8,128)(2,1)S(1)}, bf16[256,768]{1,0:T(8,128)(2,1)S(1)}, u32[]{:S(2)}, u32[]{:S(2)}) collective-permute-start(bf16[256,768]{1,0:T(8,128)(2,1)S(1)} %bitcast.142), channel_id=1, source_target_pairs={{16,0},{20,4},{24,8},{28,12},{17,1},{21,5},{25,9},{29,13},{18,2},{... | collective-permute-start | bytes 1179656 | tf_op jit(solution)/shard_map/ppermute | solution.py:304
  122.3 1.8 copy-start.10
  168.5 11.9 %copy-start.5 = (bf16[768,256]{1,0:T(8,128)(2,1)}, bf16[768,256]{1,0:T(8,128)(2,1)S(1)}, u32[]{:S(2)}) copy-start(bf16[768,256]{1,0:T(8,128)(2,1)S(1)} %convolution_convert_fusion.13.query_ref.query_turned_ref) | copy-start | bytes 1179652
  190.3 4.8 copy-start.3
  190.3 4.8 copy-start.9
  192.5 14.2 %copy-start.20 = (f32[256,768]{1,0:T(8,128)}, f32[256,768]{1,0:T(8,128)S(1)}, u32[]{:S(2)}) copy-start(f32[256,768]{1,0:T(8,128)S(1)} %get-tuple-element.68) | copy-start | bytes 2359300
  192.5 14.2 %copy-start.32 = (f32[256]{0:T(256)}, f32[256]{0:T(256)S(1)}, u32[]{:S(2)}) copy-start(f32[256]{0:T(256)S(1)} %add_rsqrt_fusion.2) | copy-start | bytes 3076
  195.1 5.8 %copy-start.17 = (bf16[768,2048]{1,0:T(8,128)(2,1)}, bf16[768,2048]{1,0:T(8,128)(2,1)S(1)}, u32[]{:S(2)}) copy-start(bf16[768,2048]{1,0:T(8,128)(2,1)S(1)} %slice.296) | copy-start | bytes 9437188
  195.1 5.8 %copy-start.19 = (bf16[1,256,768]{2,1,0:T(8,128)(2,1)S(1)}, bf16[1,256,768]{2,1,0:T(8,128)(2,1)}, u32[]{:S(2)}) copy-start(bf16[1,256,768]{2,1,0:T(8,128)(2,1)} %param.27) | copy-start | bytes 1179652
  195.1 9.1 %slice-start = ((s8[14352384]{0:T(1024)(128)(4,1)}), s8[4194304]{0:T(1024)(128)(4,1)S(1)}, s32[]{:S(2)}) async-start(s8[14352384]{0:T(1024)(128)(4,1)} %bitcast.167), calls=%async_computation.3 | async-start | bytes 8388608
  195.1 9.0 %slice-start.1 = ((s8[14352384]{0:T(1024)(128)(4,1)}), s8[4194304]{0:T(1024)(128)(4,1)S(1)}, s32[]{:S(2)}) async-start(s8[14352384]{0:T(1024)(128)(4,1)} %bitcast.167), calls=%async_computation.4 | async-start | bytes 8388608
  201.0 3.2 slice-start.2
  201.0 3.2 slice-start.3
  204.2 2.5 copy-start.35
  204.2 2.5 copy-start.36
  206.9 88.5 %copy-start.12 = (f32[256,768]{1,0:T(8,128)}, f32[256,768]{1,0:T(8,128)S(1)}, u32[]{:S(2)}) copy-start(f32[256,768]{1,0:T(8,128)S(1)} %multiply_add_fusion.1) | copy-start | bytes 2359300
  242.1 6.3 %copy-start.11 = (bf16[2304,768]{1,0:T(8,128)(2,1)S(1)}, bf16[2304,768]{1,0:T(8,128)(2,1)}, u32[]{:S(2)}) copy-start(bf16[2304,768]{1,0:T(8,128)(2,1)} %get-tuple-element.21) | copy-start | bytes 10616836
  248.4 4.2 copy-start.37
  263.2 22.4 %copy-start.24 = (bf16[768,256]{1,0:T(8,128)(2,1)S(1)}, bf16[768,256]{1,0:T(8,128)(2,1)}, u32[]{:S(2)}) copy-start(bf16[768,256]{1,0:T(8,128)(2,1)} %get-tuple-element.22) | copy-start | bytes 1179652
  264.8 35.4 %collective-permute-start.15 = (bf16[256,768]{1,0:T(8,128)(2,1)}, bf16[256,768]{1,0:T(8,128)(2,1)}, u32[]{:S(2)}, u32[]{:S(2)}) collective-permute-start(bf16[256,768]{1,0:T(8,128)(2,1)} %get-tuple-element.39), channel_id=1, source_target_pairs={{16,0},{20,4},{24,8},{28,12},{17,1},{21,5},{25,9},{29,13},{18,2},{... | collective-permute-start | bytes 1179656 | tf_op jit(solution)/shard_map/ppermute | solution.py:304
  266.1 36.1 %collective-permute-start.14 = (bf16[256,768]{1,0:T(8,128)(2,1)}, bf16[256,768]{1,0:T(8,128)(2,1)}, u32[]{:S(2)}, u32[]{:S(2)}) collective-permute-start(bf16[256,768]{1,0:T(8,128)(2,1)} %get-tuple-element.40), channel_id=1, source_target_pairs={{0,16},{4,20},{8,24},{12,28},{1,17},{5,21},{9,25},{13,29},{2,18},{... | collective-permute-start | bytes 1179656 | tf_op jit(solution)/shard_map/ppermute | solution.py:304
  276.8 26.6 %collective-permute-start.13 = (bf16[256,768]{1,0:T(8,128)(2,1)S(1)}, bf16[256,768]{1,0:T(8,128)(2,1)}, u32[]{:S(2)}, u32[]{:S(2)}) collective-permute-start(bf16[256,768]{1,0:T(8,128)(2,1)S(1)} %get-tuple-element.41), channel_id=1, source_target_pairs={{12,0},{16,4},{20,8},{24,12},{28,16},{13,1},{17,5},{21,9},{25,13},... | collective-permute-start | bytes 1179656 | tf_op jit(solution)/shard_map/ppermute | solution.py:304
  278.1 39.6 %collective-permute-start.12 = (bf16[256,768]{1,0:T(8,128)(2,1)}, bf16[256,768]{1,0:T(8,128)(2,1)}, u32[]{:S(2)}, u32[]{:S(2)}) collective-permute-start(bf16[256,768]{1,0:T(8,128)(2,1)} %get-tuple-element.42), channel_id=1, source_target_pairs={{0,12},{4,16},{8,20},{12,24},{16,28},{1,13},{5,17},{9,21},{13,25},... | collective-permute-start | bytes 1179656 | tf_op jit(solution)/shard_map/ppermute | solution.py:304
  284.4 33.4 %collective-permute-start.11 = (bf16[256,768]{1,0:T(8,128)(2,1)}, bf16[256,768]{1,0:T(8,128)(2,1)}, u32[]{:S(2)}, u32[]{:S(2)}) collective-permute-start(bf16[256,768]{1,0:T(8,128)(2,1)} %get-tuple-element.43), channel_id=1, source_target_pairs={{8,0},{12,4},{16,8},{20,12},{24,16},{28,20},{9,1},{13,5},{17,9},{2... | collective-permute-start | bytes 1179656 | tf_op jit(solution)/shard_map/ppermute | solution.py:304
  290.3 5.2 copy-start.4
  290.3 5.2 copy-start.29
  294.3 18.3 %copy-start.14 = (bf16[768,768]{1,0:T(8,128)(2,1)S(1)}, bf16[768,768]{1,0:T(8,128)(2,1)}, u32[]{:S(2)}) copy-start(bf16[768,768]{1,0:T(8,128)(2,1)} %copy.53) | copy-start | bytes 3538948
  294.3 19.6 %copy-start.33 = (bf16[768]{0:T(1024)(128)(2,1)S(1)}, bf16[768]{0:T(1024)(128)(2,1)}, u32[]{:S(2)}) copy-start(bf16[768]{0:T(1024)(128)(2,1)} %get-tuple-element.26) | copy-start | bytes 4612
  300.1 17.7 %collective-permute-start.10 = (bf16[256,768]{1,0:T(8,128)(2,1)}, bf16[256,768]{1,0:T(8,128)(2,1)}, u32[]{:S(2)}, u32[]{:S(2)}) collective-permute-start(bf16[256,768]{1,0:T(8,128)(2,1)} %get-tuple-element.44), channel_id=1, source_target_pairs={{0,8},{4,12},{8,16},{12,20},{16,24},{20,28},{1,9},{5,13},{9,17},{1... | collective-permute-start | bytes 1179656 | tf_op jit(solution)/shard_map/ppermute | solution.py:304
  302.2 15.6 %collective-permute-start.9 = (bf16[256,768]{1,0:T(8,128)(2,1)}, bf16[256,768]{1,0:T(8,128)(2,1)}, u32[]{:S(2)}, u32[]{:S(2)}) collective-permute-start(bf16[256,768]{1,0:T(8,128)(2,1)} %get-tuple-element.45), channel_id=1, source_target_pairs={{4,0},{8,4},{12,8},{16,12},{20,16},{24,20},{28,24},{5,1},{9,5},{13... | collective-permute-start | bytes 1179656 | tf_op jit(solution)/shard_map/ppermute | solution.py:304
  303.5 25.3 %collective-permute-start.8 = (bf16[256,768]{1,0:T(8,128)(2,1)}, bf16[256,768]{1,0:T(8,128)(2,1)}, u32[]{:S(2)}, u32[]{:S(2)}) collective-permute-start(bf16[256,768]{1,0:T(8,128)(2,1)} %get-tuple-element.38), channel_id=1, source_target_pairs={{0,4},{4,8},{8,12},{12,16},{16,20},{20,24},{24,28},{1,5},{5,9},{9,... | collective-permute-start | bytes 1179656 | tf_op jit(solution)/shard_map/ppermute | solution.py:304
  315.4 13.4 %copy-start.25 = (bf16[768,256]{1,0:T(8,128)(2,1)S(1)}, bf16[768,256]{1,0:T(8,128)(2,1)}, u32[]{:S(2)}) copy-start(bf16[768,256]{1,0:T(8,128)(2,1)} %get-tuple-element.22) | copy-start | bytes 1179652
  315.4 13.4 %copy-start.30 = (f32[256]{0:T(256)S(1)}, f32[256]{0:T(256)}, u32[]{:S(2)}) copy-start(f32[256]{0:T(256)} %add_rsqrt_fusion.1) | copy-start | bytes 3076
  389.6 20.3 %copy-start.15 = (bf16[256,2048]{1,0:T(8,128)(2,1)S(1)}, bf16[256,2048]{1,0:T(8,128)(2,1)}, u32[]{:S(2)}) copy-start(bf16[256,2048]{1,0:T(8,128)(2,1)} %get-tuple-element.37) | copy-start | bytes 3145732
  389.6 20.3 %copy-start.18 = (bf16[768,2048]{1,0:T(8,128)(2,1)S(1)}, bf16[768,2048]{1,0:T(8,128)(2,1)}, u32[]{:S(2)}) copy-start(bf16[768,2048]{1,0:T(8,128)(2,1)} %copy-done.17) | copy-start | bytes 9437188
  389.6 20.3 %copy-start.21 = (f32[256,768]{1,0:T(8,128)S(1)}, f32[256,768]{1,0:T(8,128)}, u32[]{:S(2)}) copy-start(f32[256,768]{1,0:T(8,128)} %copy-done.20) | copy-start | bytes 2359300
  390.6 21.7 %copy-start.34 = (f32[256]{0:T(256)S(1)}, f32[256]{0:T(256)}, u32[]{:S(2)}) copy-start(f32[256]{0:T(256)} %get-tuple-element.29) | copy-start | bytes 3076
  390.6 21.7 %copy-start.13 = (f32[256,768]{1,0:T(8,128)S(1)}, f32[256,768]{1,0:T(8,128)}, u32[]{:S(2)}) copy-start(f32[256,768]{1,0:T(8,128)} %copy-done.12) | copy-start | bytes 2359300
  390.6 21.7 %copy-start.22 = (f32[256,768]{1,0:T(8,128)S(1)}, f32[256,768]{1,0:T(8,128)}, u32[]{:S(2)}) copy-start(f32[256,768]{1,0:T(8,128)} %get-tuple-element.32) | copy-start | bytes 2359300
  390.6 21.7 %copy-start.31 = (f32[256]{0:T(256)S(1)}, f32[256]{0:T(256)}, u32[]{:S(2)}) copy-start(f32[256]{0:T(256)} %add_rsqrt_fusion.1) | copy-start | bytes 3076
  390.7 4.2 collective-permute-start.16
  394.8 3.7 collective-permute-start.17
  398.5 4.5 collective-permute-start.18
  403.0 1.2 collective-permute-start.19
  404.2 7.5 %collective-permute-start.20 = (f32[32,12]{0,1:T(8,128)S(1)}, f32[32,12]{0,1:T(8,128)S(1)}, u32[]{:S(2)}, u32[]{:S(2)}) collective-permute-start(f32[32,12]{0,1:T(8,128)S(1)} %add.202), channel_id=1, source_target_pairs={{0,2},{1,3},{2,0},{3,1},{4,6},{5,7},{6,4},{7,5},{8,10},{9,11},{10,... | collective-permute-start | bytes 4616 | tf_op jit(solution)/shard_map/ppermute | solution.py:309
  409.9 111.1 %copy-start.1 = (f32[32,12]{0,1:T(8,128)S(1)}, f32[32,12]{0,1:T(8,128)}, u32[]{:S(2)}) copy-start(f32[32,12]{0,1:T(8,128)} %param.22) | copy-start | bytes 4612
  (1 other events, 0.7 us)
Sparse Core Ops, SparseCore 0:
  15.4 147.1 all-gather.1
  348.3 167.5 reduce-scatter.3

commit v2 on v1

--- a/solution.py
+++ b/solution.py
@@ -11,6 +11,7 @@
 BIG = -1e30
 HIGHEST = lax.Precision.HIGHEST
 BOTH = ("seq", "dp")
+SMALL = pl.CostEstimate(flops=1, bytes_accessed=1, transcendentals=0)
 TILE = 128
 STEP = 4
 SPAN = STEP * TILE
@@ -45,6 +46,7 @@
         grid=(heads,),
         in_specs=[pl.BlockSpec((1, 1, width), lambda h: (h, 0, 0))],
         out_specs=pl.BlockSpec((1, tile_count, TILE, TILE), lambda h: (h, 0, 0, 0)),
+        cost_estimate=SMALL,
     )(lines.reshape(heads, 1, width))
 
 
@@ -276,26 +278,52 @@
     )(first, last, queries, queries_turned, keys, keys_turned, values, grads, grads_turned, outs, logs, key_feat, query_feat, tiles)
 
 
-def diagonal_kernel(tiles_ref, line_ref):
-    for index in range(tiles_ref.shape[1]):
-        tile = tiles_ref[0, index]
-        padded = jnp.concatenate([tile, jnp.zeros_like(tile)], axis=1)
-        size = TILE // 2
-        while size >= 8:
-            padded = padded[:size] + pltpu.roll(padded[size:], 2 * TILE - size, 1)
-            size //= 2
-        line_ref[0, index] = padded
-
-
-def diagonal_sums(tiles):
+def diagonal_kernel(range_ref, tiles_ref, line_ref):
+    heads, tile_count = tiles_ref.shape[:2]
+    for index in range(tile_count):
+        used = (index >= range_ref[0]) & (index < range_ref[1])
+
+        @pl.when(used)
+        def _():
+            for head in range(heads):
+                tile = tiles_ref[head, index]
+                padded = jnp.concatenate([tile, jnp.zeros_like(tile)], axis=1)
+                size = TILE // 2
+                while size >= 8:
+                    padded = padded[:size] + pltpu.roll(padded[size:], 2 * TILE - size, 1)
+                    size //= 2
+                line_ref[head, index] = padded
+
+        @pl.when(jnp.logical_not(used))
+        def _():
+            for head in range(heads):
+                line_ref[head, index] = jnp.zeros((8, 2 * TILE), F32)
+
+
+def diagonal_sums(tiles, used, chunk):
     heads, tile_count = tiles.shape[:2]
-    return pl.pallas_call(
-        diagonal_kernel,
-        out_shape=jax.ShapeDtypeStruct((heads, tile_count, 8, 2 * TILE), F32),
-        grid=(heads,),
-        in_specs=[pl.BlockSpec((1, tile_count, TILE, TILE), lambda h: (h, 0, 0, 0))],
-        out_specs=pl.BlockSpec((1, tile_count, 8, 2 * TILE), lambda h: (h, 0, 0, 0)),
-    )(tiles)
+    results = []
+    for start in range(0, heads, chunk):
+        results.append(
+            pl.pallas_call(
+                diagonal_kernel,
+                out_shape=jax.ShapeDtypeStruct((chunk, tile_count, 8, 2 * TILE), F32),
+                grid_spec=pltpu.PrefetchScalarGridSpec(
+                    num_scalar_prefetch=1,
+                    grid=(1,),
+                    in_specs=[
+                        pl.BlockSpec(
+                            (chunk, tile_count, TILE, TILE),
+                            functools.partial(lambda first, h, r: (first, 0, 0, 0), start // chunk),
+                        )
+                    ],
+                    out_specs=pl.BlockSpec((chunk, tile_count, 8, 2 * TILE), lambda h, r: (0, 0, 0, 0)),
+                ),
+                cost_estimate=SMALL,
+                compiler_params=pltpu.CompilerParams(vmem_limit_bytes=40 << 20),
+            )(used, tiles)
+        )
+    return jnp.concatenate(results, axis=0)
 
 
 def shifted(value, axis, steps):
@@ -304,32 +332,286 @@
     return lax.ppermute(value, axis, pairs)
 
 
-def swapped(value, axis, bit):
-    count = lax.axis_size(axis)
-    return lax.ppermute(value, axis, [(source, source ^ bit) for source in range(count)])
-
-
-def sum_everywhere(value):
-    for axis in BOTH:
-        count = lax.axis_size(axis)
-        if count & (count - 1):
-            value = lax.psum(value, axis)
-            continue
-        bit = 1
-        while bit < count:
-            value = value + swapped(value, axis, bit)
-            bit *= 2
+def flat_swap(value, mask):
+    count = lax.axis_size("seq") * lax.axis_size("dp")
+    return lax.ppermute(value, BOTH, [(source, source ^ mask) for source in range(count)])
+
+
+def groups_of(low, bits):
+    groups = []
+    if bits % 2:
+        groups.append((low, 1))
+        low, bits = low + 1, bits - 1
+    while bits:
+        groups.append((low, 2))
+        low, bits = low + 2, bits - 2
+    return groups
+
+
+def bits_of(count):
+    bits = count.bit_length() - 1
+    assert count == 1 << bits
+    return bits
+
+
+def all_groups(count):
+    return [(0, 1)] + groups_of(1, bits_of(count) - 1)
+
+
+def tie(*values):
+    return lax.optimization_barrier(values)
+
+
+def swaps(piece, group):
+    low, bits = group
+    return [flat_swap(piece, step << low) for step in range(1, 1 << bits)]
+
+
+def swap_masks(masks, group):
+    low, bits = group
+    return [mask ^ (step << low) for step in range(1, 1 << bits) for mask in masks]
+
+
+def stack_kernel(*refs):
+    target = refs[-1]
+    start = 0
+    for source in refs[:-1]:
+        target[start : start + source.shape[0]] = source[...]
+        start += source.shape[0]
+
+
+def stacked(pieces):
+    if len(pieces) == 1:
+        return pieces[0]
+    count = sum(piece.shape[0] for piece in pieces)
+    return pl.pallas_call(
+        stack_kernel,
+        out_shape=jax.ShapeDtypeStruct((count,) + pieces[0].shape[1:], pieces[0].dtype),
+        in_specs=[pl.BlockSpec(memory_space=pltpu.VMEM)] * len(pieces),
+        out_specs=pl.BlockSpec(memory_space=pltpu.VMEM),
+        cost_estimate=SMALL,
+        compiler_params=pltpu.CompilerParams(vmem_limit_bytes=40 << 20),
+    )(*pieces)
+
+
+def units_kernel(rank_ref, gate_ref, up_ref, units_ref, *, dp_count):
+    left = lax.broadcasted_iota(jnp.int32, (gate_ref.shape[0], TILE), 1) < TILE // 2
+    for side, source in enumerate((gate_ref, up_ref)):
+        span = source.shape[1] // dp_count
+        for owner in range(dp_count):
+            for pair in range(span // TILE):
+                halves_of = []
+                for odd in range(2):
+                    unit = (2 * pair + odd) * dp_count + owner
+                    tile = source[:, unit // 2 * TILE : (unit // 2 + 1) * TILE]
+                    halves_of.append(tile if unit % 2 == odd else pltpu.roll(tile, TILE // 2, 1))
+                start = side * span + pair * TILE
+                merged = jnp.where(left, halves_of[0], halves_of[1])
+                units_ref[rank_ref[0] ^ owner, :, start : start + TILE] = merged.astype(BF16)
+
+
+def units_of(gate_weight, up_weight, dp_rank, dp_count, seq_count, unit):
+    rows, hidden_width = gate_weight.shape
+    share = seq_count * unit
+    if unit != TILE // 2 or rows % 8:
+        both = jnp.stack([gate_weight.astype(BF16), up_weight.astype(BF16)], axis=1)
+        both = both.reshape(rows, 2, seq_count, dp_count, unit)
+        taken = [
+            lax.dynamic_index_in_dim(both, dp_rank ^ mask, 3, keepdims=False).reshape(rows, 2 * share)
+            for mask in range(dp_count)
+        ]
+        return jnp.stack(taken)
+    return pl.pallas_call(
+        functools.partial(units_kernel, dp_count=dp_count),
+        out_shape=jax.ShapeDtypeStruct((dp_count, rows, 2 * share), BF16),
+        in_specs=[pl.BlockSpec(memory_space=pltpu.SMEM)] + [pl.BlockSpec(memory_space=pltpu.VMEM)] * 2,
+        out_specs=pl.BlockSpec(memory_space=pltpu.VMEM),
+    )(dp_rank[None].astype(jnp.int32), gate_weight, up_weight)
+
+
+def columns_kernel(rank_ref, *refs, dp_count):
+    sources, (gate_ref, up_ref), scratch = refs[:dp_count], refs[dp_count : dp_count + 2], refs[-1]
+    for mask in range(dp_count):
+        scratch[rank_ref[0] ^ mask] = sources[mask][...].astype(F32)
+    left = lax.broadcasted_iota(jnp.int32, (gate_ref.shape[0], TILE), 1) < TILE // 2
+    for side, target in enumerate((gate_ref, up_ref)):
+        span = target.shape[1] // dp_count
+        for tile in range(target.shape[1] // TILE):
+            halves_of = []
+            for odd in range(2):
+                group, owner = divmod(2 * tile + odd, dp_count)
+                start = side * span + group // 2 * TILE
+                part = scratch[owner, :, start : start + TILE]
+                halves_of.append(part if group % 2 == odd else pltpu.roll(part, TILE // 2, 1))
+            target[:, tile * TILE : (tile + 1) * TILE] = jnp.where(left, halves_of[0], halves_of[1])
+
+
+def columns_of(parts, dp_rank, dp_count, seq_count, unit):
+    rows = parts[0].shape[0]
+    hidden_width = seq_count * dp_count * unit
+    if unit != TILE // 2 or rows % 8:
+        both = jnp.stack(parts)
+        both = jnp.stack(
+            [lax.dynamic_index_in_dim(both, dp_rank ^ index, 0, keepdims=False) for index in range(dp_count)], axis=1
+        )
+        both = both.reshape(rows, dp_count, 2, seq_count, unit).transpose(0, 2, 3, 1, 4)
+        both = both.reshape(rows, 2, hidden_width).astype(F32)
+        return both[:, 0], both[:, 1]
+    return pl.pallas_call(
+        functools.partial(columns_kernel, dp_count=dp_count),
+        out_shape=(jax.ShapeDtypeStruct((rows, hidden_width), F32),) * 2,
+        in_specs=[pl.BlockSpec(memory_space=pltpu.SMEM)] + [pl.BlockSpec(memory_space=pltpu.VMEM)] * dp_count,
+        out_specs=(pl.BlockSpec(memory_space=pltpu.VMEM),) * 2,
+        scratch_shapes=[pltpu.VMEM((dp_count,) + parts[0].shape, F32)],
+        cost_estimate=SMALL,
+    )(dp_rank[None].astype(jnp.int32), *parts)
+
+
+def shard_kernel(*refs):
+    target = refs[-1]
+    start = 0
+    for source in refs[:-1]:
+        columns = source.shape[1]
+        target[:, start : start + columns] = source[...].astype(BF16)
+        start += columns
+
+
+def side_by_side(arrays):
+    columns = sum(array.shape[1] for array in arrays)
+    return pl.pallas_call(
+        shard_kernel,
+        out_shape=jax.ShapeDtypeStruct((arrays[0].shape[0], columns), BF16),
+        in_specs=[pl.BlockSpec(memory_space=pltpu.VMEM)] * len(arrays),
+        out_specs=pl.BlockSpec(memory_space=pltpu.VMEM),
+        cost_estimate=SMALL,
+        compiler_params=pltpu.CompilerParams(vmem_limit_bytes=40 << 20),
+    )(*arrays)
+
+
+def norm_kernel(gain_ref, *refs):
+    target = refs[-1]
+    gain = gain_ref[...].astype(F32).T[:1]
+    start = 0
+    for source in refs[:-1]:
+        rows = source[...].astype(F32)
+        scale = lax.rsqrt(jnp.mean(rows * rows, axis=1, keepdims=True) + EPSILON)
+        target[start : start + source.shape[0]] = (rows * scale * gain).astype(BF16)
+        start += source.shape[0]
+
+
+def normed_rows_of(pieces, weights, block):
+    rows, width = pieces[0].shape
+    return pl.pallas_call(
+        norm_kernel,
+        out_shape=jax.ShapeDtypeStruct((len(pieces) * rows, width), BF16),
+        grid=(1,),
+        in_specs=[pl.BlockSpec((width, TILE), lambda k: (0, block))]
+        + [pl.BlockSpec((rows, width), lambda k: (0, 0))] * len(pieces),
+        out_specs=pl.BlockSpec((len(pieces) * rows, width), lambda k: (0, 0)),
+        compiler_params=pltpu.CompilerParams(vmem_limit_bytes=40 << 20),
+    )(weights, *pieces)
+
+
+def place_kernel(rank_ref, *refs, masks):
+    target = refs[-1]
+    rank = rank_ref[0]
+    for source, part in zip(refs, masks):
+        for index, mask in enumerate(part):
+            target[rank ^ mask] = source[index]
+
+
+def placed(held, masks, rank):
+    count = sum(len(part) for part in masks)
+    shape = held[0].shape[1:]
+    return pl.pallas_call(
+        functools.partial(place_kernel, masks=masks),
+        out_shape=jax.ShapeDtypeStruct((count,) + shape, held[0].dtype),
+        in_specs=[pl.BlockSpec(memory_space=pltpu.SMEM)] + [pl.BlockSpec(memory_space=pltpu.VMEM)] * len(held),
+        out_specs=pl.BlockSpec(memory_space=pltpu.VMEM),
+        cost_estimate=SMALL,
+        compiler_params=pltpu.CompilerParams(vmem_limit_bytes=40 << 20),
+    )(rank[None].astype(jnp.int32), *held)
+
+
+def place_far_kernel(rank_ref, source_ref, pair_ref, down_ref, *, dp_count):
+    for owner in range(source_ref.shape[0]):
+        for entry in range(dp_count):
+            pair_ref[owner * dp_count + (rank_ref[0] ^ entry)] = source_ref[owner, entry]
+        for entry in range(dp_count // 2):
+            down_ref[owner, entry] = source_ref[owner, dp_count + entry]
+
+
+def place_far(held, dp_rank, dp_count):
+    count = held.shape[0]
+    shape = held.shape[2:]
+    return pl.pallas_call(
+        functools.partial(place_far_kernel, dp_count=dp_count),
+        out_shape=(
+            jax.ShapeDtypeStruct((count * dp_count,) + shape, held.dtype),
+            jax.ShapeDtypeStruct((count, dp_count // 2) + shape, held.dtype),
+        ),
+        in_specs=[pl.BlockSpec(memory_space=pltpu.SMEM), pl.BlockSpec(memory_space=pltpu.VMEM)],
+        out_specs=(pl.BlockSpec(memory_space=pltpu.VMEM), pl.BlockSpec(memory_space=pltpu.VMEM)),
+        cost_estimate=SMALL,
+        compiler_params=pltpu.CompilerParams(vmem_limit_bytes=40 << 20),
+    )(dp_rank[None].astype(jnp.int32), held)
+
+
+def split_and_swap(held, mine, group):
+    low, bits = group
+    held = held.reshape((-1, 1 << bits) + held.shape[1:])
+    kept = lax.dynamic_index_in_dim(held, mine, 1, keepdims=False)
+    got = [
+        flat_swap(lax.dynamic_index_in_dim(held, mine ^ step, 1, keepdims=False), step << low)
+        for step in range(1, 1 << bits)
+    ]
+    return kept, got
+
+
+def joined(kept, got):
+    return kept.astype(F32) + sum(piece.astype(F32) for piece in got)
+
+
+def spread_dp(parts, bits):
+    held = {(mask, 0): part for mask, part in parts.items()}
+    for bit in range(bits):
+        step = 1 << bit
+        keys = sorted(key for key in held if key[0] & step)
+        sent = flat_swap(jnp.stack([held[key] for key in keys]), step)
+        held = {key: part for key, part in held.items() if not key[0] & step}
+        held.update({(goal ^ step, source ^ step): sent[k] for k, (goal, source) in enumerate(keys)})
+    return [held[(0, mask)] for mask in range(1 << bits)]
+
+
+def gather_dp(value, bits):
+    held = {0: value}
+    for bit in range(bits - 1, -1, -1):
+        held.update({mask ^ (1 << bit): flat_swap(piece, 1 << bit) for mask, piece in list(held.items())})
+    return [held[mask] for mask in range(1 << bits)]
+
+
+def scatter_dp(parts, bits):
+    held = dict(enumerate(parts))
+    for bit in range(bits):
+        step = 1 << bit
+        held = {
+            mask: piece.astype(F32) + flat_swap(held[mask ^ step].astype(BF16), step).astype(F32)
+            for mask, piece in held.items()
+            if not mask & step
+        }
+    return held[0]
+
+
+def sum_everywhere(value, groups):
+    for group in groups:
+        value = sum_in_pairs([value] + swaps(value, group))
     return value
 
 
-def rows_of(value, rows):
-    height, width = value.shape
-    columns = height * width // rows
-    if height % 8 or rows % 8 or width % TILE or columns % TILE:
-        return value.reshape(rows, columns)
-    tiles = value.reshape(height // 8, 8, width // TILE, TILE).transpose(0, 2, 1, 3)
-    tiles = tiles.reshape(rows // 8, columns // TILE, 8, TILE).transpose(0, 2, 1, 3)
-    return tiles.reshape(rows, columns)
+def sum_in_pairs(values):
+    while len(values) > 1:
+        values = [values[k] + values[k + 1] for k in range(0, len(values), 2)]
+    return values[0]
 
 
 def parts_of(value, parts, to_rows):
@@ -391,36 +673,72 @@
     center = reach * query_blocks + query_blocks - 1
     pairs = 2 if window <= 2304 else 1
 
+    dp_count = lax.axis_size("dp")
+    dp_rank = lax.axis_index("dp")
+    dp_bits = bits_of(dp_count)
+    rank = seq_rank * dp_count + dp_rank
+    groups = all_groups(device_count)
     own = blocks[0]
-    near = [shifted(own, "seq", -step) for step in range(1, reach + 1)]
-    far = [shifted(own, "seq", step) for step in range(1, reach + 1)]
-    window_blocks_low = jnp.concatenate(far[::-1] + [own] + near, axis=0)
-
-    gains = jnp.stack([first_gain.astype(BF16), second_gain.astype(BF16)], axis=1)
-    gains = jnp.pad(gains, ((0, 0), (0, TILE - 2)))
-    shard = jnp.concatenate(
-        [
-            query_weight.astype(BF16),
-            key_weight.astype(BF16),
-            value_weight.astype(BF16),
-            gains,
-            output_weight.astype(BF16),
-            gate_weight.astype(BF16),
-            up_weight.astype(BF16),
-            rows_of(down_weight.astype(BF16), shard_rows),
-        ],
-        axis=1,
-    )
-    gathered = lax.all_gather(shard, BOTH, axis=0, tiled=True)
-    down_columns = down_weight.shape[0] * width // shard_rows
-    places = [width, width, width, TILE, width, 2 * hidden_width, down_columns]
-    cuts = []
-    start = 0
-    for place in places:
-        cuts.append(gathered[:, start : start + place])
-        start += place
-    weight_query, weight_key, weight_value, gain_columns, weight_output, weight_pair, weight_down = cuts
-    weight_down = parts_of(weight_down, device_count, down_weight.shape[0])
+
+    gains = jnp.pad(jnp.stack([first_gain, second_gain], axis=1), ((0, 0), (0, TILE - 2)))
+    near_shard = side_by_side([query_weight, key_weight, value_weight, output_weight, gains])
+
+    unit = down_weight.shape[0]
+    share = seq_count * unit
+    pair_units = units_of(gate_weight, up_weight, dp_rank, dp_count, seq_count, unit)
+
+    line_width = (tile_count + 1) * TILE
+    ahead = (tile_count - center) * TILE - (max_length - 1)
+    behind = line_width - ahead - bucket_table.shape[0]
+    bucket_line = jnp.pad(bucket_table[::-1], (max(ahead, 0), max(behind, 0)), mode="edge")
+    bucket_line = bucket_line[max(-ahead, 0) : max(-ahead, 0) + line_width]
+    bucket_ids = jnp.arange(bucket_count, dtype=jnp.int32)
+    line_hot = (bucket_line[None, :] == bucket_ids[:, None]).astype(F32)
+    lines = lax.dot_general(table_weight, line_hot, (((0,), (0,)), ((), ())), precision=HIGHEST)
+
+    order = groups[::-1]
+    near_shard = near_shard[None]
+    masks = [0]
+    around = {0: own}
+    near_held = near_shard
+    stages = len(order)
+    for stage, group in enumerate(order):
+        got = swaps(near_held, group)
+        last = stage == stages - 1
+        moves = [step for step in range(1, reach + 1) if step == stage + 1 or (last and step > stage)]
+        arrived = {}
+        for step in moves:
+            arrived[step] = shifted(own, "seq", step)
+            arrived[-step] = shifted(own, "seq", -step)
+        got_masks = swap_masks(masks, group)
+        if last:
+            held, masks = [near_held] + got, [masks] + [
+                got_masks[k * len(masks) : (k + 1) * len(masks)] for k in range(len(got))
+            ]
+        else:
+            if stage == 0:
+                lines = tie(lines, got[0])[0]
+            if stage == 1:
+                tiles = bias_tiles(lines, tile_count)
+                near_held, got, arrived, tiles = tie(near_held, got, arrived, tiles)
+            else:
+                near_held, got, arrived = tie(near_held, got, arrived)
+            near_held = stacked([near_held] + got)
+            masks = masks + got_masks
+        around.update(arrived)
+    near_full = placed(held, masks, rank)
+    near_full = near_full.reshape(device_count * shard_rows, 4 * width + TILE)
+    weight_query = near_full[:, :width]
+    weight_key = near_full[:, width : 2 * width]
+    weight_value = near_full[:, 2 * width : 3 * width]
+    weight_output = near_full[:, 3 * width : 4 * width]
+    gain_columns = near_full[:, 4 * width :]
+
+    pair_parts = spread_dp({mask: pair_units[mask] for mask in range(dp_count)}, dp_bits)
+    down_parts = parts_of(down_weight.astype(BF16), 1, shard_rows * dp_count // 2)
+    down_parts = down_parts.reshape(dp_count // 2, shard_rows, 2 * share)
+    far_shard = stacked([part[None] for part in pair_parts] + [down_parts])
+    far_held = lax.all_gather(tie(far_shard, around)[0], "seq", axis=0, tiled=False)
     gain_one = gain_columns[:, 0].astype(F32)[None, :]
     gain_two = gain_columns[:, 1].astype(F32)[None, :]
 
@@ -454,19 +772,10 @@
     first = jnp.minimum(first, window_blocks - steps * STEP).astype(jnp.int32)
     steps = steps.astype(jnp.int32)
 
-    line_width = (tile_count + 1) * TILE
-    ahead = (tile_count - center) * TILE - (max_length - 1)
-    behind = line_width - ahead - bucket_table.shape[0]
-    bucket_line = jnp.pad(bucket_table[::-1], (max(ahead, 0), max(behind, 0)), mode="edge")
-    bucket_line = bucket_line[max(-ahead, 0) : max(-ahead, 0) + line_width]
-    bucket_ids = jnp.arange(bucket_count, dtype=jnp.int32)
-    line_hot = (bucket_line[None, :] == bucket_ids[:, None]).astype(F32)
-    lines = lax.dot_general(table_weight, line_hot, (((0,), (0,)), ((), ())), precision=HIGHEST)
-    tiles = bias_tiles(lines, tile_count)
-
-    window_rows = window_blocks_low.astype(F32)
-    window_scale = lax.rsqrt(jnp.mean(window_rows * window_rows, axis=1, keepdims=True) + EPSILON)
-    window_normed = (window_rows * window_scale * gain_one).astype(BF16)
+
+    window_normed = normed_rows_of(
+        [around[-step] for step in range(-reach, reach + 1)], near_full, 4 * width // TILE
+    )
     own_slice = slice(reach * row_count, (reach + 1) * row_count)
     tokens = own.astype(F32)
     scale_one = lax.rsqrt(jnp.mean(tokens * tokens, axis=1, keepdims=True) + EPSILON)
@@ -477,24 +786,30 @@
     outs, logs = attend(
         first, steps, queries_turned, keys, values_turned, key_feat, query_feat, tiles, head_dim, pairs
     )
+    far_full = place_far(tie(far_held, outs)[0], dp_rank, dp_count)
+    weight_pair = far_full[0].reshape(device_count * shard_rows, 2 * share)
+    weight_down = parts_of(far_full[1].reshape(-1, 2 * share), seq_count, unit)
     attended = (outs * valid_rows[None, :]).astype(BF16)
     middle = tokens + contract(attended, weight_output, 0, 0)
 
     scale_two = lax.rsqrt(jnp.mean(middle * middle, axis=1, keepdims=True) + EPSILON)
     second = middle * scale_two
     second_low = (second * gain_two).astype(BF16)
-    both_ways = contract(second_low, weight_pair, 1, 0)
-    gate_values, upward = both_ways[:, :hidden_width], both_ways[:, hidden_width:]
+    every_second = jnp.concatenate(gather_dp(second_low, dp_bits), axis=0)
+    every_grad = jnp.concatenate(gather_dp(cotangent[0], dp_bits), axis=0)
+    both_ways = contract(every_second, weight_pair, 1, 0)
+    gate_values, upward = both_ways[:, :share], both_ways[:, share:]
     active, slope = gelu_pair(gate_values)
     hidden = (active * upward).astype(BF16)
-    output = middle + contract(hidden, weight_down, 1, 0)
-    grad_out = cotangent[0]
-    grad_hidden = contract(grad_out, weight_down, 1, 1)
+    grad_hidden = contract(every_grad, weight_down, 1, 1)
     grad_pair = jnp.concatenate(
         [(grad_hidden * upward * slope).astype(BF16), (grad_hidden * active).astype(BF16)], axis=1
     )
-    grad_second = contract(grad_pair, weight_pair, 1, 1)
-    grad_gain_two = jnp.sum(grad_second * second, axis=0)
+    every_back = contract(grad_pair, weight_pair, 1, 1).astype(BF16)
+    grad_second = scatter_dp(jnp.split(every_back, dp_count, axis=0), dp_bits)
+    every_out = contract(hidden, weight_down, 1, 0).astype(BF16)
+    output = middle + scatter_dp(jnp.split(every_out, dp_count, axis=0), dp_bits)
+    grad_out = cotangent[0]
     scaled = grad_second * gain_two
     grad_middle = grad_out.astype(F32) + scale_two * (
         scaled - second * jnp.mean(scaled * second, axis=1, keepdims=True)
@@ -504,9 +819,21 @@
     grad_mixed_turned = (
         contract(weight_output, grad_branch, 1, 1).astype(BF16).astype(F32) * valid_rows[None, :]
     ).astype(BF16)
-    grad_down = contract(hidden, grad_out, 0, 0).astype(BF16)
-    grad_pair_weight = contract(second_low, grad_pair, 0, 0).astype(BF16)
     grad_output_weight = contract(attended, grad_branch, 1, 0).astype(BF16)
+    grad_down = contract(hidden, every_grad, 0, 0).astype(BF16)
+    grad_down = parts_of(grad_down, seq_count, shard_rows * dp_count // 2)
+    grad_pair_weight = contract(every_second, grad_pair, 0, 0).astype(BF16)
+    far_grads = jnp.concatenate(
+        [
+            grad_pair_weight.reshape(seq_count, dp_count, shard_rows, 2 * share),
+            grad_down.reshape(seq_count, dp_count // 2, shard_rows, 2 * share),
+        ],
+        axis=1,
+    )
+    far_grads, grad_mixed, grad_mixed_turned, grad_output_weight = tie(
+        far_grads, grad_mixed, grad_mixed_turned, grad_output_weight
+    )
+    far_sum = lax.psum_scatter(far_grads, "seq", scatter_dimension=0, tiled=True)[0]
 
     queries = contract(normed_own, weight_query, 1, 0).astype(BF16)
     keys_turned = contract(weight_key, window_normed, 0, 1).astype(BF16)
@@ -517,23 +844,60 @@
     )
     partial = contract(grad_keys, weight_key, 1, 1) + contract(grad_values, weight_value, 1, 1)
     partial_low = partial.astype(BF16)
-    grad_normed = partial[own_slice] + contract(grad_queries, weight_query, 0, 1)
-    for step in range(1, reach + 1):
-        ahead_part = partial_low[(reach + step) * row_count : (reach + step + 1) * row_count]
-        behind_part = partial_low[(reach - step) * row_count : (reach - step + 1) * row_count]
-        grad_normed = grad_normed + shifted(ahead_part, "seq", step).astype(F32)
-        grad_normed = grad_normed + shifted(behind_part, "seq", -step).astype(F32)
+
+    def returned_from(low_rows, step):
+        parts = []
+        for turn in (step, -step):
+            part = low_rows[(reach + turn) * row_count : (reach + turn + 1) * row_count]
+            parts.append(shifted(part, "seq", turn))
+        return parts
+
+    steps_left = list(range(1, reach + 1))
+    returned = []
+    partial_low, grad_queries, grad_keys, grad_values, tile_sums = tie(
+        partial_low, grad_queries, grad_keys, grad_values, tile_sums
+    )
+    tile_first = first - jnp.arange(query_blocks, dtype=jnp.int32) + (query_blocks - 1)
+    used = jnp.stack([jnp.min(tile_first), jnp.max(tile_first + steps * STEP)])
+    sums = diagonal_sums(tile_sums, used, 4)
+    for step in (steps_left.pop(0), steps_left.pop(-1)) if reach > 1 else steps_left:
+        returned += returned_from(partial_low, step)
     grad_query_weight = contract(normed_own, grad_queries, 0, 1).astype(BF16)
     grad_key_weight = contract(window_normed, grad_keys, 0, 0).astype(BF16)
     grad_value_weight = contract(window_normed, grad_values, 0, 0).astype(BF16)
+    near_grads = jnp.concatenate([grad_query_weight, grad_key_weight, grad_value_weight, grad_output_weight], axis=1)
+    near_held = near_grads.reshape(device_count, shard_rows, 4 * width)
+    for stage, (low, bits) in enumerate(groups):
+        kept, got = split_and_swap(near_held, (rank >> low) & ((1 << bits) - 1), (low, bits))
+        arrived = []
+        if stage and steps_left:
+            last_stage = stage == len(groups) - 1
+            for step in list(steps_left) if last_stage else steps_left[:1]:
+                steps_left.remove(step)
+                arrived += returned_from(partial_low, step)
+        if stage == 0:
+            kept, got, returned, partial_low, sums = tie(kept, got, returned, partial_low, sums)
+        elif stage == 1:
+            kept, got, arrived, partial_low, far_sum = tie(kept, got, arrived, partial_low, far_sum)
+        else:
+            kept, got, arrived, partial_low = tie(kept, got, arrived, partial_low)
+        returned = returned + arrived
+        total = joined(kept, got)
+        near_held = total.astype(BF16)
+    near_sum = total.reshape(shard_rows, 4 * width)
+    grad_normed = partial[own_slice] + contract(grad_queries, weight_query, 0, 1)
+    grad_normed = grad_normed + sum(piece.astype(F32) for piece in returned)
+    pair_back = spread_dp(
+        {mask: lax.dynamic_index_in_dim(far_sum, dp_rank ^ mask, 0, keepdims=False) for mask in range(dp_count)}, dp_bits
+    )
+    grad_gate_own, grad_up_own = columns_of(pair_back, dp_rank, dp_count, seq_count, unit)
+    grad_down_own = parts_of(far_sum[dp_count:].astype(F32).reshape(-1, 2 * share), 1, unit)
     normed_rows = tokens * scale_one
-    grad_gain_one = jnp.sum(grad_normed * normed_rows, axis=0)
     scaled_one = grad_normed * gain_one
     grad_blocks = grad_middle + scale_one * (
         scaled_one - normed_rows * jnp.mean(scaled_one * normed_rows, axis=1, keepdims=True)
     )
 
-    sums = diagonal_sums(tile_sums)
     diagonals = sum(jnp.roll(sums[:, :, row], -row, axis=2) for row in range(8))
     flipped = bucket_line.reshape(tile_count + 1, TILE)[::-1]
     bucket_at = jnp.concatenate([flipped[:-1], flipped[1:]], axis=1).reshape(-1)
@@ -541,41 +905,28 @@
     grad_table = lax.dot_general(
         bucket_hot, diagonals.reshape(heads, -1), (((0,), (1,)), ((), ())), precision=HIGHEST
     )
-    grad_table = sum_everywhere(grad_table)
-
-    grad_gains = jnp.stack([grad_gain_one, grad_gain_two], axis=1).astype(BF16)
-    grad_gains = jnp.pad(grad_gains, ((0, 0), (0, TILE - 2)))
-    grads = jnp.concatenate(
-        [
-            grad_query_weight,
-            grad_key_weight,
-            grad_value_weight,
-            grad_gains,
-            grad_output_weight,
-            grad_pair_weight,
-            parts_of(grad_down, device_count, shard_rows),
-        ],
-        axis=1,
-    )
-    summed = lax.psum_scatter(grads, BOTH, scatter_dimension=0, tiled=True).astype(F32)
-    pieces = []
-    start = 0
-    for place in [width, width, width, TILE, width, hidden_width, hidden_width, down_columns]:
-        pieces.append(summed[:, start : start + place])
-        start += place
+    grad_table = sum_everywhere(grad_table, [(bit, 1) for bit in range(bits_of(device_count))])
+
+    def gain_grad(gain, weights, grads):
+        total = sum(jnp.sum(weight.astype(BF16).astype(F32) * grad, axis=1) for weight, grad in zip(weights, grads))
+        return total / gain.astype(BF16).astype(F32)
+
+    near_parts = [near_sum[:, k * width : (k + 1) * width] for k in range(4)]
+    grad_gain_one = gain_grad(first_gain, (query_weight, key_weight, value_weight), near_parts[:3])
+    grad_gain_two = gain_grad(second_gain, (gate_weight, up_weight), (grad_gate_own, grad_up_own))
     return (
         output.astype(BF16)[None],
         grad_blocks[None],
-        pieces[3][:, 0],
-        pieces[0],
-        pieces[1],
-        pieces[2],
-        pieces[4],
+        grad_gain_one,
+        near_parts[0],
+        near_parts[1],
+        near_parts[2],
+        near_parts[3],
         grad_table,
-        pieces[3][:, 1],
-        pieces[5],
-        pieces[6],
-        rows_of(pieces[7], down_weight.shape[0]),
+        grad_gain_two,
+        grad_gate_own,
+        grad_up_own,
+        grad_down_own,
     )
 
 

time: 535 us -> 413 us (0.77)
  the two profiles are of different devices: /device:TPU:0 before, /device:TPU:4 now
where the time goes in v2:
time: 413 us; the launch traced here: 408 us
  waiting for transfers between devices  102 us (25%)
  starting transfers between devices  82.6 us (20%)
  Pallas kernels  73.6 us (18%)
  matrix products  59.7 us (14%)
  local copies, waits for them, and re-layouts  41.9 us (10%)
  other arithmetic  32.6 us (8%)
  between operations  15.7 us (4%)
    dot_general x22, matrix products, contract(): lax.dot_general(left_side, right_side, (((left_dim,), (right_dim,)), ((),...  59 us
    ppermute x16, waiting for transfers between devices, shifted(): return lax.ppermute(value, axis, pairs)  54.4 us
    ppermute x16, starting transfers between devices, shifted(): return lax.ppermute(value, axis, pairs)  43.1 us
    ppermute x35, waiting for transfers between devices, flat_swap(): lax.ppermute(value, BOTH, [(source, source ^ mask) for source in range(co...  40.3 us
    ppermute x35, starting transfers between devices, flat_swap(): lax.ppermute(value, BOTH, [(source, source ^ mask) for source in range(co...  39.2 us
    pallas_call x1, Pallas kernels, attend_back(): pl.pallas_call(kernel, out_shape=(jax.ShapeDtypeStruct((width, row_count)...  24.2 us
    unnamed x143, local copies, waits for them, and re-layouts  18.6 us
    pallas_call x3, Pallas kernels, diagonal_sums(): pl.pallas_call(diagonal_kernel, out_shape=jax.ShapeDtypeStruct((chunk, ti...  16.2 us
  transfers between devices with their start and end apart: 53, of which 18 were waited for; matrix products, arithmetic and copies ran while one was open for 19% of the time, Pallas kernels for 12%

profile of v2, /device:TPU:4, one launch (start us, length us, event | category | flops | bytes accessed | tf_op | source)
XLA Modules:
  0.0 407.6 jit_solution(17408705702918752209)
XLA Ops:
  7.2 1.9 collective-permute-start.3
  9.2 4.8 %collective-permute-start.4 = (bf16[256,768]{1,0:T(8,128)(2,1)}, bf16[256,768]{1,0:T(8,128)(2,1)S(1)}, u32[]{:S(2)}, u32[]{:S(2)}) collective-permute-start(bf16[256,768]{1,0:T(8,128)(2,1)} %bitcast.175), channel_id=1, source_target_pairs={{0,4},{4,8},{8,12},{12,16},{16,20},{20,24},{24,28},{1,5},{5,9},{9,... | collective-permute-start | bytes 1179656 | tf_op jit(solution)/shard_map/ppermute | solution.py:332
  22.8 1.8 shard_map.236
  28.4 5.7 %collective-permute-done.1.refs_2_ = bf16[1,24,3200]{2,1,0:T(8,128)(2,1)S(1)} collective-permute-done((bf16[1,24,3200]{2,1,0:T(8,128)(2,1)S(1)}, bf16[1,24,3200]{2,1,0:T(8,128)(2,1)S(1)}, u32[]{:S(2)}, u32[]{:S(2)}) %collective-permute-start.1) | collective-permute-done | bytes 153632 | tf_op jit(solution)/shard_map/ppermute | solution.py:337
  34.1 3.6 collective-permute-start.9
  40.9 2.0 collective-permute-start.7
  48.5 12.2 %shard_map.231.tiles_ref = f32[12,19,128,128]{3,2,1,0:T(8,128)} custom-call(f32[12,1,2560]{2,1,0:T(1,128)} %reshape.215.line_ref), custom_call_target="tpu_custom_call" | custom-call | flops 1 | bytes 1 | tf_op jit(solution)/shard_map/pallas_call | solution.py:43
  61.4 4.7 %collective-permute-start.11 = (bf16[256,768]{1,0:T(8,128)(2,1)S(1)}, bf16[256,768]{1,0:T(8,128)(2,1)S(1)}, u32[]{:S(2)}, u32[]{:S(2)}) collective-permute-start(bf16[256,768]{1,0:T(8,128)(2,1)S(1)} %bitcast.178), channel_id=1, source_target_pairs={{0,16},{4,20},{8,24},{12,28},{1,17},{5,21},{9,25},{13,29},{2,18},{... | collective-permute-start | bytes 1179656 | tf_op jit(solution)/shard_map/ppermute | solution.py:332
  66.1 2.0 collective-permute-start.12
  79.8 3.0 collective-permute-done.19
  89.5 6.0 %collective-permute-done.24 = bf16[256,768]{1,0:T(8,128)(2,1)} collective-permute-done((bf16[256,768]{1,0:T(8,128)(2,1)}, bf16[256,768]{1,0:T(8,128)(2,1)}, u32[]{:S(2)}, u32[]{:S(2)}) %collective-permute-start.24) | collective-permute-done | bytes 393248 | tf_op jit(solution)/shard_map/ppermute | solution.py:337
  95.5 9.9 %collective-permute-done.14.refs_8_ = bf16[256,768]{1,0:T(8,128)(2,1)} collective-permute-done((bf16[256,768]{1,0:T(8,128)(2,1)S(1)}, bf16[256,768]{1,0:T(8,128)(2,1)}, u32[]{:S(2)}, u32[]{:S(2)}) %collective-permute-start.14) | collective-permute-done | bytes 393248 | tf_op jit(solution)/shard_map/ppermute | solution.py:332
  105.8 2.1 shard_map.233
  108.0 3.9 shard_map.234
  112.7 4.6 %convolution_convert_fusion.2.value_turned_ref = bf16[768,2304]{1,0:T(8,128)(2,1)} fusion(bf16[2304,768]{1,0:T(8,128)(2,1)S(1)} %shard_map.234, bf16[768,3200]{1,0:T(8,128)(2,1)S(1)} %bitcast.161), kind=kOutput, calls=%fused_computation.3 | convolution fusion | flops 2719678464 | bytes 8257536 | tf_op jit(solution)/shard_map/dot_general | solution.py:628
  117.3 4.3 %convolution_convert_fusion.3.key_ref = bf16[2304,768]{1,0:T(8,128)(2,1)} fusion(bf16[2304,768]{1,0:T(8,128)(2,1)S(1)} %shard_map.234, bf16[768,3200]{1,0:T(8,128)(2,1)S(1)} %bitcast.162), kind=kOutput, calls=%fused_computation.4 | convolution fusion | flops 2719678464 | bytes 8257536 | tf_op jit(solution)/shard_map/dot_general | solution.py:628
  121.7 11.0 %shard_map.235 = (f32[768,256]{1,0:T(8,128)S(1)}, f32[3,4,256]{2,1,0:T(4,128)S(1)}) custom-call(s32[2]{0:T(128)S(1)} %get-tuple-element.138.first_ref, s32[2]{0:T(128)S(1)} %get-tuple-element.139.last_ref, bf16[768,256]{1,0:T(8,128)(2,1)S(1)} %convolution_convert_fusion.15.query_ref.query_turned_ref, bf16[2304,768]{1,0:T(8,128)(2,1)} %convolution_convert_fusion.3.key_ref, ...), custom_call_target="tpu_custom_call" | custom-call | flops 4026531840 | bytes 25165824 | tf_op jit(solution)/shard_map/pallas_call | solution.py:145
  133.4 2.9 collective-permute-start.16
  136.3 1.8 collective-permute-start.15
  138.1 4.4 %convolution_convert_fusion.value_ref = bf16[2304,768]{1,0:T(8,128)(2,1)} fusion(bf16[2304,768]{1,0:T(8,128)(2,1)S(1)} %shard_map.234, bf16[768,3200]{1,0:T(8,128)(2,1)S(1)} %bitcast.164), kind=kOutput, calls=%fused_computation.1 | convolution fusion | flops 2719678464 | bytes 8257536 | tf_op jit(solution)/shard_map/dot_general | solution.py:628
  142.5 2.2 collective-permute-done.16
  144.7 1.8 collective-permute-start.17
  146.5 4.6 %convolution_convert_fusion.1.key_turned_ref = bf16[768,2304]{1,0:T(8,128)(2,1)} fusion(bf16[2304,768]{1,0:T(8,128)(2,1)S(1)} %shard_map.234, bf16[768,3200]{1,0:T(8,128)(2,1)S(1)} %bitcast.165), kind=kOutput, calls=%fused_computation.2 | convolution fusion | flops 2719678464 | bytes 8257536 | tf_op jit(solution)/shard_map/dot_general | solution.py:628
  152.4 2.6 all-gather.3.cloned.1.call-done
  156.9 3.0 fusion.51
  159.9 3.6 fusion.6
  166.1 1.9 convolution_convert_fusion.6
  169.4 3.0 convolution_convert_fusion.5
  172.4 2.3 convolution_convert_fusion.11
  180.5 7.4 %collective-permute-done.28 = bf16[256,768]{1,0:T(8,128)(2,1)} collective-permute-done((bf16[256,768]{1,0:T(8,128)(2,1)}, bf16[256,768]{1,0:T(8,128)(2,1)}, u32[]{:S(2)}, u32[]{:S(2)}) %collective-permute-start.28) | collective-permute-done | bytes 393248 | tf_op jit(solution)/shard_map/ppermute | solution.py:337
  189.3 5.9 %collective-permute-done.22 = bf16[256,768]{1,0:T(8,128)(2,1)S(1)} collective-permute-done((bf16[256,768]{1,0:T(8,128)(2,1)S(1)}, bf16[256,768]{1,0:T(8,128)(2,1)S(1)}, u32[]{:S(2)}, u32[]{:S(2)}) %collective-permute-start.22) | collective-permute-done | bytes 393248 | tf_op jit(solution)/shard_map/ppermute | solution.py:337
  195.2 2.7 multiply_add_fusion.1
  198.0 1.9 convolution_convert_fusion.10
  202.5 24.2 %shard_map.239 = (bf16[768,256]{1,0:T(8,128)(2,1)}, bf16[2304,768]{1,0:T(8,128)(2,1)}, bf16[2304,768]{1,0:T(8,128)(2,1)}, f32[12,19,128,128]{3,2,1,0:T(8,128)}) custom-call(s32[2]{0:T(128)} %copy-done.35, s32[2]{0:T(128)} %copy-done.36, bf16[256,768]{1,0:T(8,128)(2,1)} %convolution_convert_fusion.14.query_ref, ...), custom_call_target="tpu_custom_call", output_to_operand_aliasing={{3}: (13, {})} | custom-call | flops 10066329600 | bytes 33554432 | tf_op jit(solution)/shard_map/pallas_call | solution.py:238
  226.7 5.2 %fusion.19 = f32[2304,768]{1,0:T(8,128)S(1)} fusion(bf16[2304,768]{1,0:T(8,128)(2,1)} %get-tuple-element.97, bf16[768,3200]{1,0:T(8,128)(2,1)S(1)} %bitcast.172), kind=kOutput, calls=%fused_computation.57 | convolution fusion | flops 2717908992 | bytes 11796480 | tf_op jit(solution)/shard_map/dot_general | solution.py:628
  231.9 5.8 %fusion.78 = (bf16[2304,768]{1,0:T(8,128)(2,1)}, f32[2304,768]{1,0:T(8,128)}) fusion(f32[2304,768]{1,0:T(8,128)S(1)} %fusion.19, bf16[2304,768]{1,0:T(8,128)(2,1)S(1)} %copy-done.38, bf16[768,3200]{1,0:T(8,128)(2,1)S(1)} %bitcast.173), kind=kOutput, calls=%fused_computation.207 | convolution fusion | flops 2721447936 | bytes 22413312 | tf_op jit(solution)/shard_map/dot_general | solution.py:628
  238.3 3.0 convolution_convert_fusion.8
  241.3 3.0 convolution_convert_fusion.7
  245.0 1.9 dynamic-slice_bitcast_fusion
  248.3 2.5 fusion.69
  250.8 4.3 %collective-permute-start.30 = (bf16[256,768]{1,0:T(8,128)(2,1)}, bf16[256,768]{1,0:T(8,128)(2,1)}, u32[]{:S(2)}, u32[]{:S(2)}) collective-permute-start(bf16[256,768]{1,0:T(8,128)(2,1)} %get-tuple-element.152), channel_id=1, source_target_pairs={{0,4},{4,8},{8,12},{12,16},{16,20},{20,24},{24,28},{1,5},{5,9},{9,... | collective-permute-start | bytes 1179656 | tf_op jit(solution)/shard_map/ppermute | solution.py:332
  255.1 2.3 collective-permute-start.31
  257.4 4.1 %collective-permute-start.32 = (bf16[256,768]{1,0:T(8,128)(2,1)}, bf16[256,768]{1,0:T(8,128)(2,1)}, u32[]{:S(2)}, u32[]{:S(2)}) collective-permute-start(bf16[256,768]{1,0:T(8,128)(2,1)} %get-tuple-element.150), channel_id=1, source_target_pairs={{0,16},{4,20},{8,24},{12,28},{1,17},{5,21},{9,25},{13,29},{2,18},{... | collective-permute-start | bytes 1179656 | tf_op jit(solution)/shard_map/ppermute | solution.py:332
  264.2 5.3 %shard_map.240 = f32[4,19,8,256]{3,2,1,0:T(8,128)S(1)} custom-call(s32[2]{0:T(128)S(1)} %pad_add_fusion.3.range_ref, f32[12,19,128,128]{3,2,1,0:T(8,128)} %get-tuple-element.100.tiles_ref), custom_call_target="tpu_custom_call" | custom-call | flops 1 | bytes 1 | tf_op jit(solution)/shard_map/pallas_call | solution.py:308
  269.5 5.3 %shard_map.241 = f32[4,19,8,256]{3,2,1,0:T(8,128)S(1)} custom-call(s32[2]{0:T(128)S(1)} %pad_add_fusion.3.range_ref, f32[12,19,128,128]{3,2,1,0:T(8,128)} %get-tuple-element.100.tiles_ref), custom_call_target="tpu_custom_call" | custom-call | flops 1 | bytes 1 | tf_op jit(solution)/shard_map/pallas_call | solution.py:308
  274.9 5.5 %shard_map.242 = f32[4,19,8,256]{3,2,1,0:T(8,128)S(1)} custom-call(s32[2]{0:T(128)S(1)} %pad_add_fusion.3.range_ref, f32[12,19,128,128]{3,2,1,0:T(8,128)} %get-tuple-element.100.tiles_ref), custom_call_target="tpu_custom_call" | custom-call | flops 1 | bytes 1 | tf_op jit(solution)/shard_map/pallas_call | solution.py:308
  281.6 15.2 %collective-permute-done.33 = bf16[256,768]{1,0:T(8,128)(2,1)} collective-permute-done((bf16[256,768]{1,0:T(8,128)(2,1)}, bf16[256,768]{1,0:T(8,128)(2,1)}, u32[]{:S(2)}, u32[]{:S(2)}) %collective-permute-start.33) | collective-permute-done | bytes 393248 | tf_op jit(solution)/shard_map/ppermute | solution.py:332
  303.6 3.5 collective-permute-done.45
  307.1 6.6 %collective-permute-start.46 = (f32[32,12]{0,1:T(8,128)S(1)}, f32[32,12]{0,1:T(8,128)S(1)}, u32[]{:S(2)}, u32[]{:S(2)}) collective-permute-start(f32[32,12]{0,1:T(8,128)S(1)} %add.316), channel_id=1, source_target_pairs={{0,4},{1,5},{2,6},{3,7},{4,0},{5,1},{6,2},{7,3},{8,12},{9,13},{10,... | collective-permute-start | bytes 4616 | tf_op jit(solution)/shard_map/ppermute | solution.py:337
  313.7 2.5 add_convert_fusion
  321.1 2.0 collective-permute-start.48
  323.1 2.1 fusion.68
  325.1 2.6 collective-permute-start.37
  329.1 1.8 fusion.26
  331.5 10.4 %collective-permute-done.37 = bf16[256,768]{1,0:T(8,128)(2,1)} collective-permute-done((bf16[256,768]{1,0:T(8,128)(2,1)}, bf16[256,768]{1,0:T(8,128)(2,1)}, u32[]{:S(2)}, u32[]{:S(2)}) %collective-permute-start.37) | collective-permute-done | bytes 393248 | tf_op jit(solution)/shard_map/ppermute | solution.py:332
  343.7 5.3 %collective-permute-done.35 = bf16[4,24,3072]{2,1,0:T(8,128)(2,1)} collective-permute-done((bf16[4,24,3072]{2,1,0:T(8,128)(2,1)}, bf16[4,24,3072]{2,1,0:T(8,128)(2,1)}, u32[]{:S(2)}, u32[]{:S(2)}) %collective-permute-start.35) | collective-permute-done | bytes 589856 | tf_op jit(solution)/shard_map/ppermute | solution.py:337
  349.0 4.2 %reduce-scatter.2.cloned.1.call-done = bf16[1,6,24,1024]{3,2,1,0:T(8,128)(2,1)} async-done(((bf16[8,6,24,1024]{3,2,1,0:T(8,128)(2,1)}), bf16[1,6,24,1024]{3,2,1,0:T(8,128)(2,1)}) %reduce-scatter.2.cloned.1.call-update) | async-done | bytes 294928 | tf_op jit(solution)/shard_map/reduce_scatter | solution.py:836
  358.6 2.0 collective-permute-start.40
  360.6 2.0 collective-permute-start.41
  363.4 2.1 fusion.67
  365.4 5.0 %collective-permute-start.42 = (bf16[256,768]{1,0:T(8,128)(2,1)}, bf16[256,768]{1,0:T(8,128)(2,1)S(1)}, u32[]{:S(2)}, u32[]{:S(2)}) collective-permute-start(bf16[256,768]{1,0:T(8,128)(2,1)} %get-tuple-element.146), channel_id=1, source_target_pairs={{0,12},{4,16},{8,20},{12,24},{16,28},{1,13},{5,17},{9,21},{13,25},... | collective-permute-start | bytes 1179656 | tf_op jit(solution)/shard_map/ppermute | solution.py:332
  377.4 5.1 %collective-permute-done.42 = bf16[256,768]{1,0:T(8,128)(2,1)S(1)} collective-permute-done((bf16[256,768]{1,0:T(8,128)(2,1)}, bf16[256,768]{1,0:T(8,128)(2,1)S(1)}, u32[]{:S(2)}, u32[]{:S(2)}) %collective-permute-start.42) | collective-permute-done | bytes 393248 | tf_op jit(solution)/shard_map/ppermute | solution.py:332
  382.5 11.0 %collective-permute-done.43 = bf16[256,768]{1,0:T(8,128)(2,1)S(1)} collective-permute-done((bf16[256,768]{1,0:T(8,128)(2,1)}, bf16[256,768]{1,0:T(8,128)(2,1)S(1)}, u32[]{:S(2)}, u32[]{:S(2)}) %collective-permute-start.43) | collective-permute-done | bytes 393248 | tf_op jit(solution)/shard_map/ppermute | solution.py:332
  396.2 2.7 fusion.30
  (328 shorter events, 97.6 us)
Async XLA Ops:
  7.2 40.3 %copy-start = (f32[32,12]{0,1:T(8,128)S(1)}, f32[32,12]{0,1:T(8,128)}, u32[]{:S(2)}) copy-start(f32[32,12]{0,1:T(8,128)} %param.22) | copy-start | bytes 4612
  7.2 35.8 %copy-start.51 = (s32[2047]{0:T(1024)S(1)}, s32[2047]{0:T(1024)}, u32[]{:S(2)}) copy-start(s32[2047]{0:T(1024)} %param.16) | copy-start | bytes 24568
  7.2 147.8 %all-gather.3.cloned.1.call-start = ((), (), s32[]{:S(2)}) async-start(), calls=%async_computation.2 | async-start | bytes 2654208 | tf_op jit(solution)/shard_map/all_gather | solution.py:741
  7.2 30.5 %collective-permute-start.3 = (bf16[256,768]{1,0:T(8,128)(2,1)}, bf16[256,768]{1,0:T(8,128)(2,1)S(1)}, u32[]{:S(2)}, u32[]{:S(2)}) collective-permute-start(bf16[256,768]{1,0:T(8,128)(2,1)} %bitcast.174), channel_id=1, source_target_pairs={{4,0},{8,4},{12,8},{16,12},{20,16},{24,20},{28,24},{5,1},{9,5},{13... | collective-permute-start | bytes 1179656 | tf_op jit(solution)/shard_map/ppermute | solution.py:332
  9.2 29.3 %collective-permute-start.4 = (bf16[256,768]{1,0:T(8,128)(2,1)}, bf16[256,768]{1,0:T(8,128)(2,1)S(1)}, u32[]{:S(2)}, u32[]{:S(2)}) collective-permute-start(bf16[256,768]{1,0:T(8,128)(2,1)} %bitcast.175), channel_id=1, source_target_pairs={{0,4},{4,8},{8,12},{12,16},{16,20},{20,24},{24,28},{1,5},{5,9},{9,... | collective-permute-start | bytes 1179656 | tf_op jit(solution)/shard_map/ppermute | solution.py:332
  18.3 8.7 %collective-permute-start = (bf16[1,24,3200]{2,1,0:T(8,128)(2,1)S(1)}, bf16[1,24,3200]{2,1,0:T(8,128)(2,1)S(1)}, u32[]{:S(2)}, u32[]{:S(2)}) collective-permute-start(bf16[1,24,3200]{2,1,0:T(8,128)(2,1)S(1)} %bitcast.184), channel_id=1, source_target_pairs={{0,8},{1,9},{2,10},{3,11},{4,12},{5,13},{6,14},{7,15},{8,0},{9,1},... | collective-permute-start | bytes 460808 | tf_op jit(solution)/shard_map/ppermute | solution.py:337
  20.0 14.1 %collective-permute-start.1 = (bf16[1,24,3200]{2,1,0:T(8,128)(2,1)S(1)}, bf16[1,24,3200]{2,1,0:T(8,128)(2,1)S(1)}, u32[]{:S(2)}, u32[]{:S(2)}) collective-permute-start(bf16[1,24,3200]{2,1,0:T(8,128)(2,1)S(1)} %bitcast.185), channel_id=1, source_target_pairs={{0,16},{1,17},{2,18},{3,19},{4,20},{5,21},{6,22},{7,23},{8,24},{9,... | collective-permute-start | bytes 460808 | tf_op jit(solution)/shard_map/ppermute | solution.py:337
  21.1 16.7 %collective-permute-start.2 = (bf16[1,24,3200]{2,1,0:T(8,128)(2,1)S(1)}, bf16[1,24,3200]{2,1,0:T(8,128)(2,1)S(1)}, u32[]{:S(2)}, u32[]{:S(2)}) collective-permute-start(bf16[1,24,3200]{2,1,0:T(8,128)(2,1)S(1)} %bitcast.186), channel_id=1, source_target_pairs={{0,24},{1,25},{2,26},{3,27},{4,28},{5,29},{6,30},{7,31},{8,16},{9,... | collective-permute-start | bytes 460808 | tf_op jit(solution)/shard_map/ppermute | solution.py:337
  27.1 33.6 %collective-permute-start.8 = (bf16[256,768]{1,0:T(8,128)(2,1)}, bf16[256,768]{1,0:T(8,128)(2,1)S(1)}, u32[]{:S(2)}, u32[]{:S(2)}) collective-permute-start(bf16[256,768]{1,0:T(8,128)(2,1)} %bitcast.176), channel_id=1, source_target_pairs={{8,0},{12,4},{16,8},{20,12},{24,16},{28,20},{9,1},{13,5},{17,9},{2... | collective-permute-start | bytes 1179656 | tf_op jit(solution)/shard_map/ppermute | solution.py:332
  34.1 32.0 %collective-permute-start.9 = (bf16[256,768]{1,0:T(8,128)(2,1)}, bf16[256,768]{1,0:T(8,128)(2,1)}, u32[]{:S(2)}, u32[]{:S(2)}) collective-permute-start(bf16[256,768]{1,0:T(8,128)(2,1)} %bitcast.177), channel_id=1, source_target_pairs={{0,8},{4,12},{8,16},{12,20},{16,24},{20,28},{1,9},{5,13},{9,17},{1... | collective-permute-start | bytes 1179656 | tf_op jit(solution)/shard_map/ppermute | solution.py:332
  39.3 28.9 %collective-permute-start.5 = (bf16[4,24,3200]{2,1,0:T(8,128)(2,1)S(1)}, bf16[4,24,3200]{2,1,0:T(8,128)(2,1)S(1)}, u32[]{:S(2)}, u32[]{:S(2)}) collective-permute-start(bf16[4,24,3200]{2,1,0:T(8,128)(2,1)S(1)} %shard_map.230.refs_0_), channel_id=1, source_target_pairs={{0,2},{1,3},{2,0},{3,1},{4,6},{5,7},{6,4},{7,5},{8,10},{9,11},{10,... | collective-permute-start | bytes 1843208 | tf_op jit(solution)/shard_map/ppermute | solution.py:337
  40.9 29.4 %collective-permute-start.6 = (bf16[4,24,3200]{2,1,0:T(8,128)(2,1)S(1)}, bf16[4,24,3200]{2,1,0:T(8,128)(2,1)S(1)}, u32[]{:S(2)}, u32[]{:S(2)}) collective-permute-start(bf16[4,24,3200]{2,1,0:T(8,128)(2,1)S(1)} %shard_map.230.refs_0_), channel_id=1, source_target_pairs={{0,4},{1,5},{2,6},{3,7},{4,0},{5,1},{6,2},{7,3},{8,12},{9,13},{10,... | collective-permute-start | bytes 1843208 | tf_op jit(solution)/shard_map/ppermute | solution.py:337
  40.9 30.3 %collective-permute-start.7 = (bf16[4,24,3200]{2,1,0:T(8,128)(2,1)S(1)}, bf16[4,24,3200]{2,1,0:T(8,128)(2,1)S(1)}, u32[]{:S(2)}, u32[]{:S(2)}) collective-permute-start(bf16[4,24,3200]{2,1,0:T(8,128)(2,1)S(1)} %shard_map.230.refs_0_), channel_id=1, source_target_pairs={{0,6},{1,7},{2,4},{3,5},{4,2},{5,3},{6,0},{7,1},{8,14},{9,15},{10,... | collective-permute-start | bytes 1843208 | tf_op jit(solution)/shard_map/ppermute | solution.py:337
  61.4 22.8 %collective-permute-start.11 = (bf16[256,768]{1,0:T(8,128)(2,1)S(1)}, bf16[256,768]{1,0:T(8,128)(2,1)S(1)}, u32[]{:S(2)}, u32[]{:S(2)}) collective-permute-start(bf16[256,768]{1,0:T(8,128)(2,1)S(1)} %bitcast.178), channel_id=1, source_target_pairs={{0,16},{4,20},{8,24},{12,28},{1,17},{5,21},{9,25},{13,29},{2,18},{... | collective-permute-start | bytes 1179656 | tf_op jit(solution)/shard_map/ppermute | solution.py:332
  66.1 23.4 %collective-permute-start.12 = (bf16[256,768]{1,0:T(8,128)(2,1)S(1)}, bf16[256,768]{1,0:T(8,128)(2,1)}, u32[]{:S(2)}, u32[]{:S(2)}) collective-permute-start(bf16[256,768]{1,0:T(8,128)(2,1)S(1)} %bitcast.179), channel_id=1, source_target_pairs={{0,12},{4,16},{8,20},{12,24},{16,28},{1,13},{5,17},{9,21},{13,25},... | collective-permute-start | bytes 1179656 | tf_op jit(solution)/shard_map/ppermute | solution.py:332
  69.0 26.6 %collective-permute-start.13 = (bf16[256,768]{1,0:T(8,128)(2,1)S(1)}, bf16[256,768]{1,0:T(8,128)(2,1)}, u32[]{:S(2)}, u32[]{:S(2)}) collective-permute-start(bf16[256,768]{1,0:T(8,128)(2,1)S(1)} %bitcast.180), channel_id=1, source_target_pairs={{12,0},{16,4},{20,8},{24,12},{28,16},{13,1},{17,5},{21,9},{25,13},... | collective-permute-start | bytes 1179656 | tf_op jit(solution)/shard_map/ppermute | solution.py:332
  71.1 6.1 %collective-permute-start.18 = (bf16[2,24,1024]{2,1,0:T(8,128)(2,1)}, bf16[2,24,1024]{2,1,0:T(8,128)(2,1)S(1)}, u32[]{:S(2)}, u32[]{:S(2)}) collective-permute-start(bf16[2,24,1024]{2,1,0:T(8,128)(2,1)} %pad_maximum_fusion.19), channel_id=1, source_target_pairs={{0,1},{1,0},{2,3},{3,2},{4,5},{5,4},{6,7},{7,6},{8,9},{9,8},{10,11... | collective-permute-start | bytes 294920 | tf_op jit(solution)/shard_map/ppermute | solution.py:337
  75.4 30.4 %collective-permute-start.10 = (bf16[16,24,3200]{2,1,0:T(8,128)(2,1)S(1)}, bf16[16,24,3200]{2,1,0:T(8,128)(2,1)}, u32[]{:S(2)}, u32[]{:S(2)}) collective-permute-start(bf16[16,24,3200]{2,1,0:T(8,128)(2,1)S(1)} %shard_map.232.refs_0_), channel_id=1, source_target_pairs={{0,1},{1,0},{2,3},{3,2},{4,5},{5,4},{6,7},{7,6},{8,9},{9,8},{10,11... | collective-permute-start | bytes 7372808 | tf_op jit(solution)/shard_map/ppermute | solution.py:337
  76.0 45.6 %copy-start.32 = (bf16[128,256]{1,0:T(8,128)(2,1)}, bf16[128,256]{1,0:T(8,128)(2,1)S(1)}, u32[]{:S(2)}) copy-start(bf16[128,256]{1,0:T(8,128)(2,1)S(1)} %fusion.54.query_feat_ref) | copy-start | bytes 196612
  77.1 44.5 %copy-start.6 = (bf16[2304,128]{1,0:T(8,128)(2,1)}, bf16[2304,128]{1,0:T(8,128)(2,1)S(1)}, u32[]{:S(2)}) copy-start(bf16[2304,128]{1,0:T(8,128)(2,1)S(1)} %select_convert_fusion.key_feat_ref) | copy-start | bytes 1769476
  78.1 4.8 %collective-permute-start.19 = (bf16[2,24,1024]{2,1,0:T(8,128)(2,1)S(1)}, bf16[2,24,1024]{2,1,0:T(8,128)(2,1)S(1)}, u32[]{:S(2)}, u32[]{:S(2)}) collective-permute-start(bf16[2,24,1024]{2,1,0:T(8,128)(2,1)S(1)} %pad_maximum_fusion.20), channel_id=1, source_target_pairs={{0,2},{1,3},{2,0},{3,1},{4,6},{5,7},{6,4},{7,5},{8,10},{9,11},{10,... | collective-permute-start | bytes 294920 | tf_op jit(solution)/shard_map/ppermute | solution.py:337
  82.9 22.6 %collective-permute-start.14 = (bf16[256,768]{1,0:T(8,128)(2,1)S(1)}, bf16[256,768]{1,0:T(8,128)(2,1)}, u32[]{:S(2)}, u32[]{:S(2)}) collective-permute-start(bf16[256,768]{1,0:T(8,128)(2,1)S(1)} %bitcast.181), channel_id=1, source_target_pairs={{16,0},{20,4},{24,8},{28,12},{17,1},{21,5},{25,9},{29,13},{18,2},{... | collective-permute-start | bytes 1179656 | tf_op jit(solution)/shard_map/ppermute | solution.py:332
  84.9 10.6 %collective-permute-start.24 = (bf16[256,768]{1,0:T(8,128)(2,1)}, bf16[256,768]{1,0:T(8,128)(2,1)}, u32[]{:S(2)}, u32[]{:S(2)}) collective-permute-start(bf16[256,768]{1,0:T(8,128)(2,1)} %bitcast.25), channel_id=1, source_target_pairs={{0,2},{1,3},{2,0},{3,1},{4,6},{5,7},{6,4},{7,5},{8,10},{9,11},{10,... | collective-permute-start | bytes 1179656 | tf_op jit(solution)/shard_map/ppermute | solution.py:337
  87.1 34.6 %copy-start.36 = (s32[2]{0:T(128)}, s32[2]{0:T(128)S(1)}, u32[]{:S(2)}) copy-start(s32[2]{0:T(128)S(1)} %get-tuple-element.139.last_ref) | copy-start | bytes 28
  89.5 70.4 %collective-permute-start.23 = (bf16[256,768]{1,0:T(8,128)(2,1)}, bf16[256,768]{1,0:T(8,128)(2,1)}, u32[]{:S(2)}, u32[]{:S(2)}) collective-permute-start(bf16[256,768]{1,0:T(8,128)(2,1)} %bitcast.25), channel_id=1, source_target_pairs={{0,1},{1,0},{2,3},{3,2},{4,5},{5,4},{6,7},{7,6},{8,9},{9,8},{10,11... | collective-permute-start | bytes 1179656 | tf_op jit(solution)/shard_map/ppermute | solution.py:337
  95.5 64.4 %collective-permute-start.25 = (bf16[256,768]{1,0:T(8,128)(2,1)}, bf16[256,768]{1,0:T(8,128)(2,1)}, u32[]{:S(2)}, u32[]{:S(2)}) collective-permute-start(bf16[256,768]{1,0:T(8,128)(2,1)} %collective-permute-done.24), channel_id=1, source_target_pairs={{0,1},{1,0},{2,3},{3,2},{4,5},{5,4},{6,7},{7,6},{8,9},{9,8},{10,11... | collective-permute-start | bytes 1179656 | tf_op jit(solution)/shard_map/ppermute | solution.py:337
  105.5 247.7 %reduce-scatter.2.cloned.1.call-start = ((), (), s32[]{:S(2)}) async-start(), calls=%async_computation.1 | async-start | bytes 2654208 | tf_op jit(solution)/shard_map/reduce_scatter | solution.py:836
  107.9 43.2 %copy-start.2 = (bf16[32,24,3200]{2,1,0:T(8,128)(2,1)}, bf16[32,24,3200]{2,1,0:T(8,128)(2,1)S(1)}, u32[]{:S(2)}) copy-start(bf16[32,24,3200]{2,1,0:T(8,128)(2,1)S(1)} %shard_map.233) | copy-start | bytes 14745604
  111.9 39.2 %copy-start.4 = (bf16[2304,768]{1,0:T(8,128)(2,1)}, bf16[2304,768]{1,0:T(8,128)(2,1)S(1)}, u32[]{:S(2)}) copy-start(bf16[2304,768]{1,0:T(8,128)(2,1)S(1)} %shard_map.234) | copy-start | bytes 10616836
  132.7 65.3 %copy-start.9 = (f32[768,256]{1,0:T(8,128)}, f32[768,256]{1,0:T(8,128)S(1)}, u32[]{:S(2)}) copy-start(f32[768,256]{1,0:T(8,128)S(1)} %get-tuple-element.83.out_ref) | copy-start | bytes 2359300
  133.4 11.2 %collective-permute-start.16 = (bf16[256,768]{1,0:T(8,128)(2,1)S(1)}, bf16[256,768]{1,0:T(8,128)(2,1)S(1)}, u32[]{:S(2)}, u32[]{:S(2)}) collective-permute-start(bf16[256,768]{1,0:T(8,128)(2,1)S(1)} %multiply_convert_fusion.2), channel_id=1, source_target_pairs={{0,2},{1,3},{2,0},{3,1},{4,6},{5,7},{6,4},{7,5},{8,10},{9,11},{10,... | collective-permute-start | bytes 1179656 | tf_op jit(solution)/shard_map/ppermute | solution.py:337
  136.3 20.6 %collective-permute-start.15 = (bf16[256,768]{1,0:T(8,128)(2,1)S(1)}, bf16[256,768]{1,0:T(8,128)(2,1)}, u32[]{:S(2)}, u32[]{:S(2)}) collective-permute-start(bf16[256,768]{1,0:T(8,128)(2,1)S(1)} %multiply_convert_fusion.2), channel_id=1, source_target_pairs={{0,1},{1,0},{2,3},{3,2},{4,5},{5,4},{6,7},{7,6},{8,9},{9,8},{10,11... | collective-permute-start | bytes 1179656 | tf_op jit(solution)/shard_map/ppermute | solution.py:337
  144.7 12.2 %collective-permute-start.17 = (bf16[256,768]{1,0:T(8,128)(2,1)S(1)}, bf16[256,768]{1,0:T(8,128)(2,1)}, u32[]{:S(2)}, u32[]{:S(2)}) collective-permute-start(bf16[256,768]{1,0:T(8,128)(2,1)S(1)} %collective-permute-done.16), channel_id=1, source_target_pairs={{0,1},{1,0},{2,3},{3,2},{4,5},{5,4},{6,7},{7,6},{8,9},{9,8},{10,11... | collective-permute-start | bytes 1179656 | tf_op jit(solution)/shard_map/ppermute | solution.py:337
  165.6 13.1 %collective-permute-start.21 = (bf16[256,768]{1,0:T(8,128)(2,1)}, bf16[256,768]{1,0:T(8,128)(2,1)}, u32[]{:S(2)}, u32[]{:S(2)}) collective-permute-start(bf16[256,768]{1,0:T(8,128)(2,1)} %get-tuple-element.168), channel_id=1, source_target_pairs={{0,1},{1,0},{2,3},{3,2},{4,5},{5,4},{6,7},{7,6},{8,9},{9,8},{10,11... | collective-permute-start | bytes 1179656 | tf_op jit(solution)/shard_map/ppermute | solution.py:337
  165.6 23.7 %collective-permute-start.20 = (bf16[256,768]{1,0:T(8,128)(2,1)}, bf16[256,768]{1,0:T(8,128)(2,1)}, u32[]{:S(2)}, u32[]{:S(2)}) collective-permute-start(bf16[256,768]{1,0:T(8,128)(2,1)} %get-tuple-element.167), channel_id=1, source_target_pairs={{0,1},{1,0},{2,3},{3,2},{4,5},{5,4},{6,7},{7,6},{8,9},{9,8},{10,11... | collective-permute-start | bytes 1179656 | tf_op jit(solution)/shard_map/ppermute | solution.py:337
  168.9 5.8 %collective-permute-start.27 = (bf16[256,768]{1,0:T(8,128)(2,1)S(1)}, bf16[256,768]{1,0:T(8,128)(2,1)S(1)}, u32[]{:S(2)}, u32[]{:S(2)}) collective-permute-start(bf16[256,768]{1,0:T(8,128)(2,1)S(1)} %get-tuple-element.166), channel_id=1, source_target_pairs={{0,1},{1,0},{2,3},{3,2},{4,5},{5,4},{6,7},{7,6},{8,9},{9,8},{10,11... | collective-permute-start | bytes 1179656 | tf_op jit(solution)/shard_map/ppermute | solution.py:337
  168.9 11.6 %collective-permute-start.26 = (bf16[256,768]{1,0:T(8,128)(2,1)}, bf16[256,768]{1,0:T(8,128)(2,1)S(1)}, u32[]{:S(2)}, u32[]{:S(2)}) collective-permute-start(bf16[256,768]{1,0:T(8,128)(2,1)} %get-tuple-element.165), channel_id=1, source_target_pairs={{0,1},{1,0},{2,3},{3,2},{4,5},{5,4},{6,7},{7,6},{8,9},{9,8},{10,11... | collective-permute-start | bytes 1179656 | tf_op jit(solution)/shard_map/ppermute | solution.py:337
  175.6 12.3 %collective-permute-start.28 = (bf16[256,768]{1,0:T(8,128)(2,1)}, bf16[256,768]{1,0:T(8,128)(2,1)}, u32[]{:S(2)}, u32[]{:S(2)}) collective-permute-start(bf16[256,768]{1,0:T(8,128)(2,1)} %add_convert_fusion.2), channel_id=1, source_target_pairs={{0,2},{1,3},{2,0},{3,1},{4,6},{5,7},{6,4},{7,5},{8,10},{9,11},{10,... | collective-permute-start | bytes 1179656 | tf_op jit(solution)/shard_map/ppermute | solution.py:337
  179.9 15.3 %collective-permute-start.22 = (bf16[256,768]{1,0:T(8,128)(2,1)S(1)}, bf16[256,768]{1,0:T(8,128)(2,1)S(1)}, u32[]{:S(2)}, u32[]{:S(2)}) collective-permute-start(bf16[256,768]{1,0:T(8,128)(2,1)S(1)} %add_convert_fusion.4), channel_id=1, source_target_pairs={{0,2},{1,3},{2,0},{3,1},{4,6},{5,7},{6,4},{7,5},{8,10},{9,11},{10,... | collective-permute-start | bytes 1179656 | tf_op jit(solution)/shard_map/ppermute | solution.py:337
  246.9 49.9 %collective-permute-start.29 = (bf16[16,24,3072]{2,1,0:T(8,128)(2,1)}, bf16[16,24,3072]{2,1,0:T(8,128)(2,1)}, u32[]{:S(2)}, u32[]{:S(2)}) collective-permute-start(bf16[16,24,3072]{2,1,0:T(8,128)(2,1)} %get-tuple-element.142), channel_id=1, source_target_pairs={{0,1},{1,0},{2,3},{3,2},{4,5},{5,4},{6,7},{7,6},{8,9},{9,8},{10,11... | collective-permute-start | bytes 7077896 | tf_op jit(solution)/shard_map/ppermute | solution.py:337
  250.8 29.8 %collective-permute-start.30 = (bf16[256,768]{1,0:T(8,128)(2,1)}, bf16[256,768]{1,0:T(8,128)(2,1)}, u32[]{:S(2)}, u32[]{:S(2)}) collective-permute-start(bf16[256,768]{1,0:T(8,128)(2,1)} %get-tuple-element.152), channel_id=1, source_target_pairs={{0,4},{4,8},{8,12},{12,16},{16,20},{20,24},{24,28},{1,5},{5,9},{9,... | collective-permute-start | bytes 1179656 | tf_op jit(solution)/shard_map/ppermute | solution.py:332
  255.1 25.5 %collective-permute-start.31 = (bf16[256,768]{1,0:T(8,128)(2,1)}, bf16[256,768]{1,0:T(8,128)(2,1)}, u32[]{:S(2)}, u32[]{:S(2)}) collective-permute-start(bf16[256,768]{1,0:T(8,128)(2,1)} %get-tuple-element.151), channel_id=1, source_target_pairs={{4,0},{8,4},{12,8},{16,12},{20,16},{24,20},{28,24},{5,1},{9,5},{13... | collective-permute-start | bytes 1179656 | tf_op jit(solution)/shard_map/ppermute | solution.py:332
  257.4 24.2 %collective-permute-start.32 = (bf16[256,768]{1,0:T(8,128)(2,1)}, bf16[256,768]{1,0:T(8,128)(2,1)}, u32[]{:S(2)}, u32[]{:S(2)}) collective-permute-start(bf16[256,768]{1,0:T(8,128)(2,1)} %get-tuple-element.150), channel_id=1, source_target_pairs={{0,16},{4,20},{8,24},{12,28},{1,17},{5,21},{9,25},{13,29},{2,18},{... | collective-permute-start | bytes 1179656 | tf_op jit(solution)/shard_map/ppermute | solution.py:332
  261.5 35.3 %collective-permute-start.33 = (bf16[256,768]{1,0:T(8,128)(2,1)}, bf16[256,768]{1,0:T(8,128)(2,1)}, u32[]{:S(2)}, u32[]{:S(2)}) collective-permute-start(bf16[256,768]{1,0:T(8,128)(2,1)} %get-tuple-element.149), channel_id=1, source_target_pairs={{16,0},{20,4},{24,8},{28,12},{17,1},{21,5},{25,9},{29,13},{18,2},{... | collective-permute-start | bytes 1179656 | tf_op jit(solution)/shard_map/ppermute | solution.py:332
  302.3 1.2 collective-permute-start.44
  303.4 3.7 collective-permute-start.45
  307.1 9.1 %collective-permute-start.46 = (f32[32,12]{0,1:T(8,128)S(1)}, f32[32,12]{0,1:T(8,128)S(1)}, u32[]{:S(2)}, u32[]{:S(2)}) collective-permute-start(f32[32,12]{0,1:T(8,128)S(1)} %add.316), channel_id=1, source_target_pairs={{0,4},{1,5},{2,6},{3,7},{4,0},{5,1},{6,2},{7,3},{8,12},{9,13},{10,... | collective-permute-start | bytes 4616 | tf_op jit(solution)/shard_map/ppermute | solution.py:337
  316.2 4.8 %collective-permute-start.47 = (f32[32,12]{0,1:T(8,128)S(1)}, f32[32,12]{0,1:T(8,128)S(1)}, u32[]{:S(2)}, u32[]{:S(2)}) collective-permute-start(f32[32,12]{0,1:T(8,128)S(1)} %add.317), channel_id=1, source_target_pairs={{0,8},{1,9},{2,10},{3,11},{4,12},{5,13},{6,14},{7,15},{8,0},{9,1},... | collective-permute-start | bytes 4616 | tf_op jit(solution)/shard_map/ppermute | solution.py:337
  317.6 26.1 %collective-permute-start.34 = (bf16[4,24,3072]{2,1,0:T(8,128)(2,1)}, bf16[4,24,3072]{2,1,0:T(8,128)(2,1)S(1)}, u32[]{:S(2)}, u32[]{:S(2)}) collective-permute-start(bf16[4,24,3072]{2,1,0:T(8,128)(2,1)} %get-tuple-element.155), channel_id=1, source_target_pairs={{0,2},{1,3},{2,0},{3,1},{4,6},{5,7},{6,4},{7,5},{8,10},{9,11},{10,... | collective-permute-start | bytes 1769480 | tf_op jit(solution)/shard_map/ppermute | solution.py:337
  319.2 29.8 %collective-permute-start.35 = (bf16[4,24,3072]{2,1,0:T(8,128)(2,1)}, bf16[4,24,3072]{2,1,0:T(8,128)(2,1)}, u32[]{:S(2)}, u32[]{:S(2)}) collective-permute-start(bf16[4,24,3072]{2,1,0:T(8,128)(2,1)} %get-tuple-element.154), channel_id=1, source_target_pairs={{0,4},{1,5},{2,6},{3,7},{4,0},{5,1},{6,2},{7,3},{8,12},{9,13},{10,... | collective-permute-start | bytes 1769480 | tf_op jit(solution)/shard_map/ppermute | solution.py:337
  320.2 28.8 %collective-permute-start.36 = (bf16[4,24,3072]{2,1,0:T(8,128)(2,1)}, bf16[4,24,3072]{2,1,0:T(8,128)(2,1)}, u32[]{:S(2)}, u32[]{:S(2)}) collective-permute-start(bf16[4,24,3072]{2,1,0:T(8,128)(2,1)} %get-tuple-element.153), channel_id=1, source_target_pairs={{0,6},{1,7},{2,4},{3,5},{4,2},{5,3},{6,0},{7,1},{8,14},{9,15},{10,... | collective-permute-start | bytes 1769480 | tf_op jit(solution)/shard_map/ppermute | solution.py:337
  321.1 6.7 %collective-permute-start.48 = (f32[32,12]{0,1:T(8,128)S(1)}, f32[32,12]{0,1:T(8,128)S(1)}, u32[]{:S(2)}, u32[]{:S(2)}) collective-permute-start(f32[32,12]{0,1:T(8,128)S(1)} %add.318), channel_id=1, source_target_pairs={{0,16},{1,17},{2,18},{3,19},{4,20},{5,21},{6,22},{7,23},{8,24},{9,... | collective-permute-start | bytes 4616 | tf_op jit(solution)/shard_map/ppermute | solution.py:337
  325.1 16.8 %collective-permute-start.37 = (bf16[256,768]{1,0:T(8,128)(2,1)}, bf16[256,768]{1,0:T(8,128)(2,1)}, u32[]{:S(2)}, u32[]{:S(2)}) collective-permute-start(bf16[256,768]{1,0:T(8,128)(2,1)} %get-tuple-element.148), channel_id=1, source_target_pairs={{0,8},{4,12},{8,16},{12,20},{16,24},{20,28},{1,9},{5,13},{9,17},{1... | collective-permute-start | bytes 1179656 | tf_op jit(solution)/shard_map/ppermute | solution.py:332
  327.8 15.9 %collective-permute-start.38 = (bf16[256,768]{1,0:T(8,128)(2,1)}, bf16[256,768]{1,0:T(8,128)(2,1)}, u32[]{:S(2)}, u32[]{:S(2)}) collective-permute-start(bf16[256,768]{1,0:T(8,128)(2,1)} %get-tuple-element.147), channel_id=1, source_target_pairs={{8,0},{12,4},{16,8},{20,12},{24,16},{28,20},{9,1},{13,5},{17,9},{2... | collective-permute-start | bytes 1179656 | tf_op jit(solution)/shard_map/ppermute | solution.py:332
  354.8 7.9 %collective-permute-start.49 = (bf16[2,24,1024]{2,1,0:T(8,128)(2,1)S(1)}, bf16[2,24,1024]{2,1,0:T(8,128)(2,1)S(1)}, u32[]{:S(2)}, u32[]{:S(2)}) collective-permute-start(bf16[2,24,1024]{2,1,0:T(8,128)(2,1)S(1)} %pad_maximum_fusion.21), channel_id=1, source_target_pairs={{0,1},{1,0},{2,3},{3,2},{4,5},{5,4},{6,7},{7,6},{8,9},{9,8},{10,11... | collective-permute-start | bytes 294920 | tf_op jit(solution)/shard_map/ppermute | solution.py:337
  357.3 38.0 %copy-start.27 = (f32[24,768]{1,0:T(8,128)S(1)}, f32[24,768]{1,0:T(8,128)}, u32[]{:S(2)}) copy-start(f32[24,768]{1,0:T(8,128)} %refs_0_.1) | copy-start | bytes 221188
  357.3 38.0 %copy-start.29 = (f32[24,768]{1,0:T(8,128)S(1)}, f32[24,768]{1,0:T(8,128)}, u32[]{:S(2)}) copy-start(f32[24,768]{1,0:T(8,128)} %refs_1_.1) | copy-start | bytes 221188
  357.3 38.0 %copy-start.31 = (f32[24,768]{1,0:T(8,128)S(1)}, f32[24,768]{1,0:T(8,128)}, u32[]{:S(2)}) copy-start(f32[24,768]{1,0:T(8,128)} %refs_2_.1) | copy-start | bytes 221188
  358.2 19.2 %collective-permute-start.39 = (bf16[1,24,3072]{2,1,0:T(8,128)(2,1)}, bf16[1,24,3072]{2,1,0:T(8,128)(2,1)S(1)}, u32[]{:S(2)}, u32[]{:S(2)}) collective-permute-start(bf16[1,24,3072]{2,1,0:T(8,128)(2,1)} %get-tuple-element.173), channel_id=1, source_target_pairs={{0,8},{1,9},{2,10},{3,11},{4,12},{5,13},{6,14},{7,15},{8,0},{9,1},... | collective-permute-start | bytes 442376 | tf_op jit(solution)/shard_map/ppermute | solution.py:337
  358.6 18.8 %collective-permute-start.40 = (bf16[1,24,3072]{2,1,0:T(8,128)(2,1)S(1)}, bf16[1,24,3072]{2,1,0:T(8,128)(2,1)}, u32[]{:S(2)}, u32[]{:S(2)}) collective-permute-start(bf16[1,24,3072]{2,1,0:T(8,128)(2,1)S(1)} %get-tuple-element.172), channel_id=1, source_target_pairs={{0,16},{1,17},{2,18},{3,19},{4,20},{5,21},{6,22},{7,23},{8,24},{9,... | collective-permute-start | bytes 442376 | tf_op jit(solution)/shard_map/ppermute | solution.py:337
  360.6 16.8 %collective-permute-start.41 = (bf16[1,24,3072]{2,1,0:T(8,128)(2,1)S(1)}, bf16[1,24,3072]{2,1,0:T(8,128)(2,1)}, u32[]{:S(2)}, u32[]{:S(2)}) collective-permute-start(bf16[1,24,3072]{2,1,0:T(8,128)(2,1)S(1)} %get-tuple-element.171), channel_id=1, source_target_pairs={{0,24},{1,25},{2,26},{3,27},{4,28},{5,29},{6,30},{7,31},{8,16},{9,... | collective-permute-start | bytes 442376 | tf_op jit(solution)/shard_map/ppermute | solution.py:337
  363.3 7.8 %collective-permute-start.50 = (bf16[2,24,1024]{2,1,0:T(8,128)(2,1)S(1)}, bf16[2,24,1024]{2,1,0:T(8,128)(2,1)S(1)}, u32[]{:S(2)}, u32[]{:S(2)}) collective-permute-start(bf16[2,24,1024]{2,1,0:T(8,128)(2,1)S(1)} %pad_maximum_fusion.22), channel_id=1, source_target_pairs={{0,2},{1,3},{2,0},{3,1},{4,6},{5,7},{6,4},{7,5},{8,10},{9,11},{10,... | collective-permute-start | bytes 294920 | tf_op jit(solution)/shard_map/ppermute | solution.py:337
  365.4 17.1 %collective-permute-start.42 = (bf16[256,768]{1,0:T(8,128)(2,1)}, bf16[256,768]{1,0:T(8,128)(2,1)S(1)}, u32[]{:S(2)}, u32[]{:S(2)}) collective-permute-start(bf16[256,768]{1,0:T(8,128)(2,1)} %get-tuple-element.146), channel_id=1, source_target_pairs={{0,12},{4,16},{8,20},{12,24},{16,28},{1,13},{5,17},{9,21},{13,25},... | collective-permute-start | bytes 1179656 | tf_op jit(solution)/shard_map/ppermute | solution.py:332
  371.1 22.4 %collective-permute-start.43 = (bf16[256,768]{1,0:T(8,128)(2,1)}, bf16[256,768]{1,0:T(8,128)(2,1)S(1)}, u32[]{:S(2)}, u32[]{:S(2)}) collective-permute-start(bf16[256,768]{1,0:T(8,128)(2,1)} %get-tuple-element.145), channel_id=1, source_target_pairs={{12,0},{16,4},{20,8},{24,12},{28,16},{13,1},{17,5},{21,9},{25,13},... | collective-permute-start | bytes 1179656 | tf_op jit(solution)/shard_map/ppermute | solution.py:332
  (48 other events, 284.3 us)
Sparse Core Ops, SparseCore 0:
  105.6 49.3 all-gather.2
  248.4 104.7 reduce-scatter.1

commit v3 on v2

--- a/solution.py
+++ b/solution.py
@@ -278,52 +278,98 @@
     )(first, last, queries, queries_turned, keys, keys_turned, values, grads, grads_turned, outs, logs, key_feat, query_feat, tiles)
 
 
-def diagonal_kernel(range_ref, tiles_ref, line_ref):
-    heads, tile_count = tiles_ref.shape[:2]
-    for index in range(tile_count):
-        used = (index >= range_ref[0]) & (index < range_ref[1])
-
-        @pl.when(used)
-        def _():
-            for head in range(heads):
-                tile = tiles_ref[head, index]
-                padded = jnp.concatenate([tile, jnp.zeros_like(tile)], axis=1)
-                size = TILE // 2
-                while size >= 8:
-                    padded = padded[:size] + pltpu.roll(padded[size:], 2 * TILE - size, 1)
-                    size //= 2
-                line_ref[head, index] = padded
-
-        @pl.when(jnp.logical_not(used))
-        def _():
-            for head in range(heads):
-                line_ref[head, index] = jnp.zeros((8, 2 * TILE), F32)
-
-
-def diagonal_sums(tiles, used, chunk):
+def table_kernel(range_ref, tiles_ref, bucket_ref, table_ref):
+    index = pl.program_id(0)
+    heads = tiles_ref.shape[0]
+
+    @pl.when(index == 0)
+    def _():
+        table_ref[...] = jnp.zeros_like(table_ref)
+
+    @pl.when((index >= range_ref[0]) & (index < range_ref[1]))
+    def _():
+        rows = []
+        for head in range(heads):
+            tile = tiles_ref[head, 0]
+            padded = jnp.concatenate([tile, jnp.zeros_like(tile)], axis=1)
+            size = TILE // 2
+            while size >= 1:
+                padded = padded[:size] + pltpu.roll(padded[size:], 2 * TILE - size, 1)
+                size //= 2
+            rows.append(padded)
+        sums = jnp.concatenate(rows, axis=0)
+        buckets = lax.broadcasted_iota(jnp.int32, (table_ref.shape[1], 2 * TILE), 0)
+        hot = (buckets == bucket_ref[0]).astype(F32)
+        table_ref[...] += lax.dot_general(
+            sums, hot, (((1,), (1,)), ((), ())), preferred_element_type=F32, precision=HIGHEST
+        )
+
+
+def table_sums(tiles, used, bucket_at, bucket_count):
     heads, tile_count = tiles.shape[:2]
-    results = []
-    for start in range(0, heads, chunk):
-        results.append(
-            pl.pallas_call(
-                diagonal_kernel,
-                out_shape=jax.ShapeDtypeStruct((chunk, tile_count, 8, 2 * TILE), F32),
-                grid_spec=pltpu.PrefetchScalarGridSpec(
-                    num_scalar_prefetch=1,
-                    grid=(1,),
-                    in_specs=[
-                        pl.BlockSpec(
-                            (chunk, tile_count, TILE, TILE),
-                            functools.partial(lambda first, h, r: (first, 0, 0, 0), start // chunk),
-                        )
-                    ],
-                    out_specs=pl.BlockSpec((chunk, tile_count, 8, 2 * TILE), lambda h, r: (0, 0, 0, 0)),
-                ),
-                cost_estimate=SMALL,
-                compiler_params=pltpu.CompilerParams(vmem_limit_bytes=40 << 20),
-            )(used, tiles)
-        )
-    return jnp.concatenate(results, axis=0)
+
+    def held(index, used_ref):
+        return jnp.minimum(jnp.maximum(index, used_ref[0]), used_ref[1] - 1)
+
+    return pl.pallas_call(
+        table_kernel,
+        out_shape=jax.ShapeDtypeStruct((heads, bucket_count), F32),
+        grid_spec=pltpu.PrefetchScalarGridSpec(
+            num_scalar_prefetch=1,
+            grid=(tile_count,),
+            in_specs=[
+                pl.BlockSpec((heads, 1, TILE, TILE), lambda t, r: (0, held(t, r), 0, 0)),
+                pl.BlockSpec((1, 1, 2 * TILE), lambda t, r: (t, 0, 0)),
+            ],
+            out_specs=pl.BlockSpec((heads, bucket_count), lambda t, r: (0, 0)),
+        ),
+        cost_estimate=SMALL,
+        compiler_params=pltpu.CompilerParams(vmem_limit_bytes=40 << 20),
+    )(used, tiles, bucket_at)
+
+
+def window_kernel(range_ref, key_ref, value_ref, key_weight_ref, value_weight_ref, out_ref):
+    index = pl.program_id(0)
+    tiles = out_ref.shape[0] // TILE
+    needed = ((index + 1) * tiles > range_ref[0]) & (index * tiles < range_ref[1])
+
+    @pl.when(needed)
+    def _():
+        out_ref[...] = (
+            contract(key_ref[...], key_weight_ref[...], 1, 1) + contract(value_ref[...], value_weight_ref[...], 1, 1)
+        ).astype(BF16)
+
+    @pl.when(jnp.logical_not(needed))
+    def _():
+        out_ref[...] = jnp.zeros_like(out_ref)
+
+
+def window_gradient(grad_keys, grad_values, weights, spots, covered, row_count):
+    window, width = grad_keys.shape
+    tiles = row_count // TILE
+
+    def rows(index, covered_ref):
+        low = lax.div(covered_ref[0], tiles)
+        high = lax.div(covered_ref[1] - 1, tiles)
+        return jnp.minimum(jnp.maximum(index, low), high), 0
+
+    return pl.pallas_call(
+        window_kernel,
+        out_shape=jax.ShapeDtypeStruct((window, width), BF16),
+        grid_spec=pltpu.PrefetchScalarGridSpec(
+            num_scalar_prefetch=1,
+            grid=(window // row_count,),
+            in_specs=[
+                pl.BlockSpec((row_count, width), rows),
+                pl.BlockSpec((row_count, width), rows),
+                pl.BlockSpec((width, width), lambda k, r: (0, spots[0])),
+                pl.BlockSpec((width, width), lambda k, r: (0, spots[1])),
+            ],
+            out_specs=pl.BlockSpec((row_count, width), lambda k, r: (k, 0)),
+        ),
+        cost_estimate=SMALL,
+        compiler_params=pltpu.CompilerParams(vmem_limit_bytes=40 << 20),
+    )(covered, grad_keys, grad_values, weights, weights)
 
 
 def shifted(value, axis, steps):
@@ -533,28 +579,33 @@
     )(rank[None].astype(jnp.int32), *held)
 
 
-def place_far_kernel(rank_ref, source_ref, pair_ref, down_ref, *, dp_count):
-    for owner in range(source_ref.shape[0]):
-        for entry in range(dp_count):
-            pair_ref[owner * dp_count + (rank_ref[0] ^ entry)] = source_ref[owner, entry]
-        for entry in range(dp_count // 2):
-            down_ref[owner, entry] = source_ref[owner, dp_count + entry]
-
-
-def place_far(held, dp_rank, dp_count):
-    count = held.shape[0]
-    shape = held.shape[2:]
-    return pl.pallas_call(
-        functools.partial(place_far_kernel, dp_count=dp_count),
+def place_far_kernel(rank_ref, *refs, masks, dp_count):
+    pair_ref, down_ref = refs[-2:]
+    rank = rank_ref[0]
+    for source, part in zip(refs, masks):
+        for index, mask in enumerate(part):
+            owner = rank ^ mask
+            for entry in range(dp_count):
+                pair_ref[owner ^ entry] = source[index, entry]
+            for entry in range(dp_count // 2):
+                down_ref[owner // dp_count, entry] = source[index, dp_count + entry]
+
+
+def place_far(held, masks, rank, dp_count):
+    count = sum(len(part) for part in masks)
+    shape = held[0].shape[2:]
+    dtype = held[0].dtype
+    return pl.pallas_call(
+        functools.partial(place_far_kernel, masks=masks, dp_count=dp_count),
         out_shape=(
-            jax.ShapeDtypeStruct((count * dp_count,) + shape, held.dtype),
-            jax.ShapeDtypeStruct((count, dp_count // 2) + shape, held.dtype),
+            jax.ShapeDtypeStruct((count * dp_count,) + shape, dtype),
+            jax.ShapeDtypeStruct((count, dp_count // 2) + shape, dtype),
         ),
-        in_specs=[pl.BlockSpec(memory_space=pltpu.SMEM), pl.BlockSpec(memory_space=pltpu.VMEM)],
+        in_specs=[pl.BlockSpec(memory_space=pltpu.SMEM)] + [pl.BlockSpec(memory_space=pltpu.VMEM)] * len(held),
         out_specs=(pl.BlockSpec(memory_space=pltpu.VMEM), pl.BlockSpec(memory_space=pltpu.VMEM)),
         cost_estimate=SMALL,
         compiler_params=pltpu.CompilerParams(vmem_limit_bytes=40 << 20),
-    )(dp_rank[None].astype(jnp.int32), held)
+    )(rank[None].astype(jnp.int32), *held)
 
 
 def split_and_swap(held, mine, group):
@@ -569,7 +620,10 @@
 
 
 def joined(kept, got):
-    return kept.astype(F32) + sum(piece.astype(F32) for piece in got)
+    values = [piece.astype(F32) for piece in [kept] + got]
+    while len(values) > 1:
+        values = [values[k] + values[k + 1] for k in range(0, len(values), 2)]
+    return values[0]
 
 
 def spread_dp(parts, bits):
@@ -600,18 +654,6 @@
             if not mask & step
         }
     return held[0]
-
-
-def sum_everywhere(value, groups):
-    for group in groups:
-        value = sum_in_pairs([value] + swaps(value, group))
-    return value
-
-
-def sum_in_pairs(values):
-    while len(values) > 1:
-        values = [values[k] + values[k + 1] for k in range(0, len(values), 2)]
-    return values[0]
 
 
 def parts_of(value, parts, to_rows):
@@ -678,6 +720,7 @@
     dp_bits = bits_of(dp_count)
     rank = seq_rank * dp_count + dp_rank
     groups = all_groups(device_count)
+    seq_groups = groups_of(dp_bits, bits_of(seq_count))
     own = blocks[0]
 
     gains = jnp.pad(jnp.stack([first_gain, second_gain], axis=1), ((0, 0), (0, TILE - 2)))
@@ -738,7 +781,10 @@
     down_parts = parts_of(down_weight.astype(BF16), 1, shard_rows * dp_count // 2)
     down_parts = down_parts.reshape(dp_count // 2, shard_rows, 2 * share)
     far_shard = stacked([part[None] for part in pair_parts] + [down_parts])
-    far_held = lax.all_gather(tie(far_shard, around)[0], "seq", axis=0, tiled=False)
+    far_shard = tie(far_shard, around)[0][None]
+    far_order = seq_groups[::-1]
+    far_first = swaps(far_shard, far_order[0])
+    far_own = [piece for group in far_order[1:2] for piece in swaps(far_shard, group)]
     gain_one = gain_columns[:, 0].astype(F32)[None, :]
     gain_two = gain_columns[:, 1].astype(F32)[None, :]
 
@@ -786,7 +832,18 @@
     outs, logs = attend(
         first, steps, queries_turned, keys, values_turned, key_feat, query_feat, tiles, head_dim, pairs
     )
-    far_full = place_far(tie(far_held, outs)[0], dp_rank, dp_count)
+    far_first = stacked(tie(far_first, outs)[0])
+    first_masks = swap_masks([0], far_order[0])
+    far_held, far_masks = [far_shard, far_first], [[0], first_masks]
+    for number, group in enumerate(far_order[1:]):
+        got, got_masks = [], []
+        for piece, part in zip(far_held, far_masks):
+            more = far_own if piece is far_shard and number == 0 else swaps(piece, group)
+            extra = swap_masks(part, group)
+            got += more
+            got_masks += [extra[k * len(part) : (k + 1) * len(part)] for k in range(len(more))]
+        far_held, far_masks = far_held + got, far_masks + got_masks
+    far_full = place_far(far_held, far_masks, rank, dp_count)
     weight_pair = far_full[0].reshape(device_count * shard_rows, 2 * share)
     weight_down = parts_of(far_full[1].reshape(-1, 2 * share), seq_count, unit)
     attended = (outs * valid_rows[None, :]).astype(BF16)
@@ -833,7 +890,8 @@
     far_grads, grad_mixed, grad_mixed_turned, grad_output_weight = tie(
         far_grads, grad_mixed, grad_mixed_turned, grad_output_weight
     )
-    far_sum = lax.psum_scatter(far_grads, "seq", scatter_dimension=0, tiled=True)[0]
+    bits = seq_groups[0][1]
+    far_kept, far_got = split_and_swap(far_grads, seq_rank & ((1 << bits) - 1), seq_groups[0])
 
     queries = contract(normed_own, weight_query, 1, 0).astype(BF16)
     keys_turned = contract(weight_key, window_normed, 0, 1).astype(BF16)
@@ -842,8 +900,14 @@
         first, steps, queries, queries_turned, keys, keys_turned, values, grad_mixed, grad_mixed_turned,
         outs, logs, key_feat, query_feat, tiles, head_dim, pairs,
     )
-    partial = contract(grad_keys, weight_key, 1, 1) + contract(grad_values, weight_value, 1, 1)
-    partial_low = partial.astype(BF16)
+    grad_queries, grad_keys, grad_values, tile_sums, far_kept, far_got = tie(
+        grad_queries, grad_keys, grad_values, tile_sums, far_kept, far_got
+    )
+    for low, bits in seq_groups[1:]:
+        far_held = joined(far_kept, far_got).astype(BF16)
+        far_kept, far_got = split_and_swap(far_held, (rank >> low) & ((1 << bits) - 1), (low, bits))
+    covered = jnp.stack([jnp.min(first), jnp.max(first + steps * STEP)])
+    partial_low = window_gradient(grad_keys, grad_values, near_full, (1, 2), covered, row_count)
 
     def returned_from(low_rows, step):
         parts = []
@@ -852,40 +916,53 @@
             parts.append(shifted(part, "seq", turn))
         return parts
 
-    steps_left = list(range(1, reach + 1))
-    returned = []
-    partial_low, grad_queries, grad_keys, grad_values, tile_sums = tie(
-        partial_low, grad_queries, grad_keys, grad_values, tile_sums
-    )
-    tile_first = first - jnp.arange(query_blocks, dtype=jnp.int32) + (query_blocks - 1)
-    used = jnp.stack([jnp.min(tile_first), jnp.max(tile_first + steps * STEP)])
-    sums = diagonal_sums(tile_sums, used, 4)
-    for step in (steps_left.pop(0), steps_left.pop(-1)) if reach > 1 else steps_left:
-        returned += returned_from(partial_low, step)
+    returned = returned_from(partial_low, 1)
     grad_query_weight = contract(normed_own, grad_queries, 0, 1).astype(BF16)
     grad_key_weight = contract(window_normed, grad_keys, 0, 0).astype(BF16)
     grad_value_weight = contract(window_normed, grad_values, 0, 0).astype(BF16)
-    near_grads = jnp.concatenate([grad_query_weight, grad_key_weight, grad_value_weight, grad_output_weight], axis=1)
-    near_held = near_grads.reshape(device_count, shard_rows, 4 * width)
+
+    tile_first = first - jnp.arange(query_blocks, dtype=jnp.int32) + (query_blocks - 1)
+    used = jnp.stack([jnp.min(tile_first), jnp.max(tile_first + steps * STEP)])
+    flipped = bucket_line.reshape(tile_count + 1, TILE)[::-1]
+    bucket_at = jnp.concatenate([flipped[:-1], flipped[1:]], axis=1)[:, None, :]
+    grad_table = table_sums(tile_sums, used, bucket_at, bucket_count).T
+    table_rows = -(-grad_table.size // TILE)
+    table_block = jnp.pad(grad_table.reshape(-1), (0, table_rows * TILE - grad_table.size)).reshape(table_rows, TILE)
+    table_block = jnp.pad(table_block, ((0, shard_rows - table_rows), (0, 0))).astype(BF16)
+    near_grads = jnp.concatenate(
+        [
+            grad_query_weight,
+            grad_key_weight,
+            grad_value_weight,
+            grad_output_weight,
+            jnp.tile(table_block, (device_count, 1)),
+        ],
+        axis=1,
+    )
+    near_grads, partial_low, returned, far_kept, far_got = tie(
+        near_grads, partial_low, returned, far_kept, far_got
+    )
+    far_sum = joined(far_kept, far_got).reshape(far_grads.shape[1:]).astype(BF16)
+
+    left = list(range(reach, 2, -1))
+    waiting = returned_from(partial_low, 2) if reach > 1 else []
+    near_held = near_grads.reshape(device_count, shard_rows, 4 * width + TILE)
     for stage, (low, bits) in enumerate(groups):
         kept, got = split_and_swap(near_held, (rank >> low) & ((1 << bits) - 1), (low, bits))
-        arrived = []
-        if stage and steps_left:
-            last_stage = stage == len(groups) - 1
-            for step in list(steps_left) if last_stage else steps_left[:1]:
-                steps_left.remove(step)
-                arrived += returned_from(partial_low, step)
         if stage == 0:
-            kept, got, returned, partial_low, sums = tie(kept, got, returned, partial_low, sums)
-        elif stage == 1:
-            kept, got, arrived, partial_low, far_sum = tie(kept, got, arrived, partial_low, far_sum)
+            kept, got, partial_low = tie(kept, got, partial_low)
         else:
-            kept, got, arrived, partial_low = tie(kept, got, arrived, partial_low)
-        returned = returned + arrived
+            arrived = returned_from(partial_low, left.pop(0)) if left else []
+            kept, got, arrived, waiting, partial_low, far_sum = tie(
+                kept, got, arrived, waiting, partial_low, far_sum
+            )
+            returned, waiting = returned + arrived + waiting, []
         total = joined(kept, got)
         near_held = total.astype(BF16)
-    near_sum = total.reshape(shard_rows, 4 * width)
-    grad_normed = partial[own_slice] + contract(grad_queries, weight_query, 0, 1)
+    for step in left:
+        returned = returned + returned_from(partial_low, step)
+    near_sum = total.reshape(shard_rows, 4 * width + TILE)
+    grad_normed = partial_low[own_slice].astype(F32) + contract(grad_queries, weight_query, 0, 1)
     grad_normed = grad_normed + sum(piece.astype(F32) for piece in returned)
     pair_back = spread_dp(
         {mask: lax.dynamic_index_in_dim(far_sum, dp_rank ^ mask, 0, keepdims=False) for mask in range(dp_count)}, dp_bits
@@ -898,14 +975,7 @@
         scaled_one - normed_rows * jnp.mean(scaled_one * normed_rows, axis=1, keepdims=True)
     )
 
-    diagonals = sum(jnp.roll(sums[:, :, row], -row, axis=2) for row in range(8))
-    flipped = bucket_line.reshape(tile_count + 1, TILE)[::-1]
-    bucket_at = jnp.concatenate([flipped[:-1], flipped[1:]], axis=1).reshape(-1)
-    bucket_hot = (bucket_at[:, None] == bucket_ids[None, :]).astype(F32)
-    grad_table = lax.dot_general(
-        bucket_hot, diagonals.reshape(heads, -1), (((0,), (1,)), ((), ())), precision=HIGHEST
-    )
-    grad_table = sum_everywhere(grad_table, [(bit, 1) for bit in range(bits_of(device_count))])
+    grad_table = near_sum[:table_rows, 4 * width :].reshape(-1)[: table_weight.size].reshape(table_weight.shape)
 
     def gain_grad(gain, weights, grads):
         total = sum(jnp.sum(weight.astype(BF16).astype(F32) * grad, axis=1) for weight, grad in zip(weights, grads))

time: 413 us -> 387 us (0.937)
  the two profiles are of different devices: /device:TPU:4 before, /device:TPU:0 now
where the time goes in v3:
time: 387 us; the launch traced here: 380 us
  starting transfers between devices  93.7 us (24%)
  waiting for transfers between devices  89.3 us (23%)
  Pallas kernels  79.7 us (21%)
  matrix products  45.1 us (12%)
  local copies, waits for them, and re-layouts  40.5 us (10%)
  other arithmetic  29.8 us (8%)
    ppermute x39, waiting for transfers between devices, flat_swap(): lax.ppermute(value, BOTH, [(source, source ^ mask) for source in range(co...  59.9 us
    ppermute x39, starting transfers between devices, flat_swap(): lax.ppermute(value, BOTH, [(source, source ^ mask) for source in range(co...  47 us
    ppermute x16, starting transfers between devices, shifted(): return lax.ppermute(value, axis, pairs)  46.7 us
    dot_general x20, matrix products, contract(): lax.dot_general(left_side, right_side, (((left_dim,), (right_dim,)), ((),...  44.9 us
    ppermute x16, waiting for transfers between devices, shifted(): return lax.ppermute(value, axis, pairs)  29.3 us
    pallas_call x1, Pallas kernels, attend_back(): pl.pallas_call(kernel, out_shape=(jax.ShapeDtypeStruct((width, row_count)...  25.9 us
    unnamed x112, local copies, waits for them, and re-layouts  18.8 us
    pallas_call x1, Pallas kernels, attend(): pl.pallas_call(kernel, out_shape=(jax.ShapeDtypeStruct((width, row_count)...  12.3 us
  transfers between devices with their start and end apart: 55, of which 13 were waited for; matrix products, arithmetic and copies ran while one was open for 20% of the time, Pallas kernels for 21%

profile of v3, /device:TPU:0, one launch (start us, length us, event | category | flops | bytes accessed | tf_op | source)
XLA Modules:
  0.0 380.1 jit_solution(7418138582805852061)
XLA Ops:
  2.1 5.5 %collective-permute-start.4 = (bf16[256,768]{1,0:T(8,128)(2,1)}, bf16[256,768]{1,0:T(8,128)(2,1)S(1)}, u32[]{:S(2)}, u32[]{:S(2)}) collective-permute-start(bf16[256,768]{1,0:T(8,128)(2,1)} %bitcast.137), channel_id=1, source_target_pairs={{0,4},{4,8},{8,12},{12,16},{16,20},{20,24},{24,28},{1,5},{5,9},{9,... | collective-permute-start | bytes 1179656 | tf_op jit(solution)/shard_map/ppermute | solution.py:378
  12.0 2.1 collective-permute-start
  14.1 2.6 collective-permute-start.1
  16.7 1.8 shard_map.236
  18.5 1.5 fusion.62
  23.8 4.0 %collective-permute-done.1.refs_2_ = bf16[1,24,3200]{2,1,0:T(8,128)(2,1)S(1)} collective-permute-done((bf16[1,24,3200]{2,1,0:T(8,128)(2,1)S(1)}, bf16[1,24,3200]{2,1,0:T(8,128)(2,1)S(1)}, u32[]{:S(2)}, u32[]{:S(2)}) %collective-permute-start.1) | collective-permute-done | bytes 153632 | tf_op jit(solution)/shard_map/ppermute | solution.py:383
  27.9 2.5 collective-permute-start.9
  31.9 1.6 collective-permute-start.5
  33.4 4.1 %collective-permute-start.6 = (bf16[4,24,3200]{2,1,0:T(8,128)(2,1)S(1)}, bf16[4,24,3200]{2,1,0:T(8,128)(2,1)S(1)}, u32[]{:S(2)}, u32[]{:S(2)}) collective-permute-start(bf16[4,24,3200]{2,1,0:T(8,128)(2,1)S(1)} %shard_map.230.refs_0_), channel_id=1, source_target_pairs={{0,4},{1,5},{2,6},{3,7},{4,0},{5,1},{6,2},{7,3},{8,12},{9,13},{10,... | collective-permute-start | bytes 1843208 | tf_op jit(solution)/shard_map/ppermute | solution.py:383
  41.6 12.2 %shard_map.231.tiles_ref = f32[12,19,128,128]{3,2,1,0:T(8,128)} custom-call(f32[12,1,2560]{2,1,0:T(1,128)} %reshape.229.line_ref), custom_call_target="tpu_custom_call" | custom-call | flops 1 | bytes 1 | tf_op jit(solution)/shard_map/pallas_call | solution.py:43
  54.5 5.3 %collective-permute-start.11 = (bf16[256,768]{1,0:T(8,128)(2,1)S(1)}, bf16[256,768]{1,0:T(8,128)(2,1)}, u32[]{:S(2)}, u32[]{:S(2)}) collective-permute-start(bf16[256,768]{1,0:T(8,128)(2,1)S(1)} %bitcast.140), channel_id=1, source_target_pairs={{0,16},{4,20},{8,24},{12,28},{1,17},{5,21},{9,25},{13,29},{2,18},{... | collective-permute-start | bytes 1179656 | tf_op jit(solution)/shard_map/ppermute | solution.py:378
  59.9 3.5 collective-permute-start.12
  72.3 1.7 select_convert_fusion.key_feat_ref
  77.4 1.6 collective-permute-start.19
  80.3 1.9 collective-permute-done.19
  82.2 1.5 collective-permute-start.14
  87.2 1.9 pad_add_fusion.3.range_ref
  91.6 1.6 collective-permute-start.29
  93.1 10.3 %collective-permute-done.14.refs_8_ = bf16[256,768]{1,0:T(8,128)(2,1)} collective-permute-done((bf16[256,768]{1,0:T(8,128)(2,1)S(1)}, bf16[256,768]{1,0:T(8,128)(2,1)}, u32[]{:S(2)}, u32[]{:S(2)}) %collective-permute-start.14) | collective-permute-done | bytes 393248 | tf_op jit(solution)/shard_map/ppermute | solution.py:378
  103.4 4.4 %collective-permute-start.22 = (bf16[1,6,24,1024]{3,2,1,0:T(8,128)(2,1)S(1)}, bf16[1,6,24,1024]{3,2,1,0:T(8,128)(2,1)}, u32[]{:S(2)}, u32[]{:S(2)}) collective-permute-start(bf16[1,6,24,1024]{3,2,1,0:T(8,128)(2,1)S(1)} %bitcast.147), channel_id=1, source_target_pairs={{0,24},{1,25},{2,26},{3,27},{4,28},{5,29},{6,30},{7,31},{8,16},{9,... | collective-permute-start | bytes 884744 | tf_op jit(solution)/shard_map/ppermute | solution.py:383
  108.9 2.1 shard_map.233
  111.1 4.4 %shard_map.234 = bf16[2304,768]{1,0:T(8,128)(2,1)S(1)} custom-call(bf16[768,3200]{1,0:T(8,128)(2,1)S(1)} %bitcast.122, bf16[256,768]{1,0:T(8,128)(2,1)} %collective-permute-done.11.refs_0_, bf16[256,768]{1,0:T(8,128)(2,1)} %collective-permute-done.12.refs_1_, bf16[256,768]{1,0:T(8,128)(2,1)} %collective-permute-done.9.refs_2_, ...), custom_call_target="tpu_custom_call" | custom-call | tf_op jit(solution)/shard_map/pallas_call | solution.py:550
  115.4 4.5 %convolution_convert_fusion.2.value_turned_ref = bf16[768,2304]{1,0:T(8,128)(2,1)} fusion(bf16[2304,768]{1,0:T(8,128)(2,1)S(1)} %shard_map.234, bf16[768,3200]{1,0:T(8,128)(2,1)S(1)} %bitcast.123), kind=kOutput, calls=%fused_computation.2 | convolution fusion | flops 2719678464 | bytes 8257536 | tf_op jit(solution)/shard_map/dot_general | solution.py:670
  119.9 4.3 %convolution_convert_fusion.3.key_ref = bf16[2304,768]{1,0:T(8,128)(2,1)} fusion(bf16[2304,768]{1,0:T(8,128)(2,1)S(1)} %shard_map.234, bf16[768,3200]{1,0:T(8,128)(2,1)S(1)} %bitcast.124), kind=kOutput, calls=%fused_computation.3 | convolution fusion | flops 2719678464 | bytes 8257536 | tf_op jit(solution)/shard_map/dot_general | solution.py:670
  125.1 12.3 %shard_map.235 = (f32[768,256]{1,0:T(8,128)S(1)}, f32[3,4,256]{2,1,0:T(4,128)S(1)}) custom-call(s32[2]{0:T(128)S(1)} %get-tuple-element.196.first_ref, s32[2]{0:T(128)S(1)} %get-tuple-element.197.last_ref, bf16[768,256]{1,0:T(8,128)(2,1)S(1)} %convolution_convert_fusion.15.query_ref.query_turned_ref, bf16[2304,768]{1,0:T(8,128)(2,1)} %convolution_convert_fusion.3.key_ref, ...), custom_call_target="tpu_custom_call" | custom-call | flops 4026531840 | bytes 25165824 | tf_op jit(solution)/shard_map/pallas_call | solution.py:145
  141.5 4.4 %convolution_convert_fusion.value_ref = bf16[2304,768]{1,0:T(8,128)(2,1)} fusion(bf16[2304,768]{1,0:T(8,128)(2,1)S(1)} %shard_map.234, bf16[768,3200]{1,0:T(8,128)(2,1)S(1)} %bitcast.128), kind=kOutput, calls=%fused_computation | convolution fusion | flops 2719678464 | bytes 8257536 | tf_op jit(solution)/shard_map/dot_general | solution.py:670
  146.8 4.7 %convolution_convert_fusion.1.key_turned_ref = bf16[768,2304]{1,0:T(8,128)(2,1)} fusion(bf16[2304,768]{1,0:T(8,128)(2,1)S(1)} %shard_map.234, bf16[768,3200]{1,0:T(8,128)(2,1)S(1)} %bitcast.129), kind=kOutput, calls=%fused_computation.1 | convolution fusion | flops 2719678464 | bytes 8257536 | tf_op jit(solution)/shard_map/dot_general | solution.py:670
  152.2 10.3 %collective-permute-done.24.refs_3_ = bf16[3,6,24,1024]{3,2,1,0:T(8,128)(2,1)S(1)} collective-permute-done((bf16[3,6,24,1024]{3,2,1,0:T(8,128)(2,1)S(1)}, bf16[3,6,24,1024]{3,2,1,0:T(8,128)(2,1)S(1)}, u32[]{:S(2)}, u32[]{:S(2)}) %collective-permute-start.24) | collective-permute-done | bytes 884768 | tf_op jit(solution)/shard_map/ppermute | solution.py:383
  163.6 1.9 fusion.41
  165.5 3.3 fusion.6
  170.5 1.9 convolution_convert_fusion.6
  173.0 1.8 convolution_convert_fusion.5
  174.8 2.0 convolution_convert_fusion.11
  177.0 2.0 collective-permute-start.33
  179.4 9.5 %collective-permute-done.33 = bf16[256,768]{1,0:T(8,128)(2,1)S(1)} collective-permute-done((bf16[256,768]{1,0:T(8,128)(2,1)S(1)}, bf16[256,768]{1,0:T(8,128)(2,1)S(1)}, u32[]{:S(2)}, u32[]{:S(2)}) %collective-permute-start.33) | collective-permute-done | bytes 393248 | tf_op jit(solution)/shard_map/ppermute | solution.py:383
  189.3 7.4 %collective-permute-done.27 = bf16[256,768]{1,0:T(8,128)(2,1)S(1)} collective-permute-done((bf16[256,768]{1,0:T(8,128)(2,1)S(1)}, bf16[256,768]{1,0:T(8,128)(2,1)S(1)}, u32[]{:S(2)}, u32[]{:S(2)}) %collective-permute-start.27) | collective-permute-done | bytes 393248 | tf_op jit(solution)/shard_map/ppermute | solution.py:383
  198.0 1.5 convolution_convert_fusion.10
  199.5 1.6 fusion.12.grad_turned_ref
  202.4 1.7 dynamic-slice_bitcast_fusion.2
  206.3 25.9 %shard_map.240 = (bf16[768,256]{1,0:T(8,128)(2,1)}, bf16[2304,768]{1,0:T(8,128)(2,1)}, bf16[2304,768]{1,0:T(8,128)(2,1)}, f32[12,19,128,128]{3,2,1,0:T(8,128)}) custom-call(s32[2]{0:T(128)} %copy-done.33, s32[2]{0:T(128)} %copy-done.34, bf16[256,768]{1,0:T(8,128)(2,1)} %convolution_convert_fusion.14.query_ref, ...), custom_call_target="tpu_custom_call", output_to_operand_aliasing={{3}: (13, {})} | custom-call | flops 10066329600 | bytes 33554432 | tf_op jit(solution)/shard_map/pallas_call | solution.py:238
  233.7 3.7 collective-permute-start.37
  239.9 2.0 copy-done.6
  241.9 5.8 %shard_map.242 = bf16[2304,768]{1,0:T(8,128)(2,1)S(1)} custom-call(s32[2]{0:T(128)S(1)} %pad_add_fusion.4.range_ref, bf16[2304,768]{1,0:T(8,128)(2,1)S(1)} %copy-done.6, bf16[2304,768]{1,0:T(8,128)(2,1)S(1)} %copy-done.5, bf16[768,3200]{1,0:T(8,128)(2,1)} %bitcast.133, bf16[768,3200]{1,0:T(8,128)(2,1)} %bitcast.134), custom_call_target="tpu_custom_call" | custom-call | flops 1 | bytes 1 | tf_op jit(solution)/shard_map/pallas_call | solution.py:356
  248.6 3.5 collective-permute-start.35
  253.9 3.1 fusion.8
  257.0 3.1 fusion.7
  260.1 10.9 %shard_map.241 = f32[12,32]{1,0:T(8,128)S(1)} custom-call(s32[2]{0:T(128)S(1)} %copy-done.35, f32[12,19,128,128]{3,2,1,0:T(8,128)} %get-tuple-element.112.tiles_ref, s32[19,1,256]{2,1,0:T(1,128)S(1)} %copy-done.31), custom_call_target="tpu_custom_call" | custom-call | flops 1 | bytes 1 | tf_op jit(solution)/shard_map/pallas_call | solution.py:314
  271.3 2.5 constant_dynamic-update-slice_fusion.1
  274.6 5.0 %dynamic-slice_bitcast_fusion = (bf16[16,24,3200]{2,1,0:T(8,128)(2,1)}, bf16[16,24,3200]{2,1,0:T(8,128)(2,1)}) fusion(bf16[16,2,24,3200]{3,2,1,0:T(8,128)(2,1)} %bitcast.161, s32[]{:T(128)S(6)} %select_n.102, s32[]{:T(128)S(6)} %select_n.101), kind=kLoop, calls=%fused_computation.8 | loop fusion | bytes 9830408 | tf_op jit(solution)/shard_map/jit(dynamic_index_in_dim)/squeeze | solution.py:616
  280.9 5.2 %collective-permute-start.46 = (bf16[256,768]{1,0:T(8,128)(2,1)S(1)}, bf16[256,768]{1,0:T(8,128)(2,1)S(1)}, u32[]{:S(2)}, u32[]{:S(2)}) collective-permute-start(bf16[256,768]{1,0:T(8,128)(2,1)S(1)} %get-tuple-element.206), channel_id=1, source_target_pairs={{0,8},{4,12},{8,16},{12,20},{16,24},{20,28},{1,9},{5,13},{9,17},{1... | collective-permute-start | bytes 1179656 | tf_op jit(solution)/shard_map/ppermute | solution.py:378
  287.4 3.0 add_convert_fusion
  290.7 4.9 %collective-permute-start.41 = (bf16[4,24,3200]{2,1,0:T(8,128)(2,1)S(1)}, bf16[4,24,3200]{2,1,0:T(8,128)(2,1)S(1)}, u32[]{:S(2)}, u32[]{:S(2)}) collective-permute-start(bf16[4,24,3200]{2,1,0:T(8,128)(2,1)S(1)} %get-tuple-element.213), channel_id=1, source_target_pairs={{0,2},{1,3},{2,0},{3,1},{4,6},{5,7},{6,4},{7,5},{8,10},{9,11},{10,... | collective-permute-start | bytes 1843208 | tf_op jit(solution)/shard_map/ppermute | solution.py:383
  297.4 7.8 %collective-permute-start.44 = (bf16[256,768]{1,0:T(8,128)(2,1)S(1)}, bf16[256,768]{1,0:T(8,128)(2,1)S(1)}, u32[]{:S(2)}, u32[]{:S(2)}) collective-permute-start(bf16[256,768]{1,0:T(8,128)(2,1)S(1)} %get-tuple-element.208), channel_id=1, source_target_pairs={{0,16},{4,20},{8,24},{12,28},{1,17},{5,21},{9,25},{13,29},{2,18},{... | collective-permute-start | bytes 1179656 | tf_op jit(solution)/shard_map/ppermute | solution.py:378
  307.9 5.6 %collective-permute-done.44 = bf16[256,768]{1,0:T(8,128)(2,1)S(1)} collective-permute-done((bf16[256,768]{1,0:T(8,128)(2,1)S(1)}, bf16[256,768]{1,0:T(8,128)(2,1)S(1)}, u32[]{:S(2)}, u32[]{:S(2)}) %collective-permute-start.44) | collective-permute-done | bytes 393248 | tf_op jit(solution)/shard_map/ppermute | solution.py:378
  313.5 13.4 %collective-permute-done.45 = bf16[256,768]{1,0:T(8,128)(2,1)S(1)} collective-permute-done((bf16[256,768]{1,0:T(8,128)(2,1)S(1)}, bf16[256,768]{1,0:T(8,128)(2,1)S(1)}, u32[]{:S(2)}, u32[]{:S(2)}) %collective-permute-start.45) | collective-permute-done | bytes 393248 | tf_op jit(solution)/shard_map/ppermute | solution.py:378
  327.0 2.8 collective-permute-start.51
  331.5 2.0 collective-permute-start.48
  333.5 5.8 %collective-permute-start.49 = (bf16[1,24,3200]{2,1,0:T(8,128)(2,1)S(1)}, bf16[1,24,3200]{2,1,0:T(8,128)(2,1)S(1)}, u32[]{:S(2)}, u32[]{:S(2)}) collective-permute-start(bf16[1,24,3200]{2,1,0:T(8,128)(2,1)S(1)} %get-tuple-element.228), channel_id=1, source_target_pairs={{0,16},{1,17},{2,18},{3,19},{4,20},{5,21},{6,22},{7,23},{8,24},{9,... | collective-permute-start | bytes 460808 | tf_op jit(solution)/shard_map/ppermute | solution.py:383
  339.3 1.8 fusion.26
  341.1 1.7 collective-permute-done.48
  342.8 21.2 %collective-permute-done.49 = bf16[1,24,3200]{2,1,0:T(8,128)(2,1)S(1)} collective-permute-done((bf16[1,24,3200]{2,1,0:T(8,128)(2,1)S(1)}, bf16[1,24,3200]{2,1,0:T(8,128)(2,1)S(1)}, u32[]{:S(2)}, u32[]{:S(2)}) %collective-permute-start.49) | collective-permute-done | bytes 153632 | tf_op jit(solution)/shard_map/ppermute | solution.py:383
  364.9 1.9 fusion.30
  372.3 2.5 collective-permute-done.54
  375.5 1.8 shard_map.243
  (280 shorter events, 78.4 us)
Async XLA Ops:
  0.6 40.0 %copy-start = (f32[32,12]{0,1:T(8,128)S(1)}, f32[32,12]{0,1:T(8,128)}, u32[]{:S(2)}) copy-start(f32[32,12]{0,1:T(8,128)} %param.22) | copy-start | bytes 4612
  0.7 37.8 %copy-start.49 = (s32[2047]{0:T(1024)S(1)}, s32[2047]{0:T(1024)}, u32[]{:S(2)}) copy-start(s32[2047]{0:T(1024)} %param.16) | copy-start | bytes 24568
  0.7 29.6 %collective-permute-start.3 = (bf16[256,768]{1,0:T(8,128)(2,1)}, bf16[256,768]{1,0:T(8,128)(2,1)S(1)}, u32[]{:S(2)}, u32[]{:S(2)}) collective-permute-start(bf16[256,768]{1,0:T(8,128)(2,1)} %bitcast.136), channel_id=1, source_target_pairs={{4,0},{8,4},{12,8},{16,12},{20,16},{24,20},{28,24},{5,1},{9,5},{13... | collective-permute-start | bytes 1179656 | tf_op jit(solution)/shard_map/ppermute | solution.py:378
  2.1 29.0 %collective-permute-start.4 = (bf16[256,768]{1,0:T(8,128)(2,1)}, bf16[256,768]{1,0:T(8,128)(2,1)S(1)}, u32[]{:S(2)}, u32[]{:S(2)}) collective-permute-start(bf16[256,768]{1,0:T(8,128)(2,1)} %bitcast.137), channel_id=1, source_target_pairs={{0,4},{4,8},{8,12},{12,16},{16,20},{20,24},{24,28},{1,5},{5,9},{9,... | collective-permute-start | bytes 1179656 | tf_op jit(solution)/shard_map/ppermute | solution.py:378
  12.0 10.6 %collective-permute-start = (bf16[1,24,3200]{2,1,0:T(8,128)(2,1)S(1)}, bf16[1,24,3200]{2,1,0:T(8,128)(2,1)S(1)}, u32[]{:S(2)}, u32[]{:S(2)}) collective-permute-start(bf16[1,24,3200]{2,1,0:T(8,128)(2,1)S(1)} %bitcast.150), channel_id=1, source_target_pairs={{0,8},{1,9},{2,10},{3,11},{4,12},{5,13},{6,14},{7,15},{8,0},{9,1},... | collective-permute-start | bytes 460808 | tf_op jit(solution)/shard_map/ppermute | solution.py:383
  14.1 13.8 %collective-permute-start.1 = (bf16[1,24,3200]{2,1,0:T(8,128)(2,1)S(1)}, bf16[1,24,3200]{2,1,0:T(8,128)(2,1)S(1)}, u32[]{:S(2)}, u32[]{:S(2)}) collective-permute-start(bf16[1,24,3200]{2,1,0:T(8,128)(2,1)S(1)} %bitcast.151), channel_id=1, source_target_pairs={{0,16},{1,17},{2,18},{3,19},{4,20},{5,21},{6,22},{7,23},{8,24},{9,... | collective-permute-start | bytes 460808 | tf_op jit(solution)/shard_map/ppermute | solution.py:383
  16.7 13.6 %collective-permute-start.2 = (bf16[1,24,3200]{2,1,0:T(8,128)(2,1)S(1)}, bf16[1,24,3200]{2,1,0:T(8,128)(2,1)S(1)}, u32[]{:S(2)}, u32[]{:S(2)}) collective-permute-start(bf16[1,24,3200]{2,1,0:T(8,128)(2,1)S(1)} %bitcast.152), channel_id=1, source_target_pairs={{0,24},{1,25},{2,26},{3,27},{4,28},{5,29},{6,30},{7,31},{8,16},{9,... | collective-permute-start | bytes 460808 | tf_op jit(solution)/shard_map/ppermute | solution.py:383
  22.5 31.3 %collective-permute-start.8 = (bf16[256,768]{1,0:T(8,128)(2,1)}, bf16[256,768]{1,0:T(8,128)(2,1)S(1)}, u32[]{:S(2)}, u32[]{:S(2)}) collective-permute-start(bf16[256,768]{1,0:T(8,128)(2,1)} %bitcast.138), channel_id=1, source_target_pairs={{8,0},{12,4},{16,8},{20,12},{24,16},{28,20},{9,1},{13,5},{17,9},{2... | collective-permute-start | bytes 1179656 | tf_op jit(solution)/shard_map/ppermute | solution.py:378
  27.9 32.0 %collective-permute-start.9 = (bf16[256,768]{1,0:T(8,128)(2,1)}, bf16[256,768]{1,0:T(8,128)(2,1)}, u32[]{:S(2)}, u32[]{:S(2)}) collective-permute-start(bf16[256,768]{1,0:T(8,128)(2,1)} %bitcast.139), channel_id=1, source_target_pairs={{0,8},{4,12},{8,16},{12,20},{16,24},{20,28},{1,9},{5,13},{9,17},{1... | collective-permute-start | bytes 1179656 | tf_op jit(solution)/shard_map/ppermute | solution.py:378
  31.9 31.4 %collective-permute-start.5 = (bf16[4,24,3200]{2,1,0:T(8,128)(2,1)S(1)}, bf16[4,24,3200]{2,1,0:T(8,128)(2,1)S(1)}, u32[]{:S(2)}, u32[]{:S(2)}) collective-permute-start(bf16[4,24,3200]{2,1,0:T(8,128)(2,1)S(1)} %shard_map.230.refs_0_), channel_id=1, source_target_pairs={{0,2},{1,3},{2,0},{3,1},{4,6},{5,7},{6,4},{7,5},{8,10},{9,11},{10,... | collective-permute-start | bytes 1843208 | tf_op jit(solution)/shard_map/ppermute | solution.py:383
  33.4 32.0 %collective-permute-start.6 = (bf16[4,24,3200]{2,1,0:T(8,128)(2,1)S(1)}, bf16[4,24,3200]{2,1,0:T(8,128)(2,1)S(1)}, u32[]{:S(2)}, u32[]{:S(2)}) collective-permute-start(bf16[4,24,3200]{2,1,0:T(8,128)(2,1)S(1)} %shard_map.230.refs_0_), channel_id=1, source_target_pairs={{0,4},{1,5},{2,6},{3,7},{4,0},{5,1},{6,2},{7,3},{8,12},{9,13},{10,... | collective-permute-start | bytes 1843208 | tf_op jit(solution)/shard_map/ppermute | solution.py:383
  37.5 28.8 %collective-permute-start.7 = (bf16[4,24,3200]{2,1,0:T(8,128)(2,1)S(1)}, bf16[4,24,3200]{2,1,0:T(8,128)(2,1)S(1)}, u32[]{:S(2)}, u32[]{:S(2)}) collective-permute-start(bf16[4,24,3200]{2,1,0:T(8,128)(2,1)S(1)} %shard_map.230.refs_0_), channel_id=1, source_target_pairs={{0,6},{1,7},{2,4},{3,5},{4,2},{5,3},{6,0},{7,1},{8,14},{9,15},{10,... | collective-permute-start | bytes 1843208 | tf_op jit(solution)/shard_map/ppermute | solution.py:383
  54.5 37.0 %collective-permute-start.11 = (bf16[256,768]{1,0:T(8,128)(2,1)S(1)}, bf16[256,768]{1,0:T(8,128)(2,1)}, u32[]{:S(2)}, u32[]{:S(2)}) collective-permute-start(bf16[256,768]{1,0:T(8,128)(2,1)S(1)} %bitcast.140), channel_id=1, source_target_pairs={{0,16},{4,20},{8,24},{12,28},{1,17},{5,21},{9,25},{13,29},{2,18},{... | collective-permute-start | bytes 1179656 | tf_op jit(solution)/shard_map/ppermute | solution.py:378
  59.9 33.3 %collective-permute-start.12 = (bf16[256,768]{1,0:T(8,128)(2,1)S(1)}, bf16[256,768]{1,0:T(8,128)(2,1)}, u32[]{:S(2)}, u32[]{:S(2)}) collective-permute-start(bf16[256,768]{1,0:T(8,128)(2,1)S(1)} %bitcast.141), channel_id=1, source_target_pairs={{0,12},{4,16},{8,20},{12,24},{16,28},{1,13},{5,17},{9,21},{13,25},... | collective-permute-start | bytes 1179656 | tf_op jit(solution)/shard_map/ppermute | solution.py:378
  64.1 29.0 %collective-permute-start.13 = (bf16[256,768]{1,0:T(8,128)(2,1)S(1)}, bf16[256,768]{1,0:T(8,128)(2,1)}, u32[]{:S(2)}, u32[]{:S(2)}) collective-permute-start(bf16[256,768]{1,0:T(8,128)(2,1)S(1)} %bitcast.142), channel_id=1, source_target_pairs={{12,0},{16,4},{20,8},{24,12},{28,16},{13,1},{17,5},{21,9},{25,13},... | collective-permute-start | bytes 1179656 | tf_op jit(solution)/shard_map/ppermute | solution.py:378
  66.3 9.6 %collective-permute-start.18 = (bf16[2,24,1024]{2,1,0:T(8,128)(2,1)}, bf16[2,24,1024]{2,1,0:T(8,128)(2,1)}, u32[]{:S(2)}, u32[]{:S(2)}) collective-permute-start(bf16[2,24,1024]{2,1,0:T(8,128)(2,1)} %pad_maximum_fusion.10), channel_id=1, source_target_pairs={{0,1},{1,0},{2,3},{3,2},{4,5},{5,4},{6,7},{7,6},{8,9},{9,8},{10,11... | collective-permute-start | bytes 294920 | tf_op jit(solution)/shard_map/ppermute | solution.py:383
  70.5 37.3 %collective-permute-start.10 = (bf16[16,24,3200]{2,1,0:T(8,128)(2,1)S(1)}, bf16[16,24,3200]{2,1,0:T(8,128)(2,1)}, u32[]{:S(2)}, u32[]{:S(2)}) collective-permute-start(bf16[16,24,3200]{2,1,0:T(8,128)(2,1)S(1)} %shard_map.232.refs_0_), channel_id=1, source_target_pairs={{0,1},{1,0},{2,3},{3,2},{4,5},{5,4},{6,7},{7,6},{8,9},{9,8},{10,11... | collective-permute-start | bytes 7372808 | tf_op jit(solution)/shard_map/ppermute | solution.py:383
  74.0 50.8 %copy-start.7 = (bf16[2304,128]{1,0:T(8,128)(2,1)}, bf16[2304,128]{1,0:T(8,128)(2,1)S(1)}, u32[]{:S(2)}) copy-start(bf16[2304,128]{1,0:T(8,128)(2,1)S(1)} %select_convert_fusion.key_feat_ref) | copy-start | bytes 1769476
  74.7 50.1 %copy-start.33 = (s32[2]{0:T(128)}, s32[2]{0:T(128)S(1)}, u32[]{:S(2)}) copy-start(s32[2]{0:T(128)S(1)} %get-tuple-element.196.first_ref) | copy-start | bytes 28
  74.7 50.1 %copy-start.34 = (s32[2]{0:T(128)}, s32[2]{0:T(128)S(1)}, u32[]{:S(2)}) copy-start(s32[2]{0:T(128)S(1)} %get-tuple-element.197.last_ref) | copy-start | bytes 28
  77.4 4.8 %collective-permute-start.19 = (bf16[2,24,1024]{2,1,0:T(8,128)(2,1)S(1)}, bf16[2,24,1024]{2,1,0:T(8,128)(2,1)S(1)}, u32[]{:S(2)}, u32[]{:S(2)}) collective-permute-start(bf16[2,24,1024]{2,1,0:T(8,128)(2,1)S(1)} %pad_maximum_fusion.11), channel_id=1, source_target_pairs={{0,2},{1,3},{2,0},{3,1},{4,6},{5,7},{6,4},{7,5},{8,10},{9,11},{10,... | collective-permute-start | bytes 294920 | tf_op jit(solution)/shard_map/ppermute | solution.py:383
  82.2 21.2 %collective-permute-start.14 = (bf16[256,768]{1,0:T(8,128)(2,1)S(1)}, bf16[256,768]{1,0:T(8,128)(2,1)}, u32[]{:S(2)}, u32[]{:S(2)}) collective-permute-start(bf16[256,768]{1,0:T(8,128)(2,1)S(1)} %bitcast.143), channel_id=1, source_target_pairs={{16,0},{20,4},{24,8},{28,12},{17,1},{21,5},{25,9},{29,13},{18,2},{... | collective-permute-start | bytes 1179656 | tf_op jit(solution)/shard_map/ppermute | solution.py:378
  91.6 59.9 %collective-permute-start.29 = (bf16[256,768]{1,0:T(8,128)(2,1)}, bf16[256,768]{1,0:T(8,128)(2,1)}, u32[]{:S(2)}, u32[]{:S(2)}) collective-permute-start(bf16[256,768]{1,0:T(8,128)(2,1)} %bitcast.165), channel_id=1, source_target_pairs={{0,2},{1,3},{2,0},{3,1},{4,6},{5,7},{6,4},{7,5},{8,10},{9,11},{10,... | collective-permute-start | bytes 1179656 | tf_op jit(solution)/shard_map/ppermute | solution.py:383
  103.4 35.6 %collective-permute-start.20 = (bf16[1,6,24,1024]{3,2,1,0:T(8,128)(2,1)S(1)}, bf16[1,6,24,1024]{3,2,1,0:T(8,128)(2,1)}, u32[]{:S(2)}, u32[]{:S(2)}) collective-permute-start(bf16[1,6,24,1024]{3,2,1,0:T(8,128)(2,1)S(1)} %bitcast.145), channel_id=1, source_target_pairs={{0,8},{1,9},{2,10},{3,11},{4,12},{5,13},{6,14},{7,15},{8,0},{9,1},... | collective-permute-start | bytes 884744 | tf_op jit(solution)/shard_map/ppermute | solution.py:383
  103.4 35.7 %collective-permute-start.21 = (bf16[1,6,24,1024]{3,2,1,0:T(8,128)(2,1)S(1)}, bf16[1,6,24,1024]{3,2,1,0:T(8,128)(2,1)}, u32[]{:S(2)}, u32[]{:S(2)}) collective-permute-start(bf16[1,6,24,1024]{3,2,1,0:T(8,128)(2,1)S(1)} %bitcast.146), channel_id=1, source_target_pairs={{0,16},{1,17},{2,18},{3,19},{4,20},{5,21},{6,22},{7,23},{8,24},{9,... | collective-permute-start | bytes 884744 | tf_op jit(solution)/shard_map/ppermute | solution.py:383
  103.4 35.7 %collective-permute-start.22 = (bf16[1,6,24,1024]{3,2,1,0:T(8,128)(2,1)S(1)}, bf16[1,6,24,1024]{3,2,1,0:T(8,128)(2,1)}, u32[]{:S(2)}, u32[]{:S(2)}) collective-permute-start(bf16[1,6,24,1024]{3,2,1,0:T(8,128)(2,1)S(1)} %bitcast.147), channel_id=1, source_target_pairs={{0,24},{1,25},{2,26},{3,27},{4,28},{5,29},{6,30},{7,31},{8,16},{9,... | collective-permute-start | bytes 884744 | tf_op jit(solution)/shard_map/ppermute | solution.py:383
  107.8 44.3 %collective-permute-start.23 = (bf16[1,6,24,1024]{3,2,1,0:T(8,128)(2,1)S(1)}, bf16[1,6,24,1024]{3,2,1,0:T(8,128)(2,1)}, u32[]{:S(2)}, u32[]{:S(2)}) collective-permute-start(bf16[1,6,24,1024]{3,2,1,0:T(8,128)(2,1)S(1)} %bitcast.148), channel_id=1, source_target_pairs={{0,4},{1,5},{2,6},{3,7},{4,0},{5,1},{6,2},{7,3},{8,12},{9,13},{10,... | collective-permute-start | bytes 884744 | tf_op jit(solution)/shard_map/ppermute | solution.py:383
  111.0 94.0 %copy-start.2 = (bf16[32,24,3200]{2,1,0:T(8,128)(2,1)}, bf16[32,24,3200]{2,1,0:T(8,128)(2,1)S(1)}, u32[]{:S(2)}) copy-start(bf16[32,24,3200]{2,1,0:T(8,128)(2,1)S(1)} %shard_map.233) | copy-start | bytes 14745604
  137.4 60.6 %copy-start.8 = (f32[768,256]{1,0:T(8,128)}, f32[768,256]{1,0:T(8,128)S(1)}, u32[]{:S(2)}) copy-start(f32[768,256]{1,0:T(8,128)S(1)} %get-tuple-element.93.out_ref) | copy-start | bytes 2359300
  139.0 7.8 %collective-permute-start.16 = (bf16[256,768]{1,0:T(8,128)(2,1)S(1)}, bf16[256,768]{1,0:T(8,128)(2,1)S(1)}, u32[]{:S(2)}, u32[]{:S(2)}) collective-permute-start(bf16[256,768]{1,0:T(8,128)(2,1)S(1)} %multiply_convert_fusion.2), channel_id=1, source_target_pairs={{0,2},{1,3},{2,0},{3,1},{4,6},{5,7},{6,4},{7,5},{8,10},{9,11},{10,... | collective-permute-start | bytes 1179656 | tf_op jit(solution)/shard_map/ppermute | solution.py:383
  139.1 24.5 %collective-permute-start.15 = (bf16[256,768]{1,0:T(8,128)(2,1)S(1)}, bf16[256,768]{1,0:T(8,128)(2,1)S(1)}, u32[]{:S(2)}, u32[]{:S(2)}) collective-permute-start(bf16[256,768]{1,0:T(8,128)(2,1)S(1)} %multiply_convert_fusion.2), channel_id=1, source_target_pairs={{0,1},{1,0},{2,3},{3,2},{4,5},{5,4},{6,7},{7,6},{8,9},{9,8},{10,11... | collective-permute-start | bytes 1179656 | tf_op jit(solution)/shard_map/ppermute | solution.py:383
  140.4 22.1 %collective-permute-start.24 = (bf16[3,6,24,1024]{3,2,1,0:T(8,128)(2,1)S(1)}, bf16[3,6,24,1024]{3,2,1,0:T(8,128)(2,1)S(1)}, u32[]{:S(2)}, u32[]{:S(2)}) collective-permute-start(bf16[3,6,24,1024]{3,2,1,0:T(8,128)(2,1)S(1)} %shard_map.238.refs_1_), channel_id=1, source_target_pairs={{0,4},{1,5},{2,6},{3,7},{4,0},{5,1},{6,2},{7,3},{8,12},{9,13},{10,... | collective-permute-start | bytes 2654216 | tf_op jit(solution)/shard_map/ppermute | solution.py:383
  146.8 16.8 %collective-permute-start.17 = (bf16[256,768]{1,0:T(8,128)(2,1)S(1)}, bf16[256,768]{1,0:T(8,128)(2,1)S(1)}, u32[]{:S(2)}, u32[]{:S(2)}) collective-permute-start(bf16[256,768]{1,0:T(8,128)(2,1)S(1)} %collective-permute-done.16), channel_id=1, source_target_pairs={{0,1},{1,0},{2,3},{3,2},{4,5},{5,4},{6,7},{7,6},{8,9},{9,8},{10,11... | collective-permute-start | bytes 1179656 | tf_op jit(solution)/shard_map/ppermute | solution.py:383
  151.5 14.0 %collective-permute-start.28 = (bf16[256,768]{1,0:T(8,128)(2,1)S(1)}, bf16[256,768]{1,0:T(8,128)(2,1)S(1)}, u32[]{:S(2)}, u32[]{:S(2)}) collective-permute-start(bf16[256,768]{1,0:T(8,128)(2,1)S(1)} %bitcast.166), channel_id=1, source_target_pairs={{0,1},{1,0},{2,3},{3,2},{4,5},{5,4},{6,7},{7,6},{8,9},{9,8},{10,11... | collective-permute-start | bytes 1179656 | tf_op jit(solution)/shard_map/ppermute | solution.py:383
  152.1 13.4 %collective-permute-start.30 = (bf16[256,768]{1,0:T(8,128)(2,1)}, bf16[256,768]{1,0:T(8,128)(2,1)S(1)}, u32[]{:S(2)}, u32[]{:S(2)}) collective-permute-start(bf16[256,768]{1,0:T(8,128)(2,1)} %collective-permute-done.29), channel_id=1, source_target_pairs={{0,1},{1,0},{2,3},{3,2},{4,5},{5,4},{6,7},{7,6},{8,9},{9,8},{10,11... | collective-permute-start | bytes 1179656 | tf_op jit(solution)/shard_map/ppermute | solution.py:383
  169.9 9.3 %collective-permute-start.26 = (bf16[256,768]{1,0:T(8,128)(2,1)S(1)}, bf16[256,768]{1,0:T(8,128)(2,1)S(1)}, u32[]{:S(2)}, u32[]{:S(2)}) collective-permute-start(bf16[256,768]{1,0:T(8,128)(2,1)S(1)} %get-tuple-element.220), channel_id=1, source_target_pairs={{0,1},{1,0},{2,3},{3,2},{4,5},{5,4},{6,7},{7,6},{8,9},{9,8},{10,11... | collective-permute-start | bytes 1179656 | tf_op jit(solution)/shard_map/ppermute | solution.py:383
  170.0 19.3 %collective-permute-start.25 = (bf16[256,768]{1,0:T(8,128)(2,1)S(1)}, bf16[256,768]{1,0:T(8,128)(2,1)S(1)}, u32[]{:S(2)}, u32[]{:S(2)}) collective-permute-start(bf16[256,768]{1,0:T(8,128)(2,1)S(1)} %get-tuple-element.219), channel_id=1, source_target_pairs={{0,1},{1,0},{2,3},{3,2},{4,5},{5,4},{6,7},{7,6},{8,9},{9,8},{10,11... | collective-permute-start | bytes 1179656 | tf_op jit(solution)/shard_map/ppermute | solution.py:383
  172.4 4.4 %collective-permute-start.32 = (bf16[256,768]{1,0:T(8,128)(2,1)S(1)}, bf16[256,768]{1,0:T(8,128)(2,1)S(1)}, u32[]{:S(2)}, u32[]{:S(2)}) collective-permute-start(bf16[256,768]{1,0:T(8,128)(2,1)S(1)} %get-tuple-element.218), channel_id=1, source_target_pairs={{0,1},{1,0},{2,3},{3,2},{4,5},{5,4},{6,7},{7,6},{8,9},{9,8},{10,11... | collective-permute-start | bytes 1179656 | tf_op jit(solution)/shard_map/ppermute | solution.py:383
  172.6 6.9 %collective-permute-start.31 = (bf16[256,768]{1,0:T(8,128)(2,1)S(1)}, bf16[256,768]{1,0:T(8,128)(2,1)S(1)}, u32[]{:S(2)}, u32[]{:S(2)}) collective-permute-start(bf16[256,768]{1,0:T(8,128)(2,1)S(1)} %get-tuple-element.217), channel_id=1, source_target_pairs={{0,1},{1,0},{2,3},{3,2},{4,5},{5,4},{6,7},{7,6},{8,9},{9,8},{10,11... | collective-permute-start | bytes 1179656 | tf_op jit(solution)/shard_map/ppermute | solution.py:383
  177.0 12.0 %collective-permute-start.33 = (bf16[256,768]{1,0:T(8,128)(2,1)S(1)}, bf16[256,768]{1,0:T(8,128)(2,1)S(1)}, u32[]{:S(2)}, u32[]{:S(2)}) collective-permute-start(bf16[256,768]{1,0:T(8,128)(2,1)S(1)} %add_convert_fusion.3), channel_id=1, source_target_pairs={{0,2},{1,3},{2,0},{3,1},{4,6},{5,7},{6,4},{7,5},{8,10},{9,11},{10,... | collective-permute-start | bytes 1179656 | tf_op jit(solution)/shard_map/ppermute | solution.py:383
  179.3 17.5 %collective-permute-start.27 = (bf16[256,768]{1,0:T(8,128)(2,1)S(1)}, bf16[256,768]{1,0:T(8,128)(2,1)S(1)}, u32[]{:S(2)}, u32[]{:S(2)}) collective-permute-start(bf16[256,768]{1,0:T(8,128)(2,1)S(1)} %add_convert_fusion.5), channel_id=1, source_target_pairs={{0,2},{1,3},{2,0},{3,1},{4,6},{5,7},{6,4},{7,5},{8,10},{9,11},{10,... | collective-permute-start | bytes 1179656 | tf_op jit(solution)/shard_map/ppermute | solution.py:383
  204.1 28.1 %collective-permute-start.34 = (bf16[4,6,24,1024]{3,2,1,0:T(8,128)(2,1)}, bf16[4,6,24,1024]{3,2,1,0:T(8,128)(2,1)S(1)}, u32[]{:S(2)}, u32[]{:S(2)}) collective-permute-start(bf16[4,6,24,1024]{3,2,1,0:T(8,128)(2,1)} %get-tuple-element.215), channel_id=1, source_target_pairs={{0,4},{1,5},{2,6},{3,7},{4,0},{5,1},{6,2},{7,3},{8,12},{9,13},{10,... | collective-permute-start | bytes 3538952 | tf_op jit(solution)/shard_map/ppermute | solution.py:383
  233.7 40.8 %collective-permute-start.37 = (bf16[1,6,24,1024]{3,2,1,0:T(8,128)(2,1)}, bf16[1,6,24,1024]{3,2,1,0:T(8,128)(2,1)}, u32[]{:S(2)}, u32[]{:S(2)}) collective-permute-start(bf16[1,6,24,1024]{3,2,1,0:T(8,128)(2,1)} %get-tuple-element.223), channel_id=1, source_target_pairs={{0,8},{1,9},{2,10},{3,11},{4,12},{5,13},{6,14},{7,15},{8,0},{9,1},... | collective-permute-start | bytes 884744 | tf_op jit(solution)/shard_map/ppermute | solution.py:383
  237.5 37.1 %collective-permute-start.38 = (bf16[1,6,24,1024]{3,2,1,0:T(8,128)(2,1)}, bf16[1,6,24,1024]{3,2,1,0:T(8,128)(2,1)}, u32[]{:S(2)}, u32[]{:S(2)}) collective-permute-start(bf16[1,6,24,1024]{3,2,1,0:T(8,128)(2,1)} %get-tuple-element.222), channel_id=1, source_target_pairs={{0,16},{1,17},{2,18},{3,19},{4,20},{5,21},{6,22},{7,23},{8,24},{9,... | collective-permute-start | bytes 884744 | tf_op jit(solution)/shard_map/ppermute | solution.py:383
  238.9 35.7 %collective-permute-start.39 = (bf16[1,6,24,1024]{3,2,1,0:T(8,128)(2,1)}, bf16[1,6,24,1024]{3,2,1,0:T(8,128)(2,1)}, u32[]{:S(2)}, u32[]{:S(2)}) collective-permute-start(bf16[1,6,24,1024]{3,2,1,0:T(8,128)(2,1)} %get-tuple-element.221), channel_id=1, source_target_pairs={{0,24},{1,25},{2,26},{3,27},{4,28},{5,29},{6,30},{7,31},{8,16},{9,... | collective-permute-start | bytes 884744 | tf_op jit(solution)/shard_map/ppermute | solution.py:383
  248.6 26.0 %collective-permute-start.35 = (bf16[256,768]{1,0:T(8,128)(2,1)}, bf16[256,768]{1,0:T(8,128)(2,1)}, u32[]{:S(2)}, u32[]{:S(2)}) collective-permute-start(bf16[256,768]{1,0:T(8,128)(2,1)} %get-tuple-element.210), channel_id=1, source_target_pairs={{0,4},{4,8},{8,12},{12,16},{16,20},{20,24},{24,28},{1,5},{5,9},{9,... | collective-permute-start | bytes 1179656 | tf_op jit(solution)/shard_map/ppermute | solution.py:378
  252.1 22.5 %collective-permute-start.36 = (bf16[256,768]{1,0:T(8,128)(2,1)}, bf16[256,768]{1,0:T(8,128)(2,1)}, u32[]{:S(2)}, u32[]{:S(2)}) collective-permute-start(bf16[256,768]{1,0:T(8,128)(2,1)} %get-tuple-element.209), channel_id=1, source_target_pairs={{4,0},{8,4},{12,8},{16,12},{20,16},{24,20},{28,24},{5,1},{9,5},{13... | collective-permute-start | bytes 1179656 | tf_op jit(solution)/shard_map/ppermute | solution.py:378
  279.6 7.7 %collective-permute-start.40 = (bf16[16,24,3200]{2,1,0:T(8,128)(2,1)}, bf16[16,24,3200]{2,1,0:T(8,128)(2,1)}, u32[]{:S(2)}, u32[]{:S(2)}) collective-permute-start(bf16[16,24,3200]{2,1,0:T(8,128)(2,1)} %get-tuple-element.200), channel_id=1, source_target_pairs={{0,1},{1,0},{2,3},{3,2},{4,5},{5,4},{6,7},{7,6},{8,9},{9,8},{10,11... | collective-permute-start | bytes 7372808 | tf_op jit(solution)/shard_map/ppermute | solution.py:383
  280.9 16.5 %collective-permute-start.46 = (bf16[256,768]{1,0:T(8,128)(2,1)S(1)}, bf16[256,768]{1,0:T(8,128)(2,1)S(1)}, u32[]{:S(2)}, u32[]{:S(2)}) collective-permute-start(bf16[256,768]{1,0:T(8,128)(2,1)S(1)} %get-tuple-element.206), channel_id=1, source_target_pairs={{0,8},{4,12},{8,16},{12,20},{16,24},{20,28},{1,9},{5,13},{9,17},{1... | collective-permute-start | bytes 1179656 | tf_op jit(solution)/shard_map/ppermute | solution.py:378
  286.1 19.1 %collective-permute-start.47 = (bf16[256,768]{1,0:T(8,128)(2,1)S(1)}, bf16[256,768]{1,0:T(8,128)(2,1)S(1)}, u32[]{:S(2)}, u32[]{:S(2)}) collective-permute-start(bf16[256,768]{1,0:T(8,128)(2,1)S(1)} %get-tuple-element.205), channel_id=1, source_target_pairs={{8,0},{12,4},{16,8},{20,12},{24,16},{28,20},{9,1},{13,5},{17,9},{2... | collective-permute-start | bytes 1179656 | tf_op jit(solution)/shard_map/ppermute | solution.py:378
  290.7 36.2 %collective-permute-start.41 = (bf16[4,24,3200]{2,1,0:T(8,128)(2,1)S(1)}, bf16[4,24,3200]{2,1,0:T(8,128)(2,1)S(1)}, u32[]{:S(2)}, u32[]{:S(2)}) collective-permute-start(bf16[4,24,3200]{2,1,0:T(8,128)(2,1)S(1)} %get-tuple-element.213), channel_id=1, source_target_pairs={{0,2},{1,3},{2,0},{3,1},{4,6},{5,7},{6,4},{7,5},{8,10},{9,11},{10,... | collective-permute-start | bytes 1843208 | tf_op jit(solution)/shard_map/ppermute | solution.py:383
  295.6 31.3 %collective-permute-start.42 = (bf16[4,24,3200]{2,1,0:T(8,128)(2,1)S(1)}, bf16[4,24,3200]{2,1,0:T(8,128)(2,1)S(1)}, u32[]{:S(2)}, u32[]{:S(2)}) collective-permute-start(bf16[4,24,3200]{2,1,0:T(8,128)(2,1)S(1)} %get-tuple-element.212), channel_id=1, source_target_pairs={{0,4},{1,5},{2,6},{3,7},{4,0},{5,1},{6,2},{7,3},{8,12},{9,13},{10,... | collective-permute-start | bytes 1843208 | tf_op jit(solution)/shard_map/ppermute | solution.py:383
  296.9 30.0 %collective-permute-start.43 = (bf16[4,24,3200]{2,1,0:T(8,128)(2,1)S(1)}, bf16[4,24,3200]{2,1,0:T(8,128)(2,1)S(1)}, u32[]{:S(2)}, u32[]{:S(2)}) collective-permute-start(bf16[4,24,3200]{2,1,0:T(8,128)(2,1)S(1)} %get-tuple-element.211), channel_id=1, source_target_pairs={{0,6},{1,7},{2,4},{3,5},{4,2},{5,3},{6,0},{7,1},{8,14},{9,15},{10,... | collective-permute-start | bytes 1843208 | tf_op jit(solution)/shard_map/ppermute | solution.py:383
  297.4 16.1 %collective-permute-start.44 = (bf16[256,768]{1,0:T(8,128)(2,1)S(1)}, bf16[256,768]{1,0:T(8,128)(2,1)S(1)}, u32[]{:S(2)}, u32[]{:S(2)}) collective-permute-start(bf16[256,768]{1,0:T(8,128)(2,1)S(1)} %get-tuple-element.208), channel_id=1, source_target_pairs={{0,16},{4,20},{8,24},{12,28},{1,17},{5,21},{9,25},{13,29},{2,18},{... | collective-permute-start | bytes 1179656 | tf_op jit(solution)/shard_map/ppermute | solution.py:378
  305.2 21.7 %collective-permute-start.45 = (bf16[256,768]{1,0:T(8,128)(2,1)S(1)}, bf16[256,768]{1,0:T(8,128)(2,1)S(1)}, u32[]{:S(2)}, u32[]{:S(2)}) collective-permute-start(bf16[256,768]{1,0:T(8,128)(2,1)S(1)} %get-tuple-element.207), channel_id=1, source_target_pairs={{16,0},{20,4},{24,8},{28,12},{17,1},{21,5},{25,9},{29,13},{18,2},{... | collective-permute-start | bytes 1179656 | tf_op jit(solution)/shard_map/ppermute | solution.py:378
  327.0 37.1 %collective-permute-start.51 = (bf16[256,768]{1,0:T(8,128)(2,1)S(1)}, bf16[256,768]{1,0:T(8,128)(2,1)S(1)}, u32[]{:S(2)}, u32[]{:S(2)}) collective-permute-start(bf16[256,768]{1,0:T(8,128)(2,1)S(1)} %get-tuple-element.204), channel_id=1, source_target_pairs={{0,12},{4,16},{8,20},{12,24},{16,28},{1,13},{5,17},{9,21},{13,25},... | collective-permute-start | bytes 1179656 | tf_op jit(solution)/shard_map/ppermute | solution.py:378
  329.8 34.3 %collective-permute-start.52 = (bf16[256,768]{1,0:T(8,128)(2,1)S(1)}, bf16[256,768]{1,0:T(8,128)(2,1)S(1)}, u32[]{:S(2)}, u32[]{:S(2)}) collective-permute-start(bf16[256,768]{1,0:T(8,128)(2,1)S(1)} %get-tuple-element.203), channel_id=1, source_target_pairs={{12,0},{16,4},{20,8},{24,12},{28,16},{13,1},{17,5},{21,9},{25,13},... | collective-permute-start | bytes 1179656 | tf_op jit(solution)/shard_map/ppermute | solution.py:378
  331.5 33.4 %copy-start.4 = (bf16[1,256,768]{2,1,0:T(8,128)(2,1)S(1)}, bf16[1,256,768]{2,1,0:T(8,128)(2,1)}, u32[]{:S(2)}) copy-start(bf16[1,256,768]{2,1,0:T(8,128)(2,1)} %param.14) | copy-start | bytes 1179652
  331.5 33.4 %copy-start.48 = (f32[768]{0:T(1024)S(1)}, f32[768]{0:T(1024)}, u32[]{:S(2)}) copy-start(f32[768]{0:T(1024)} %get-tuple-element.182) | copy-start | bytes 9220
  331.5 11.3 %collective-permute-start.48 = (bf16[1,24,3200]{2,1,0:T(8,128)(2,1)S(1)}, bf16[1,24,3200]{2,1,0:T(8,128)(2,1)S(1)}, u32[]{:S(2)}, u32[]{:S(2)}) collective-permute-start(bf16[1,24,3200]{2,1,0:T(8,128)(2,1)S(1)} %get-tuple-element.229), channel_id=1, source_target_pairs={{0,8},{1,9},{2,10},{3,11},{4,12},{5,13},{6,14},{7,15},{8,0},{9,1},... | collective-permute-start | bytes 460808 | tf_op jit(solution)/shard_map/ppermute | solution.py:383
  333.5 30.6 %collective-permute-start.49 = (bf16[1,24,3200]{2,1,0:T(8,128)(2,1)S(1)}, bf16[1,24,3200]{2,1,0:T(8,128)(2,1)S(1)}, u32[]{:S(2)}, u32[]{:S(2)}) collective-permute-start(bf16[1,24,3200]{2,1,0:T(8,128)(2,1)S(1)} %get-tuple-element.228), channel_id=1, source_target_pairs={{0,16},{1,17},{2,18},{3,19},{4,20},{5,21},{6,22},{7,23},{8,24},{9,... | collective-permute-start | bytes 460808 | tf_op jit(solution)/shard_map/ppermute | solution.py:383
  339.3 24.8 %collective-permute-start.50 = (bf16[1,24,3200]{2,1,0:T(8,128)(2,1)S(1)}, bf16[1,24,3200]{2,1,0:T(8,128)(2,1)S(1)}, u32[]{:S(2)}, u32[]{:S(2)}) collective-permute-start(bf16[1,24,3200]{2,1,0:T(8,128)(2,1)S(1)} %get-tuple-element.227), channel_id=1, source_target_pairs={{0,24},{1,25},{2,26},{3,27},{4,28},{5,29},{6,30},{7,31},{8,16},{9,... | collective-permute-start | bytes 460808 | tf_op jit(solution)/shard_map/ppermute | solution.py:383
  364.8 4.2 %collective-permute-start.53 = (bf16[2,24,1024]{2,1,0:T(8,128)(2,1)S(1)}, bf16[2,24,1024]{2,1,0:T(8,128)(2,1)S(1)}, u32[]{:S(2)}, u32[]{:S(2)}) collective-permute-start(bf16[2,24,1024]{2,1,0:T(8,128)(2,1)S(1)} %pad_maximum_fusion.12), channel_id=1, source_target_pairs={{0,1},{1,0},{2,3},{3,2},{4,5},{5,4},{6,7},{7,6},{8,9},{9,8},{10,11... | collective-permute-start | bytes 294920 | tf_op jit(solution)/shard_map/ppermute | solution.py:383
  369.6 5.2 %collective-permute-start.54 = (bf16[2,24,1024]{2,1,0:T(8,128)(2,1)S(1)}, bf16[2,24,1024]{2,1,0:T(8,128)(2,1)S(1)}, u32[]{:S(2)}, u32[]{:S(2)}) collective-permute-start(bf16[2,24,1024]{2,1,0:T(8,128)(2,1)S(1)} %pad_maximum_fusion.13), channel_id=1, source_target_pairs={{0,2},{1,3},{2,0},{3,1},{4,6},{5,7},{6,4},{7,5},{8,10},{9,11},{10,... | collective-permute-start | bytes 294920 | tf_op jit(solution)/shard_map/ppermute | solution.py:383
  (45 other events, 253.7 us)

commit v4 on v3

--- a/solution.py
+++ b/solution.py
@@ -558,6 +558,35 @@
     )(weights, *pieces)
 
 
+def halves_kernel(rank_ref, *refs):
+    sources, table_ref, (kept_ref, sent_ref) = refs[:-3], refs[-3], refs[-2:]
+    mine = rank_ref[0] & 1
+    for index in range(kept_ref.shape[0]):
+        for target, side in ((kept_ref, mine), (sent_ref, 1 - mine)):
+            start = 0
+            for source in sources:
+                target[index, :, start : start + source.shape[2]] = source[2 * index + side]
+                start += source.shape[2]
+            target[index, :, start:] = table_ref[...]
+
+
+def core_halves(grads, table_block, rank, count):
+    rows = grads[0].shape[0] // count
+    columns = sum(grad.shape[1] for grad in grads) + TILE
+    if rows % 8:
+        held = jnp.concatenate(grads + [jnp.tile(table_block, (count, 1))], axis=1).reshape(-1, 2, rows, columns)
+        return [lax.dynamic_index_in_dim(held, (rank & 1) ^ side, 1, keepdims=False) for side in range(2)]
+    return pl.pallas_call(
+        halves_kernel,
+        out_shape=(jax.ShapeDtypeStruct((count // 2, rows, columns), BF16),) * 2,
+        in_specs=[pl.BlockSpec(memory_space=pltpu.SMEM)]
+        + [pl.BlockSpec(memory_space=pltpu.VMEM)] * (len(grads) + 1),
+        out_specs=(pl.BlockSpec(memory_space=pltpu.VMEM),) * 2,
+        cost_estimate=SMALL,
+        compiler_params=pltpu.CompilerParams(vmem_limit_bytes=40 << 20),
+    )(rank[None].astype(jnp.int32), *[grad.reshape(count, rows, -1) for grad in grads], table_block)
+
+
 def place_kernel(rank_ref, *refs, masks):
     target = refs[-1]
     rank = rank_ref[0]
@@ -864,8 +893,6 @@
     )
     every_back = contract(grad_pair, weight_pair, 1, 1).astype(BF16)
     grad_second = scatter_dp(jnp.split(every_back, dp_count, axis=0), dp_bits)
-    every_out = contract(hidden, weight_down, 1, 0).astype(BF16)
-    output = middle + scatter_dp(jnp.split(every_out, dp_count, axis=0), dp_bits)
     grad_out = cotangent[0]
     scaled = grad_second * gain_two
     grad_middle = grad_out.astype(F32) + scale_two * (
@@ -887,9 +914,11 @@
         ],
         axis=1,
     )
-    far_grads, grad_mixed, grad_mixed_turned, grad_output_weight = tie(
-        far_grads, grad_mixed, grad_mixed_turned, grad_output_weight
-    )
+    every_out = contract(hidden, weight_down, 1, 0).astype(BF16)
+    far_grads, grad_mixed, grad_mixed_turned, grad_output_weight, every_out = tie(
+        far_grads, grad_mixed, grad_mixed_turned, grad_output_weight, every_out
+    )
+    out_parts = jnp.split(every_out, dp_count, axis=0)
     bits = seq_groups[0][1]
     far_kept, far_got = split_and_swap(far_grads, seq_rank & ((1 << bits) - 1), seq_groups[0])
 
@@ -900,6 +929,9 @@
         first, steps, queries, queries_turned, keys, keys_turned, values, grad_mixed, grad_mixed_turned,
         outs, logs, key_feat, query_feat, tiles, head_dim, pairs,
     )
+    out_parts = [out_parts[0]] + [flat_swap(out_parts[mask], mask) for mask in range(1, dp_count)]
+    grad_queries, out_parts = tie(grad_queries, out_parts)
+    output = middle + sum(part.astype(F32) for part in out_parts)
     grad_queries, grad_keys, grad_values, tile_sums, far_kept, far_got = tie(
         grad_queries, grad_keys, grad_values, tile_sums, far_kept, far_got
     )
@@ -917,6 +949,8 @@
         return parts
 
     returned = returned_from(partial_low, 1)
+    if reach > 2:
+        returned = returned + returned_from(partial_low, reach - 1)
     grad_query_weight = contract(normed_own, grad_queries, 0, 1).astype(BF16)
     grad_key_weight = contract(window_normed, grad_keys, 0, 0).astype(BF16)
     grad_value_weight = contract(window_normed, grad_values, 0, 0).astype(BF16)
@@ -929,26 +963,19 @@
     table_rows = -(-grad_table.size // TILE)
     table_block = jnp.pad(grad_table.reshape(-1), (0, table_rows * TILE - grad_table.size)).reshape(table_rows, TILE)
     table_block = jnp.pad(table_block, ((0, shard_rows - table_rows), (0, 0))).astype(BF16)
-    near_grads = jnp.concatenate(
-        [
-            grad_query_weight,
-            grad_key_weight,
-            grad_value_weight,
-            grad_output_weight,
-            jnp.tile(table_block, (device_count, 1)),
-        ],
-        axis=1,
-    )
-    near_grads, partial_low, returned, far_kept, far_got = tie(
-        near_grads, partial_low, returned, far_kept, far_got
-    )
+    kept, sent = core_halves(
+        [grad_query_weight, grad_key_weight, grad_value_weight, grad_output_weight], table_block, rank, device_count
+    )
+    kept, sent, partial_low, returned, far_kept, far_got = tie(kept, sent, partial_low, returned, far_kept, far_got)
     far_sum = joined(far_kept, far_got).reshape(far_grads.shape[1:]).astype(BF16)
 
-    left = list(range(reach, 2, -1))
-    waiting = returned_from(partial_low, 2) if reach > 1 else []
-    near_held = near_grads.reshape(device_count, shard_rows, 4 * width + TILE)
+    left = [step for step in range(reach, 2, -1) if step != reach - 1]
+    waiting = returned_from(partial_low, 2) if reach == 2 or reach > 3 else []
     for stage, (low, bits) in enumerate(groups):
-        kept, got = split_and_swap(near_held, (rank >> low) & ((1 << bits) - 1), (low, bits))
+        if stage == 0:
+            got = [flat_swap(sent, 1)]
+        else:
+            kept, got = split_and_swap(near_held, (rank >> low) & ((1 << bits) - 1), (low, bits))
         if stage == 0:
             kept, got, partial_low = tie(kept, got, partial_low)
         else:
@@ -956,6 +983,13 @@
             kept, got, arrived, waiting, partial_low, far_sum = tie(
                 kept, got, arrived, waiting, partial_low, far_sum
             )
+            if stage == 1:
+                pair_back = spread_dp(
+                    {mask: lax.dynamic_index_in_dim(far_sum, dp_rank ^ mask, 0, keepdims=False) for mask in range(dp_count)},
+                    dp_bits,
+                )
+            if stage == 2:
+                kept, pair_back = tie(kept, pair_back)
             returned, waiting = returned + arrived + waiting, []
         total = joined(kept, got)
         near_held = total.astype(BF16)
@@ -964,9 +998,6 @@
     near_sum = total.reshape(shard_rows, 4 * width + TILE)
     grad_normed = partial_low[own_slice].astype(F32) + contract(grad_queries, weight_query, 0, 1)
     grad_normed = grad_normed + sum(piece.astype(F32) for piece in returned)
-    pair_back = spread_dp(
-        {mask: lax.dynamic_index_in_dim(far_sum, dp_rank ^ mask, 0, keepdims=False) for mask in range(dp_count)}, dp_bits
-    )
     grad_gate_own, grad_up_own = columns_of(pair_back, dp_rank, dp_count, seq_count, unit)
     grad_down_own = parts_of(far_sum[dp_count:].astype(F32).reshape(-1, 2 * share), 1, unit)
     normed_rows = tokens * scale_one

time: 387 us -> 369 us (0.953)
  waiting for transfers between devices: 89.3 us -> 67.4 us
  starting transfers between devices: 93.7 us -> 112 us
  Pallas kernels: 79.7 us -> 69.5 us
  local copies, waits for them, and re-layouts: 40.5 us -> 32.1 us
    ppermute x39, waiting for transfers between devices: 59.9 us -> 36.5 us  [flat_swap(): lax.ppermute(value, BOTH, [(source, source ^ mask) for source in range(co...]
    ppermute x16, starting transfers between devices: 46.7 us -> 58.2 us  [shifted(): return lax.ppermute(value, axis, pairs)]
    ppermute x39, starting transfers between devices: 47 us -> 53.4 us  [flat_swap(): lax.ppermute(value, BOTH, [(source, source ^ mask) for source in range(co...]
    squeeze x5 -> x4, local copies, waits for them, and re-layouts: 8.15 us -> 2.58 us  [split_and_swap(): lax.dynamic_index_in_dim(held, mine ^ step, 1, keepdims=False)]
    pallas_call x1, Pallas kernels: 10.9 us -> 6.5 us  [table_sums(): pl.pallas_call(table_kernel, out_shape=jax.ShapeDtypeStruct((heads, bucke...]
    unnamed x112 -> x123, local copies, waits for them, and re-layouts: 18.8 us -> 19.1 us
  transfers between devices with their start and end apart: 55 -> 55, of which waited for: 13 -> 13; matrix products, arithmetic and copies ran while one was open for 20% -> 20% of each run, Pallas kernels for 21% -> 19%
where the time goes in v4:
time: 369 us; the launch traced here: 362 us
  starting transfers between devices  112 us (30%)
  Pallas kernels  69.5 us (19%)
  waiting for transfers between devices  67.4 us (18%)
  matrix products  48.5 us (13%)
  local copies, waits for them, and re-layouts  32.1 us (9%)
  other arithmetic  31 us (8%)
    ppermute x16, starting transfers between devices, shifted(): return lax.ppermute(value, axis, pairs)  58.2 us
    ppermute x39, starting transfers between devices, flat_swap(): lax.ppermute(value, BOTH, [(source, source ^ mask) for source in range(co...  53.4 us
    dot_general x20, matrix products, contract(): lax.dot_general(left_side, right_side, (((left_dim,), (right_dim,)), ((),...  48.3 us
    ppermute x39, waiting for transfers between devices, flat_swap(): lax.ppermute(value, BOTH, [(source, source ^ mask) for source in range(co...  36.5 us
    ppermute x16, waiting for transfers between devices, shifted(): return lax.ppermute(value, axis, pairs)  30.9 us
    pallas_call x1, Pallas kernels, attend_back(): pl.pallas_call(kernel, out_shape=(jax.ShapeDtypeStruct((width, row_count)...  22.4 us
    unnamed x123, local copies, waits for them, and re-layouts  19.1 us
    pallas_call x1, Pallas kernels, bias_tiles(): pl.pallas_call(tiles_kernel, out_shape=jax.ShapeDtypeStruct((heads, tile_...  12.2 us
  transfers between devices with their start and end apart: 55, of which 13 were waited for; matrix products, arithmetic and copies ran while one was open for 20% of the time, Pallas kernels for 19%

profile of v4, /device:TPU:0, one launch (start us, length us, event | category | flops | bytes accessed | tf_op | source)
XLA Modules:
  0.0 362.0 jit_solution(737950749775907671)
XLA Ops:
  2.1 5.5 %collective-permute-start.4 = (bf16[256,768]{1,0:T(8,128)(2,1)}, bf16[256,768]{1,0:T(8,128)(2,1)S(1)}, u32[]{:S(2)}, u32[]{:S(2)}) collective-permute-start(bf16[256,768]{1,0:T(8,128)(2,1)} %bitcast.135), channel_id=1, source_target_pairs={{0,4},{4,8},{8,12},{12,16},{16,20},{20,24},{24,28},{1,5},{5,9},{9,... | collective-permute-start | bytes 1179656 | tf_op jit(solution)/shard_map/ppermute | solution.py:378
  12.0 2.1 collective-permute-start
  14.1 2.6 collective-permute-start.1
  16.7 1.8 shard_map.236
  23.8 4.0 %collective-permute-done.1.refs_2_ = bf16[1,24,3200]{2,1,0:T(8,128)(2,1)S(1)} collective-permute-done((bf16[1,24,3200]{2,1,0:T(8,128)(2,1)S(1)}, bf16[1,24,3200]{2,1,0:T(8,128)(2,1)S(1)}, u32[]{:S(2)}, u32[]{:S(2)}) %collective-permute-start.1) | collective-permute-done | bytes 153632 | tf_op jit(solution)/shard_map/ppermute | solution.py:383
  27.9 2.5 collective-permute-start.9
  31.9 1.6 collective-permute-start.5
  33.5 4.1 %collective-permute-start.6 = (bf16[4,24,3200]{2,1,0:T(8,128)(2,1)S(1)}, bf16[4,24,3200]{2,1,0:T(8,128)(2,1)S(1)}, u32[]{:S(2)}, u32[]{:S(2)}) collective-permute-start(bf16[4,24,3200]{2,1,0:T(8,128)(2,1)S(1)} %shard_map.230.refs_0_), channel_id=1, source_target_pairs={{0,4},{1,5},{2,6},{3,7},{4,0},{5,1},{6,2},{7,3},{8,12},{9,13},{10,... | collective-permute-start | bytes 1843208 | tf_op jit(solution)/shard_map/ppermute | solution.py:383
  42.2 12.2 %shard_map.231.tiles_ref = f32[12,19,128,128]{3,2,1,0:T(8,128)} custom-call(f32[12,1,2560]{2,1,0:T(1,128)} %reshape.237.line_ref), custom_call_target="tpu_custom_call" | custom-call | flops 1 | bytes 1 | tf_op jit(solution)/shard_map/pallas_call | solution.py:43
  55.1 5.3 %collective-permute-start.11 = (bf16[256,768]{1,0:T(8,128)(2,1)S(1)}, bf16[256,768]{1,0:T(8,128)(2,1)}, u32[]{:S(2)}, u32[]{:S(2)}) collective-permute-start(bf16[256,768]{1,0:T(8,128)(2,1)S(1)} %bitcast.138), channel_id=1, source_target_pairs={{0,16},{4,20},{8,24},{12,28},{1,17},{5,21},{9,25},{13,29},{2,18},{... | collective-permute-start | bytes 1179656 | tf_op jit(solution)/shard_map/ppermute | solution.py:378
  60.4 3.5 collective-permute-start.12
  74.0 2.3 select_convert_fusion.key_feat_ref
  77.9 1.6 collective-permute-start.22
  79.5 3.2 collective-permute-done.22
  89.3 1.6 collective-permute-start.19
  90.9 13.1 %collective-permute-done.14.refs_8_ = bf16[256,768]{1,0:T(8,128)(2,1)} collective-permute-done((bf16[256,768]{1,0:T(8,128)(2,1)S(1)}, bf16[256,768]{1,0:T(8,128)(2,1)}, u32[]{:S(2)}, u32[]{:S(2)}) %collective-permute-start.14) | collective-permute-done | bytes 393248 | tf_op jit(solution)/shard_map/ppermute | solution.py:378
  103.9 4.4 %collective-permute-start.25 = (bf16[1,6,24,1024]{3,2,1,0:T(8,128)(2,1)S(1)}, bf16[1,6,24,1024]{3,2,1,0:T(8,128)(2,1)}, u32[]{:S(2)}, u32[]{:S(2)}) collective-permute-start(bf16[1,6,24,1024]{3,2,1,0:T(8,128)(2,1)S(1)} %bitcast.147), channel_id=1, source_target_pairs={{0,24},{1,25},{2,26},{3,27},{4,28},{5,29},{6,30},{7,31},{8,16},{9,... | collective-permute-start | bytes 884744 | tf_op jit(solution)/shard_map/ppermute | solution.py:383
  109.5 2.2 shard_map.233
  111.7 4.3 %shard_map.234 = bf16[2304,768]{1,0:T(8,128)(2,1)S(1)} custom-call(bf16[768,3200]{1,0:T(8,128)(2,1)S(1)} %bitcast.120, bf16[256,768]{1,0:T(8,128)(2,1)} %collective-permute-done.11.refs_0_, bf16[256,768]{1,0:T(8,128)(2,1)} %collective-permute-done.12.refs_1_, bf16[256,768]{1,0:T(8,128)(2,1)} %collective-permute-done.9.refs_2_, ...), custom_call_target="tpu_custom_call" | custom-call | tf_op jit(solution)/shard_map/pallas_call | solution.py:550
  116.0 4.5 %convolution_convert_fusion.2.value_turned_ref = bf16[768,2304]{1,0:T(8,128)(2,1)} fusion(bf16[2304,768]{1,0:T(8,128)(2,1)S(1)} %shard_map.234, bf16[768,3200]{1,0:T(8,128)(2,1)S(1)} %bitcast.121), kind=kOutput, calls=%fused_computation.2 | convolution fusion | flops 2719678464 | bytes 8257536 | tf_op jit(solution)/shard_map/dot_general | solution.py:699
  120.6 4.3 %convolution_convert_fusion.3.key_ref = bf16[2304,768]{1,0:T(8,128)(2,1)} fusion(bf16[2304,768]{1,0:T(8,128)(2,1)S(1)} %shard_map.234, bf16[768,3200]{1,0:T(8,128)(2,1)S(1)} %bitcast.122), kind=kOutput, calls=%fused_computation.3 | convolution fusion | flops 2719678464 | bytes 8257536 | tf_op jit(solution)/shard_map/dot_general | solution.py:699
  126.0 9.8 %shard_map.235 = (f32[768,256]{1,0:T(8,128)S(1)}, f32[3,4,256]{2,1,0:T(4,128)S(1)}) custom-call(s32[2]{0:T(128)S(1)} %get-tuple-element.224.first_ref, s32[2]{0:T(128)S(1)} %get-tuple-element.225.last_ref, bf16[768,256]{1,0:T(8,128)(2,1)S(1)} %convolution_convert_fusion.15.query_ref.query_turned_ref, bf16[2304,768]{1,0:T(8,128)(2,1)} %convolution_convert_fusion.3.key_ref, ...), custom_call_target="tpu_custom_call" | custom-call | flops 4026531840 | bytes 25165824 | tf_op jit(solution)/shard_map/pallas_call | solution.py:145
  136.8 4.0 %collective-permute-start.16 = (bf16[256,768]{1,0:T(8,128)(2,1)S(1)}, bf16[256,768]{1,0:T(8,128)(2,1)S(1)}, u32[]{:S(2)}, u32[]{:S(2)}) collective-permute-start(bf16[256,768]{1,0:T(8,128)(2,1)S(1)} %multiply_convert_fusion.2), channel_id=1, source_target_pairs={{0,2},{1,3},{2,0},{3,1},{4,6},{5,7},{6,4},{7,5},{8,10},{9,11},{10,... | collective-permute-start | bytes 1179656 | tf_op jit(solution)/shard_map/ppermute | solution.py:383
  142.1 2.9 collective-permute-start.27
  145.0 4.4 %convolution_convert_fusion.value_ref = bf16[2304,768]{1,0:T(8,128)(2,1)} fusion(bf16[2304,768]{1,0:T(8,128)(2,1)S(1)} %shard_map.234, bf16[768,3200]{1,0:T(8,128)(2,1)S(1)} %bitcast.126), kind=kOutput, calls=%fused_computation | convolution fusion | flops 2719678464 | bytes 8257536 | tf_op jit(solution)/shard_map/dot_general | solution.py:699
  149.6 4.7 %convolution_convert_fusion.1.key_turned_ref = bf16[768,2304]{1,0:T(8,128)(2,1)} fusion(bf16[2304,768]{1,0:T(8,128)(2,1)S(1)} %shard_map.234, bf16[768,3200]{1,0:T(8,128)(2,1)S(1)} %bitcast.127), kind=kOutput, calls=%fused_computation.1 | convolution fusion | flops 2719678464 | bytes 8257536 | tf_op jit(solution)/shard_map/dot_general | solution.py:699
  156.0 9.3 %collective-permute-done.27.refs_3_ = bf16[3,6,24,1024]{3,2,1,0:T(8,128)(2,1)S(1)} collective-permute-done((bf16[3,6,24,1024]{3,2,1,0:T(8,128)(2,1)S(1)}, bf16[3,6,24,1024]{3,2,1,0:T(8,128)(2,1)S(1)}, u32[]{:S(2)}, u32[]{:S(2)}) %collective-permute-start.27) | collective-permute-done | bytes 884768 | tf_op jit(solution)/shard_map/ppermute | solution.py:383
  166.4 1.8 fusion.38
  168.3 3.4 fusion.6
  171.7 1.9 convolution_convert_fusion.5
  174.2 1.8 convolution_convert_fusion.6
  176.0 2.1 convolution_convert_fusion.11
  178.2 2.0 collective-permute-start.30
  181.5 8.1 %collective-permute-done.30 = bf16[256,768]{1,0:T(8,128)(2,1)S(1)} collective-permute-done((bf16[256,768]{1,0:T(8,128)(2,1)S(1)}, bf16[256,768]{1,0:T(8,128)(2,1)S(1)}, u32[]{:S(2)}, u32[]{:S(2)}) %collective-permute-start.30) | collective-permute-done | bytes 393248 | tf_op jit(solution)/shard_map/ppermute | solution.py:383
  194.1 1.7 fusion.12.grad_ref
  197.0 1.7 collective-permute-start.34
  199.6 1.7 collective-permute-start.32
  201.5 22.4 %shard_map.240 = (bf16[768,256]{1,0:T(8,128)(2,1)}, bf16[2304,768]{1,0:T(8,128)(2,1)}, bf16[2304,768]{1,0:T(8,128)(2,1)}, f32[12,19,128,128]{3,2,1,0:T(8,128)}) custom-call(s32[2]{0:T(128)} %copy-done.41, s32[2]{0:T(128)} %copy-done.42, bf16[256,768]{1,0:T(8,128)(2,1)} %convolution_convert_fusion.14.query_ref, ...), custom_call_target="tpu_custom_call", output_to_operand_aliasing={{3}: (13, {})} | custom-call | flops 10066329600 | bytes 33554432 | tf_op jit(solution)/shard_map/pallas_call | solution.py:238
  226.3 3.1 collective-permute-start.39
  229.4 2.4 collective-permute-start.41
  231.8 4.1 %convolution_convert_fusion.7 = bf16[768,768]{1,0:T(8,128)(2,1)} fusion(bf16[2304,768]{1,0:T(8,128)(2,1)S(1)} %shard_map.234, bf16[2304,768]{1,0:T(8,128)(2,1)S(1)} %copy-done.9), kind=kOutput, calls=%fused_computation.26 | convolution fusion | flops 2718498816 | bytes 8257536 | tf_op jit(solution)/shard_map/dot_general | solution.py:699
  235.9 4.0 %convolution_convert_fusion.8 = bf16[768,768]{1,0:T(8,128)(2,1)} fusion(bf16[2304,768]{1,0:T(8,128)(2,1)S(1)} %shard_map.234, bf16[2304,768]{1,0:T(8,128)(2,1)S(1)} %copy-done.8), kind=kOutput, calls=%fused_computation.27 | convolution fusion | flops 2718498816 | bytes 8257536 | tf_op jit(solution)/shard_map/dot_general | solution.py:699
  239.9 4.2 %shard_map.243 = bf16[2304,768]{1,0:T(8,128)(2,1)S(1)} custom-call(s32[2]{0:T(128)S(1)} %pad_add_fusion.4.range_ref, bf16[2304,768]{1,0:T(8,128)(2,1)S(1)} %copy-done.8, bf16[2304,768]{1,0:T(8,128)(2,1)S(1)} %copy-done.9, bf16[768,3200]{1,0:T(8,128)(2,1)} %bitcast.131, bf16[768,3200]{1,0:T(8,128)(2,1)} %bitcast.132), custom_call_target="tpu_custom_call" | custom-call | flops 1 | bytes 1 | tf_op jit(solution)/shard_map/pallas_call | solution.py:356
  245.3 9.0 %collective-permute-start.35 = (bf16[256,768]{1,0:T(8,128)(2,1)}, bf16[256,768]{1,0:T(8,128)(2,1)}, u32[]{:S(2)}, u32[]{:S(2)}) collective-permute-start(bf16[256,768]{1,0:T(8,128)(2,1)} %get-tuple-element.236), channel_id=1, source_target_pairs={{0,4},{4,8},{8,12},{12,16},{16,20},{20,24},{24,28},{1,5},{5,9},{9,... | collective-permute-start | bytes 1179656 | tf_op jit(solution)/shard_map/ppermute | solution.py:378
  255.6 6.5 %shard_map.241 = f32[12,32]{1,0:T(8,128)S(1)} custom-call(s32[2]{0:T(128)S(1)} %pad_add_fusion.3.range_ref, f32[12,19,128,128]{3,2,1,0:T(8,128)} %get-tuple-element.132.tiles_ref, s32[19,1,256]{2,1,0:T(1,128)S(1)} %copy-done.39), custom_call_target="tpu_custom_call" | custom-call | flops 1 | bytes 1 | tf_op jit(solution)/shard_map/pallas_call | solution.py:314
  262.1 10.6 %collective-permute-start.37 = (bf16[256,768]{1,0:T(8,128)(2,1)}, bf16[256,768]{1,0:T(8,128)(2,1)}, u32[]{:S(2)}, u32[]{:S(2)}) collective-permute-start(bf16[256,768]{1,0:T(8,128)(2,1)} %get-tuple-element.234), channel_id=1, source_target_pairs={{0,12},{4,16},{8,20},{12,24},{16,28},{1,13},{5,17},{9,21},{13,25},... | collective-permute-start | bytes 1179656 | tf_op jit(solution)/shard_map/ppermute | solution.py:378
  274.4 1.7 convolution_convert_fusion.9
  278.7 1.8 shard_map.242
  281.9 1.7 collective-permute-done.38
  284.9 2.6 fusion.33
  287.5 6.0 %collective-permute-start.48 = (bf16[256,768]{1,0:T(8,128)(2,1)S(1)}, bf16[256,768]{1,0:T(8,128)(2,1)S(1)}, u32[]{:S(2)}, u32[]{:S(2)}) collective-permute-start(bf16[256,768]{1,0:T(8,128)(2,1)S(1)} %get-tuple-element.230), channel_id=1, source_target_pairs={{0,8},{4,12},{8,16},{12,20},{16,24},{20,28},{1,9},{5,13},{9,17},{1... | collective-permute-start | bytes 1179656 | tf_op jit(solution)/shard_map/ppermute | solution.py:378
  294.9 2.3 add_convert_fusion
  297.6 7.8 %collective-permute-start.44 = (bf16[4,24,3200]{2,1,0:T(8,128)(2,1)S(1)}, bf16[4,24,3200]{2,1,0:T(8,128)(2,1)S(1)}, u32[]{:S(2)}, u32[]{:S(2)}) collective-permute-start(bf16[4,24,3200]{2,1,0:T(8,128)(2,1)S(1)} %get-tuple-element.238), channel_id=1, source_target_pairs={{0,4},{1,5},{2,6},{3,7},{4,0},{5,1},{6,2},{7,3},{8,12},{9,13},{10,... | collective-permute-start | bytes 1843208 | tf_op jit(solution)/shard_map/ppermute | solution.py:383
  305.5 5.1 %collective-permute-start.46 = (bf16[256,768]{1,0:T(8,128)(2,1)S(1)}, bf16[256,768]{1,0:T(8,128)(2,1)S(1)}, u32[]{:S(2)}, u32[]{:S(2)}) collective-permute-start(bf16[256,768]{1,0:T(8,128)(2,1)S(1)} %get-tuple-element.232), channel_id=1, source_target_pairs={{0,16},{4,20},{8,24},{12,28},{1,17},{5,21},{9,25},{13,29},{2,18},{... | collective-permute-start | bytes 1179656 | tf_op jit(solution)/shard_map/ppermute | solution.py:378
  311.9 1.8 fusion.23
  315.1 2.9 collective-permute-done.46
  318.0 13.2 %collective-permute-done.47 = bf16[256,768]{1,0:T(8,128)(2,1)S(1)} collective-permute-done((bf16[256,768]{1,0:T(8,128)(2,1)S(1)}, bf16[256,768]{1,0:T(8,128)(2,1)S(1)}, u32[]{:S(2)}, u32[]{:S(2)}) %collective-permute-start.47) | collective-permute-done | bytes 393248 | tf_op jit(solution)/shard_map/ppermute | solution.py:378
  333.6 2.4 collective-permute-start.50
  336.7 1.8 collective-permute-start.52
  339.2 1.6 collective-permute-start.54
  340.8 2.4 collective-permute-done.50
  343.2 7.3 %collective-permute-done.51 = bf16[1,24,3200]{2,1,0:T(8,128)(2,1)S(1)} collective-permute-done((bf16[1,24,3200]{2,1,0:T(8,128)(2,1)S(1)}, bf16[1,24,3200]{2,1,0:T(8,128)(2,1)S(1)}, u32[]{:S(2)}, u32[]{:S(2)}) %collective-permute-start.51) | collective-permute-done | bytes 153632 | tf_op jit(solution)/shard_map/ppermute | solution.py:383
  350.4 2.1 fusion.27
  356.1 1.8 shard_map.244
  (288 shorter events, 79.6 us)
Async XLA Ops:
  0.6 40.0 %copy-start = (f32[32,12]{0,1:T(8,128)S(1)}, f32[32,12]{0,1:T(8,128)}, u32[]{:S(2)}) copy-start(f32[32,12]{0,1:T(8,128)} %param.22) | copy-start | bytes 4612
  0.7 37.9 %copy-start.53 = (s32[2047]{0:T(1024)S(1)}, s32[2047]{0:T(1024)}, u32[]{:S(2)}) copy-start(s32[2047]{0:T(1024)} %param.16) | copy-start | bytes 24568
  0.7 29.7 %collective-permute-start.3 = (bf16[256,768]{1,0:T(8,128)(2,1)}, bf16[256,768]{1,0:T(8,128)(2,1)S(1)}, u32[]{:S(2)}, u32[]{:S(2)}) collective-permute-start(bf16[256,768]{1,0:T(8,128)(2,1)} %bitcast.134), channel_id=1, source_target_pairs={{4,0},{8,4},{12,8},{16,12},{20,16},{24,20},{28,24},{5,1},{9,5},{13... | collective-permute-start | bytes 1179656 | tf_op jit(solution)/shard_map/ppermute | solution.py:378
  2.1 29.0 %collective-permute-start.4 = (bf16[256,768]{1,0:T(8,128)(2,1)}, bf16[256,768]{1,0:T(8,128)(2,1)S(1)}, u32[]{:S(2)}, u32[]{:S(2)}) collective-permute-start(bf16[256,768]{1,0:T(8,128)(2,1)} %bitcast.135), channel_id=1, source_target_pairs={{0,4},{4,8},{8,12},{12,16},{16,20},{20,24},{24,28},{1,5},{5,9},{9,... | collective-permute-start | bytes 1179656 | tf_op jit(solution)/shard_map/ppermute | solution.py:378
  12.0 10.6 %collective-permute-start = (bf16[1,24,3200]{2,1,0:T(8,128)(2,1)S(1)}, bf16[1,24,3200]{2,1,0:T(8,128)(2,1)S(1)}, u32[]{:S(2)}, u32[]{:S(2)}) collective-permute-start(bf16[1,24,3200]{2,1,0:T(8,128)(2,1)S(1)} %bitcast.152), channel_id=1, source_target_pairs={{0,8},{1,9},{2,10},{3,11},{4,12},{5,13},{6,14},{7,15},{8,0},{9,1},... | collective-permute-start | bytes 460808 | tf_op jit(solution)/shard_map/ppermute | solution.py:383
  14.1 13.8 %collective-permute-start.1 = (bf16[1,24,3200]{2,1,0:T(8,128)(2,1)S(1)}, bf16[1,24,3200]{2,1,0:T(8,128)(2,1)S(1)}, u32[]{:S(2)}, u32[]{:S(2)}) collective-permute-start(bf16[1,24,3200]{2,1,0:T(8,128)(2,1)S(1)} %bitcast.153), channel_id=1, source_target_pairs={{0,16},{1,17},{2,18},{3,19},{4,20},{5,21},{6,22},{7,23},{8,24},{9,... | collective-permute-start | bytes 460808 | tf_op jit(solution)/shard_map/ppermute | solution.py:383
  16.7 13.6 %collective-permute-start.2 = (bf16[1,24,3200]{2,1,0:T(8,128)(2,1)S(1)}, bf16[1,24,3200]{2,1,0:T(8,128)(2,1)S(1)}, u32[]{:S(2)}, u32[]{:S(2)}) collective-permute-start(bf16[1,24,3200]{2,1,0:T(8,128)(2,1)S(1)} %bitcast.154), channel_id=1, source_target_pairs={{0,24},{1,25},{2,26},{3,27},{4,28},{5,29},{6,30},{7,31},{8,16},{9,... | collective-permute-start | bytes 460808 | tf_op jit(solution)/shard_map/ppermute | solution.py:383
  22.5 31.8 %collective-permute-start.8 = (bf16[256,768]{1,0:T(8,128)(2,1)}, bf16[256,768]{1,0:T(8,128)(2,1)S(1)}, u32[]{:S(2)}, u32[]{:S(2)}) collective-permute-start(bf16[256,768]{1,0:T(8,128)(2,1)} %bitcast.136), channel_id=1, source_target_pairs={{8,0},{12,4},{16,8},{20,12},{24,16},{28,20},{9,1},{13,5},{17,9},{2... | collective-permute-start | bytes 1179656 | tf_op jit(solution)/shard_map/ppermute | solution.py:378
  27.9 32.6 %collective-permute-start.9 = (bf16[256,768]{1,0:T(8,128)(2,1)}, bf16[256,768]{1,0:T(8,128)(2,1)}, u32[]{:S(2)}, u32[]{:S(2)}) collective-permute-start(bf16[256,768]{1,0:T(8,128)(2,1)} %bitcast.137), channel_id=1, source_target_pairs={{0,8},{4,12},{8,16},{12,20},{16,24},{20,28},{1,9},{5,13},{9,17},{1... | collective-permute-start | bytes 1179656 | tf_op jit(solution)/shard_map/ppermute | solution.py:378
  31.9 32.0 %collective-permute-start.5 = (bf16[4,24,3200]{2,1,0:T(8,128)(2,1)S(1)}, bf16[4,24,3200]{2,1,0:T(8,128)(2,1)S(1)}, u32[]{:S(2)}, u32[]{:S(2)}) collective-permute-start(bf16[4,24,3200]{2,1,0:T(8,128)(2,1)S(1)} %shard_map.230.refs_0_), channel_id=1, source_target_pairs={{0,2},{1,3},{2,0},{3,1},{4,6},{5,7},{6,4},{7,5},{8,10},{9,11},{10,... | collective-permute-start | bytes 1843208 | tf_op jit(solution)/shard_map/ppermute | solution.py:383
  33.5 32.6 %collective-permute-start.6 = (bf16[4,24,3200]{2,1,0:T(8,128)(2,1)S(1)}, bf16[4,24,3200]{2,1,0:T(8,128)(2,1)S(1)}, u32[]{:S(2)}, u32[]{:S(2)}) collective-permute-start(bf16[4,24,3200]{2,1,0:T(8,128)(2,1)S(1)} %shard_map.230.refs_0_), channel_id=1, source_target_pairs={{0,4},{1,5},{2,6},{3,7},{4,0},{5,1},{6,2},{7,3},{8,12},{9,13},{10,... | collective-permute-start | bytes 1843208 | tf_op jit(solution)/shard_map/ppermute | solution.py:383
  37.5 29.4 %collective-permute-start.7 = (bf16[4,24,3200]{2,1,0:T(8,128)(2,1)S(1)}, bf16[4,24,3200]{2,1,0:T(8,128)(2,1)S(1)}, u32[]{:S(2)}, u32[]{:S(2)}) collective-permute-start(bf16[4,24,3200]{2,1,0:T(8,128)(2,1)S(1)} %shard_map.230.refs_0_), channel_id=1, source_target_pairs={{0,6},{1,7},{2,4},{3,5},{4,2},{5,3},{6,0},{7,1},{8,14},{9,15},{10,... | collective-permute-start | bytes 1843208 | tf_op jit(solution)/shard_map/ppermute | solution.py:383
  42.2 34.2 %copy-start.57 = (s32[2]{0:T(128)S(1)}, s32[2]{0:T(128)}, u32[]{:S(2)}) copy-start(s32[2]{0:T(128)} %get-tuple-element.288) | copy-start | bytes 28
  55.1 34.1 %collective-permute-start.11 = (bf16[256,768]{1,0:T(8,128)(2,1)S(1)}, bf16[256,768]{1,0:T(8,128)(2,1)}, u32[]{:S(2)}, u32[]{:S(2)}) collective-permute-start(bf16[256,768]{1,0:T(8,128)(2,1)S(1)} %bitcast.138), channel_id=1, source_target_pairs={{0,16},{4,20},{8,24},{12,28},{1,17},{5,21},{9,25},{13,29},{2,18},{... | collective-permute-start | bytes 1179656 | tf_op jit(solution)/shard_map/ppermute | solution.py:378
  60.4 30.4 %collective-permute-start.12 = (bf16[256,768]{1,0:T(8,128)(2,1)S(1)}, bf16[256,768]{1,0:T(8,128)(2,1)}, u32[]{:S(2)}, u32[]{:S(2)}) collective-permute-start(bf16[256,768]{1,0:T(8,128)(2,1)S(1)} %bitcast.139), channel_id=1, source_target_pairs={{0,12},{4,16},{8,20},{12,24},{16,28},{1,13},{5,17},{9,21},{13,25},... | collective-permute-start | bytes 1179656 | tf_op jit(solution)/shard_map/ppermute | solution.py:378
  64.8 26.1 %collective-permute-start.13 = (bf16[256,768]{1,0:T(8,128)(2,1)S(1)}, bf16[256,768]{1,0:T(8,128)(2,1)}, u32[]{:S(2)}, u32[]{:S(2)}) collective-permute-start(bf16[256,768]{1,0:T(8,128)(2,1)S(1)} %bitcast.140), channel_id=1, source_target_pairs={{12,0},{16,4},{20,8},{24,12},{28,16},{13,1},{17,5},{21,9},{25,13},... | collective-permute-start | bytes 1179656 | tf_op jit(solution)/shard_map/ppermute | solution.py:378
  66.9 10.2 %collective-permute-start.21 = (bf16[2,24,1024]{2,1,0:T(8,128)(2,1)}, bf16[2,24,1024]{2,1,0:T(8,128)(2,1)}, u32[]{:S(2)}, u32[]{:S(2)}) collective-permute-start(bf16[2,24,1024]{2,1,0:T(8,128)(2,1)} %pad_maximum_fusion.10), channel_id=1, source_target_pairs={{0,1},{1,0},{2,3},{3,2},{4,5},{5,4},{6,7},{7,6},{8,9},{9,8},{10,11... | collective-permute-start | bytes 294920 | tf_op jit(solution)/shard_map/ppermute | solution.py:383
  72.2 36.1 %collective-permute-start.10 = (bf16[16,24,3200]{2,1,0:T(8,128)(2,1)S(1)}, bf16[16,24,3200]{2,1,0:T(8,128)(2,1)}, u32[]{:S(2)}, u32[]{:S(2)}) collective-permute-start(bf16[16,24,3200]{2,1,0:T(8,128)(2,1)S(1)} %shard_map.232.refs_0_), channel_id=1, source_target_pairs={{0,1},{1,0},{2,3},{3,2},{4,5},{5,4},{6,7},{7,6},{8,9},{9,8},{10,11... | collective-permute-start | bytes 7372808 | tf_op jit(solution)/shard_map/ppermute | solution.py:383
  77.0 48.4 %copy-start.41 = (s32[2]{0:T(128)}, s32[2]{0:T(128)S(1)}, u32[]{:S(2)}) copy-start(s32[2]{0:T(128)S(1)} %get-tuple-element.224.first_ref) | copy-start | bytes 28
  77.0 48.4 %copy-start.42 = (s32[2]{0:T(128)}, s32[2]{0:T(128)S(1)}, u32[]{:S(2)}) copy-start(s32[2]{0:T(128)S(1)} %get-tuple-element.225.last_ref) | copy-start | bytes 28
  77.9 4.8 %collective-permute-start.22 = (bf16[2,24,1024]{2,1,0:T(8,128)(2,1)S(1)}, bf16[2,24,1024]{2,1,0:T(8,128)(2,1)S(1)}, u32[]{:S(2)}, u32[]{:S(2)}) collective-permute-start(bf16[2,24,1024]{2,1,0:T(8,128)(2,1)S(1)} %pad_maximum_fusion.11), channel_id=1, source_target_pairs={{0,2},{1,3},{2,0},{3,1},{4,6},{5,7},{6,4},{7,5},{8,10},{9,11},{10,... | collective-permute-start | bytes 294920 | tf_op jit(solution)/shard_map/ppermute | solution.py:383
  82.7 21.2 %collective-permute-start.14 = (bf16[256,768]{1,0:T(8,128)(2,1)S(1)}, bf16[256,768]{1,0:T(8,128)(2,1)}, u32[]{:S(2)}, u32[]{:S(2)}) collective-permute-start(bf16[256,768]{1,0:T(8,128)(2,1)S(1)} %bitcast.141), channel_id=1, source_target_pairs={{16,0},{20,4},{24,8},{28,12},{17,1},{21,5},{25,9},{29,13},{18,2},{... | collective-permute-start | bytes 1179656 | tf_op jit(solution)/shard_map/ppermute | solution.py:378
  89.3 66.2 %collective-permute-start.19 = (bf16[256,768]{1,0:T(8,128)(2,1)}, bf16[256,768]{1,0:T(8,128)(2,1)}, u32[]{:S(2)}, u32[]{:S(2)}) collective-permute-start(bf16[256,768]{1,0:T(8,128)(2,1)} %bitcast.11), channel_id=1, source_target_pairs={{0,2},{1,3},{2,0},{3,1},{4,6},{5,7},{6,4},{7,5},{8,10},{9,11},{10,... | collective-permute-start | bytes 1179656 | tf_op jit(solution)/shard_map/ppermute | solution.py:383
  103.9 32.9 %collective-permute-start.23 = (bf16[1,6,24,1024]{3,2,1,0:T(8,128)(2,1)S(1)}, bf16[1,6,24,1024]{3,2,1,0:T(8,128)(2,1)}, u32[]{:S(2)}, u32[]{:S(2)}) collective-permute-start(bf16[1,6,24,1024]{3,2,1,0:T(8,128)(2,1)S(1)} %bitcast.145), channel_id=1, source_target_pairs={{0,8},{1,9},{2,10},{3,11},{4,12},{5,13},{6,14},{7,15},{8,0},{9,1},... | collective-permute-start | bytes 884744 | tf_op jit(solution)/shard_map/ppermute | solution.py:383
  103.9 36.9 %collective-permute-start.24 = (bf16[1,6,24,1024]{3,2,1,0:T(8,128)(2,1)S(1)}, bf16[1,6,24,1024]{3,2,1,0:T(8,128)(2,1)}, u32[]{:S(2)}, u32[]{:S(2)}) collective-permute-start(bf16[1,6,24,1024]{3,2,1,0:T(8,128)(2,1)S(1)} %bitcast.146), channel_id=1, source_target_pairs={{0,16},{1,17},{2,18},{3,19},{4,20},{5,21},{6,22},{7,23},{8,24},{9,... | collective-permute-start | bytes 884744 | tf_op jit(solution)/shard_map/ppermute | solution.py:383
  103.9 36.9 %collective-permute-start.25 = (bf16[1,6,24,1024]{3,2,1,0:T(8,128)(2,1)S(1)}, bf16[1,6,24,1024]{3,2,1,0:T(8,128)(2,1)}, u32[]{:S(2)}, u32[]{:S(2)}) collective-permute-start(bf16[1,6,24,1024]{3,2,1,0:T(8,128)(2,1)S(1)} %bitcast.147), channel_id=1, source_target_pairs={{0,24},{1,25},{2,26},{3,27},{4,28},{5,29},{6,30},{7,31},{8,16},{9,... | collective-permute-start | bytes 884744 | tf_op jit(solution)/shard_map/ppermute | solution.py:383
  108.3 47.5 %collective-permute-start.26 = (bf16[1,6,24,1024]{3,2,1,0:T(8,128)(2,1)S(1)}, bf16[1,6,24,1024]{3,2,1,0:T(8,128)(2,1)}, u32[]{:S(2)}, u32[]{:S(2)}) collective-permute-start(bf16[1,6,24,1024]{3,2,1,0:T(8,128)(2,1)S(1)} %bitcast.148), channel_id=1, source_target_pairs={{0,4},{1,5},{2,6},{3,7},{4,0},{5,1},{6,2},{7,3},{8,12},{9,13},{10,... | collective-permute-start | bytes 884744 | tf_op jit(solution)/shard_map/ppermute | solution.py:383
  111.6 82.4 %copy-start.2 = (bf16[32,24,3200]{2,1,0:T(8,128)(2,1)}, bf16[32,24,3200]{2,1,0:T(8,128)(2,1)S(1)}, u32[]{:S(2)}) copy-start(bf16[32,24,3200]{2,1,0:T(8,128)(2,1)S(1)} %shard_map.233) | copy-start | bytes 14745604
  116.0 119.8 %copy-start.7 = (bf16[2304,768]{1,0:T(8,128)(2,1)}, bf16[2304,768]{1,0:T(8,128)(2,1)S(1)}, u32[]{:S(2)}) copy-start(bf16[2304,768]{1,0:T(8,128)(2,1)S(1)} %shard_map.234) | copy-start | bytes 10616836
  135.8 55.5 %copy-start.17 = (f32[768,256]{1,0:T(8,128)}, f32[768,256]{1,0:T(8,128)S(1)}, u32[]{:S(2)}) copy-start(f32[768,256]{1,0:T(8,128)S(1)} %get-tuple-element.107.out_ref) | copy-start | bytes 2359300
  136.4 53.5 %copy-start.44 = (f32[256,768]{1,0:T(8,128)}, f32[256,768]{1,0:T(8,128)S(1)}, u32[]{:S(2)}) copy-start(f32[256,768]{1,0:T(8,128)S(1)} %get-tuple-element.286) | copy-start | bytes 2359300
  136.8 12.5 %collective-permute-start.16 = (bf16[256,768]{1,0:T(8,128)(2,1)S(1)}, bf16[256,768]{1,0:T(8,128)(2,1)S(1)}, u32[]{:S(2)}, u32[]{:S(2)}) collective-permute-start(bf16[256,768]{1,0:T(8,128)(2,1)S(1)} %multiply_convert_fusion.2), channel_id=1, source_target_pairs={{0,2},{1,3},{2,0},{3,1},{4,6},{5,7},{6,4},{7,5},{8,10},{9,11},{10,... | collective-permute-start | bytes 1179656 | tf_op jit(solution)/shard_map/ppermute | solution.py:383
  140.8 25.6 %collective-permute-start.15 = (bf16[256,768]{1,0:T(8,128)(2,1)S(1)}, bf16[256,768]{1,0:T(8,128)(2,1)S(1)}, u32[]{:S(2)}, u32[]{:S(2)}) collective-permute-start(bf16[256,768]{1,0:T(8,128)(2,1)S(1)} %multiply_convert_fusion.2), channel_id=1, source_target_pairs={{0,1},{1,0},{2,3},{3,2},{4,5},{5,4},{6,7},{7,6},{8,9},{9,8},{10,11... | collective-permute-start | bytes 1179656 | tf_op jit(solution)/shard_map/ppermute | solution.py:383
  142.1 23.2 %collective-permute-start.27 = (bf16[3,6,24,1024]{3,2,1,0:T(8,128)(2,1)S(1)}, bf16[3,6,24,1024]{3,2,1,0:T(8,128)(2,1)S(1)}, u32[]{:S(2)}, u32[]{:S(2)}) collective-permute-start(bf16[3,6,24,1024]{3,2,1,0:T(8,128)(2,1)S(1)} %shard_map.238.refs_1_), channel_id=1, source_target_pairs={{0,4},{1,5},{2,6},{3,7},{4,0},{5,1},{6,2},{7,3},{8,12},{9,13},{10,... | collective-permute-start | bytes 2654216 | tf_op jit(solution)/shard_map/ppermute | solution.py:383
  149.4 17.0 %collective-permute-start.17 = (bf16[256,768]{1,0:T(8,128)(2,1)S(1)}, bf16[256,768]{1,0:T(8,128)(2,1)S(1)}, u32[]{:S(2)}, u32[]{:S(2)}) collective-permute-start(bf16[256,768]{1,0:T(8,128)(2,1)S(1)} %collective-permute-done.16), channel_id=1, source_target_pairs={{0,1},{1,0},{2,3},{3,2},{4,5},{5,4},{6,7},{7,6},{8,9},{9,8},{10,11... | collective-permute-start | bytes 1179656 | tf_op jit(solution)/shard_map/ppermute | solution.py:383
  155.5 12.8 %collective-permute-start.18 = (bf16[256,768]{1,0:T(8,128)(2,1)}, bf16[256,768]{1,0:T(8,128)(2,1)S(1)}, u32[]{:S(2)}, u32[]{:S(2)}) collective-permute-start(bf16[256,768]{1,0:T(8,128)(2,1)} %bitcast.11), channel_id=1, source_target_pairs={{0,1},{1,0},{2,3},{3,2},{4,5},{5,4},{6,7},{7,6},{8,9},{9,8},{10,11... | collective-permute-start | bytes 1179656 | tf_op jit(solution)/shard_map/ppermute | solution.py:383
  155.8 12.5 %collective-permute-start.20 = (bf16[256,768]{1,0:T(8,128)(2,1)}, bf16[256,768]{1,0:T(8,128)(2,1)S(1)}, u32[]{:S(2)}, u32[]{:S(2)}) collective-permute-start(bf16[256,768]{1,0:T(8,128)(2,1)} %collective-permute-done.19), channel_id=1, source_target_pairs={{0,1},{1,0},{2,3},{3,2},{4,5},{5,4},{6,7},{7,6},{8,9},{9,8},{10,11... | collective-permute-start | bytes 1179656 | tf_op jit(solution)/shard_map/ppermute | solution.py:383
  173.6 4.5 %collective-permute-start.29 = (bf16[256,768]{1,0:T(8,128)(2,1)S(1)}, bf16[256,768]{1,0:T(8,128)(2,1)S(1)}, u32[]{:S(2)}, u32[]{:S(2)}) collective-permute-start(bf16[256,768]{1,0:T(8,128)(2,1)S(1)} %get-tuple-element.248), channel_id=1, source_target_pairs={{0,1},{1,0},{2,3},{3,2},{4,5},{5,4},{6,7},{7,6},{8,9},{9,8},{10,11... | collective-permute-start | bytes 1179656 | tf_op jit(solution)/shard_map/ppermute | solution.py:383
  173.7 7.8 %collective-permute-start.28 = (bf16[256,768]{1,0:T(8,128)(2,1)S(1)}, bf16[256,768]{1,0:T(8,128)(2,1)S(1)}, u32[]{:S(2)}, u32[]{:S(2)}) collective-permute-start(bf16[256,768]{1,0:T(8,128)(2,1)S(1)} %get-tuple-element.247), channel_id=1, source_target_pairs={{0,1},{1,0},{2,3},{3,2},{4,5},{5,4},{6,7},{7,6},{8,9},{9,8},{10,11... | collective-permute-start | bytes 1179656 | tf_op jit(solution)/shard_map/ppermute | solution.py:383
  178.2 11.4 %collective-permute-start.30 = (bf16[256,768]{1,0:T(8,128)(2,1)S(1)}, bf16[256,768]{1,0:T(8,128)(2,1)S(1)}, u32[]{:S(2)}, u32[]{:S(2)}) collective-permute-start(bf16[256,768]{1,0:T(8,128)(2,1)S(1)} %add_convert_fusion.4), channel_id=1, source_target_pairs={{0,2},{1,3},{2,0},{3,1},{4,6},{5,7},{6,4},{7,5},{8,10},{9,11},{10,... | collective-permute-start | bytes 1179656 | tf_op jit(solution)/shard_map/ppermute | solution.py:383
  197.0 27.5 %collective-permute-start.34 = (bf16[4,6,24,1024]{3,2,1,0:T(8,128)(2,1)}, bf16[4,6,24,1024]{3,2,1,0:T(8,128)(2,1)S(1)}, u32[]{:S(2)}, u32[]{:S(2)}) collective-permute-start(bf16[4,6,24,1024]{3,2,1,0:T(8,128)(2,1)} %get-tuple-element.241), channel_id=1, source_target_pairs={{0,4},{1,5},{2,6},{3,7},{4,0},{5,1},{6,2},{7,3},{8,12},{9,13},{10,... | collective-permute-start | bytes 3538952 | tf_op jit(solution)/shard_map/ppermute | solution.py:383
  199.6 24.3 %collective-permute-start.31 = (bf16[256,768]{1,0:T(8,128)(2,1)S(1)}, bf16[256,768]{1,0:T(8,128)(2,1)S(1)}, u32[]{:S(2)}, u32[]{:S(2)}) collective-permute-start(bf16[256,768]{1,0:T(8,128)(2,1)S(1)} %get-tuple-element.245), channel_id=1, source_target_pairs={{0,1},{1,0},{2,3},{3,2},{4,5},{5,4},{6,7},{7,6},{8,9},{9,8},{10,11... | collective-permute-start | bytes 1179656 | tf_op jit(solution)/shard_map/ppermute | solution.py:383
  199.6 24.3 %collective-permute-start.32 = (bf16[256,768]{1,0:T(8,128)(2,1)S(1)}, bf16[256,768]{1,0:T(8,128)(2,1)S(1)}, u32[]{:S(2)}, u32[]{:S(2)}) collective-permute-start(bf16[256,768]{1,0:T(8,128)(2,1)S(1)} %get-tuple-element.244), channel_id=1, source_target_pairs={{0,2},{1,3},{2,0},{3,1},{4,6},{5,7},{6,4},{7,5},{8,10},{9,11},{10,... | collective-permute-start | bytes 1179656 | tf_op jit(solution)/shard_map/ppermute | solution.py:383
  201.4 22.6 %collective-permute-start.33 = (bf16[256,768]{1,0:T(8,128)(2,1)S(1)}, bf16[256,768]{1,0:T(8,128)(2,1)}, u32[]{:S(2)}, u32[]{:S(2)}) collective-permute-start(bf16[256,768]{1,0:T(8,128)(2,1)S(1)} %get-tuple-element.243), channel_id=1, source_target_pairs={{0,3},{1,2},{2,1},{3,0},{4,7},{5,6},{6,5},{7,4},{8,11},{9,10},{10,... | collective-permute-start | bytes 1179656 | tf_op jit(solution)/shard_map/ppermute | solution.py:383
  226.3 35.8 %collective-permute-start.39 = (bf16[1,6,24,1024]{3,2,1,0:T(8,128)(2,1)S(1)}, bf16[1,6,24,1024]{3,2,1,0:T(8,128)(2,1)}, u32[]{:S(2)}, u32[]{:S(2)}) collective-permute-start(bf16[1,6,24,1024]{3,2,1,0:T(8,128)(2,1)S(1)} %get-tuple-element.251), channel_id=1, source_target_pairs={{0,8},{1,9},{2,10},{3,11},{4,12},{5,13},{6,14},{7,15},{8,0},{9,1},... | collective-permute-start | bytes 884744 | tf_op jit(solution)/shard_map/ppermute | solution.py:383
  229.4 43.3 %collective-permute-start.40 = (bf16[1,6,24,1024]{3,2,1,0:T(8,128)(2,1)S(1)}, bf16[1,6,24,1024]{3,2,1,0:T(8,128)(2,1)}, u32[]{:S(2)}, u32[]{:S(2)}) collective-permute-start(bf16[1,6,24,1024]{3,2,1,0:T(8,128)(2,1)S(1)} %get-tuple-element.250), channel_id=1, source_target_pairs={{0,16},{1,17},{2,18},{3,19},{4,20},{5,21},{6,22},{7,23},{8,24},{9,... | collective-permute-start | bytes 884744 | tf_op jit(solution)/shard_map/ppermute | solution.py:383
  229.4 52.5 %collective-permute-start.41 = (bf16[1,6,24,1024]{3,2,1,0:T(8,128)(2,1)}, bf16[1,6,24,1024]{3,2,1,0:T(8,128)(2,1)}, u32[]{:S(2)}, u32[]{:S(2)}) collective-permute-start(bf16[1,6,24,1024]{3,2,1,0:T(8,128)(2,1)} %get-tuple-element.249), channel_id=1, source_target_pairs={{0,24},{1,25},{2,26},{3,27},{4,28},{5,29},{6,30},{7,31},{8,16},{9,... | collective-permute-start | bytes 884744 | tf_op jit(solution)/shard_map/ppermute | solution.py:383
  245.3 36.6 %collective-permute-start.35 = (bf16[256,768]{1,0:T(8,128)(2,1)}, bf16[256,768]{1,0:T(8,128)(2,1)}, u32[]{:S(2)}, u32[]{:S(2)}) collective-permute-start(bf16[256,768]{1,0:T(8,128)(2,1)} %get-tuple-element.236), channel_id=1, source_target_pairs={{0,4},{4,8},{8,12},{12,16},{16,20},{20,24},{24,28},{1,5},{5,9},{9,... | collective-permute-start | bytes 1179656 | tf_op jit(solution)/shard_map/ppermute | solution.py:378
  254.3 27.6 %collective-permute-start.36 = (bf16[256,768]{1,0:T(8,128)(2,1)}, bf16[256,768]{1,0:T(8,128)(2,1)}, u32[]{:S(2)}, u32[]{:S(2)}) collective-permute-start(bf16[256,768]{1,0:T(8,128)(2,1)} %get-tuple-element.235), channel_id=1, source_target_pairs={{4,0},{8,4},{12,8},{16,12},{20,16},{24,20},{28,24},{5,1},{9,5},{13... | collective-permute-start | bytes 1179656 | tf_op jit(solution)/shard_map/ppermute | solution.py:378
  262.1 19.8 %collective-permute-start.37 = (bf16[256,768]{1,0:T(8,128)(2,1)}, bf16[256,768]{1,0:T(8,128)(2,1)}, u32[]{:S(2)}, u32[]{:S(2)}) collective-permute-start(bf16[256,768]{1,0:T(8,128)(2,1)} %get-tuple-element.234), channel_id=1, source_target_pairs={{0,12},{4,16},{8,20},{12,24},{16,28},{1,13},{5,17},{9,21},{13,25},... | collective-permute-start | bytes 1179656 | tf_op jit(solution)/shard_map/ppermute | solution.py:378
  272.7 10.9 %collective-permute-start.38 = (bf16[256,768]{1,0:T(8,128)(2,1)}, bf16[256,768]{1,0:T(8,128)(2,1)}, u32[]{:S(2)}, u32[]{:S(2)}) collective-permute-start(bf16[256,768]{1,0:T(8,128)(2,1)} %get-tuple-element.233), channel_id=1, source_target_pairs={{12,0},{16,4},{20,8},{24,12},{28,16},{13,1},{17,5},{21,9},{25,13},... | collective-permute-start | bytes 1179656 | tf_op jit(solution)/shard_map/ppermute | solution.py:378
  283.6 11.3 %collective-permute-start.42 = (bf16[16,24,3200]{2,1,0:T(8,128)(2,1)}, bf16[16,24,3200]{2,1,0:T(8,128)(2,1)}, u32[]{:S(2)}, u32[]{:S(2)}) collective-permute-start(bf16[16,24,3200]{2,1,0:T(8,128)(2,1)} %get-tuple-element.138), channel_id=1, source_target_pairs={{0,1},{1,0},{2,3},{3,2},{4,5},{5,4},{6,7},{7,6},{8,9},{9,8},{10,11... | collective-permute-start | bytes 7372808 | tf_op jit(solution)/shard_map/ppermute | solution.py:383
  287.5 18.0 %collective-permute-start.48 = (bf16[256,768]{1,0:T(8,128)(2,1)S(1)}, bf16[256,768]{1,0:T(8,128)(2,1)S(1)}, u32[]{:S(2)}, u32[]{:S(2)}) collective-permute-start(bf16[256,768]{1,0:T(8,128)(2,1)S(1)} %get-tuple-element.230), channel_id=1, source_target_pairs={{0,8},{4,12},{8,16},{12,20},{16,24},{20,28},{1,9},{5,13},{9,17},{1... | collective-permute-start | bytes 1179656 | tf_op jit(solution)/shard_map/ppermute | solution.py:378
  293.5 17.0 %collective-permute-start.49 = (bf16[256,768]{1,0:T(8,128)(2,1)S(1)}, bf16[256,768]{1,0:T(8,128)(2,1)S(1)}, u32[]{:S(2)}, u32[]{:S(2)}) collective-permute-start(bf16[256,768]{1,0:T(8,128)(2,1)S(1)} %get-tuple-element.229), channel_id=1, source_target_pairs={{8,0},{12,4},{16,8},{20,12},{24,16},{28,20},{9,1},{13,5},{17,9},{2... | collective-permute-start | bytes 1179656 | tf_op jit(solution)/shard_map/ppermute | solution.py:378
  297.5 33.7 %collective-permute-start.43 = (bf16[4,24,3200]{2,1,0:T(8,128)(2,1)S(1)}, bf16[4,24,3200]{2,1,0:T(8,128)(2,1)S(1)}, u32[]{:S(2)}, u32[]{:S(2)}) collective-permute-start(bf16[4,24,3200]{2,1,0:T(8,128)(2,1)S(1)} %get-tuple-element.239), channel_id=1, source_target_pairs={{0,2},{1,3},{2,0},{3,1},{4,6},{5,7},{6,4},{7,5},{8,10},{9,11},{10,... | collective-permute-start | bytes 1843208 | tf_op jit(solution)/shard_map/ppermute | solution.py:383
  297.6 34.9 %collective-permute-start.44 = (bf16[4,24,3200]{2,1,0:T(8,128)(2,1)S(1)}, bf16[4,24,3200]{2,1,0:T(8,128)(2,1)S(1)}, u32[]{:S(2)}, u32[]{:S(2)}) collective-permute-start(bf16[4,24,3200]{2,1,0:T(8,128)(2,1)S(1)} %get-tuple-element.238), channel_id=1, source_target_pairs={{0,4},{1,5},{2,6},{3,7},{4,0},{5,1},{6,2},{7,3},{8,12},{9,13},{10,... | collective-permute-start | bytes 1843208 | tf_op jit(solution)/shard_map/ppermute | solution.py:383
  305.4 27.1 %collective-permute-start.45 = (bf16[4,24,3200]{2,1,0:T(8,128)(2,1)S(1)}, bf16[4,24,3200]{2,1,0:T(8,128)(2,1)S(1)}, u32[]{:S(2)}, u32[]{:S(2)}) collective-permute-start(bf16[4,24,3200]{2,1,0:T(8,128)(2,1)S(1)} %get-tuple-element.237), channel_id=1, source_target_pairs={{0,6},{1,7},{2,4},{3,5},{4,2},{5,3},{6,0},{7,1},{8,14},{9,15},{10,... | collective-permute-start | bytes 1843208 | tf_op jit(solution)/shard_map/ppermute | solution.py:383
  305.5 12.5 %collective-permute-start.46 = (bf16[256,768]{1,0:T(8,128)(2,1)S(1)}, bf16[256,768]{1,0:T(8,128)(2,1)S(1)}, u32[]{:S(2)}, u32[]{:S(2)}) collective-permute-start(bf16[256,768]{1,0:T(8,128)(2,1)S(1)} %get-tuple-element.232), channel_id=1, source_target_pairs={{0,16},{4,20},{8,24},{12,28},{1,17},{5,21},{9,25},{13,29},{2,18},{... | collective-permute-start | bytes 1179656 | tf_op jit(solution)/shard_map/ppermute | solution.py:378
  310.6 20.6 %collective-permute-start.47 = (bf16[256,768]{1,0:T(8,128)(2,1)S(1)}, bf16[256,768]{1,0:T(8,128)(2,1)S(1)}, u32[]{:S(2)}, u32[]{:S(2)}) collective-permute-start(bf16[256,768]{1,0:T(8,128)(2,1)S(1)} %get-tuple-element.231), channel_id=1, source_target_pairs={{16,0},{20,4},{24,8},{28,12},{17,1},{21,5},{25,9},{29,13},{18,2},{... | collective-permute-start | bytes 1179656 | tf_op jit(solution)/shard_map/ppermute | solution.py:378
  333.1 5.4 %collective-permute-start.53 = (bf16[2,24,1024]{2,1,0:T(8,128)(2,1)S(1)}, bf16[2,24,1024]{2,1,0:T(8,128)(2,1)S(1)}, u32[]{:S(2)}, u32[]{:S(2)}) collective-permute-start(bf16[2,24,1024]{2,1,0:T(8,128)(2,1)S(1)} %pad_maximum_fusion.12), channel_id=1, source_target_pairs={{0,1},{1,0},{2,3},{3,2},{4,5},{5,4},{6,7},{7,6},{8,9},{9,8},{10,11... | collective-permute-start | bytes 294920 | tf_op jit(solution)/shard_map/ppermute | solution.py:383
  333.6 9.5 %collective-permute-start.50 = (bf16[1,24,3200]{2,1,0:T(8,128)(2,1)S(1)}, bf16[1,24,3200]{2,1,0:T(8,128)(2,1)S(1)}, u32[]{:S(2)}, u32[]{:S(2)}) collective-permute-start(bf16[1,24,3200]{2,1,0:T(8,128)(2,1)S(1)} %get-tuple-element.255), channel_id=1, source_target_pairs={{0,8},{1,9},{2,10},{3,11},{4,12},{5,13},{6,14},{7,15},{8,0},{9,1},... | collective-permute-start | bytes 460808 | tf_op jit(solution)/shard_map/ppermute | solution.py:383
  336.1 14.3 %collective-permute-start.51 = (bf16[1,24,3200]{2,1,0:T(8,128)(2,1)S(1)}, bf16[1,24,3200]{2,1,0:T(8,128)(2,1)S(1)}, u32[]{:S(2)}, u32[]{:S(2)}) collective-permute-start(bf16[1,24,3200]{2,1,0:T(8,128)(2,1)S(1)} %get-tuple-element.254), channel_id=1, source_target_pairs={{0,16},{1,17},{2,18},{3,19},{4,20},{5,21},{6,22},{7,23},{8,24},{9,... | collective-permute-start | bytes 460808 | tf_op jit(solution)/shard_map/ppermute | solution.py:383
  336.7 13.7 %collective-permute-start.52 = (bf16[1,24,3200]{2,1,0:T(8,128)(2,1)S(1)}, bf16[1,24,3200]{2,1,0:T(8,128)(2,1)S(1)}, u32[]{:S(2)}, u32[]{:S(2)}) collective-permute-start(bf16[1,24,3200]{2,1,0:T(8,128)(2,1)S(1)} %get-tuple-element.253), channel_id=1, source_target_pairs={{0,24},{1,25},{2,26},{3,27},{4,28},{5,29},{6,30},{7,31},{8,16},{9,... | collective-permute-start | bytes 460808 | tf_op jit(solution)/shard_map/ppermute | solution.py:383
  339.2 15.3 %collective-permute-start.54 = (bf16[2,24,1024]{2,1,0:T(8,128)(2,1)S(1)}, bf16[2,24,1024]{2,1,0:T(8,128)(2,1)S(1)}, u32[]{:S(2)}, u32[]{:S(2)}) collective-permute-start(bf16[2,24,1024]{2,1,0:T(8,128)(2,1)S(1)} %pad_maximum_fusion.13), channel_id=1, source_target_pairs={{0,2},{1,3},{2,0},{3,1},{4,6},{5,7},{6,4},{7,5},{8,10},{9,11},{10,... | collective-permute-start | bytes 294920 | tf_op jit(solution)/shard_map/ppermute | solution.py:383
  (51 other events, 256.8 us)

commit v5 on v4

--- a/solution.py
+++ b/solution.py
@@ -810,7 +810,7 @@
     down_parts = parts_of(down_weight.astype(BF16), 1, shard_rows * dp_count // 2)
     down_parts = down_parts.reshape(dp_count // 2, shard_rows, 2 * share)
     far_shard = stacked([part[None] for part in pair_parts] + [down_parts])
-    far_shard = tie(far_shard, around)[0][None]
+    far_shard = tie(far_shard, near_held)[0][None]
     far_order = seq_groups[::-1]
     far_first = swaps(far_shard, far_order[0])
     far_own = [piece for group in far_order[1:2] for piece in swaps(far_shard, group)]
@@ -862,6 +862,10 @@
         first, steps, queries_turned, keys, values_turned, key_feat, query_feat, tiles, head_dim, pairs
     )
     far_first = stacked(tie(far_first, outs)[0])
+    grad_held = {0: cotangent[0]}
+    for bit in range(dp_bits - 1, 0, -1):
+        grad_held.update({mask ^ (1 << bit): flat_swap(piece, 1 << bit) for mask, piece in list(grad_held.items())})
+    outs, grad_held = tie(outs, grad_held)
     first_masks = swap_masks([0], far_order[0])
     far_held, far_masks = [far_shard, far_first], [[0], first_masks]
     for number, group in enumerate(far_order[1:]):
@@ -882,7 +886,8 @@
     second = middle * scale_two
     second_low = (second * gain_two).astype(BF16)
     every_second = jnp.concatenate(gather_dp(second_low, dp_bits), axis=0)
-    every_grad = jnp.concatenate(gather_dp(cotangent[0], dp_bits), axis=0)
+    grad_held.update({mask ^ 1: flat_swap(piece, 1) for mask, piece in list(grad_held.items())})
+    every_grad = jnp.concatenate([grad_held[mask] for mask in range(dp_count)], axis=0)
     both_ways = contract(every_second, weight_pair, 1, 0)
     gate_values, upward = both_ways[:, :share], both_ways[:, share:]
     active, slope = gelu_pair(gate_values)

time: 369 us -> 368 us (level)
  starting transfers between devices: 112 us -> 99.1 us
  Pallas kernels: 69.5 us -> 79 us
  local copies, waits for them, and re-layouts: 32.1 us -> 36.2 us
    ppermute x16, starting transfers between devices: 58.2 us -> 43.3 us  [shifted(): return lax.ppermute(value, axis, pairs)]
    ppermute x39, waiting for transfers between devices: 36.5 us -> 43.4 us  [flat_swap(): lax.ppermute(value, BOTH, [(source, source ^ mask) for source in range(co...]
    ppermute x16, waiting for transfers between devices: 30.9 us -> 24.5 us  [shifted(): return lax.ppermute(value, axis, pairs)]
    unnamed x123 -> x122, local copies, waits for them, and re-layouts: 19.1 us -> 20.8 us
  transfers between devices with their start and end apart: 55 -> 55, of which waited for: 13 -> 14; matrix products, arithmetic and copies ran while one was open for 20% -> 21% of each run, Pallas kernels for 19% -> 21%
where the time goes in v5:
time: 368 us; the launch traced here: 361 us
  starting transfers between devices  99.1 us (27%)
  Pallas kernels  79 us (21%)
  waiting for transfers between devices  68 us (18%)
  matrix products  46.6 us (13%)
  local copies, waits for them, and re-layouts  36.2 us (10%)
  other arithmetic  30.6 us (8%)
    ppermute x39, starting transfers between devices, flat_swap(): lax.ppermute(value, BOTH, [(source, source ^ mask) for source in range(co...  55.8 us
    dot_general x20, matrix products, contract(): lax.dot_general(left_side, right_side, (((left_dim,), (right_dim,)), ((),...  46.3 us
    ppermute x39, waiting for transfers between devices, flat_swap(): lax.ppermute(value, BOTH, [(source, source ^ mask) for source in range(co...  43.4 us
    ppermute x16, starting transfers between devices, shifted(): return lax.ppermute(value, axis, pairs)  43.3 us
    pallas_call x1, Pallas kernels, attend_back(): pl.pallas_call(kernel, out_shape=(jax.ShapeDtypeStruct((width, row_count)...  26.1 us
    ppermute x16, waiting for transfers between devices, shifted(): return lax.ppermute(value, axis, pairs)  24.5 us
    unnamed x122, local copies, waits for them, and re-layouts  20.8 us
    pallas_call x1, Pallas kernels, attend(): pl.pallas_call(kernel, out_shape=(jax.ShapeDtypeStruct((width, row_count)...  12.3 us
  transfers between devices with their start and end apart: 55, of which 14 were waited for; matrix products, arithmetic and copies ran while one was open for 21% of the time, Pallas kernels for 21%

profile of v5, /device:TPU:0, one launch (start us, length us, event | category | flops | bytes accessed | tf_op | source)
XLA Modules:
  0.0 361.2 jit_solution(14088000411136974182)
XLA Ops:
  2.1 5.5 %collective-permute-start.4 = (bf16[256,768]{1,0:T(8,128)(2,1)}, bf16[256,768]{1,0:T(8,128)(2,1)S(1)}, u32[]{:S(2)}, u32[]{:S(2)}) collective-permute-start(bf16[256,768]{1,0:T(8,128)(2,1)} %bitcast.137), channel_id=1, source_target_pairs={{0,4},{4,8},{8,12},{12,16},{16,20},{20,24},{24,28},{1,5},{5,9},{9,... | collective-permute-start | bytes 1179656 | tf_op jit(solution)/shard_map/ppermute | solution.py:378
  12.0 2.1 collective-permute-start
  14.1 2.6 collective-permute-start.1
  16.7 1.8 shard_map.236
  18.5 1.5 fusion.55
  23.8 4.0 %collective-permute-done.1.refs_2_ = bf16[1,24,3200]{2,1,0:T(8,128)(2,1)S(1)} collective-permute-done((bf16[1,24,3200]{2,1,0:T(8,128)(2,1)S(1)}, bf16[1,24,3200]{2,1,0:T(8,128)(2,1)S(1)}, u32[]{:S(2)}, u32[]{:S(2)}) %collective-permute-start.1) | collective-permute-done | bytes 153632 | tf_op jit(solution)/shard_map/ppermute | solution.py:383
  27.9 2.5 collective-permute-start.9
  31.9 1.6 collective-permute-start.5
  33.4 4.1 %collective-permute-start.6 = (bf16[4,24,3200]{2,1,0:T(8,128)(2,1)S(1)}, bf16[4,24,3200]{2,1,0:T(8,128)(2,1)S(1)}, u32[]{:S(2)}, u32[]{:S(2)}) collective-permute-start(bf16[4,24,3200]{2,1,0:T(8,128)(2,1)S(1)} %shard_map.230.refs_0_), channel_id=1, source_target_pairs={{0,4},{1,5},{2,6},{3,7},{4,0},{5,1},{6,2},{7,3},{8,12},{9,13},{10,... | collective-permute-start | bytes 1843208 | tf_op jit(solution)/shard_map/ppermute | solution.py:383
  41.6 12.2 %shard_map.231.tiles_ref = f32[12,19,128,128]{3,2,1,0:T(8,128)} custom-call(f32[12,1,2560]{2,1,0:T(1,128)} %reshape.237.line_ref), custom_call_target="tpu_custom_call" | custom-call | flops 1 | bytes 1 | tf_op jit(solution)/shard_map/pallas_call | solution.py:43
  54.5 5.3 %collective-permute-start.11 = (bf16[256,768]{1,0:T(8,128)(2,1)S(1)}, bf16[256,768]{1,0:T(8,128)(2,1)}, u32[]{:S(2)}, u32[]{:S(2)}) collective-permute-start(bf16[256,768]{1,0:T(8,128)(2,1)S(1)} %bitcast.140), channel_id=1, source_target_pairs={{0,16},{4,20},{8,24},{12,28},{1,17},{5,21},{9,25},{13,29},{2,18},{... | collective-permute-start | bytes 1179656 | tf_op jit(solution)/shard_map/ppermute | solution.py:378
  59.9 3.5 collective-permute-start.12
  72.3 1.7 select_convert_fusion.key_feat_ref
  77.4 1.6 collective-permute-start.22
  80.3 1.9 collective-permute-done.22
  93.2 2.1 shard_map.233
  95.4 4.4 %collective-permute-start.24 = (bf16[1,6,24,1024]{3,2,1,0:T(8,128)(2,1)}, bf16[1,6,24,1024]{3,2,1,0:T(8,128)(2,1)S(1)}, u32[]{:S(2)}, u32[]{:S(2)}) collective-permute-start(bf16[1,6,24,1024]{3,2,1,0:T(8,128)(2,1)} %bitcast.18.refs_0_), channel_id=1, source_target_pairs={{0,16},{1,17},{2,18},{3,19},{4,20},{5,21},{6,22},{7,23},{8,24},{9,... | collective-permute-start | bytes 884744 | tf_op jit(solution)/shard_map/ppermute | solution.py:383
  101.2 2.4 collective-permute-done.14.refs_8_
  103.7 2.9 shard_map.234
  106.6 4.7 %convolution_convert_fusion.2.value_turned_ref = bf16[768,2304]{1,0:T(8,128)(2,1)} fusion(bf16[2304,768]{1,0:T(8,128)(2,1)S(1)} %shard_map.234, bf16[768,3200]{1,0:T(8,128)(2,1)S(1)} %bitcast.123), kind=kOutput, calls=%fused_computation.2 | convolution fusion | flops 2719678464 | bytes 8257536 | tf_op jit(solution)/shard_map/dot_general | solution.py:699
  111.3 4.3 %convolution_convert_fusion.3.key_ref = bf16[2304,768]{1,0:T(8,128)(2,1)} fusion(bf16[2304,768]{1,0:T(8,128)(2,1)S(1)} %shard_map.234, bf16[768,3200]{1,0:T(8,128)(2,1)S(1)} %bitcast.124), kind=kOutput, calls=%fused_computation.3 | convolution fusion | flops 2719678464 | bytes 8257536 | tf_op jit(solution)/shard_map/dot_general | solution.py:699
  117.0 12.3 %shard_map.235 = (f32[768,256]{1,0:T(8,128)S(1)}, f32[3,4,256]{2,1,0:T(4,128)S(1)}) custom-call(s32[2]{0:T(128)S(1)} %get-tuple-element.230.first_ref, s32[2]{0:T(128)S(1)} %get-tuple-element.231.last_ref, bf16[768,256]{1,0:T(8,128)(2,1)S(1)} %convolution_convert_fusion.15.query_ref.query_turned_ref, bf16[2304,768]{1,0:T(8,128)(2,1)} %convolution_convert_fusion.3.key_ref, ...), custom_call_target="tpu_custom_call" | custom-call | flops 4026531840 | bytes 25165824 | tf_op jit(solution)/shard_map/pallas_call | solution.py:145
  130.2 1.6 copy-done.7
  131.9 4.3 %convolution_convert_fusion.value_ref = bf16[2304,768]{1,0:T(8,128)(2,1)} fusion(bf16[2304,768]{1,0:T(8,128)(2,1)S(1)} %copy-done.7, bf16[768,3200]{1,0:T(8,128)(2,1)S(1)} %bitcast.128), kind=kOutput, calls=%fused_computation | convolution fusion | flops 2719678464 | bytes 8257536 | tf_op jit(solution)/shard_map/dot_general | solution.py:699
  136.3 2.3 collective-permute-start.27
  138.6 4.5 %convolution_convert_fusion.1.key_turned_ref = bf16[768,2304]{1,0:T(8,128)(2,1)} fusion(bf16[2304,768]{1,0:T(8,128)(2,1)S(1)} %copy-done.7, bf16[768,3200]{1,0:T(8,128)(2,1)S(1)} %bitcast.129), kind=kOutput, calls=%fused_computation.1 | convolution fusion | flops 2719678464 | bytes 8257536 | tf_op jit(solution)/shard_map/dot_general | solution.py:699
  146.4 17.7 %collective-permute-done.26.refs_2_ = bf16[1,6,24,1024]{3,2,1,0:T(8,128)(2,1)S(1)} collective-permute-done((bf16[1,6,24,1024]{3,2,1,0:T(8,128)(2,1)}, bf16[1,6,24,1024]{3,2,1,0:T(8,128)(2,1)S(1)}, u32[]{:S(2)}, u32[]{:S(2)}) %collective-permute-start.26) | collective-permute-done | bytes 294944 | tf_op jit(solution)/shard_map/ppermute | solution.py:383
  165.2 1.9 fusion.38
  167.1 2.7 fusion.6
  169.9 1.9 convolution_convert_fusion.5
  173.3 1.9 convolution_convert_fusion.6
  175.3 1.5 collective-permute-start.30
  178.1 8.4 %collective-permute-done.30 = bf16[256,768]{1,0:T(8,128)(2,1)S(1)} collective-permute-done((bf16[256,768]{1,0:T(8,128)(2,1)S(1)}, bf16[256,768]{1,0:T(8,128)(2,1)S(1)}, u32[]{:S(2)}, u32[]{:S(2)}) %collective-permute-start.30) | collective-permute-done | bytes 393248 | tf_op jit(solution)/shard_map/ppermute | solution.py:383
  187.2 1.5 convolution_convert_fusion.10
  191.5 1.8 collective-permute-start.34
  196.0 26.1 %shard_map.240 = (bf16[768,256]{1,0:T(8,128)(2,1)}, bf16[2304,768]{1,0:T(8,128)(2,1)}, bf16[2304,768]{1,0:T(8,128)(2,1)}, f32[12,19,128,128]{3,2,1,0:T(8,128)}) custom-call(s32[2]{0:T(128)} %copy-done.40, s32[2]{0:T(128)} %copy-done.41, bf16[256,768]{1,0:T(8,128)(2,1)} %convolution_convert_fusion.14.query_ref, ...), custom_call_target="tpu_custom_call", output_to_operand_aliasing={{3}: (13, {})} | custom-call | flops 10066329600 | bytes 33554432 | tf_op jit(solution)/shard_map/pallas_call | solution.py:238
  223.6 1.9 collective-permute-start.39
  225.5 2.2 collective-permute-start.40
  229.1 4.1 %convolution_convert_fusion.7 = bf16[768,768]{1,0:T(8,128)(2,1)} fusion(bf16[2304,768]{1,0:T(8,128)(2,1)S(1)} %copy-done.7, bf16[2304,768]{1,0:T(8,128)(2,1)S(1)} %copy-done.9), kind=kOutput, calls=%fused_computation.25 | convolution fusion | flops 2718498816 | bytes 8257536 | tf_op jit(solution)/shard_map/dot_general | solution.py:699
  233.2 4.1 %convolution_convert_fusion.8 = bf16[768,768]{1,0:T(8,128)(2,1)} fusion(bf16[2304,768]{1,0:T(8,128)(2,1)S(1)} %copy-done.7, bf16[2304,768]{1,0:T(8,128)(2,1)S(1)} %copy-done.8), kind=kOutput, calls=%fused_computation.26 | convolution fusion | flops 2718498816 | bytes 8257536 | tf_op jit(solution)/shard_map/dot_general | solution.py:699
  237.4 5.8 %shard_map.243 = bf16[2304,768]{1,0:T(8,128)(2,1)S(1)} custom-call(s32[2]{0:T(128)S(1)} %pad_add_fusion.4.range_ref, bf16[2304,768]{1,0:T(8,128)(2,1)S(1)} %copy-done.8, bf16[2304,768]{1,0:T(8,128)(2,1)S(1)} %copy-done.9, bf16[768,3200]{1,0:T(8,128)(2,1)} %bitcast.133, bf16[768,3200]{1,0:T(8,128)(2,1)} %bitcast.134), custom_call_target="tpu_custom_call" | custom-call | flops 1 | bytes 1 | tf_op jit(solution)/shard_map/pallas_call | solution.py:356
  244.4 2.9 collective-permute-start.35
  248.7 10.2 %shard_map.241 = f32[12,32]{1,0:T(8,128)S(1)} custom-call(s32[2]{0:T(128)S(1)} %pad_add_fusion.3.range_ref, f32[12,19,128,128]{3,2,1,0:T(8,128)} %get-tuple-element.138.tiles_ref, s32[19,1,256]{2,1,0:T(1,128)S(1)} %copy-done.38), custom_call_target="tpu_custom_call" | custom-call | flops 1 | bytes 1 | tf_op jit(solution)/shard_map/pallas_call | solution.py:314
  258.9 6.0 %collective-permute-start.37 = (bf16[256,768]{1,0:T(8,128)(2,1)}, bf16[256,768]{1,0:T(8,128)(2,1)}, u32[]{:S(2)}, u32[]{:S(2)}) collective-permute-start(bf16[256,768]{1,0:T(8,128)(2,1)} %get-tuple-element.240), channel_id=1, source_target_pairs={{0,12},{4,16},{8,20},{12,24},{16,28},{1,13},{5,17},{9,21},{13,25},... | collective-permute-start | bytes 1179656 | tf_op jit(solution)/shard_map/ppermute | solution.py:378
  266.6 1.7 convolution_convert_fusion.9
  270.9 1.7 shard_map.242
  274.1 2.3 collective-permute-done.37
  276.4 3.0 collective-permute-done.38
  280.6 2.7 fusion.33
  283.4 2.2 collective-permute-start.48
  286.9 2.3 add_convert_fusion
  289.5 5.5 %collective-permute-start.43 = (bf16[4,24,3200]{2,1,0:T(8,128)(2,1)S(1)}, bf16[4,24,3200]{2,1,0:T(8,128)(2,1)S(1)}, u32[]{:S(2)}, u32[]{:S(2)}) collective-permute-start(bf16[4,24,3200]{2,1,0:T(8,128)(2,1)S(1)} %get-tuple-element.245), channel_id=1, source_target_pairs={{0,2},{1,3},{2,0},{3,1},{4,6},{5,7},{6,4},{7,5},{8,10},{9,11},{10,... | collective-permute-start | bytes 1843208 | tf_op jit(solution)/shard_map/ppermute | solution.py:383
  295.0 9.2 %collective-permute-start.44 = (bf16[4,24,3200]{2,1,0:T(8,128)(2,1)S(1)}, bf16[4,24,3200]{2,1,0:T(8,128)(2,1)S(1)}, u32[]{:S(2)}, u32[]{:S(2)}) collective-permute-start(bf16[4,24,3200]{2,1,0:T(8,128)(2,1)S(1)} %get-tuple-element.244), channel_id=1, source_target_pairs={{0,4},{1,5},{2,6},{3,7},{4,0},{5,1},{6,2},{7,3},{8,12},{9,13},{10,... | collective-permute-start | bytes 1843208 | tf_op jit(solution)/shard_map/ppermute | solution.py:383
  304.3 4.8 %collective-permute-start.46 = (bf16[256,768]{1,0:T(8,128)(2,1)S(1)}, bf16[256,768]{1,0:T(8,128)(2,1)S(1)}, u32[]{:S(2)}, u32[]{:S(2)}) collective-permute-start(bf16[256,768]{1,0:T(8,128)(2,1)S(1)} %get-tuple-element.238), channel_id=1, source_target_pairs={{0,16},{4,20},{8,24},{12,28},{1,17},{5,21},{9,25},{13,29},{2,18},{... | collective-permute-start | bytes 1179656 | tf_op jit(solution)/shard_map/ppermute | solution.py:378
  310.4 1.8 fusion.23
  313.5 3.5 collective-permute-done.46
  317.0 13.2 %collective-permute-done.47 = bf16[256,768]{1,0:T(8,128)(2,1)S(1)} collective-permute-done((bf16[256,768]{1,0:T(8,128)(2,1)S(1)}, bf16[256,768]{1,0:T(8,128)(2,1)S(1)}, u32[]{:S(2)}, u32[]{:S(2)}) %collective-permute-start.47) | collective-permute-done | bytes 393248 | tf_op jit(solution)/shard_map/ppermute | solution.py:378
  332.8 2.4 collective-permute-start.50
  335.7 2.0 collective-permute-start.52
  338.3 2.0 collective-permute-start.54
  340.3 1.8 collective-permute-done.50
  342.2 7.4 %collective-permute-done.51 = bf16[1,24,3200]{2,1,0:T(8,128)(2,1)S(1)} collective-permute-done((bf16[1,24,3200]{2,1,0:T(8,128)(2,1)S(1)}, bf16[1,24,3200]{2,1,0:T(8,128)(2,1)S(1)}, u32[]{:S(2)}, u32[]{:S(2)}) %collective-permute-start.51) | collective-permute-done | bytes 153632 | tf_op jit(solution)/shard_map/ppermute | solution.py:383
  349.6 2.1 fusion.27
  355.2 1.8 shard_map.244
  (288 shorter events, 85.6 us)
Async XLA Ops:
  0.6 40.0 %copy-start = (f32[32,12]{0,1:T(8,128)S(1)}, f32[32,12]{0,1:T(8,128)}, u32[]{:S(2)}) copy-start(f32[32,12]{0,1:T(8,128)} %param.22) | copy-start | bytes 4612
  0.7 37.8 %copy-start.53 = (s32[2047]{0:T(1024)S(1)}, s32[2047]{0:T(1024)}, u32[]{:S(2)}) copy-start(s32[2047]{0:T(1024)} %param.16) | copy-start | bytes 24568
  0.7 29.6 %collective-permute-start.3 = (bf16[256,768]{1,0:T(8,128)(2,1)}, bf16[256,768]{1,0:T(8,128)(2,1)S(1)}, u32[]{:S(2)}, u32[]{:S(2)}) collective-permute-start(bf16[256,768]{1,0:T(8,128)(2,1)} %bitcast.136), channel_id=1, source_target_pairs={{4,0},{8,4},{12,8},{16,12},{20,16},{24,20},{28,24},{5,1},{9,5},{13... | collective-permute-start | bytes 1179656 | tf_op jit(solution)/shard_map/ppermute | solution.py:378
  2.1 29.0 %collective-permute-start.4 = (bf16[256,768]{1,0:T(8,128)(2,1)}, bf16[256,768]{1,0:T(8,128)(2,1)S(1)}, u32[]{:S(2)}, u32[]{:S(2)}) collective-permute-start(bf16[256,768]{1,0:T(8,128)(2,1)} %bitcast.137), channel_id=1, source_target_pairs={{0,4},{4,8},{8,12},{12,16},{16,20},{20,24},{24,28},{1,5},{5,9},{9,... | collective-permute-start | bytes 1179656 | tf_op jit(solution)/shard_map/ppermute | solution.py:378
  12.0 10.6 %collective-permute-start = (bf16[1,24,3200]{2,1,0:T(8,128)(2,1)S(1)}, bf16[1,24,3200]{2,1,0:T(8,128)(2,1)S(1)}, u32[]{:S(2)}, u32[]{:S(2)}) collective-permute-start(bf16[1,24,3200]{2,1,0:T(8,128)(2,1)S(1)} %bitcast.149), channel_id=1, source_target_pairs={{0,8},{1,9},{2,10},{3,11},{4,12},{5,13},{6,14},{7,15},{8,0},{9,1},... | collective-permute-start | bytes 460808 | tf_op jit(solution)/shard_map/ppermute | solution.py:383
  14.1 13.8 %collective-permute-start.1 = (bf16[1,24,3200]{2,1,0:T(8,128)(2,1)S(1)}, bf16[1,24,3200]{2,1,0:T(8,128)(2,1)S(1)}, u32[]{:S(2)}, u32[]{:S(2)}) collective-permute-start(bf16[1,24,3200]{2,1,0:T(8,128)(2,1)S(1)} %bitcast.150), channel_id=1, source_target_pairs={{0,16},{1,17},{2,18},{3,19},{4,20},{5,21},{6,22},{7,23},{8,24},{9,... | collective-permute-start | bytes 460808 | tf_op jit(solution)/shard_map/ppermute | solution.py:383
  16.7 13.6 %collective-permute-start.2 = (bf16[1,24,3200]{2,1,0:T(8,128)(2,1)S(1)}, bf16[1,24,3200]{2,1,0:T(8,128)(2,1)S(1)}, u32[]{:S(2)}, u32[]{:S(2)}) collective-permute-start(bf16[1,24,3200]{2,1,0:T(8,128)(2,1)S(1)} %bitcast.151), channel_id=1, source_target_pairs={{0,24},{1,25},{2,26},{3,27},{4,28},{5,29},{6,30},{7,31},{8,16},{9,... | collective-permute-start | bytes 460808 | tf_op jit(solution)/shard_map/ppermute | solution.py:383
  22.5 31.2 %collective-permute-start.8 = (bf16[256,768]{1,0:T(8,128)(2,1)}, bf16[256,768]{1,0:T(8,128)(2,1)S(1)}, u32[]{:S(2)}, u32[]{:S(2)}) collective-permute-start(bf16[256,768]{1,0:T(8,128)(2,1)} %bitcast.138), channel_id=1, source_target_pairs={{8,0},{12,4},{16,8},{20,12},{24,16},{28,20},{9,1},{13,5},{17,9},{2... | collective-permute-start | bytes 1179656 | tf_op jit(solution)/shard_map/ppermute | solution.py:378
  27.9 32.0 %collective-permute-start.9 = (bf16[256,768]{1,0:T(8,128)(2,1)}, bf16[256,768]{1,0:T(8,128)(2,1)}, u32[]{:S(2)}, u32[]{:S(2)}) collective-permute-start(bf16[256,768]{1,0:T(8,128)(2,1)} %bitcast.139), channel_id=1, source_target_pairs={{0,8},{4,12},{8,16},{12,20},{16,24},{20,28},{1,9},{5,13},{9,17},{1... | collective-permute-start | bytes 1179656 | tf_op jit(solution)/shard_map/ppermute | solution.py:378
  31.9 31.5 %collective-permute-start.5 = (bf16[4,24,3200]{2,1,0:T(8,128)(2,1)S(1)}, bf16[4,24,3200]{2,1,0:T(8,128)(2,1)S(1)}, u32[]{:S(2)}, u32[]{:S(2)}) collective-permute-start(bf16[4,24,3200]{2,1,0:T(8,128)(2,1)S(1)} %shard_map.230.refs_0_), channel_id=1, source_target_pairs={{0,2},{1,3},{2,0},{3,1},{4,6},{5,7},{6,4},{7,5},{8,10},{9,11},{10,... | collective-permute-start | bytes 1843208 | tf_op jit(solution)/shard_map/ppermute | solution.py:383
  33.4 32.0 %collective-permute-start.6 = (bf16[4,24,3200]{2,1,0:T(8,128)(2,1)S(1)}, bf16[4,24,3200]{2,1,0:T(8,128)(2,1)S(1)}, u32[]{:S(2)}, u32[]{:S(2)}) collective-permute-start(bf16[4,24,3200]{2,1,0:T(8,128)(2,1)S(1)} %shard_map.230.refs_0_), channel_id=1, source_target_pairs={{0,4},{1,5},{2,6},{3,7},{4,0},{5,1},{6,2},{7,3},{8,12},{9,13},{10,... | collective-permute-start | bytes 1843208 | tf_op jit(solution)/shard_map/ppermute | solution.py:383
  37.5 28.8 %collective-permute-start.7 = (bf16[4,24,3200]{2,1,0:T(8,128)(2,1)S(1)}, bf16[4,24,3200]{2,1,0:T(8,128)(2,1)S(1)}, u32[]{:S(2)}, u32[]{:S(2)}) collective-permute-start(bf16[4,24,3200]{2,1,0:T(8,128)(2,1)S(1)} %shard_map.230.refs_0_), channel_id=1, source_target_pairs={{0,6},{1,7},{2,4},{3,5},{4,2},{5,3},{6,0},{7,1},{8,14},{9,15},{10,... | collective-permute-start | bytes 1843208 | tf_op jit(solution)/shard_map/ppermute | solution.py:383
  41.6 32.4 %copy-start.56 = (s32[2]{0:T(128)S(1)}, s32[2]{0:T(128)}, u32[]{:S(2)}) copy-start(s32[2]{0:T(128)} %get-tuple-element.294) | copy-start | bytes 28
  54.5 40.8 %collective-permute-start.11 = (bf16[256,768]{1,0:T(8,128)(2,1)S(1)}, bf16[256,768]{1,0:T(8,128)(2,1)}, u32[]{:S(2)}, u32[]{:S(2)}) collective-permute-start(bf16[256,768]{1,0:T(8,128)(2,1)S(1)} %bitcast.140), channel_id=1, source_target_pairs={{0,16},{4,20},{8,24},{12,28},{1,17},{5,21},{9,25},{13,29},{2,18},{... | collective-permute-start | bytes 1179656 | tf_op jit(solution)/shard_map/ppermute | solution.py:378
  59.9 35.5 %collective-permute-start.12 = (bf16[256,768]{1,0:T(8,128)(2,1)S(1)}, bf16[256,768]{1,0:T(8,128)(2,1)}, u32[]{:S(2)}, u32[]{:S(2)}) collective-permute-start(bf16[256,768]{1,0:T(8,128)(2,1)S(1)} %bitcast.141), channel_id=1, source_target_pairs={{0,12},{4,16},{8,20},{12,24},{16,28},{1,13},{5,17},{9,21},{13,25},... | collective-permute-start | bytes 1179656 | tf_op jit(solution)/shard_map/ppermute | solution.py:378
  64.1 35.6 %collective-permute-start.13 = (bf16[256,768]{1,0:T(8,128)(2,1)S(1)}, bf16[256,768]{1,0:T(8,128)(2,1)}, u32[]{:S(2)}, u32[]{:S(2)}) collective-permute-start(bf16[256,768]{1,0:T(8,128)(2,1)S(1)} %bitcast.142), channel_id=1, source_target_pairs={{12,0},{16,4},{20,8},{24,12},{28,16},{13,1},{17,5},{21,9},{25,13},... | collective-permute-start | bytes 1179656 | tf_op jit(solution)/shard_map/ppermute | solution.py:378
  66.3 9.7 %collective-permute-start.21 = (bf16[2,24,1024]{2,1,0:T(8,128)(2,1)}, bf16[2,24,1024]{2,1,0:T(8,128)(2,1)}, u32[]{:S(2)}, u32[]{:S(2)}) collective-permute-start(bf16[2,24,1024]{2,1,0:T(8,128)(2,1)} %pad_maximum_fusion.7), channel_id=1, source_target_pairs={{0,1},{1,0},{2,3},{3,2},{4,5},{5,4},{6,7},{7,6},{8,9},{9,8},{10,11... | collective-permute-start | bytes 294920 | tf_op jit(solution)/shard_map/ppermute | solution.py:383
  70.5 21.1 %collective-permute-start.10 = (bf16[16,24,3200]{2,1,0:T(8,128)(2,1)S(1)}, bf16[16,24,3200]{2,1,0:T(8,128)(2,1)}, u32[]{:S(2)}, u32[]{:S(2)}) collective-permute-start(bf16[16,24,3200]{2,1,0:T(8,128)(2,1)S(1)} %shard_map.232.refs_0_), channel_id=1, source_target_pairs={{0,1},{1,0},{2,3},{3,2},{4,5},{5,4},{6,7},{7,6},{8,9},{9,8},{10,11... | collective-permute-start | bytes 7372808 | tf_op jit(solution)/shard_map/ppermute | solution.py:383
  74.0 43.0 %copy-start.12 = (bf16[2304,128]{1,0:T(8,128)(2,1)}, bf16[2304,128]{1,0:T(8,128)(2,1)S(1)}, u32[]{:S(2)}) copy-start(bf16[2304,128]{1,0:T(8,128)(2,1)S(1)} %select_convert_fusion.key_feat_ref) | copy-start | bytes 1769476
  74.8 42.2 %copy-start.40 = (s32[2]{0:T(128)}, s32[2]{0:T(128)S(1)}, u32[]{:S(2)}) copy-start(s32[2]{0:T(128)S(1)} %get-tuple-element.230.first_ref) | copy-start | bytes 28
  74.8 42.2 %copy-start.41 = (s32[2]{0:T(128)}, s32[2]{0:T(128)S(1)}, u32[]{:S(2)}) copy-start(s32[2]{0:T(128)S(1)} %get-tuple-element.231.last_ref) | copy-start | bytes 28
  77.4 4.8 %collective-permute-start.22 = (bf16[2,24,1024]{2,1,0:T(8,128)(2,1)S(1)}, bf16[2,24,1024]{2,1,0:T(8,128)(2,1)S(1)}, u32[]{:S(2)}, u32[]{:S(2)}) collective-permute-start(bf16[2,24,1024]{2,1,0:T(8,128)(2,1)S(1)} %pad_maximum_fusion.8), channel_id=1, source_target_pairs={{0,2},{1,3},{2,0},{3,1},{4,6},{5,7},{6,4},{7,5},{8,10},{9,11},{10,... | collective-permute-start | bytes 294920 | tf_op jit(solution)/shard_map/ppermute | solution.py:383
  82.2 21.4 %collective-permute-start.14 = (bf16[256,768]{1,0:T(8,128)(2,1)S(1)}, bf16[256,768]{1,0:T(8,128)(2,1)}, u32[]{:S(2)}, u32[]{:S(2)}) collective-permute-start(bf16[256,768]{1,0:T(8,128)(2,1)S(1)} %bitcast.143), channel_id=1, source_target_pairs={{16,0},{20,4},{24,8},{28,12},{17,1},{21,5},{25,9},{29,13},{18,2},{... | collective-permute-start | bytes 1179656 | tf_op jit(solution)/shard_map/ppermute | solution.py:378
  91.7 37.6 %collective-permute-start.15 = (bf16[256,768]{1,0:T(8,128)(2,1)}, bf16[256,768]{1,0:T(8,128)(2,1)}, u32[]{:S(2)}, u32[]{:S(2)}) collective-permute-start(bf16[256,768]{1,0:T(8,128)(2,1)} %bitcast.161), channel_id=1, source_target_pairs={{0,2},{1,3},{2,0},{3,1},{4,6},{5,7},{6,4},{7,5},{8,10},{9,11},{10,... | collective-permute-start | bytes 1179656 | tf_op jit(solution)/shard_map/ppermute | solution.py:383
  95.3 94.7 %copy-start.2 = (bf16[32,24,3200]{2,1,0:T(8,128)(2,1)}, bf16[32,24,3200]{2,1,0:T(8,128)(2,1)S(1)}, u32[]{:S(2)}) copy-start(bf16[32,24,3200]{2,1,0:T(8,128)(2,1)S(1)} %shard_map.233) | copy-start | bytes 14745604
  95.3 40.9 %collective-permute-start.23 = (bf16[1,6,24,1024]{3,2,1,0:T(8,128)(2,1)}, bf16[1,6,24,1024]{3,2,1,0:T(8,128)(2,1)S(1)}, u32[]{:S(2)}, u32[]{:S(2)}) collective-permute-start(bf16[1,6,24,1024]{3,2,1,0:T(8,128)(2,1)} %bitcast.18.refs_0_), channel_id=1, source_target_pairs={{0,8},{1,9},{2,10},{3,11},{4,12},{5,13},{6,14},{7,15},{8,0},{9,1},... | collective-permute-start | bytes 884744 | tf_op jit(solution)/shard_map/ppermute | solution.py:383
  95.4 40.8 %collective-permute-start.24 = (bf16[1,6,24,1024]{3,2,1,0:T(8,128)(2,1)}, bf16[1,6,24,1024]{3,2,1,0:T(8,128)(2,1)S(1)}, u32[]{:S(2)}, u32[]{:S(2)}) collective-permute-start(bf16[1,6,24,1024]{3,2,1,0:T(8,128)(2,1)} %bitcast.18.refs_0_), channel_id=1, source_target_pairs={{0,16},{1,17},{2,18},{3,19},{4,20},{5,21},{6,22},{7,23},{8,24},{9,... | collective-permute-start | bytes 884744 | tf_op jit(solution)/shard_map/ppermute | solution.py:383
  99.8 36.4 %collective-permute-start.25 = (bf16[1,6,24,1024]{3,2,1,0:T(8,128)(2,1)}, bf16[1,6,24,1024]{3,2,1,0:T(8,128)(2,1)S(1)}, u32[]{:S(2)}, u32[]{:S(2)}) collective-permute-start(bf16[1,6,24,1024]{3,2,1,0:T(8,128)(2,1)} %bitcast.18.refs_0_), channel_id=1, source_target_pairs={{0,24},{1,25},{2,26},{3,27},{4,28},{5,29},{6,30},{7,31},{8,16},{9,... | collective-permute-start | bytes 884744 | tf_op jit(solution)/shard_map/ppermute | solution.py:383
  129.3 57.9 %copy-start.15 = (f32[768,256]{1,0:T(8,128)}, f32[768,256]{1,0:T(8,128)S(1)}, u32[]{:S(2)}) copy-start(f32[768,256]{1,0:T(8,128)S(1)} %get-tuple-element.111.out_ref) | copy-start | bytes 2359300
  129.9 56.9 %copy-start.43 = (f32[256,768]{1,0:T(8,128)}, f32[256,768]{1,0:T(8,128)S(1)}, u32[]{:S(2)}) copy-start(f32[256,768]{1,0:T(8,128)S(1)} %get-tuple-element.292) | copy-start | bytes 2359300
  130.1 14.7 %collective-permute-start.17 = (bf16[256,768]{1,0:T(8,128)(2,1)S(1)}, bf16[256,768]{1,0:T(8,128)(2,1)S(1)}, u32[]{:S(2)}, u32[]{:S(2)}) collective-permute-start(bf16[256,768]{1,0:T(8,128)(2,1)S(1)} %multiply_convert_fusion.2), channel_id=1, source_target_pairs={{0,2},{1,3},{2,0},{3,1},{4,6},{5,7},{6,4},{7,5},{8,10},{9,11},{10,... | collective-permute-start | bytes 1179656 | tf_op jit(solution)/shard_map/ppermute | solution.py:383
  130.2 35.0 %collective-permute-start.16 = (bf16[256,768]{1,0:T(8,128)(2,1)S(1)}, bf16[256,768]{1,0:T(8,128)(2,1)S(1)}, u32[]{:S(2)}, u32[]{:S(2)}) collective-permute-start(bf16[256,768]{1,0:T(8,128)(2,1)S(1)} %multiply_convert_fusion.2), channel_id=1, source_target_pairs={{0,1},{1,0},{2,3},{3,2},{4,5},{5,4},{6,7},{7,6},{8,9},{9,8},{10,11... | collective-permute-start | bytes 1179656 | tf_op jit(solution)/shard_map/ppermute | solution.py:383
  136.3 27.8 %collective-permute-start.27 = (bf16[3,6,24,1024]{3,2,1,0:T(8,128)(2,1)S(1)}, bf16[3,6,24,1024]{3,2,1,0:T(8,128)(2,1)S(1)}, u32[]{:S(2)}, u32[]{:S(2)}) collective-permute-start(bf16[3,6,24,1024]{3,2,1,0:T(8,128)(2,1)S(1)} %shard_map.238.refs_1_), channel_id=1, source_target_pairs={{0,4},{1,5},{2,6},{3,7},{4,0},{5,1},{6,2},{7,3},{8,12},{9,13},{10,... | collective-permute-start | bytes 2654216 | tf_op jit(solution)/shard_map/ppermute | solution.py:383
  143.0 2.2 collective-permute-start.19
  143.0 3.3 collective-permute-start.20
  144.8 20.4 %collective-permute-start.18 = (bf16[256,768]{1,0:T(8,128)(2,1)S(1)}, bf16[256,768]{1,0:T(8,128)(2,1)S(1)}, u32[]{:S(2)}, u32[]{:S(2)}) collective-permute-start(bf16[256,768]{1,0:T(8,128)(2,1)S(1)} %collective-permute-done.17), channel_id=1, source_target_pairs={{0,1},{1,0},{2,3},{3,2},{4,5},{5,4},{6,7},{7,6},{8,9},{9,8},{10,11... | collective-permute-start | bytes 1179656 | tf_op jit(solution)/shard_map/ppermute | solution.py:383
  145.3 18.8 %collective-permute-start.26 = (bf16[1,6,24,1024]{3,2,1,0:T(8,128)(2,1)}, bf16[1,6,24,1024]{3,2,1,0:T(8,128)(2,1)S(1)}, u32[]{:S(2)}, u32[]{:S(2)}) collective-permute-start(bf16[1,6,24,1024]{3,2,1,0:T(8,128)(2,1)} %bitcast.18.refs_0_), channel_id=1, source_target_pairs={{0,4},{1,5},{2,6},{3,7},{4,0},{5,1},{6,2},{7,3},{8,12},{9,13},{10,... | collective-permute-start | bytes 884744 | tf_op jit(solution)/shard_map/ppermute | solution.py:383
  171.8 3.4 collective-permute-start.29
  171.9 6.2 %collective-permute-start.28 = (bf16[256,768]{1,0:T(8,128)(2,1)S(1)}, bf16[256,768]{1,0:T(8,128)(2,1)S(1)}, u32[]{:S(2)}, u32[]{:S(2)}) collective-permute-start(bf16[256,768]{1,0:T(8,128)(2,1)S(1)} %get-tuple-element.253), channel_id=1, source_target_pairs={{0,1},{1,0},{2,3},{3,2},{4,5},{5,4},{6,7},{7,6},{8,9},{9,8},{10,11... | collective-permute-start | bytes 1179656 | tf_op jit(solution)/shard_map/ppermute | solution.py:383
  175.3 11.2 %collective-permute-start.30 = (bf16[256,768]{1,0:T(8,128)(2,1)S(1)}, bf16[256,768]{1,0:T(8,128)(2,1)S(1)}, u32[]{:S(2)}, u32[]{:S(2)}) collective-permute-start(bf16[256,768]{1,0:T(8,128)(2,1)S(1)} %add_convert_fusion.4), channel_id=1, source_target_pairs={{0,2},{1,3},{2,0},{3,1},{4,6},{5,7},{6,4},{7,5},{8,10},{9,11},{10,... | collective-permute-start | bytes 1179656 | tf_op jit(solution)/shard_map/ppermute | solution.py:383
  191.5 30.6 %collective-permute-start.34 = (bf16[4,6,24,1024]{3,2,1,0:T(8,128)(2,1)S(1)}, bf16[4,6,24,1024]{3,2,1,0:T(8,128)(2,1)S(1)}, u32[]{:S(2)}, u32[]{:S(2)}) collective-permute-start(bf16[4,6,24,1024]{3,2,1,0:T(8,128)(2,1)S(1)} %get-tuple-element.247), channel_id=1, source_target_pairs={{0,4},{1,5},{2,6},{3,7},{4,0},{5,1},{6,2},{7,3},{8,12},{9,13},{10,... | collective-permute-start | bytes 3538952 | tf_op jit(solution)/shard_map/ppermute | solution.py:383
  194.1 27.9 %collective-permute-start.31 = (bf16[256,768]{1,0:T(8,128)(2,1)S(1)}, bf16[256,768]{1,0:T(8,128)(2,1)}, u32[]{:S(2)}, u32[]{:S(2)}) collective-permute-start(bf16[256,768]{1,0:T(8,128)(2,1)S(1)} %get-tuple-element.251), channel_id=1, source_target_pairs={{0,1},{1,0},{2,3},{3,2},{4,5},{5,4},{6,7},{7,6},{8,9},{9,8},{10,11... | collective-permute-start | bytes 1179656 | tf_op jit(solution)/shard_map/ppermute | solution.py:383
  194.1 27.9 %collective-permute-start.32 = (bf16[256,768]{1,0:T(8,128)(2,1)S(1)}, bf16[256,768]{1,0:T(8,128)(2,1)}, u32[]{:S(2)}, u32[]{:S(2)}) collective-permute-start(bf16[256,768]{1,0:T(8,128)(2,1)S(1)} %get-tuple-element.250), channel_id=1, source_target_pairs={{0,2},{1,3},{2,0},{3,1},{4,6},{5,7},{6,4},{7,5},{8,10},{9,11},{10,... | collective-permute-start | bytes 1179656 | tf_op jit(solution)/shard_map/ppermute | solution.py:383
  195.6 26.5 %collective-permute-start.33 = (bf16[256,768]{1,0:T(8,128)(2,1)S(1)}, bf16[256,768]{1,0:T(8,128)(2,1)}, u32[]{:S(2)}, u32[]{:S(2)}) collective-permute-start(bf16[256,768]{1,0:T(8,128)(2,1)S(1)} %get-tuple-element.249), channel_id=1, source_target_pairs={{0,3},{1,2},{2,1},{3,0},{4,7},{5,6},{6,5},{7,4},{8,11},{9,10},{10,... | collective-permute-start | bytes 1179656 | tf_op jit(solution)/shard_map/ppermute | solution.py:383
  223.6 35.3 %collective-permute-start.39 = (bf16[1,6,24,1024]{3,2,1,0:T(8,128)(2,1)S(1)}, bf16[1,6,24,1024]{3,2,1,0:T(8,128)(2,1)}, u32[]{:S(2)}, u32[]{:S(2)}) collective-permute-start(bf16[1,6,24,1024]{3,2,1,0:T(8,128)(2,1)S(1)} %get-tuple-element.257), channel_id=1, source_target_pairs={{0,8},{1,9},{2,10},{3,11},{4,12},{5,13},{6,14},{7,15},{8,0},{9,1},... | collective-permute-start | bytes 884744 | tf_op jit(solution)/shard_map/ppermute | solution.py:383
  225.5 39.4 %collective-permute-start.40 = (bf16[1,6,24,1024]{3,2,1,0:T(8,128)(2,1)S(1)}, bf16[1,6,24,1024]{3,2,1,0:T(8,128)(2,1)}, u32[]{:S(2)}, u32[]{:S(2)}) collective-permute-start(bf16[1,6,24,1024]{3,2,1,0:T(8,128)(2,1)S(1)} %get-tuple-element.256), channel_id=1, source_target_pairs={{0,16},{1,17},{2,18},{3,19},{4,20},{5,21},{6,22},{7,23},{8,24},{9,... | collective-permute-start | bytes 884744 | tf_op jit(solution)/shard_map/ppermute | solution.py:383
  227.7 46.4 %collective-permute-start.41 = (bf16[1,6,24,1024]{3,2,1,0:T(8,128)(2,1)}, bf16[1,6,24,1024]{3,2,1,0:T(8,128)(2,1)}, u32[]{:S(2)}, u32[]{:S(2)}) collective-permute-start(bf16[1,6,24,1024]{3,2,1,0:T(8,128)(2,1)} %get-tuple-element.255), channel_id=1, source_target_pairs={{0,24},{1,25},{2,26},{3,27},{4,28},{5,29},{6,30},{7,31},{8,16},{9,... | collective-permute-start | bytes 884744 | tf_op jit(solution)/shard_map/ppermute | solution.py:383
  244.4 29.6 %collective-permute-start.35 = (bf16[256,768]{1,0:T(8,128)(2,1)}, bf16[256,768]{1,0:T(8,128)(2,1)}, u32[]{:S(2)}, u32[]{:S(2)}) collective-permute-start(bf16[256,768]{1,0:T(8,128)(2,1)} %get-tuple-element.242), channel_id=1, source_target_pairs={{0,4},{4,8},{8,12},{12,16},{16,20},{20,24},{24,28},{1,5},{5,9},{9,... | collective-permute-start | bytes 1179656 | tf_op jit(solution)/shard_map/ppermute | solution.py:378
  247.4 26.7 %collective-permute-start.36 = (bf16[256,768]{1,0:T(8,128)(2,1)}, bf16[256,768]{1,0:T(8,128)(2,1)}, u32[]{:S(2)}, u32[]{:S(2)}) collective-permute-start(bf16[256,768]{1,0:T(8,128)(2,1)} %get-tuple-element.241), channel_id=1, source_target_pairs={{4,0},{8,4},{12,8},{16,12},{20,16},{24,20},{28,24},{5,1},{9,5},{13... | collective-permute-start | bytes 1179656 | tf_op jit(solution)/shard_map/ppermute | solution.py:378
  258.9 17.6 %collective-permute-start.37 = (bf16[256,768]{1,0:T(8,128)(2,1)}, bf16[256,768]{1,0:T(8,128)(2,1)}, u32[]{:S(2)}, u32[]{:S(2)}) collective-permute-start(bf16[256,768]{1,0:T(8,128)(2,1)} %get-tuple-element.240), channel_id=1, source_target_pairs={{0,12},{4,16},{8,20},{12,24},{16,28},{1,13},{5,17},{9,21},{13,25},... | collective-permute-start | bytes 1179656 | tf_op jit(solution)/shard_map/ppermute | solution.py:378
  264.9 14.6 %collective-permute-start.38 = (bf16[256,768]{1,0:T(8,128)(2,1)}, bf16[256,768]{1,0:T(8,128)(2,1)}, u32[]{:S(2)}, u32[]{:S(2)}) collective-permute-start(bf16[256,768]{1,0:T(8,128)(2,1)} %get-tuple-element.239), channel_id=1, source_target_pairs={{12,0},{16,4},{20,8},{24,12},{28,16},{13,1},{17,5},{21,9},{25,13},... | collective-permute-start | bytes 1179656 | tf_op jit(solution)/shard_map/ppermute | solution.py:378
  279.4 7.5 %collective-permute-start.42 = (bf16[16,24,3200]{2,1,0:T(8,128)(2,1)}, bf16[16,24,3200]{2,1,0:T(8,128)(2,1)}, u32[]{:S(2)}, u32[]{:S(2)}) collective-permute-start(bf16[16,24,3200]{2,1,0:T(8,128)(2,1)} %get-tuple-element.144), channel_id=1, source_target_pairs={{0,1},{1,0},{2,3},{3,2},{4,5},{5,4},{6,7},{7,6},{8,9},{9,8},{10,11... | collective-permute-start | bytes 7372808 | tf_op jit(solution)/shard_map/ppermute | solution.py:383
  283.4 20.9 %collective-permute-start.48 = (bf16[256,768]{1,0:T(8,128)(2,1)S(1)}, bf16[256,768]{1,0:T(8,128)(2,1)S(1)}, u32[]{:S(2)}, u32[]{:S(2)}) collective-permute-start(bf16[256,768]{1,0:T(8,128)(2,1)S(1)} %get-tuple-element.236), channel_id=1, source_target_pairs={{0,8},{4,12},{8,16},{12,20},{16,24},{20,28},{1,9},{5,13},{9,17},{1... | collective-permute-start | bytes 1179656 | tf_op jit(solution)/shard_map/ppermute | solution.py:378
  285.6 23.5 %collective-permute-start.49 = (bf16[256,768]{1,0:T(8,128)(2,1)S(1)}, bf16[256,768]{1,0:T(8,128)(2,1)S(1)}, u32[]{:S(2)}, u32[]{:S(2)}) collective-permute-start(bf16[256,768]{1,0:T(8,128)(2,1)S(1)} %get-tuple-element.235), channel_id=1, source_target_pairs={{8,0},{12,4},{16,8},{20,12},{24,16},{28,20},{9,1},{13,5},{17,9},{2... | collective-permute-start | bytes 1179656 | tf_op jit(solution)/shard_map/ppermute | solution.py:378
  289.5 40.7 %collective-permute-start.43 = (bf16[4,24,3200]{2,1,0:T(8,128)(2,1)S(1)}, bf16[4,24,3200]{2,1,0:T(8,128)(2,1)S(1)}, u32[]{:S(2)}, u32[]{:S(2)}) collective-permute-start(bf16[4,24,3200]{2,1,0:T(8,128)(2,1)S(1)} %get-tuple-element.245), channel_id=1, source_target_pairs={{0,2},{1,3},{2,0},{3,1},{4,6},{5,7},{6,4},{7,5},{8,10},{9,11},{10,... | collective-permute-start | bytes 1843208 | tf_op jit(solution)/shard_map/ppermute | solution.py:383
  295.0 36.6 %collective-permute-start.44 = (bf16[4,24,3200]{2,1,0:T(8,128)(2,1)S(1)}, bf16[4,24,3200]{2,1,0:T(8,128)(2,1)S(1)}, u32[]{:S(2)}, u32[]{:S(2)}) collective-permute-start(bf16[4,24,3200]{2,1,0:T(8,128)(2,1)S(1)} %get-tuple-element.244), channel_id=1, source_target_pairs={{0,4},{1,5},{2,6},{3,7},{4,0},{5,1},{6,2},{7,3},{8,12},{9,13},{10,... | collective-permute-start | bytes 1843208 | tf_op jit(solution)/shard_map/ppermute | solution.py:383
  304.2 27.4 %collective-permute-start.45 = (bf16[4,24,3200]{2,1,0:T(8,128)(2,1)S(1)}, bf16[4,24,3200]{2,1,0:T(8,128)(2,1)S(1)}, u32[]{:S(2)}, u32[]{:S(2)}) collective-permute-start(bf16[4,24,3200]{2,1,0:T(8,128)(2,1)S(1)} %get-tuple-element.243), channel_id=1, source_target_pairs={{0,6},{1,7},{2,4},{3,5},{4,2},{5,3},{6,0},{7,1},{8,14},{9,15},{10,... | collective-permute-start | bytes 1843208 | tf_op jit(solution)/shard_map/ppermute | solution.py:383
  304.3 12.7 %collective-permute-start.46 = (bf16[256,768]{1,0:T(8,128)(2,1)S(1)}, bf16[256,768]{1,0:T(8,128)(2,1)S(1)}, u32[]{:S(2)}, u32[]{:S(2)}) collective-permute-start(bf16[256,768]{1,0:T(8,128)(2,1)S(1)} %get-tuple-element.238), channel_id=1, source_target_pairs={{0,16},{4,20},{8,24},{12,28},{1,17},{5,21},{9,25},{13,29},{2,18},{... | collective-permute-start | bytes 1179656 | tf_op jit(solution)/shard_map/ppermute | solution.py:378
  309.1 21.1 %collective-permute-start.47 = (bf16[256,768]{1,0:T(8,128)(2,1)S(1)}, bf16[256,768]{1,0:T(8,128)(2,1)S(1)}, u32[]{:S(2)}, u32[]{:S(2)}) collective-permute-start(bf16[256,768]{1,0:T(8,128)(2,1)S(1)} %get-tuple-element.237), channel_id=1, source_target_pairs={{16,0},{20,4},{24,8},{28,12},{17,1},{21,5},{25,9},{29,13},{18,2},{... | collective-permute-start | bytes 1179656 | tf_op jit(solution)/shard_map/ppermute | solution.py:378
  332.3 5.4 %collective-permute-start.53 = (bf16[2,24,1024]{2,1,0:T(8,128)(2,1)S(1)}, bf16[2,24,1024]{2,1,0:T(8,128)(2,1)S(1)}, u32[]{:S(2)}, u32[]{:S(2)}) collective-permute-start(bf16[2,24,1024]{2,1,0:T(8,128)(2,1)S(1)} %pad_maximum_fusion.9), channel_id=1, source_target_pairs={{0,1},{1,0},{2,3},{3,2},{4,5},{5,4},{6,7},{7,6},{8,9},{9,8},{10,11... | collective-permute-start | bytes 294920 | tf_op jit(solution)/shard_map/ppermute | solution.py:383
  332.8 9.4 %collective-permute-start.50 = (bf16[1,24,3200]{2,1,0:T(8,128)(2,1)S(1)}, bf16[1,24,3200]{2,1,0:T(8,128)(2,1)S(1)}, u32[]{:S(2)}, u32[]{:S(2)}) collective-permute-start(bf16[1,24,3200]{2,1,0:T(8,128)(2,1)S(1)} %get-tuple-element.261), channel_id=1, source_target_pairs={{0,8},{1,9},{2,10},{3,11},{4,12},{5,13},{6,14},{7,15},{8,0},{9,1},... | collective-permute-start | bytes 460808 | tf_op jit(solution)/shard_map/ppermute | solution.py:383
  335.2 14.3 %collective-permute-start.51 = (bf16[1,24,3200]{2,1,0:T(8,128)(2,1)S(1)}, bf16[1,24,3200]{2,1,0:T(8,128)(2,1)S(1)}, u32[]{:S(2)}, u32[]{:S(2)}) collective-permute-start(bf16[1,24,3200]{2,1,0:T(8,128)(2,1)S(1)} %get-tuple-element.260), channel_id=1, source_target_pairs={{0,16},{1,17},{2,18},{3,19},{4,20},{5,21},{6,22},{7,23},{8,24},{9,... | collective-permute-start | bytes 460808 | tf_op jit(solution)/shard_map/ppermute | solution.py:383
  335.7 13.9 %collective-permute-start.52 = (bf16[1,24,3200]{2,1,0:T(8,128)(2,1)S(1)}, bf16[1,24,3200]{2,1,0:T(8,128)(2,1)S(1)}, u32[]{:S(2)}, u32[]{:S(2)}) collective-permute-start(bf16[1,24,3200]{2,1,0:T(8,128)(2,1)S(1)} %get-tuple-element.259), channel_id=1, source_target_pairs={{0,24},{1,25},{2,26},{3,27},{4,28},{5,29},{6,30},{7,31},{8,16},{9,... | collective-permute-start | bytes 460808 | tf_op jit(solution)/shard_map/ppermute | solution.py:383
  338.3 15.3 %collective-permute-start.54 = (bf16[2,24,1024]{2,1,0:T(8,128)(2,1)S(1)}, bf16[2,24,1024]{2,1,0:T(8,128)(2,1)S(1)}, u32[]{:S(2)}, u32[]{:S(2)}) collective-permute-start(bf16[2,24,1024]{2,1,0:T(8,128)(2,1)S(1)} %pad_maximum_fusion.10), channel_id=1, source_target_pairs={{0,2},{1,3},{2,0},{3,1},{4,6},{5,7},{6,4},{7,5},{8,10},{9,11},{10,... | collective-permute-start | bytes 294920 | tf_op jit(solution)/shard_map/ppermute | solution.py:383
  (49 other events, 261.7 us)
